TPU v7x, 32 devices: a whole 2x2x4 slice. The times are simulated.
32 devices in a mesh: dp: 8 (over z, x), tp: 4 (over y, core).
Axes of the slice: x: 2, y: 2, z: 4, core: 2. Of those that a mesh axis runs over, the one named last changes fastest.
Arguments:
- tokens: bfloat16 [4096, 2048], P('dp'), may hold values from -6 to 6
- positions: int32 [4096], P('dp'), may hold values from 0 to 2047, as said below
- norm1_gain: float32 [2048], replicated, may hold values from 0.5 to 1.5
- w_query: bfloat16 [2048, 2048], P(None, 'tp'), may hold values from -0.125 to 0.125
- w_key: bfloat16 [2048, 256], P(None, 'tp'), may hold values from -0.125 to 0.125
- w_value: bfloat16 [2048, 256], P(None, 'tp'), may hold values from -0.125 to 0.125
- w_out: bfloat16 [2048, 2048], P('tp'), may hold values from -0.5 to 0.5
- norm2_gain: float32 [2048], replicated, may hold values from 0.5 to 1.5
- w_gate: bfloat16 [2048, 5632], P(None, 'tp'), may hold values from -0.125 to 0.125
- w_up: bfloat16 [2048, 5632], P(None, 'tp'), may hold values from -0.125 to 0.125
- w_down: bfloat16 [5632, 2048], P('tp'), may hold values from -0.078125 to 0.078125
- cotangent: bfloat16 [4096, 2048], P('dp'), may hold values from -6 to 6
Outputs:
- output: bfloat16 [4096, 2048], P(('dp', 'tp'))
- input_grad: float32 [4096, 2048], P(('dp', 'tp'))
- grad_norm1_gain: float32 [2048], P('dp')
- grad_query: float32 [2048, 2048], P('dp', 'tp')
- grad_key: float32 [2048, 256], P('dp', 'tp')
- grad_value: float32 [2048, 256], P('dp', 'tp')
- grad_out: float32 [2048, 2048], P('tp', 'dp')
- grad_norm2_gain: float32 [2048], P('dp')
- grad_gate: float32 [2048, 5632], P('dp', 'tp')
- grad_up: float32 [2048, 5632], P('dp', 'tp')
- grad_down: float32 [5632, 2048], P('tp', 'dp')
Inputs may be any that keep to these rules, and one draw needn't show every extreme that they name: Each packed sequence of 2048 tokens holds whole documents; positions count up by one from 0 within a document, a position of 0 starts a document. Every sequence starts with a document, and documents other than that first one start only within the sequence's last 512 tokens. The first sequence is a single document.
All inputs are finite; a program needn't handle non-finite values.
Results may differ from a plain program's by a relative error of at most 0.015.
Values may be sent and summed in bfloat16 or wider, within the bound.
No kernel may reach another device: no remote copies, remote signals or barrier semaphores. Data moves between devices by JAX's collectives and lax.ppermute only.
A program may use at most 320 MiB of HBM per device.

v0:
```python
import jax
import jax.numpy as jnp
from jax import lax
from jax.sharding import PartitionSpec as P

SPAN = 4


epsilon = 1e-05
far_below = -1e30


def shifted(block, axis, distance):
    devices = range(lax.axis_size(axis))
    route = [(i - distance, i) for i in devices if i - distance in devices]
    return lax.ppermute(block, axis, route)


def angle_tables(positions, head_size):
    halfway = head_size // 2
    frequency = jnp.exp(
        -jnp.log(10000.0) * (2.0 * jnp.arange(halfway, dtype=jnp.float32) / head_size)
    )
    angles = positions.astype(jnp.float32)[:, None] * frequency[None, :]
    return (
        jnp.concatenate([jnp.cos(angles), jnp.cos(angles)], -1),
        jnp.concatenate([jnp.sin(angles), jnp.sin(angles)], -1),
    )


def rotate(values, cosine, sine_table):
    middle_at = values.shape[-1] // 2
    turned = jnp.concatenate([-values[..., middle_at:], values[..., :middle_at]], -1)
    return values * cosine + turned * sine_table


def unrotate(grads, cosine, sine_table):
    middle_at = grads.shape[-1] // 2
    scaled = grads * sine_table
    turned = jnp.concatenate([scaled[..., middle_at:], -scaled[..., :middle_at]], -1)
    return grads * cosine + turned


def product(left, right):
    return jnp.dot(left, right, preferred_element_type=jnp.float32)


def contract_rows(left, right):
    return lax.dot_general(
        left, right, (((0,), (0,)), ((), ())), preferred_element_type=jnp.float32
    )


def contract_cols(left, right):
    return lax.dot_general(
        left, right, (((1,), (1,)), ((), ())), preferred_element_type=jnp.float32
    )


def norm_back(grad_rows, values, scale_rows, gain):
    scaled = grad_rows * gain
    inner_mean = jnp.mean(scaled * values, -1, keepdims=True)
    return (
        scale_rows * (scaled - values * scale_rows * scale_rows * inner_mean),
        jnp.sum(grad_rows * values * scale_rows, 0),
    )


def shards(
    tokens,
    positions,
    norm1_gain,
    w_query,
    w_key,
    w_value,
    w_out,
    norm2_gain,
    w_gate,
    w_up,
    w_down,
    cotangent,
):
    rows_here = tokens.shape[0]
    head_size = w_key.shape[1]
    head_count = w_query.shape[1] // head_size
    own_rows = rows_here // lax.axis_size("tp")
    own_start = lax.axis_index("tp") * own_rows
    ranking = lax.axis_index("dp") % SPAN
    block_rows = min(512, rows_here)
    block_count = rows_here // block_rows
    factor = head_size ** (-0.5)
    key_total_rows = SPAN * rows_here
    inputs = tokens.astype(jnp.float32)
    scale_one = lax.rsqrt(jnp.mean(inputs * inputs, -1, keepdims=True) + epsilon)
    normed_one = (inputs * scale_one * norm1_gain).astype(jnp.bfloat16)
    cosine, sine_table = angle_tables(positions, head_size)
    queries = product(normed_one, w_query).reshape(rows_here, head_count, head_size)
    queries = rotate(queries, cosine[:, None, :], sine_table[:, None, :]).astype(jnp.bfloat16)
    key_new = rotate(product(normed_one, w_key), cosine, sine_table).astype(jnp.bfloat16)
    value_new = product(normed_one, w_value).astype(jnp.bfloat16)
    paired = jnp.concatenate([key_new, value_new], 1)
    earlier_parts = []
    for distance in range(SPAN - 1, 0, -1):
        earlier_parts.append(shifted(paired, "dp", distance))
    key_value = jnp.concatenate(earlier_parts + [paired], 0)
    key_rows = key_value[:, :head_size]
    value_rows = key_value[:, head_size:]
    query_at = jnp.arange(rows_here, dtype=jnp.int32) + ranking * rows_here
    doc_start = query_at - positions
    key_at = jnp.arange(key_total_rows, dtype=jnp.int32) + (ranking - SPAN + 1) * rows_here

    def block_scores():
        allowed = (key_at[None, :] <= query_at[:, None]) & (key_at[None, :] >= doc_start[:, None])
        scores = (
            jnp.einsum("qhd,kd->qhk", queries, key_rows, preferred_element_type=jnp.float32)
            * factor
        )
        return (queries, jnp.where(allowed[:, None, :], scores, far_below))

    def forward_block(number):
        ignored, scores = block_scores()
        row_max = jnp.max(scores, -1, keepdims=True)
        weights = jnp.exp(scores - row_max)
        row_sum = jnp.sum(weights, -1, keepdims=True)
        probs_low = (weights / row_sum).astype(jnp.bfloat16)
        mixed = jnp.einsum("qhk,kd->qhd", probs_low, value_rows, preferred_element_type=jnp.float32)
        return (mixed, row_max, row_sum)

    mixed_all, row_maxes, row_sums = lax.map(forward_block, jnp.arange(block_count))
    attended = mixed_all.reshape(rows_here, head_count * head_size).astype(jnp.bfloat16)
    attn_term = product(attended, w_out)
    middle = inputs + lax.psum(attn_term, "tp")
    scale_two = lax.rsqrt(jnp.mean(middle * middle, -1, keepdims=True) + epsilon)
    normed_two = (middle * scale_two * norm2_gain).astype(jnp.bfloat16)
    middle_own = lax.dynamic_slice_in_dim(middle, own_start, own_rows, 0)
    gate_pre = product(normed_two, w_gate)
    up_pre = product(normed_two, w_up)
    sigma = jax.nn.sigmoid(gate_pre)
    active = gate_pre * sigma
    hidden = (active * up_pre).astype(jnp.bfloat16)
    down_term = product(hidden, w_down)
    ffn_own = lax.dynamic_slice_in_dim(
        lax.psum(down_term.astype(jnp.bfloat16), "tp").astype(jnp.float32), own_start, own_rows, 0
    )
    output_rows = (middle_own + ffn_own).astype(jnp.bfloat16)
    grad_down = contract_rows(hidden, cotangent)
    grad_hidden = contract_cols(cotangent, w_down)
    grad_gate_pre = (grad_hidden * up_pre * sigma * (1.0 + gate_pre * (1.0 - sigma))).astype(
        jnp.bfloat16
    )
    grad_up_pre = (grad_hidden * active).astype(jnp.bfloat16)
    grad_gate = contract_rows(normed_two, grad_gate_pre)
    grad_up = contract_rows(normed_two, grad_up_pre)
    normed_two_term = contract_cols(grad_gate_pre, w_gate) + contract_cols(grad_up_pre, w_up)
    grad_normed_two = lax.psum(normed_two_term, "tp")
    grad_mid_norm, gain_two_grad = norm_back(grad_normed_two, middle, scale_two, norm2_gain)
    grad_middle = cotangent.astype(jnp.float32) + grad_mid_norm
    branch_grad = grad_middle.astype(jnp.bfloat16)
    grad_middle_own = lax.dynamic_slice_in_dim(grad_middle, own_start, own_rows, 0)
    grad_out = contract_rows(attended, branch_grad)
    grad_mixed = (
        contract_cols(branch_grad, w_out)
        .astype(jnp.bfloat16)
        .reshape(rows_here, head_count, head_size)
    )

    def backward_block(carry, number):
        key_acc, value_acc = carry
        query_block, scores = block_scores()
        probs = jnp.exp(scores - row_maxes[number]) / row_sums[number]
        probs_low = probs.astype(jnp.bfloat16)
        grad_probs = jnp.einsum(
            "qhd,kd->qhk", grad_mixed, value_rows, preferred_element_type=jnp.float32
        )
        inner_sum = jnp.sum(probs * grad_probs, -1, keepdims=True)
        grad_scores = (probs * (grad_probs - inner_sum)).astype(jnp.bfloat16)
        grad_query_block = (
            jnp.einsum("qhk,kd->qhd", grad_scores, key_rows, preferred_element_type=jnp.float32)
            * factor
        )
        key_acc = (
            key_acc
            + jnp.einsum(
                "qhk,qhd->kd", grad_scores, query_block, preferred_element_type=jnp.float32
            )
            * factor
        )
        value_acc = value_acc + jnp.einsum(
            "qhk,qhd->kd", probs_low, grad_mixed, preferred_element_type=jnp.float32
        )
        return ((key_acc, value_acc), grad_query_block)

    zero_rows = jnp.zeros((key_total_rows, head_size), jnp.float32)
    (key_acc, value_acc), grad_queries = lax.scan(
        backward_block, (zero_rows, zero_rows), jnp.arange(block_count)
    )
    own_from = (SPAN - 1) * rows_here
    key_total = key_acc[own_from:]
    value_total = value_acc[own_from:]
    for distance in range(1, SPAN):
        begin_at = (SPAN - 1 - distance) * rows_here
        sending = jnp.concatenate(
            [key_acc[begin_at : begin_at + rows_here], value_acc[begin_at : begin_at + rows_here]],
            1,
        )
        returned = shifted(sending, "dp", -distance)
        key_total = key_total + returned[:, :head_size]
        value_total = value_total + returned[:, head_size:]
    key_grad = unrotate(key_total, cosine, sine_table).astype(jnp.bfloat16)
    value_grad = value_total.astype(jnp.bfloat16)
    query_grad = unrotate(
        grad_queries.reshape(rows_here, head_count, head_size),
        cosine[:, None, :],
        sine_table[:, None, :],
    )
    query_grad = query_grad.astype(jnp.bfloat16).reshape(rows_here, head_count * head_size)
    grad_query = contract_rows(normed_one, query_grad)
    grad_key = contract_rows(normed_one, key_grad)
    grad_value = contract_rows(normed_one, value_grad)
    normed_one_term = (
        contract_cols(query_grad, w_query)
        + contract_cols(key_grad, w_key)
        + contract_cols(value_grad, w_value)
    )
    grad_normed_one = lax.psum(normed_one_term, "tp")
    grad_in_norm, gain_one_grad = norm_back(grad_normed_one, inputs, scale_one, norm1_gain)
    grad_in_norm_own = lax.dynamic_slice_in_dim(grad_in_norm, own_start, own_rows, 0)
    input_rows = grad_middle_own + grad_in_norm_own
    summed = (
        lax.psum_scatter(gain_one_grad, "dp", scatter_dimension=0, tiled=True),
        lax.psum_scatter(grad_query, "dp", scatter_dimension=0, tiled=True),
        lax.psum_scatter(grad_key, "dp", scatter_dimension=0, tiled=True),
        lax.psum_scatter(grad_value, "dp", scatter_dimension=0, tiled=True),
        lax.psum_scatter(grad_out, "dp", scatter_dimension=1, tiled=True),
        lax.psum_scatter(gain_two_grad, "dp", scatter_dimension=0, tiled=True),
        lax.psum_scatter(grad_gate, "dp", scatter_dimension=0, tiled=True),
        lax.psum_scatter(grad_up, "dp", scatter_dimension=0, tiled=True),
        lax.psum_scatter(grad_down, "dp", scatter_dimension=1, tiled=True),
    )
    return (
        output_rows,
        input_rows,
        summed[0],
        summed[1],
        summed[2],
        summed[3],
        summed[4],
        summed[5],
        summed[6],
        summed[7],
        summed[8],
    )


def solution(mesh):
    placed = (
        P("dp", None),
        P("dp"),
        P(),
        P(None, "tp"),
        P(None, "tp"),
        P(None, "tp"),
        P("tp", None),
        P(),
        P(None, "tp"),
        P(None, "tp"),
        P("tp", None),
        P("dp", None),
    )
    return jax.shard_map(
        shards,
        mesh=mesh,
        in_specs=placed,
        out_specs=(
            P(("dp", "tp"), None),
            P(("dp", "tp"), None),
            P("dp"),
            P("dp", "tp"),
            P("dp", "tp"),
            P("dp", "tp"),
            P("tp", "dp"),
            P("dp"),
            P("dp", "tp"),
            P("dp", "tp"),
            P("tp", "dp"),
        ),
        check_vma=False,
    )
```

profile of v0, /device:TPU:0, one launch (start us, length us, event | category | flops | bytes accessed | tf_op | source)
XLA Modules:
  0.0 1429.0 jit_solution(7808374068309831273)
XLA Ops:
  7.3 2.2 fusion.9
  9.5 4.2 convert_multiply_fusion.2
  13.7 0.8 convolution_convert_fusion.2
  15.1 0.8 fusion.49
  16.2 4.9 collective-permute-start.2
  21.1 3.5 collective-permute-start.1
  24.6 5.1 collective-permute-start
  29.7 3.5 fusion.48
  33.3 1.9 compare_and_fusion
  35.6 1.1 maximum_maximum_fusion
  36.7 16.8 %fusion.47 = (f32[512,8]{0,1:T(8,128)S(1)}, f32[512,8,2048]{2,0,1:T(8,128)}) fusion(pred[512,2048]{1,0:T(8,128)(4,1)} %compare_and_fusion, bf16[512,8,64]{0,2,1:T(8,128)(2,1)S(1)} %fusion.27, bf16[2048,128]{0,1:T(8,128)(2,1)S(1)} %maximum_maximum_fusion), kind=kOutput, calls=%fused_computation.108 | convolution fusion | flops 1107298304 | bytes 35405824 | tf_op jit(solution)/shard_map/while/body/eval_jaxpr/sub | solution.py:123
  53.5 13.3 fusion.20
  66.8 0.8 copy-done.8
  67.6 3.3 fusion.50
  71.5 84.3 %all-reduce.8.cloned.1.call-done = f32[512,2048]{1,0:T(8,128)} async-done(((f32[512,2048]{1,0:T(8,128)}), f32[512,2048]{1,0:T(8,128)}) %all-reduce.8.cloned.1.call-update) | async-done | bytes 4194320 | tf_op jit(solution)/shard_map/psum | solution.py:132
  155.7 3.5 multiply_reduce_fusion.3
  159.7 10.0 fusion.52
  169.8 5.0 fusion.51
  174.8 8.0 multiply_convert_fusion.3
  182.8 4.9 fusion.53
  187.8 5.2 convolution_add_fusion
  193.2 85.6 %all-reduce.12.cloned.1.call-done = f32[512,2048]{1,0:T(8,128)} async-done(((f32[512,2048]{1,0:T(8,128)}), f32[512,2048]{1,0:T(8,128)}) %all-reduce.12.cloned.1.call-update) | async-done | bytes 4194320 | tf_op jit(solution)/shard_map/psum | solution.py:155
  278.8 5.2 multiply_reduce_fusion.1
  284.7 2.8 multiply_add_fusion
  287.5 2.0 copy-done.6
  289.6 1.3 convolution_convert_fusion.1
  290.9 12.3 fusion.16
  303.2 21.3 %multiply_reduce_fusion = (f32[512,8]{0,1:T(8,128)S(1)}, f32[512,8,2048]{2,0,1:T(8,128)}) fusion(f32[512,8,2048]{2,0,1:T(8,128)} %get-tuple-element.122, f32[512,8]{0,1:T(8,128)S(1)} %get-tuple-element.121, bf16[512,8,64]{0,2,1:T(8,128)(2,1)S(1)} %bitcast.92, bf16[2048,128]{0,1:T(8,128)(2,1)S(1)} %maximum_maximum_fusion), kind=kOutput, calls=%fused_computation.2 | convolution fusion | flops 1098903552 | bytes 67928064 | tf_op jit(solution)/shard_map/while/body/eval_jaxpr/qhd,kd->qhk/dot_general | solution.py:172
  324.5 27.6 %multiply_convert_fusion = bf16[512,8,2048]{2,0,1:T(8,128)(2,1)} fusion(f32[512,8,2048]{2,0,1:T(8,128)} %get-tuple-element.124, f32[512,8]{0,1:T(8,128)S(1)} %get-tuple-element.123, f32[512,8,2048]{2,0,1:T(8,128)} %get-tuple-element.122, f32[512,8]{0,1:T(8,128)S(1)} %get-tuple-element.121), kind=kLoop, calls=%fused_computation.1 | loop fusion | flops 33554432 | bytes 83918848 | tf_op jit(solution)/shard_map/while/body/eval_jaxpr/convert_element_type | solution.py:176
  352.2 8.9 fusion.19
  361.2 1.3 collective-permute-start.4
  362.5 1.3 collective-permute-start.5
  363.8 1.3 collective-permute-start.3
  365.1 7.4 convolution_convert_fusion
  373.1 4.4 collective-permute-done.5
  377.6 1.8 collective-permute-done.3
  379.3 1.0 fusion.39
  380.4 11.4 broadcast_multiply_fusion.1
  392.0 0.7 fusion.55
  393.6 1.3 fusion.54
  394.9 2.7 add_add_fusion
  397.7 1.5 copy-done.3
  399.2 1.3 fusion.60
  400.6 1.3 fusion.61
  401.9 5.5 fusion.29
  407.5 3.3 fusion.56
  410.8 1.6 copy-done.13
  412.8 6.2 fusion.58
  419.4 1.0 copy-done.34
  420.4 6.2 fusion.57
  426.7 1.5 copy-done.16
  428.6 6.0 fusion.59
  436.6 2.5 add_convert_fusion
  439.1 78.1 %all-reduce.14.cloned.1.call-done = f32[512,2048]{1,0:T(8,128)} async-done(((f32[512,2048]{1,0:T(8,128)}), f32[512,2048]{1,0:T(8,128)}) %all-reduce.14.cloned.1.call-update) | async-done | bytes 4194320 | tf_op jit(solution)/shard_map/psum | solution.py:225
  517.3 6.2 fusion.12
  523.5 37.2 %all-reduce.2 = (f32[2048]{0:T(1024)S(1)}, f32[2048]{0:T(1024)S(1)}) all-reduce(f32[2048]{0:T(1024)S(1)} %get-tuple-element.69, f32[2048]{0:T(1024)S(1)} %copy-done.27), channel_id=2, replica_groups=mesh['dp'=8,'tp'=4] {'dp'}, use_global_device_ids=true, to_apply=%region_12.13.clone | all-reduce | flops 4096 | bytes 32768
  562.0 3.1 fusion.24
  565.1 18.5 %reduce-scatter.10.cloned.1.call-done = f32[256,64]{0,1:T(8,128)} async-done(((f32[2048,64]{0,1:T(8,128)}), f32[256,64]{0,1:T(8,128)}) %reduce-scatter.10.cloned.1.call-update) | async-done | bytes 65552 | tf_op jit(solution)/shard_map/reduce_scatter | solution.py:232
  583.6 65.5 %reduce-scatter.12.cloned.1.call-done = f32[256,64]{0,1:T(8,128)} async-done(((f32[2048,64]{0,1:T(8,128)}), f32[256,64]{0,1:T(8,128)}) %reduce-scatter.12.cloned.1.call-update) | async-done | bytes 65552 | tf_op jit(solution)/shard_map/reduce_scatter | solution.py:233
  649.1 91.6 %reduce-scatter.14.cloned.1.call-done = f32[512,256]{1,0:T(8,128)} async-done(((f32[512,2048]{1,0:T(8,128)}), f32[512,256]{1,0:T(8,128)}) %reduce-scatter.14.cloned.1.call-update) | async-done | bytes 524304 | tf_op jit(solution)/shard_map/reduce_scatter | solution.py:234
  740.7 92.5 %reduce-scatter.8.cloned.1.call-done = f32[256,512]{1,0:T(8,128)} async-done(((f32[2048,512]{1,0:T(8,128)}), f32[256,512]{1,0:T(8,128)}) %reduce-scatter.8.cloned.1.call-update) | async-done | bytes 524304 | tf_op jit(solution)/shard_map/reduce_scatter | solution.py:231
  833.2 196.6 %reduce-scatter.18.cloned.1.call-done = f32[256,1408]{1,0:T(8,128)} async-done(((f32[2048,1408]{1,0:T(8,128)}), f32[256,1408]{1,0:T(8,128)}) %reduce-scatter.18.cloned.1.call-update) | async-done | bytes 1441808 | tf_op jit(solution)/shard_map/reduce_scatter | solution.py:237
  1029.8 195.8 %reduce-scatter.16.cloned.1.call-done = f32[256,1408]{1,0:T(8,128)} async-done(((f32[2048,1408]{1,0:T(8,128)}), f32[256,1408]{1,0:T(8,128)}) %reduce-scatter.16.cloned.1.call-update) | async-done | bytes 1441808 | tf_op jit(solution)/shard_map/reduce_scatter | solution.py:236
  1225.6 196.4 %reduce-scatter.20.cloned.1.call-done = f32[1408,256]{1,0:T(8,128)} async-done(((f32[1408,2048]{1,0:T(8,128)}), f32[1408,256]{1,0:T(8,128)}) %reduce-scatter.20.cloned.1.call-update) | async-done | bytes 1441808 | tf_op jit(solution)/shard_map/reduce_scatter | solution.py:238
  (138 shorter events, 9.2 us)
Async XLA Ops:
  7.2 60.4 %copy-start = (bf16[512,2048]{1,0:T(8,128)(2,1)S(1)}, bf16[512,2048]{1,0:T(8,128)(2,1)}, u32[]{:S(2)}) copy-start(bf16[512,2048]{1,0:T(8,128)(2,1)} %param.18) | copy-start | bytes 6291460
  7.2 148.5 %all-reduce.8.cloned.1.call-start = ((), (), s32[]{:S(2)}) async-start(), calls=%async_computation.7 | async-start | bytes 8388608 | tf_op jit(solution)/shard_map/psum | solution.py:132
  9.5 4.2 copy-start.28
  9.5 4.2 copy-start.19
  9.5 5.5 copy-start.17
  13.7 1.3 copy-start.2
  13.7 2.1 copy-start.30
  16.2 17.1 %copy-start.21 = (f32[512,32]{0,1:T(8,128)}, f32[512,32]{0,1:T(8,128)S(1)}, u32[]{:S(2)}) copy-start(f32[512,32]{0,1:T(8,128)S(1)} %get-tuple-element.118) | copy-start | bytes 196612
  16.2 17.1 %copy-start.23 = (f32[512,32]{0,1:T(8,128)}, f32[512,32]{0,1:T(8,128)S(1)}, u32[]{:S(2)}) copy-start(f32[512,32]{0,1:T(8,128)S(1)} %get-tuple-element.117) | copy-start | bytes 196612
  16.2 19.3 %collective-permute-start.2 = (bf16[512,128]{0,1:T(8,128)(2,1)S(1)}, bf16[512,128]{0,1:T(8,128)(2,1)S(1)}, u32[]{:S(2)}, u32[]{:S(2)}) collective-permute-start(bf16[512,128]{0,1:T(8,128)(2,1)S(1)} %pad_maximum_fusion.5), channel_id=1, source_target_pairs={{0,4},{4,8},{8,12},{12,16},{16,20},{20,24},{24,28},{1,5},{5,9},{9,... | collective-permute-start | bytes 393224 | tf_op jit(solution)/shard_map/ppermute | solution.py:16
  21.1 14.5 %collective-permute-start.1 = (bf16[512,128]{0,1:T(8,128)(2,1)S(1)}, bf16[512,128]{0,1:T(8,128)(2,1)S(1)}, u32[]{:S(2)}, u32[]{:S(2)}) collective-permute-start(bf16[512,128]{0,1:T(8,128)(2,1)S(1)} %pad_maximum_fusion.5), channel_id=1, source_target_pairs={{0,8},{4,12},{8,16},{12,20},{16,24},{20,28},{1,9},{5,13},{9,17},{1... | collective-permute-start | bytes 393224 | tf_op jit(solution)/shard_map/ppermute | solution.py:16
  24.6 11.0 collective-permute-start
  35.5 18.0 %copy-start.10 = (bf16[512,8,64]{0,2,1:T(8,128)(2,1)}, bf16[512,8,64]{0,2,1:T(8,128)(2,1)S(1)}, u32[]{:S(2)}) copy-start(bf16[512,8,64]{0,2,1:T(8,128)(2,1)S(1)} %fusion.27) | copy-start | bytes 1572868
  66.8 0.8 copy-start.8
  70.9 88.3 %copy-start.25 = (f32[2048]{0:T(1024)S(1)}, f32[2048]{0:T(1024)}, u32[]{:S(2)}) copy-start(f32[2048]{0:T(1024)} %param.19) | copy-start | bytes 24580
  70.9 207.8 %all-reduce.12.cloned.1.call-start = ((), (), s32[]{:S(2)}) async-start(), calls=%async_computation.9 | async-start | bytes 8388608 | tf_op jit(solution)/shard_map/psum | solution.py:155
  159.2 10.5 copy-start.4
  159.2 10.5 slice-start
  159.7 10.1 copy-start.12
  159.7 10.1 slice-start.1
  159.7 15.1 %slice-start.4 = ((s8[5767168]{0:T(1024)(128)(4,1)}), s8[4194304]{0:T(1024)(128)(4,1)S(1)}, s32[]{:S(2)}) async-start(s8[5767168]{0:T(1024)(128)(4,1)} %bitcast.89), calls=%async_computation.22 | async-start | bytes 8388608
  169.8 5.0 copy-start.15
  169.8 5.0 slice-start.5
  169.8 18.0 %slice-start.2 = ((s8[5767168]{0:T(1024)(128)(4,1)}), s8[4194304]{0:T(1024)(128)(4,1)S(1)}, s32[]{:S(2)}) async-start(s8[5767168]{0:T(1024)(128)(4,1)} %bitcast.87), calls=%async_computation.20 | async-start | bytes 8388608
  174.8 13.0 slice-start.3
  182.8 5.0 copy-start.35
  193.0 243.6 %all-reduce.10.cloned.1.call-start = ((), (), s32[]{:S(2)}) async-start(), calls=%async_computation.8 | async-start | bytes 4194304 | tf_op jit(solution)/shard_map/psum | solution.py:143
  278.8 5.3 copy-start.5
  278.8 5.9 copy-start.7
  287.5 2.1 copy-start.6
  324.5 27.7 %copy-start.11 = (bf16[512,8,64]{0,2,1:T(8,128)(2,1)S(1)}, bf16[512,8,64]{0,2,1:T(8,128)(2,1)}, u32[]{:S(2)}) copy-start(bf16[512,8,64]{0,2,1:T(8,128)(2,1)} %copy-done.10) | copy-start | bytes 1572868
  352.2 12.9 copy-start.32
  361.2 12.0 collective-permute-start.4
  362.5 15.1 %collective-permute-start.5 = (f32[512,128]{0,1:T(8,128)S(1)}, f32[512,128]{0,1:T(8,128)S(1)}, u32[]{:S(2)}, u32[]{:S(2)}) collective-permute-start(f32[512,128]{0,1:T(8,128)S(1)} %pad_maximum_fusion.2), channel_id=1, source_target_pairs={{12,0},{16,4},{20,8},{24,12},{28,16},{13,1},{17,5},{21,9},{25,13},... | collective-permute-start | bytes 786440 | tf_op jit(solution)/shard_map/ppermute | solution.py:16
  363.8 15.5 %collective-permute-start.3 = (f32[512,128]{0,1:T(8,128)S(1)}, f32[512,128]{0,1:T(8,128)}, u32[]{:S(2)}, u32[]{:S(2)}) collective-permute-start(f32[512,128]{0,1:T(8,128)S(1)} %pad_maximum_fusion), channel_id=1, source_target_pairs={{4,0},{8,4},{12,8},{16,12},{20,16},{24,20},{28,24},{5,1},{9,5},{13... | collective-permute-start | bytes 786440 | tf_op jit(solution)/shard_map/ppermute | solution.py:16
  365.1 14.2 copy-start.22
  372.6 144.7 %all-reduce.14.cloned.1.call-start = ((), (), s32[]{:S(2)}) async-start(), calls=%async_computation.10 | async-start | bytes 8388608 | tf_op jit(solution)/shard_map/psum | solution.py:225
  380.4 11.6 copy-start.24
  380.4 11.6 copy-start.18
  392.0 1.6 copy-start.14
  393.6 1.3 copy-start.20
  397.6 1.6 copy-start.3
  397.6 4.3 copy-start.9
  397.6 185.9 %reduce-scatter.10.cloned.1.call-start = ((), (), s32[]{:S(2)}) async-start(), calls=%async_computation.12 | async-start | bytes 589824 | tf_op jit(solution)/shard_map/reduce_scatter | solution.py:232
  400.5 248.6 %reduce-scatter.12.cloned.1.call-start = ((), (), s32[]{:S(2)}) async-start(), calls=%async_computation.13 | async-start | bytes 589824 | tf_op jit(solution)/shard_map/reduce_scatter | solution.py:233
  401.9 338.8 %reduce-scatter.14.cloned.1.call-start = ((), (), s32[]{:S(2)}) async-start(), calls=%async_computation.14 | async-start | bytes 4718592 | tf_op jit(solution)/shard_map/reduce_scatter | solution.py:234
  407.4 425.8 %reduce-scatter.8.cloned.1.call-start = ((), (), s32[]{:S(2)}) async-start(), calls=%async_computation.11 | async-start | bytes 4718592 | tf_op jit(solution)/shard_map/reduce_scatter | solution.py:231
  410.7 1.7 copy-start.13
  410.7 2.1 copy-start.36
  410.8 619.0 %reduce-scatter.18.cloned.1.call-start = ((), (), s32[]{:S(2)}) async-start(), calls=%async_computation.16 | async-start | bytes 12976128 | tf_op jit(solution)/shard_map/reduce_scatter | solution.py:237
  419.1 1.4 copy-start.34
  419.1 806.5 %reduce-scatter.16.cloned.1.call-start = ((), (), s32[]{:S(2)}) async-start(), calls=%async_computation.15 | async-start | bytes 12976128 | tf_op jit(solution)/shard_map/reduce_scatter | solution.py:236
  426.6 1.6 copy-start.16
  426.6 2.0 copy-start.33
  426.6 995.4 %reduce-scatter.20.cloned.1.call-start = ((), (), s32[]{:S(2)}) async-start(), calls=%async_computation.17 | async-start | bytes 12976128 | tf_op jit(solution)/shard_map/reduce_scatter | solution.py:238
  434.6 0.7 copy-start.29
  434.6 0.8 copy-start.31
  434.6 82.7 %copy-start.26 = (f32[2048]{0:T(1024)S(1)}, f32[2048]{0:T(1024)}, u32[]{:S(2)}) copy-start(f32[2048]{0:T(1024)} %param.14) | copy-start | bytes 24580
  439.1 84.4 %copy-start.27 = (f32[2048]{0:T(1024)S(1)}, f32[2048]{0:T(1024)}, u32[]{:S(2)}) copy-start(f32[2048]{0:T(1024)} %get-tuple-element.67) | copy-start | bytes 24580
  517.3 904.7 %copy-start.1 = (bf16[512,2048]{1,0:T(8,128)(2,1)S(1)}, bf16[512,2048]{1,0:T(8,128)(2,1)}, u32[]{:S(2)}) copy-start(bf16[512,2048]{1,0:T(8,128)(2,1)} %param.18) | copy-start | bytes 6291460
Sparse Core Ops, SparseCore 0:
  71.0 84.6 all-reduce.7
  193.1 85.6 all-reduce.11
  372.7 56.5 all-reduce.9
  431.7 85.5 all-reduce.13
  521.0 62.4 reduce-scatter.9
  587.7 61.3 reduce-scatter.11
  653.3 87.3 reduce-scatter.13
  745.3 87.8 reduce-scatter.7
  837.3 192.3 reduce-scatter.17
  1033.8 191.7 reduce-scatter.15
  1229.8 192.1 reduce-scatter.19
where the time goes:
time: 1440 us; the launch traced here: 1430 us
  waiting for transfers between devices  1110 us (77%)
  matrix products  169 us (12%)
  other arithmetic  63.2 us (4%)
  blocking collectives  37.2 us (3%)
  starting transfers between devices  18.9 us (1%)
  between operations  15.6 us (1%)
    reduce_scatter x1, waiting for transfers between devices, shards(): lax.psum_scatter(grad_up, 'dp', scatter_dimension=0, tiled=True)  197 us
    reduce_scatter x1, waiting for transfers between devices, shards(): lax.psum_scatter(grad_down, 'dp', scatter_dimension=1, tiled=True)  196 us
    reduce_scatter x1, waiting for transfers between devices, shards(): lax.psum_scatter(grad_gate, 'dp', scatter_dimension=0, tiled=True)  196 us
    reduce_scatter x1, waiting for transfers between devices, shards(): lax.psum_scatter(grad_query, 'dp', scatter_dimension=0, tiled=True)  92.5 us
    reduce_scatter x1, waiting for transfers between devices, shards(): lax.psum_scatter(grad_out, 'dp', scatter_dimension=1, tiled=True)  91.6 us
    psum x1, waiting for transfers between devices, shards(): grad_normed_two = lax.psum(normed_two_term, 'tp')  85.6 us
    psum x1, waiting for transfers between devices, shards(): middle = inputs + lax.psum(attn_term, 'tp')  84.3 us
    psum x1, waiting for transfers between devices, shards(): grad_normed_one = lax.psum(normed_one_term, 'tp')  78.1 us
  transfers between devices with their start and end apart: 17, of which 13 were waited for; matrix products, arithmetic and copies ran while one was open for 5% of the time, Pallas kernels for 0%

commit v1 on v0

v1 whole, which is shorter than its diff:
```python
import functools

import jax
import jax.numpy as jnp
from jax import lax
from jax.experimental import pallas as pl
from jax.experimental.pallas import tpu as pltpu
from jax.sharding import PartitionSpec as P

SPAN = 4
EPSILON = 1e-05
FAR_BELOW = -1e30
LOW = jnp.bfloat16
ROW_MASKS = (0, 2, 1, 3)


def flip(block, axis, mask):
    return lax.ppermute(block, axis, [(i, i ^ mask) for i in range(lax.axis_size(axis))])


def dot(left, right, left_dim, right_dim):
    return lax.dot_general(
        left,
        right,
        (((left_dim,), (right_dim,)), ((), ())),
        preferred_element_type=jnp.float32,
    )


def own_mask(pos, begin, keys, queries):
    key_at = lax.broadcasted_iota(jnp.int32, (keys, queries), 0)
    query_at = lax.broadcasted_iota(jnp.int32, (keys, queries), 1) + begin
    return (key_at <= query_at) & (key_at >= query_at - pos)


def forward_kernel(
    heads, size, rank_ref, pos_ref, q_ref, kv0, kv1, kv2, kv3, o_ref, lse_ref, keys, vals, top, acc
):
    rank = rank_ref[0]
    rows = pos_ref.shape[1]
    half = rows // 2

    @pl.when(pl.program_id(0) == 0)
    def _():
        for m, kv in enumerate((kv0, kv1, kv2, kv3)):
            keys[m] = kv[:size, :].T
            vals[m, :size, :] = kv[size:, :]
            vals[m, size:, :] = jnp.ones((16, rows), LOW)

    pos = pos_ref[...]
    for part in range(2):
        cols = slice(part * half, (part + 1) * half)
        count = (part + 1) * half
        mask = own_mask(pos[:, cols], part * half, count, half)
        for h in range(heads):
            scores = dot(keys[0, :count, :], q_ref[h * size : (h + 1) * size, cols], 1, 0)
            scores = jnp.where(mask, scores, FAR_BELOW)
            peak = jnp.max(scores, 0, keepdims=True)
            weights = jnp.exp(scores - peak).astype(LOW)
            acc[h, :, cols] = dot(vals[0, :, :count], weights, 1, 0)
            top[h, :, cols] = peak
    seen = pos > lax.broadcasted_iota(jnp.int32, (1, rows), 1)
    for m in range(1, SPAN):

        @pl.when((rank ^ m) < rank)
        def _():
            for h in range(heads):
                scores = dot(keys[m], q_ref[h * size : (h + 1) * size, :], 1, 0)
                old = top[h]
                peak = jnp.where(seen, jnp.maximum(old, jnp.max(scores, 0, keepdims=True)), old)
                weights = jnp.exp(scores - jnp.where(seen, peak, -FAR_BELOW)).astype(LOW)
                acc[h] = acc[h] * jnp.exp(old - peak) + dot(vals[m], weights, 1, 0)
                top[h] = peak

    for h in range(heads):
        total = acc[h, size : size + 1, :]
        o_ref[h * size : (h + 1) * size, :] = (acc[h, :size, :] / total).astype(LOW)
        lse_ref[h] = top[h] + jnp.log(total)


def backward_kernel(
    heads,
    size,
    rank_ref,
    pos_ref,
    q_ref,
    do_ref,
    o_ref,
    lse_ref,
    cos_ref,
    sin_ref,
    kv0,
    kv1,
    kv2,
    kv3,
    dq_ref,
    g0,
    g1,
    g2,
    g3,
    keys,
    vals,
    dq,
    total,
):
    rank = rank_ref[0]
    rows = pos_ref.shape[1]
    half = rows // 2
    blocks = (kv0, kv1, kv2, kv3)
    step = pl.program_id(0)

    @pl.when(step == 0)
    def _():
        for m, kv in enumerate(blocks):
            keys[m] = kv[:size, :].T
            vals[m] = kv[size:, :].T
        total[...] = jnp.zeros_like(total)

    pos = pos_ref[...]
    seen = pos > lax.broadcasted_iota(jnp.int32, (1, rows), 1)
    deltas = []
    for h in range(heads):
        span = slice(h * size, (h + 1) * size)
        deltas.append(
            jnp.sum(
                do_ref[span, :].astype(jnp.float32) * o_ref[span, :].astype(jnp.float32),
                0,
                keepdims=True,
            )
        )
    for part in range(2):
        cols = slice(part * half, (part + 1) * half)
        count = (part + 1) * half
        mask = own_mask(pos[:, cols], part * half, count, half)
        for h in range(heads):
            span = slice(h * size, (h + 1) * size)
            query, grad = q_ref[span, cols], do_ref[span, cols]
            scores = dot(keys[0, :count, :], query, 1, 0)
            probs = jnp.exp(jnp.where(mask, scores, FAR_BELOW) - lse_ref[h, :, cols])
            grad_probs = dot(vals[0, :count, :], grad, 1, 0)
            grad_scores = (probs * (grad_probs - deltas[h][:, cols])).astype(LOW)
            total[0, :size, :count] += dot(query, grad_scores, 1, 1)
            total[0, size:, :count] += dot(grad, probs.astype(LOW), 1, 1)
            dq[h, :, cols] = dot(kv0[:size, :count], grad_scores, 1, 0)
    for m in range(1, SPAN):

        @pl.when((rank ^ m) < rank)
        def _():
            for h in range(heads):
                span = slice(h * size, (h + 1) * size)
                query, grad = q_ref[span, :], do_ref[span, :]
                scores = dot(keys[m], query, 1, 0)
                probs = jnp.exp(scores - jnp.where(seen, lse_ref[h], -FAR_BELOW))
                grad_probs = dot(vals[m], grad, 1, 0)
                grad_scores = (probs * (grad_probs - deltas[h])).astype(LOW)
                total[m, :size, :] += dot(query, grad_scores, 1, 1)
                total[m, size:, :] += dot(grad, probs.astype(LOW), 1, 1)
                dq[h] += dot(blocks[m][:size, :], grad_scores, 1, 0)

    middle_at = size // 2
    cosine, sine = cos_ref[...], sin_ref[...]
    for h in range(heads):
        first = dq[h, :middle_at, :] * size ** (-0.5)
        second = dq[h, middle_at:, :] * size ** (-0.5)
        base = h * size
        dq_ref[base : base + middle_at, :] = (first * cosine + second * sine).astype(LOW)
        dq_ref[base + middle_at : base + size, :] = (second * cosine - first * sine).astype(LOW)

    @pl.when(step == pl.num_programs(0) - 1)
    def _():
        g0[...] = total[0]
        for m, out in ((1, g1), (2, g2), (3, g3)):
            out[...] = total[m].astype(LOW)


def attention_forward(rank, pos, queries, blocks, size, heads):
    wide, rows = queries.shape
    count = wide // size
    whole = pl.BlockSpec((2 * size, rows), lambda i, r: (0, 0))
    some = pl.BlockSpec((heads * size, rows), lambda i, r: (i, 0))
    return pl.pallas_call(
        functools.partial(forward_kernel, heads, size),
        out_shape=(
            jax.ShapeDtypeStruct((wide, rows), LOW),
            jax.ShapeDtypeStruct((count, 1, rows), jnp.float32),
        ),
        grid_spec=pltpu.PrefetchScalarGridSpec(
            num_scalar_prefetch=1,
            grid=(count // heads,),
            in_specs=[pl.BlockSpec((1, rows), lambda i, r: (0, 0)), some] + [whole] * SPAN,
            out_specs=[some, pl.BlockSpec((heads, 1, rows), lambda i, r: (i, 0, 0))],
            scratch_shapes=[
                pltpu.VMEM((SPAN, rows, size), LOW),
                pltpu.VMEM((SPAN, size + 16, rows), LOW),
                pltpu.VMEM((heads, 1, rows), jnp.float32),
                pltpu.VMEM((heads, size + 16, rows), jnp.float32),
            ],
        ),
        compiler_params=pltpu.CompilerParams(vmem_limit_bytes=48 << 20),
        cost_estimate=pl.CostEstimate(
            flops=16 * wide * rows * rows * SPAN // 2,
            bytes_accessed=4 * wide * rows,
            transcendentals=count * rows * rows * SPAN,
        ),
        name="attention_forward",
    )(rank, pos, queries, *blocks)


def attention_backward(rank, pos, queries, grads, attended, lse, cosine, sine, blocks, size, heads):
    wide, rows = queries.shape
    count = wide // size
    whole = pl.BlockSpec((2 * size, rows), lambda i, r: (0, 0))
    table = pl.BlockSpec((size // 2, rows), lambda i, r: (0, 0))
    some = pl.BlockSpec((heads * size, rows), lambda i, r: (i, 0))
    return pl.pallas_call(
        functools.partial(backward_kernel, heads, size),
        out_shape=(
            jax.ShapeDtypeStruct((wide, rows), LOW),
            jax.ShapeDtypeStruct((2 * size, rows), jnp.float32),
        )
        + (jax.ShapeDtypeStruct((2 * size, rows), LOW),) * (SPAN - 1),
        grid_spec=pltpu.PrefetchScalarGridSpec(
            num_scalar_prefetch=1,
            grid=(count // heads,),
            in_specs=[
                pl.BlockSpec((1, rows), lambda i, r: (0, 0)),
                some,
                some,
                some,
                pl.BlockSpec((heads, 1, rows), lambda i, r: (i, 0, 0)),
                table,
                table,
            ]
            + [whole] * SPAN,
            out_specs=[some] + [whole] * SPAN,
            scratch_shapes=[
                pltpu.VMEM((SPAN, rows, size), LOW),
                pltpu.VMEM((SPAN, rows, size), LOW),
                pltpu.VMEM((heads, size, rows), jnp.float32),
                pltpu.VMEM((SPAN, 2 * size, rows), jnp.float32),
            ],
        ),
        compiler_params=pltpu.CompilerParams(vmem_limit_bytes=48 << 20),
        cost_estimate=pl.CostEstimate(
            flops=40 * wide * rows * rows * SPAN // 2,
            bytes_accessed=10 * wide * rows,
            transcendentals=count * rows * rows * SPAN,
        ),
        name="attention_backward",
    )(rank, pos, queries, grads, attended, lse, cosine, sine, *blocks)


def block_order(bits, first):
    used = list(range(first, bits))
    count = 1 << len(used)
    return [
        sum(((j >> (len(used) - 1 - k)) & 1) << b for k, b in enumerate(used)) for j in range(count)
    ]


def pick(values, masks, place, blocks, dim):
    size = values.shape[dim] // blocks
    return jnp.concatenate(
        [lax.dynamic_slice_in_dim(values, (place ^ m) * size, size, dim) for m in masks], dim
    )


def exchange_sum(part, count, bits, first, dim):
    got = []
    size = None
    for bit in range(first, bits):
        lo = count // 2
        send = part(lo, count)
        size = send.shape[dim] // (count - lo)
        for other in got:
            send = send + lax.slice_in_dim(other, lo * size, count * size, axis=dim)
        got.append(flip(send.astype(LOW), "dp", 1 << bit))
        count = lo
    total = part(0, 1)
    for other in got:
        total = total + lax.slice_in_dim(other, 0, total.shape[dim], axis=dim)
    return total


def pair_terms(pairs, size, left_first):
    def part(lo, hi):
        total = None
        for x, g in pairs:
            cut = x[:, lo * size : hi * size]
            term = dot(cut, g, 0, 0) if left_first else dot(g, cut, 0, 0)
            total = term if total is None else total + term
        return total

    return part


def turn(values, cosine, sine):
    half = cosine.shape[0]
    heads = values.shape[0] // (2 * half)
    pieces = values.reshape(heads, 2, half, values.shape[1])
    first, second = pieces[:, 0], pieces[:, 1]
    return jnp.stack(
        [first * cosine - second * sine, second * cosine + first * sine], 1
    ).reshape(values.shape)


def turn_back(grads, cosine, sine):
    return turn(grads, cosine, -sine)


def norm_back(grad_rows, values, scale_rows, gain):
    scaled = grad_rows * gain
    inner_mean = jnp.mean(scaled * values, -1, keepdims=True)
    return (
        scale_rows * (scaled - values * scale_rows * scale_rows * inner_mean),
        jnp.sum(grad_rows * values * scale_rows, 0),
    )


def shards(
    tokens,
    positions,
    norm1_gain,
    w_query,
    w_key,
    w_value,
    w_out,
    norm2_gain,
    w_gate,
    w_up,
    w_down,
    cotangent,
):
    rows_here, width = tokens.shape
    size = w_key.shape[1]
    dp = lax.axis_size("dp")
    bits = dp.bit_length() - 1
    place = lax.axis_index("dp")
    spot = lax.axis_index("tp")
    tp_masks = range(lax.axis_size("tp"))
    own_rows = rows_here // lax.axis_size("tp")
    block = width // dp
    rank = (place % SPAN).astype(jnp.int32).reshape(1)
    pos = positions.reshape(1, rows_here)

    def own(values):
        return lax.dynamic_slice_in_dim(values, spot * own_rows, own_rows, 0)

    inputs = tokens.astype(jnp.float32)
    scale_one = lax.rsqrt(jnp.mean(inputs * inputs, -1, keepdims=True) + EPSILON)
    normed_one = (inputs * scale_one * norm1_gain).astype(LOW)
    half = size // 2
    frequency = jnp.exp(
        -jnp.log(10000.0) * (2.0 * jnp.arange(half, dtype=jnp.float32) / size)
    )
    angles = frequency[:, None] * positions.astype(jnp.float32)[None, :]
    cosine, sine = jnp.cos(angles), jnp.sin(angles)
    key_new = turn(dot(w_key, normed_one, 0, 1), cosine, sine)
    value_new = dot(w_value, normed_one, 0, 1)
    paired = jnp.concatenate([key_new, value_new], 0).astype(LOW)
    blocks = [paired] + [flip(paired, "dp", m) for m in range(1, SPAN)]
    queries = (turn(dot(w_query, normed_one, 0, 1), cosine, sine) * size ** (-0.5)).astype(LOW)

    out_core = flip(w_out, "tp", 1)
    out_far = flip(w_out, "tp", 2)
    outs = [w_out, out_core, out_far, flip(out_far, "tp", 1)]

    attended, lse = attention_forward(rank, pos, queries, blocks, size, 2)

    def token_block(values, mask):
        return lax.dynamic_slice_in_dim(values, (spot ^ mask) * own_rows, own_rows, 1)

    att_pieces = [token_block(attended, m) for m in tp_masks]
    att_mine = [att_pieces[0]] + [flip(att_pieces[m], "tp", m) for m in tp_masks if m]
    branch = sum(dot(a, w, 0, 0) for a, w in zip(att_mine, outs))

    middle = own(inputs) + branch
    scale_two = lax.rsqrt(jnp.mean(middle * middle, -1, keepdims=True) + EPSILON)

    def all_rows(mine):
        pair = jnp.concatenate([mine, flip(mine, "tp", 2)], 0)
        return jnp.concatenate([pair, flip(pair, "tp", 1)], 0)

    def sum_rows(part):
        near = flip(part(2, 4).astype(LOW), "tp", 1)
        pair = part(0, 2) + near
        return pair[:own_rows] + flip(pair[own_rows:].astype(LOW), "tp", 2)

    normed_two = all_rows((middle * scale_two * norm2_gain).astype(LOW))
    gate_pre = dot(normed_two, w_gate, 1, 0)
    up_pre = dot(normed_two, w_up, 1, 0)
    cot = pick(cotangent, ROW_MASKS, spot, len(tp_masks), 0)
    grad_hidden = dot(cot, w_down, 1, 1)
    sigma = jax.nn.sigmoid(gate_pre)
    active = gate_pre * sigma
    hidden = (active * up_pre).astype(LOW)
    grad_gate_pre = (grad_hidden * up_pre * sigma * (1.0 + gate_pre * (1.0 - sigma))).astype(LOW)
    grad_up_pre = (grad_hidden * active).astype(LOW)

    def rows_of(values, lo, hi):
        return values[lo * own_rows : hi * own_rows]

    grad_normed_two = sum_rows(
        lambda lo, hi: dot(rows_of(grad_gate_pre, lo, hi), w_gate, 1, 1)
        + dot(rows_of(grad_up_pre, lo, hi), w_up, 1, 1)
    )
    down = sum_rows(lambda lo, hi: dot(rows_of(hidden, lo, hi), w_down, 1, 0))
    output_rows = (middle + down).astype(LOW)

    half_order = block_order(bits, 1)
    half_count = len(half_order)

    def gathered(x, grads, left_first=True):
        mine = pick(x, half_order, place, dp, 1)
        theirs = flip(pick(x, half_order, place ^ 1, dp, 1), "dp", 1)
        return [
            exchange_sum(
                pair_terms([(mine, g), (theirs, flip(g, "dp", 1))], block, left_first),
                half_count,
                bits,
                1,
                0 if left_first else 1,
            )
            for g in grads
        ]

    (grad_down,) = gathered(cot, [hidden], False)
    grad_gate, grad_up = gathered(normed_two, [grad_gate_pre, grad_up_pre])

    grad_mid_norm, gain_two = norm_back(grad_normed_two, middle, scale_two, norm2_gain)
    grad_middle = own(cotangent).astype(jnp.float32) + grad_mid_norm
    branch_grad = grad_middle.astype(LOW)
    grad_pieces = [dot(w, branch_grad, 1, 1).astype(LOW) for w in outs]
    grad_mine = [grad_pieces[0]] + [flip(grad_pieces[m], "tp", m) for m in tp_masks if m]
    ordered = jnp.zeros(attended.shape, LOW)
    for m in tp_masks:
        ordered = lax.dynamic_update_slice_in_dim(
            ordered, grad_mine[m], (spot ^ m) * own_rows, 1
        )
    grads = attention_backward(
        rank, pos, queries, ordered, attended, lse, cosine, sine, blocks, size, 2
    )
    grad_query_rows, kv_total = grads[0], grads[1]

    branch_all = pick(all_rows(branch_grad), block_order(bits, 0), place, dp, 1)
    att_all = jnp.concatenate([att_pieces[m] for m in ROW_MASKS], 1)
    grad_out = exchange_sum(
        lambda lo, hi: dot(att_all, branch_all[:, lo * block : hi * block], 1, 0),
        dp,
        bits,
        0,
        1,
    )

    for m in range(1, SPAN):
        kv_total = kv_total + flip(grads[m + 1], "dp", m)
    key_grad = turn_back(kv_total[:size], cosine, sine)
    grad_kv_rows = jnp.concatenate([key_grad, kv_total[size:]], 0).astype(LOW)

    query_core = flip(w_query, "tp", 1)
    query_far = flip(w_query, "tp", 2)
    query_all = [w_query, query_core, query_far, flip(query_far, "tp", 1)]
    w_kv = jnp.concatenate([w_key, w_value], 1)
    kv_far = flip(w_kv, "tp", 2)
    kv_all = [w_kv, flip(w_kv, "tp", 1), kv_far, flip(kv_far, "tp", 1)]
    grad_normed_one = None
    for m in tp_masks:
        piece_q = token_block(grad_query_rows, m)
        piece_kv = token_block(grad_kv_rows, m)
        if m:
            piece_q, piece_kv = flip(piece_q, "tp", m), flip(piece_kv, "tp", m)
        term = dot(piece_q, query_all[m], 0, 1) + dot(piece_kv, kv_all[m], 0, 1)
        grad_normed_one = term if grad_normed_one is None else grad_normed_one + term
    grad_in_norm, gain_one = norm_back(
        grad_normed_one, own(inputs), own(scale_one), norm1_gain
    )
    input_rows = grad_middle + grad_in_norm

    grad_rows = jnp.concatenate([grad_query_rows, grad_kv_rows], 0).T
    (grad_proj,) = gathered(normed_one, [grad_rows])
    wide = w_query.shape[1]

    gains = pick(jnp.stack([gain_one, gain_two]), block_order(bits, 0), place, dp, 1)
    for m in (1, 2):
        gains = gains + flip(gains, "tp", m)
    count = dp
    for bit in range(bits):
        count //= 2
        gains = gains[:, : count * block] + flip(gains[:, count * block :], "dp", 1 << bit)

    return (
        output_rows,
        input_rows,
        gains[0],
        grad_proj[:, :wide],
        grad_proj[:, wide : wide + size],
        grad_proj[:, wide + size :],
        grad_out,
        gains[1],
        grad_gate,
        grad_up,
        grad_down,
    )


def solution(mesh):
    placed = (
        P("dp", None),
        P("dp"),
        P(),
        P(None, "tp"),
        P(None, "tp"),
        P(None, "tp"),
        P("tp", None),
        P(),
        P(None, "tp"),
        P(None, "tp"),
        P("tp", None),
        P("dp", None),
    )
    return jax.shard_map(
        shards,
        mesh=mesh,
        in_specs=placed,
        out_specs=(
            P(("dp", "tp"), None),
            P(("dp", "tp"), None),
            P("dp"),
            P("dp", "tp"),
            P("dp", "tp"),
            P("dp", "tp"),
            P("tp", "dp"),
            P("dp"),
            P("dp", "tp"),
            P("dp", "tp"),
            P("tp", "dp"),
        ),
        check_vma=False,
    )
```

time: 1440 us -> 581 us (0.40)
  waiting for transfers between devices: 1110 us -> 317 us
  starting transfers between devices: 18.9 us -> 86.2 us
  matrix products: 169 us -> 124 us
  other arithmetic: 63.2 us -> 18.2 us
  blocking collectives: 37.2 us -> 0 us
    reduce_scatter x7 -> x0, waiting for transfers between devices: 857 us -> none  [the longest x1 197 us: shards(): lax.psum_scatter(grad_up, 'dp', scatter_dimension=0, tiled=True)]
    ppermute x6 -> x58, waiting for transfers between devices: 6.49 us -> 317 us  [flip(): lax.ppermute(block, axis, [(i, i ^ mask) for i in range(lax.axis_size(axi...]
    psum x4 -> x0, waiting for transfers between devices: 248 us -> none  [the longest x1 85.6 us: shards(): grad_normed_two = lax.psum(normed_two_term, 'tp')]
    ppermute x6 -> x58, starting transfers between devices: 17.3 us -> 86.2 us  [flip(): lax.ppermute(block, axis, [(i, i ^ mask) for i in range(lax.axis_size(axi...]
    unnamed x1 -> x0, blocking collectives: 37.2 us -> none
    dot_general x26 -> x56, matrix products: 152 us -> 124 us  [dot(): lax.dot_general(left, right, (((left_dim,), (right_dim,)), ((), ())), pre...]
    convert_element_type x6, other arithmetic: 31.2 us -> 5.5 us  [the longest x1 2.47 us: shards(): inputs = tokens.astype(jnp.float32)]
    sub x1 -> x0, matrix products: 16.8 us -> none  [forward_block(): weights = jnp.exp(scores - row_max)]
  transfers between devices with their start and end apart: 17 -> 58, of which waited for: 13 -> 25; matrix products, arithmetic and copies ran while one was open for 5% -> 27% of each run, Pallas kernels for 0% -> 2%
where the time goes in v1:
time: 581 us; the launch traced here: 576 us
  waiting for transfers between devices  317 us (55%)
  matrix products  124 us (21%)
  starting transfers between devices  86.2 us (15%)
  other arithmetic  18.2 us (3%)
  local copies, waits for them, and re-layouts  15.3 us (3%)
  Pallas kernels  13.2 us (2%)
    ppermute x58, waiting for transfers between devices, flip(): lax.ppermute(block, axis, [(i, i ^ mask) for i in range(lax.axis_size(axi...  317 us
    dot_general x56, matrix products, dot(): lax.dot_general(left, right, (((left_dim,), (right_dim,)), ((), ())), pre...  124 us
    ppermute x58, starting transfers between devices, flip(): lax.ppermute(block, axis, [(i, i ^ mask) for i in range(lax.axis_size(axi...  86.2 us
  transfers between devices with their start and end apart: 58, of which 25 were waited for; matrix products, arithmetic and copies ran while one was open for 27% of the time, Pallas kernels for 2%

profile of v1, /device:TPU:0, one launch (start us, length us, event | category | flops | bytes accessed | tf_op | source)
XLA Modules:
  0.0 576.4 jit_solution(1023630725608595583)
XLA Ops:
  0.7 3.0 collective-permute-start.6
  3.7 2.1 multiply_reduce_fusion
  12.6 2.9 constant_dynamic-slice_fusion.46
  15.8 2.9 fusion.164
  18.8 30.9 %collective-permute-done.6 = bf16[512,2048]{1,0:T(8,128)(2,1)} collective-permute-done((bf16[512,2048]{1,0:T(8,128)(2,1)}, bf16[512,2048]{1,0:T(8,128)(2,1)}, u32[]{:S(2)}, u32[]{:S(2)}) %collective-permute-start.6) | collective-permute-done | bytes 2097184 | tf_op jit(solution)/shard_map/ppermute | solution.py:18
  50.5 6.2 %attention_forward.1 = (bf16[512,512]{1,0:T(8,128)(2,1)S(1)}, f32[8,1,512]{2,1,0:T(1,128)S(1)}) custom-call(s32[1]{0:T(128)} %bitcast.rank_ref, s32[1,512]{1,0:T(1,128)S(1)} %bitcast.98, bf16[512,512]{1,0:T(8,128)(2,1)S(1)} %bitcast.96, bf16[128,512]{1,0:T(8,128)(2,1)S(1)} %pad_maximum_fusion.13.kv0, bf16[128,512]{1,0:T(8,128)(2,1)S(1)} %collective-permute-done.kv1, ...), custom_call_target="tpu_custom_call" | custom-call | flops 4294967296 | bytes 1048576 | tf_op jit(solution)/shard_map/attention_forward/pallas_call | solution.py:181
  61.7 2.5 convert_element_type.177
  64.5 2.1 fusion.167
  66.6 2.1 fusion.166
  68.7 2.1 fusion.21
  70.8 2.6 multiply_reduce_fusion.5
  79.3 8.5 %collective-permute-done.9 = bf16[128,2048]{1,0:T(8,128)(2,1)S(1)} collective-permute-done((bf16[128,2048]{1,0:T(8,128)(2,1)S(1)}, bf16[128,2048]{1,0:T(8,128)(2,1)S(1)}, u32[]{:S(2)}, u32[]{:S(2)}) %collective-permute-start.9) | collective-permute-done | bytes 524320 | tf_op jit(solution)/shard_map/ppermute | solution.py:18
  91.8 7.4 %fusion.158 = f32[512,1408]{1,0:T(8,128)S(1)} fusion(bf16[1408,2048]{1,0:T(8,128)(2,1)} %param.22, bf16[128,2048]{1,0:T(8,128)(2,1)} %get-tuple-element.71, bf16[128,2048]{1,0:T(8,128)(2,1)} %get-tuple-element.72, bf16[128,2048]{1,0:T(8,128)(2,1)} %copy-done.24, bf16[128,2048]{1,0:T(8,128)(2,1)} %copy-done.20), kind=kOutput, calls=%fused_computation.304 | convolution fusion | flops 2961178624 | bytes 10747904 | tf_op jit(solution)/shard_map/dot_general | solution.py:22
  99.2 6.7 %fusion.159 = f32[512,1408]{1,0:T(8,128)S(1)} fusion(bf16[2048,1408]{1,0:T(8,128)(2,1)} %param.21, bf16[256,2048]{1,0:T(8,128)(2,1)} %collective-permute-done.10, bf16[128,2048]{1,0:T(8,128)(2,1)S(1)} %copy-done.23, bf16[128,2048]{1,0:T(8,128)(2,1)S(1)} %multiply_convert_fusion.4), kind=kOutput, calls=%fused_computation.305 | convolution fusion | flops 2959081472 | bytes 10747904 | tf_op jit(solution)/shard_map/dot_general | solution.py:22
  105.9 5.8 %multiply_convert_fusion.1 = (bf16[512,1408]{1,0:T(8,128)(2,1)S(1)}, bf16[512,1408]{1,0:T(8,128)(2,1)S(1)}, bf16[512,1408]{1,0:T(8,128)(2,1)S(1)}) fusion(f32[512,1408]{1,0:T(8,128)S(1)} %fusion.158, f32[512,1408]{1,0:T(8,128)S(1)} %fusion.159, bf16[2048,1408]{1,0:T(8,128)(2,1)S(1)} %bitcast.129, bf16[256,2048]{1,0:T(8,128)(2,1)} %collective-permute-done.10, ...), kind=kOutput, calls=%fused_computation.8 | convolution fusion | flops 2969894912 | bytes 17956864 | tf_op jit(solution)/shard_map/dot_general | solution.py:22
  113.6 5.8 %collective-permute-start.48 = (bf16[512,1408]{1,0:T(8,128)(2,1)S(1)}, bf16[512,1408]{1,0:T(8,128)(2,1)S(1)}, u32[]{:S(2)}, u32[]{:S(2)}) collective-permute-start(bf16[512,1408]{1,0:T(8,128)(2,1)S(1)} %get-tuple-element.43), channel_id=1, source_target_pairs={{0,4},{4,0},{8,12},{12,8},{16,20},{20,16},{24,28},{28,24},{1,5},{5... | collective-permute-start | bytes 4325384 | tf_op jit(solution)/shard_map/ppermute | solution.py:18
  123.4 5.5 fusion.13
  129.1 4.6 convolution_convert_fusion
  135.0 2.7 fusion.86
  137.7 3.2 fusion.53
  140.9 3.0 fusion.84
  145.0 2.0 collective-permute-start.47
  147.0 4.8 convert_add_fusion
  152.0 4.9 convert_add_fusion.1
  157.0 48.2 %collective-permute-done.47 = bf16[512,1024]{1,0:T(8,128)(2,1)S(1)} collective-permute-done((bf16[512,1024]{1,0:T(8,128)(2,1)S(1)}, bf16[512,1024]{1,0:T(8,128)(2,1)S(1)}, u32[]{:S(2)}, u32[]{:S(2)}) %collective-permute-start.47) | collective-permute-done | bytes 1048608 | tf_op jit(solution)/shard_map/ppermute | solution.py:18
  206.7 1.9 collective-permute-start.55
  210.3 2.1 fusion
  213.0 2.2 fusion.1
  215.2 43.2 %collective-permute-done.55 = bf16[512,1024]{1,0:T(8,128)(2,1)S(1)} collective-permute-done((bf16[512,1024]{1,0:T(8,128)(2,1)S(1)}, bf16[512,1024]{1,0:T(8,128)(2,1)S(1)}, u32[]{:S(2)}, u32[]{:S(2)}) %collective-permute-start.55) | collective-permute-done | bytes 1048608 | tf_op jit(solution)/shard_map/ppermute | solution.py:18
  259.9 2.1 fusion.2
  265.8 9.3 %collective-permute-done.12 = bf16[128,2048]{1,0:T(8,128)(2,1)S(1)} collective-permute-done((bf16[128,2048]{1,0:T(8,128)(2,1)S(1)}, bf16[128,2048]{1,0:T(8,128)(2,1)S(1)}, u32[]{:S(2)}, u32[]{:S(2)}) %collective-permute-start.12) | collective-permute-done | bytes 524320 | tf_op jit(solution)/shard_map/ppermute | solution.py:18
  276.7 2.4 fusion.32
  279.0 2.3 fusion.33
  281.4 2.3 fusion.34
  285.3 2.3 fusion.35
  289.7 3.4 collective-permute-done.17
  293.2 6.9 %attention_backward.1 = (bf16[512,512]{1,0:T(8,128)(2,1)S(1)}, f32[128,512]{1,0:T(8,128)S(1)}, bf16[128,512]{1,0:T(8,128)(2,1)S(1)}, bf16[128,512]{1,0:T(8,128)(2,1)S(1)}, bf16[128,512]{1,0:T(8,128)(2,1)S(1)}) custom-call(s32[1]{0:T(128)} %bitcast.rank_ref, s32[1,512]{1,0:T(1,128)S(1)} %bitcast.99, bf16[512,512]{1,0:T(8,128)(2,1)S(1)} %bitcast.97, ...), custom_call_target="tpu_custom_call" | custom-call | flops 10737418240 | bytes 2621440 | tf_op jit(solution)/shard_map/attention_backward/pallas_call | solution.py:215
  300.2 29.7 %collective-permute-start.20 = (bf16[128,512]{1,0:T(8,128)(2,1)S(1)}, bf16[128,512]{1,0:T(8,128)(2,1)S(1)}, u32[]{:S(2)}, u32[]{:S(2)}) collective-permute-start(bf16[128,512]{1,0:T(8,128)(2,1)S(1)} %get-tuple-element.24), channel_id=1, source_target_pairs={{0,12},{4,8},{8,4},{12,0},{16,28},{20,24},{24,20},{28,16},{1,13},{... | collective-permute-start | bytes 393224 | tf_op jit(solution)/shard_map/ppermute | solution.py:18
  331.4 2.8 collective-permute-done.20
  339.2 7.9 %collective-permute-done.28 = bf16[2048,128]{0,1:T(8,128)(2,1)S(1)} collective-permute-done((bf16[2048,128]{0,1:T(8,128)(2,1)S(1)}, bf16[2048,128]{0,1:T(8,128)(2,1)S(1)}, u32[]{:S(2)}, u32[]{:S(2)}) %collective-permute-start.28) | collective-permute-done | bytes 524320 | tf_op jit(solution)/shard_map/ppermute | solution.py:18
  349.8 2.4 convolution_add_fusion.13
  352.2 2.5 fusion.19
  356.6 3.4 collective-permute-done.25
  360.1 2.6 fusion.18
  366.6 1.9 collective-permute-done.29
  370.2 2.2 collective-permute-start.33
  374.3 6.7 %collective-permute-done.34 = f32[2,2048]{1,0:T(2,128)S(1)} collective-permute-done((f32[2,2048]{1,0:T(2,128)S(1)}, f32[2,2048]{1,0:T(2,128)S(1)}, u32[]{:S(2)}, u32[]{:S(2)}) %collective-permute-start.34) | collective-permute-done | bytes 16416 | tf_op jit(solution)/shard_map/ppermute | solution.py:18
  381.1 2.1 collective-permute-start.35
  386.0 26.5 %collective-permute-done.36 = f32[2,512]{1,0:T(2,128)S(1)} collective-permute-done((f32[2,512]{1,0:T(2,128)S(1)}, f32[2,512]{1,0:T(2,128)S(1)}, u32[]{:S(2)}, u32[]{:S(2)}) %collective-permute-start.36) | collective-permute-done | bytes 4128 | tf_op jit(solution)/shard_map/ppermute | solution.py:18
  412.6 2.6 collective-permute-start.37
  420.7 11.2 %collective-permute-done.39 = bf16[512,640]{0,1:T(8,128)(2,1)S(1)} collective-permute-done((bf16[512,640]{0,1:T(8,128)(2,1)S(1)}, bf16[512,640]{0,1:T(8,128)(2,1)S(1)}, u32[]{:S(2)}, u32[]{:S(2)}) %collective-permute-start.39) | collective-permute-done | bytes 655392 | tf_op jit(solution)/shard_map/ppermute | solution.py:18
  435.4 2.3 collective-permute-start.50
  444.4 53.5 %collective-permute-done.40 = bf16[512,640]{1,0:T(8,128)(2,1)S(1)} collective-permute-done((bf16[512,640]{1,0:T(8,128)(2,1)S(1)}, bf16[512,640]{1,0:T(8,128)(2,1)S(1)}, u32[]{:S(2)}, u32[]{:S(2)}) %collective-permute-start.40) | collective-permute-done | bytes 655392 | tf_op jit(solution)/shard_map/ppermute | solution.py:18
  498.4 1.9 collective-permute-start.41
  500.3 2.6 fusion.16
  504.0 28.4 %collective-permute-done.41 = bf16[256,640]{1,0:T(8,128)(2,1)S(1)} collective-permute-done((bf16[256,640]{1,0:T(8,128)(2,1)S(1)}, bf16[256,640]{1,0:T(8,128)(2,1)S(1)}, u32[]{:S(2)}, u32[]{:S(2)}) %collective-permute-start.41) | collective-permute-done | bytes 327712 | tf_op jit(solution)/shard_map/ppermute | solution.py:18
  535.5 1.9 add_convert_fusion
  537.7 3.3 fusion.12
  541.0 5.8 collective-permute-done.57
  546.8 3.0 fusion.6
  549.8 8.0 %collective-permute-done.45 = bf16[512,512]{1,0:T(8,128)(2,1)S(1)} collective-permute-done((bf16[512,512]{1,0:T(8,128)(2,1)S(1)}, bf16[512,512]{1,0:T(8,128)(2,1)S(1)}, u32[]{:S(2)}, u32[]{:S(2)}) %collective-permute-start.45) | collective-permute-done | bytes 524320 | tf_op jit(solution)/shard_map/ppermute | solution.py:18
  560.0 2.7 fusion.9
  562.7 11.2 %collective-permute-done.46 = bf16[512,256]{1,0:T(8,128)(2,1)S(1)} collective-permute-done((bf16[512,256]{1,0:T(8,128)(2,1)S(1)}, bf16[512,256]{1,0:T(8,128)(2,1)S(1)}, u32[]{:S(2)}, u32[]{:S(2)}) %collective-permute-start.46) | collective-permute-done | bytes 262176 | tf_op jit(solution)/shard_map/ppermute | solution.py:18
  573.9 2.1 fusion.28
  (304 shorter events, 89.9 us)
Async XLA Ops:
  0.7 49.0 %collective-permute-start.6 = (bf16[512,2048]{1,0:T(8,128)(2,1)}, bf16[512,2048]{1,0:T(8,128)(2,1)}, u32[]{:S(2)}, u32[]{:S(2)}) collective-permute-start(bf16[512,2048]{1,0:T(8,128)(2,1)} %param.18), channel_id=1, source_target_pairs={{0,2},{1,3},{2,0},{3,1},{4,6},{5,7},{6,4},{7,5},{8,10},{9,11},{10,... | collective-permute-start | bytes 6291464 | tf_op jit(solution)/shard_map/ppermute | solution.py:18
  9.1 40.9 %collective-permute-start = (bf16[128,512]{1,0:T(8,128)(2,1)S(1)}, bf16[128,512]{1,0:T(8,128)(2,1)S(1)}, u32[]{:S(2)}, u32[]{:S(2)}) collective-permute-start(bf16[128,512]{1,0:T(8,128)(2,1)S(1)} %pad_maximum_fusion.13.kv0), channel_id=1, source_target_pairs={{0,4},{4,0},{8,12},{12,8},{16,20},{20,16},{24,28},{28,24},{1,5},{5... | collective-permute-start | bytes 393224 | tf_op jit(solution)/shard_map/ppermute | solution.py:18
  10.6 39.9 %collective-permute-start.1 = (bf16[128,512]{1,0:T(8,128)(2,1)S(1)}, bf16[128,512]{1,0:T(8,128)(2,1)S(1)}, u32[]{:S(2)}, u32[]{:S(2)}) collective-permute-start(bf16[128,512]{1,0:T(8,128)(2,1)S(1)} %pad_maximum_fusion.13.kv0), channel_id=1, source_target_pairs={{0,8},{4,12},{8,0},{12,4},{16,24},{20,28},{24,16},{28,20},{1,9},{5... | collective-permute-start | bytes 393224 | tf_op jit(solution)/shard_map/ppermute | solution.py:18
  12.2 38.3 %collective-permute-start.2 = (bf16[128,512]{1,0:T(8,128)(2,1)S(1)}, bf16[128,512]{1,0:T(8,128)(2,1)S(1)}, u32[]{:S(2)}, u32[]{:S(2)}) collective-permute-start(bf16[128,512]{1,0:T(8,128)(2,1)S(1)} %pad_maximum_fusion.13.kv0), channel_id=1, source_target_pairs={{0,12},{4,8},{8,4},{12,0},{16,28},{20,24},{24,20},{28,16},{1,13},{... | collective-permute-start | bytes 393224 | tf_op jit(solution)/shard_map/ppermute | solution.py:18
  12.6 54.0 %collective-permute-start.4 = (bf16[512,2048]{1,0:T(8,128)(2,1)}, bf16[512,2048]{1,0:T(8,128)(2,1)}, u32[]{:S(2)}, u32[]{:S(2)}) collective-permute-start(bf16[512,2048]{1,0:T(8,128)(2,1)} %param.18), channel_id=1, source_target_pairs={{0,1},{1,0},{2,3},{3,2},{4,5},{5,4},{6,7},{7,6},{8,9},{9,8},{10,11... | collective-permute-start | bytes 6291464 | tf_op jit(solution)/shard_map/ppermute | solution.py:18
  49.6 21.1 %collective-permute-start.8 = (bf16[512,2048]{1,0:T(8,128)(2,1)}, bf16[512,2048]{1,0:T(8,128)(2,1)}, u32[]{:S(2)}, u32[]{:S(2)}) collective-permute-start(bf16[512,2048]{1,0:T(8,128)(2,1)} %collective-permute-done.6), channel_id=1, source_target_pairs={{0,1},{1,0},{2,3},{3,2},{4,5},{5,4},{6,7},{7,6},{8,9},{9,8},{10,11... | collective-permute-start | bytes 6291464 | tf_op jit(solution)/shard_map/ppermute | solution.py:18
  49.9 298.0 %collective-permute-start.22 = (bf16[2048,512]{1,0:T(8,128)(2,1)}, bf16[2048,512]{1,0:T(8,128)(2,1)}, u32[]{:S(2)}, u32[]{:S(2)}) collective-permute-start(bf16[2048,512]{1,0:T(8,128)(2,1)} %param.15), channel_id=1, source_target_pairs={{0,1},{1,0},{2,3},{3,2},{4,5},{5,4},{6,7},{7,6},{8,9},{9,8},{10,11... | collective-permute-start | bytes 6291464 | tf_op jit(solution)/shard_map/ppermute | solution.py:18
  57.6 6.6 %collective-permute-start.5 = (bf16[512,128]{1,0:T(8,128)(2,1)S(1)}, bf16[512,128]{1,0:T(8,128)(2,1)S(1)}, u32[]{:S(2)}, u32[]{:S(2)}) collective-permute-start(bf16[512,128]{1,0:T(8,128)(2,1)S(1)} %get-tuple-element.82), channel_id=1, source_target_pairs={{0,2},{1,3},{2,0},{3,1},{4,6},{5,7},{6,4},{7,5},{8,10},{9,11},{10,... | collective-permute-start | bytes 393224 | tf_op jit(solution)/shard_map/ppermute | solution.py:18
  64.1 2.5 collective-permute-start.3
  64.2 6.6 %collective-permute-start.7 = (bf16[512,128]{1,0:T(8,128)(2,1)S(1)}, bf16[512,128]{1,0:T(8,128)(2,1)S(1)}, u32[]{:S(2)}, u32[]{:S(2)}) collective-permute-start(bf16[512,128]{1,0:T(8,128)(2,1)S(1)} %get-tuple-element.81), channel_id=1, source_target_pairs={{0,3},{1,2},{2,1},{3,0},{4,7},{5,6},{6,5},{7,4},{8,11},{9,10},{10,... | collective-permute-start | bytes 393224 | tf_op jit(solution)/shard_map/ppermute | solution.py:18
  73.6 14.2 %collective-permute-start.9 = (bf16[128,2048]{1,0:T(8,128)(2,1)S(1)}, bf16[128,2048]{1,0:T(8,128)(2,1)S(1)}, u32[]{:S(2)}, u32[]{:S(2)}) collective-permute-start(bf16[128,2048]{1,0:T(8,128)(2,1)S(1)} %multiply_convert_fusion.4), channel_id=1, source_target_pairs={{0,2},{1,3},{2,0},{3,1},{4,6},{5,7},{6,4},{7,5},{8,10},{9,11},{10,... | collective-permute-start | bytes 1572872 | tf_op jit(solution)/shard_map/ppermute | solution.py:18
  88.9 10.3 %collective-permute-start.10 = (bf16[256,2048]{1,0:T(8,128)(2,1)}, bf16[256,2048]{1,0:T(8,128)(2,1)}, u32[]{:S(2)}, u32[]{:S(2)}) collective-permute-start(bf16[256,2048]{1,0:T(8,128)(2,1)} %pad_maximum_fusion.3), channel_id=1, source_target_pairs={{0,1},{1,0},{2,3},{3,2},{4,5},{5,4},{6,7},{7,6},{8,9},{9,8},{10,11... | collective-permute-start | bytes 3145736 | tf_op jit(solution)/shard_map/ppermute | solution.py:18
  111.7 322.1 %copy-start.8 = (bf16[512,1408]{1,0:T(8,128)(2,1)}, bf16[512,1408]{1,0:T(8,128)(2,1)S(1)}, u32[]{:S(2)}) copy-start(bf16[512,1408]{1,0:T(8,128)(2,1)S(1)} %get-tuple-element.43) | copy-start | bytes 4325380
  111.7 325.9 %copy-start.6 = (bf16[512,1408]{1,0:T(8,128)(2,1)}, bf16[512,1408]{1,0:T(8,128)(2,1)S(1)}, u32[]{:S(2)}) copy-start(bf16[512,1408]{1,0:T(8,128)(2,1)S(1)} %get-tuple-element.42) | copy-start | bytes 4325380
  113.6 93.1 %collective-permute-start.48 = (bf16[512,1408]{1,0:T(8,128)(2,1)S(1)}, bf16[512,1408]{1,0:T(8,128)(2,1)S(1)}, u32[]{:S(2)}, u32[]{:S(2)}) collective-permute-start(bf16[512,1408]{1,0:T(8,128)(2,1)S(1)} %get-tuple-element.43), channel_id=1, source_target_pairs={{0,4},{4,0},{8,12},{12,8},{16,20},{20,16},{24,28},{28,24},{1,5},{5... | collective-permute-start | bytes 4325384 | tf_op jit(solution)/shard_map/ppermute | solution.py:18
  121.1 316.6 %copy-start.13 = (bf16[512,2048]{1,0:T(8,128)(2,1)}, bf16[512,2048]{1,0:T(8,128)(2,1)S(1)}, u32[]{:S(2)}) copy-start(bf16[512,2048]{1,0:T(8,128)(2,1)S(1)} %pad_maximum_fusion) | copy-start | bytes 6291460
  121.3 91.2 %collective-permute-start.51 = (bf16[512,1408]{1,0:T(8,128)(2,1)S(1)}, bf16[512,1408]{1,0:T(8,128)(2,1)S(1)}, u32[]{:S(2)}, u32[]{:S(2)}) collective-permute-start(bf16[512,1408]{1,0:T(8,128)(2,1)S(1)} %get-tuple-element.42), channel_id=1, source_target_pairs={{0,4},{4,0},{8,12},{12,8},{16,20},{20,16},{24,28},{28,24},{1,5},{5... | collective-permute-start | bytes 4325384 | tf_op jit(solution)/shard_map/ppermute | solution.py:18
  128.9 15.1 %collective-permute-start.13 = (bf16[256,2048]{1,0:T(8,128)(2,1)}, bf16[256,2048]{1,0:T(8,128)(2,1)S(1)}, u32[]{:S(2)}, u32[]{:S(2)}) collective-permute-start(bf16[256,2048]{1,0:T(8,128)(2,1)} %fusion.13), channel_id=1, source_target_pairs={{0,1},{1,0},{2,3},{3,2},{4,5},{5,4},{6,7},{7,6},{8,9},{9,8},{10,11... | collective-permute-start | bytes 3145736 | tf_op jit(solution)/shard_map/ppermute | solution.py:18
  133.7 18.2 %collective-permute-start.11 = (bf16[256,2048]{1,0:T(8,128)(2,1)S(1)}, bf16[256,2048]{1,0:T(8,128)(2,1)}, u32[]{:S(2)}, u32[]{:S(2)}) collective-permute-start(bf16[256,2048]{1,0:T(8,128)(2,1)S(1)} %convolution_convert_fusion), channel_id=1, source_target_pairs={{0,1},{1,0},{2,3},{3,2},{4,5},{5,4},{6,7},{7,6},{8,9},{9,8},{10,11... | collective-permute-start | bytes 3145736 | tf_op jit(solution)/shard_map/ppermute | solution.py:18
  145.0 60.2 %collective-permute-start.47 = (bf16[512,1024]{1,0:T(8,128)(2,1)S(1)}, bf16[512,1024]{1,0:T(8,128)(2,1)S(1)}, u32[]{:S(2)}, u32[]{:S(2)}) collective-permute-start(bf16[512,1024]{1,0:T(8,128)(2,1)S(1)} %pad_maximum_fusion.6), channel_id=1, source_target_pairs={{0,4},{4,0},{8,12},{12,8},{16,20},{20,16},{24,28},{28,24},{1,5},{5... | collective-permute-start | bytes 3145736 | tf_op jit(solution)/shard_map/ppermute | solution.py:18
  151.9 54.8 %copy-start.41 = (bf16[512,1024]{1,0:T(8,128)(2,1)S(1)}, bf16[512,1024]{1,0:T(8,128)(2,1)}, u32[]{:S(2)}) copy-start(bf16[512,1024]{1,0:T(8,128)(2,1)} %pad_maximum_fusion.7) | copy-start | bytes 3145732
  152.0 107.9 %collective-permute-start.54 = (bf16[512,1408]{1,0:T(8,128)(2,1)S(1)}, bf16[512,1408]{1,0:T(8,128)(2,1)S(1)}, u32[]{:S(2)}, u32[]{:S(2)}) collective-permute-start(bf16[512,1408]{1,0:T(8,128)(2,1)S(1)} %get-tuple-element.44), channel_id=1, source_target_pairs={{0,4},{4,0},{8,12},{12,8},{16,20},{20,16},{24,28},{28,24},{1,5},{5... | collective-permute-start | bytes 4325384 | tf_op jit(solution)/shard_map/ppermute | solution.py:18
  205.2 126.1 %collective-permute-start.26 = (bf16[2048,512]{1,0:T(8,128)(2,1)}, bf16[2048,512]{1,0:T(8,128)(2,1)}, u32[]{:S(2)}, u32[]{:S(2)}) collective-permute-start(bf16[2048,512]{1,0:T(8,128)(2,1)} %param.15), channel_id=1, source_target_pairs={{0,2},{1,3},{2,0},{3,1},{4,6},{5,7},{6,4},{7,5},{8,10},{9,11},{10,... | collective-permute-start | bytes 6291464 | tf_op jit(solution)/shard_map/ppermute | solution.py:18
  206.7 51.7 %collective-permute-start.55 = (bf16[512,1024]{1,0:T(8,128)(2,1)S(1)}, bf16[512,1024]{1,0:T(8,128)(2,1)S(1)}, u32[]{:S(2)}, u32[]{:S(2)}) collective-permute-start(bf16[512,1024]{1,0:T(8,128)(2,1)S(1)} %copy-done.41), channel_id=1, source_target_pairs={{0,4},{4,0},{8,12},{12,8},{16,20},{20,16},{24,28},{28,24},{1,5},{5... | collective-permute-start | bytes 3145736 | tf_op jit(solution)/shard_map/ppermute | solution.py:18
  212.5 52.9 %collective-permute-start.14 = (bf16[128,2048]{1,0:T(8,128)(2,1)S(1)}, bf16[128,2048]{1,0:T(8,128)(2,1)S(1)}, u32[]{:S(2)}, u32[]{:S(2)}) collective-permute-start(bf16[128,2048]{1,0:T(8,128)(2,1)S(1)} %slice.351), channel_id=1, source_target_pairs={{0,2},{1,3},{2,0},{3,1},{4,6},{5,7},{6,4},{7,5},{8,10},{9,11},{10,... | collective-permute-start | bytes 1572872 | tf_op jit(solution)/shard_map/ppermute | solution.py:18
  258.4 16.8 %collective-permute-start.12 = (bf16[128,2048]{1,0:T(8,128)(2,1)S(1)}, bf16[128,2048]{1,0:T(8,128)(2,1)S(1)}, u32[]{:S(2)}, u32[]{:S(2)}) collective-permute-start(bf16[128,2048]{1,0:T(8,128)(2,1)S(1)} %slice.352), channel_id=1, source_target_pairs={{0,2},{1,3},{2,0},{3,1},{4,6},{5,7},{6,4},{7,5},{8,10},{9,11},{10,... | collective-permute-start | bytes 1572872 | tf_op jit(solution)/shard_map/ppermute | solution.py:18
  259.9 240.4 %copy-start.10 = (bf16[512,1408]{1,0:T(8,128)(2,1)}, bf16[512,1408]{1,0:T(8,128)(2,1)S(1)}, u32[]{:S(2)}) copy-start(bf16[512,1408]{1,0:T(8,128)(2,1)S(1)} %collective-permute-done.54) | copy-start | bytes 4325380
  281.4 6.7 %collective-permute-start.15 = (bf16[512,128]{1,0:T(8,128)(2,1)S(1)}, bf16[512,128]{1,0:T(8,128)(2,1)S(1)}, u32[]{:S(2)}, u32[]{:S(2)}) collective-permute-start(bf16[512,128]{1,0:T(8,128)(2,1)S(1)} %fusion.33), channel_id=1, source_target_pairs={{0,1},{1,0},{2,3},{3,2},{4,5},{5,4},{6,7},{7,6},{8,9},{9,8},{10,11... | collective-permute-start | bytes 393224 | tf_op jit(solution)/shard_map/ppermute | solution.py:18
  283.7 6.0 %collective-permute-start.16 = (bf16[512,128]{1,0:T(8,128)(2,1)S(1)}, bf16[512,128]{1,0:T(8,128)(2,1)S(1)}, u32[]{:S(2)}, u32[]{:S(2)}) collective-permute-start(bf16[512,128]{1,0:T(8,128)(2,1)S(1)} %fusion.34), channel_id=1, source_target_pairs={{0,2},{1,3},{2,0},{3,1},{4,6},{5,7},{6,4},{7,5},{8,10},{9,11},{10,... | collective-permute-start | bytes 393224 | tf_op jit(solution)/shard_map/ppermute | solution.py:18
  287.6 5.6 collective-permute-start.17
  300.2 34.0 %collective-permute-start.20 = (bf16[128,512]{1,0:T(8,128)(2,1)S(1)}, bf16[128,512]{1,0:T(8,128)(2,1)S(1)}, u32[]{:S(2)}, u32[]{:S(2)}) collective-permute-start(bf16[128,512]{1,0:T(8,128)(2,1)S(1)} %get-tuple-element.24), channel_id=1, source_target_pairs={{0,12},{4,8},{8,4},{12,0},{16,28},{20,24},{24,20},{28,16},{1,13},{... | collective-permute-start | bytes 393224 | tf_op jit(solution)/shard_map/ppermute | solution.py:18
  329.9 5.9 %collective-permute-start.19 = (bf16[128,512]{1,0:T(8,128)(2,1)S(1)}, bf16[128,512]{1,0:T(8,128)(2,1)S(1)}, u32[]{:S(2)}, u32[]{:S(2)}) collective-permute-start(bf16[128,512]{1,0:T(8,128)(2,1)S(1)} %get-tuple-element.23), channel_id=1, source_target_pairs={{0,8},{4,12},{8,0},{12,4},{16,24},{20,28},{24,16},{28,20},{1,9},{5... | collective-permute-start | bytes 393224 | tf_op jit(solution)/shard_map/ppermute | solution.py:18
  329.9 6.6 %collective-permute-start.18 = (bf16[128,512]{1,0:T(8,128)(2,1)S(1)}, bf16[128,512]{1,0:T(8,128)(2,1)S(1)}, u32[]{:S(2)}, u32[]{:S(2)}) collective-permute-start(bf16[128,512]{1,0:T(8,128)(2,1)S(1)} %get-tuple-element.22), channel_id=1, source_target_pairs={{0,4},{4,0},{8,12},{12,8},{16,20},{20,16},{24,28},{28,24},{1,5},{5... | collective-permute-start | bytes 393224 | tf_op jit(solution)/shard_map/ppermute | solution.py:18
  331.3 6.8 %collective-permute-start.24 = (bf16[2048,128]{0,1:T(8,128)(2,1)S(1)}, bf16[2048,128]{0,1:T(8,128)(2,1)S(1)}, u32[]{:S(2)}, u32[]{:S(2)}) collective-permute-start(bf16[2048,128]{0,1:T(8,128)(2,1)S(1)} %copy-done.35), channel_id=1, source_target_pairs={{0,1},{1,0},{2,3},{3,2},{4,5},{5,4},{6,7},{7,6},{8,9},{9,8},{10,11... | collective-permute-start | bytes 1572872 | tf_op jit(solution)/shard_map/ppermute | solution.py:18
  334.2 13.0 %collective-permute-start.28 = (bf16[2048,128]{0,1:T(8,128)(2,1)S(1)}, bf16[2048,128]{0,1:T(8,128)(2,1)S(1)}, u32[]{:S(2)}, u32[]{:S(2)}) collective-permute-start(bf16[2048,128]{0,1:T(8,128)(2,1)S(1)} %copy-done.35), channel_id=1, source_target_pairs={{0,2},{1,3},{2,0},{3,1},{4,6},{5,7},{6,4},{7,5},{8,10},{9,11},{10,... | collective-permute-start | bytes 1572872 | tf_op jit(solution)/shard_map/ppermute | solution.py:18
  335.8 29.3 %collective-permute-start.30 = (bf16[2048,512]{1,0:T(8,128)(2,1)}, bf16[2048,512]{1,0:T(8,128)(2,1)S(1)}, u32[]{:S(2)}, u32[]{:S(2)}) collective-permute-start(bf16[2048,512]{1,0:T(8,128)(2,1)} %collective-permute-done.26), channel_id=1, source_target_pairs={{0,1},{1,0},{2,3},{3,2},{4,5},{5,4},{6,7},{7,6},{8,9},{9,8},{10,11... | collective-permute-start | bytes 6291464 | tf_op jit(solution)/shard_map/ppermute | solution.py:18
  337.3 9.8 %collective-permute-start.23 = (bf16[128,128]{1,0:T(8,128)(2,1)S(1)}, bf16[128,128]{1,0:T(8,128)(2,1)S(1)}, u32[]{:S(2)}, u32[]{:S(2)}) collective-permute-start(bf16[128,128]{1,0:T(8,128)(2,1)S(1)} %get-tuple-element.90), channel_id=1, source_target_pairs={{0,1},{1,0},{2,3},{3,2},{4,5},{5,4},{6,7},{7,6},{8,9},{9,8},{10,11... | collective-permute-start | bytes 98312 | tf_op jit(solution)/shard_map/ppermute | solution.py:18
  338.5 80.5 %collective-permute-start.38 = (bf16[512,1024]{1,0:T(8,128)(2,1)S(1)}, bf16[512,1024]{1,0:T(8,128)(2,1)S(1)}, u32[]{:S(2)}, u32[]{:S(2)}) collective-permute-start(bf16[512,1024]{1,0:T(8,128)(2,1)S(1)} %copy-done.40), channel_id=1, source_target_pairs={{0,4},{4,0},{8,12},{12,8},{16,20},{20,16},{24,28},{28,24},{1,5},{5... | collective-permute-start | bytes 3145736 | tf_op jit(solution)/shard_map/ppermute | solution.py:18
  347.1 15.5 %collective-permute-start.32 = (bf16[2048,128]{0,1:T(8,128)(2,1)S(1)}, bf16[2048,128]{0,1:T(8,128)(2,1)S(1)}, u32[]{:S(2)}, u32[]{:S(2)}) collective-permute-start(bf16[2048,128]{0,1:T(8,128)(2,1)S(1)} %collective-permute-done.28), channel_id=1, source_target_pairs={{0,1},{1,0},{2,3},{3,2},{4,5},{5,4},{6,7},{7,6},{8,9},{9,8},{10,11... | collective-permute-start | bytes 1572872 | tf_op jit(solution)/shard_map/ppermute | solution.py:18
  347.2 2.1 collective-permute-start.21
  348.0 85.8 %collective-permute-start.49 = (bf16[512,1408]{1,0:T(8,128)(2,1)S(1)}, bf16[512,1408]{1,0:T(8,128)(2,1)S(1)}, u32[]{:S(2)}, u32[]{:S(2)}) collective-permute-start(bf16[512,1408]{1,0:T(8,128)(2,1)S(1)} %copy-done.34), channel_id=1, source_target_pairs={{0,8},{4,12},{8,0},{12,4},{16,24},{20,28},{24,16},{28,20},{1,9},{5... | collective-permute-start | bytes 4325384 | tf_op jit(solution)/shard_map/ppermute | solution.py:18
  349.2 5.4 collective-permute-start.27
  354.7 5.3 collective-permute-start.25
  360.0 3.7 collective-permute-start.31
  362.7 75.0 %collective-permute-start.52 = (bf16[512,1408]{1,0:T(8,128)(2,1)S(1)}, bf16[512,1408]{1,0:T(8,128)(2,1)S(1)}, u32[]{:S(2)}, u32[]{:S(2)}) collective-permute-start(bf16[512,1408]{1,0:T(8,128)(2,1)S(1)} %copy-done.33), channel_id=1, source_target_pairs={{0,8},{4,12},{8,0},{12,4},{16,24},{20,28},{24,16},{28,20},{1,9},{5... | collective-permute-start | bytes 4325384 | tf_op jit(solution)/shard_map/ppermute | solution.py:18
  363.7 4.9 collective-permute-start.29
  365.1 53.2 %collective-permute-start.42 = (bf16[128,2048]{1,0:T(8,128)(2,1)S(1)}, bf16[128,2048]{1,0:T(8,128)(2,1)S(1)}, u32[]{:S(2)}, u32[]{:S(2)}) collective-permute-start(bf16[128,2048]{1,0:T(8,128)(2,1)S(1)} %get-tuple-element.40), channel_id=1, source_target_pairs={{0,2},{1,3},{2,0},{3,1},{4,6},{5,7},{6,4},{7,5},{8,10},{9,11},{10,... | collective-permute-start | bytes 1572872 | tf_op jit(solution)/shard_map/ppermute | solution.py:18
  370.2 3.5 collective-permute-start.33
  373.8 7.3 %collective-permute-start.34 = (f32[2,2048]{1,0:T(2,128)S(1)}, f32[2,2048]{1,0:T(2,128)S(1)}, u32[]{:S(2)}, u32[]{:S(2)}) collective-permute-start(f32[2,2048]{1,0:T(2,128)S(1)} %add.366), channel_id=1, source_target_pairs={{0,2},{1,3},{2,0},{3,1},{4,6},{5,7},{6,4},{7,5},{8,10},{9,11},{10,... | collective-permute-start | bytes 49160 | tf_op jit(solution)/shard_map/ppermute | solution.py:18
  381.1 3.7 collective-permute-start.35
  384.8 27.7 %collective-permute-start.36 = (f32[2,512]{1,0:T(2,128)S(1)}, f32[2,512]{1,0:T(2,128)S(1)}, u32[]{:S(2)}, u32[]{:S(2)}) collective-permute-start(f32[2,512]{1,0:T(2,128)S(1)} %slice.238), channel_id=1, source_target_pairs={{0,8},{4,12},{8,0},{12,4},{16,24},{20,28},{24,16},{28,20},{1,9},{5... | collective-permute-start | bytes 12296 | tf_op jit(solution)/shard_map/ppermute | solution.py:18
  412.6 4.5 collective-permute-start.37
  417.0 14.9 %collective-permute-start.39 = (bf16[512,640]{0,1:T(8,128)(2,1)S(1)}, bf16[512,640]{0,1:T(8,128)(2,1)S(1)}, u32[]{:S(2)}, u32[]{:S(2)}) collective-permute-start(bf16[512,640]{0,1:T(8,128)(2,1)S(1)} %fusion.157), channel_id=1, source_target_pairs={{0,4},{4,0},{8,12},{12,8},{16,20},{20,16},{24,28},{28,24},{1,5},{5... | collective-permute-start | bytes 1966088 | tf_op jit(solution)/shard_map/ppermute | solution.py:18
  418.3 21.5 %collective-permute-start.43 = (bf16[256,2048]{1,0:T(8,128)(2,1)S(1)}, bf16[256,2048]{1,0:T(8,128)(2,1)S(1)}, u32[]{:S(2)}, u32[]{:S(2)}) collective-permute-start(bf16[256,2048]{1,0:T(8,128)(2,1)S(1)} %pad_maximum_fusion.5), channel_id=1, source_target_pairs={{0,1},{1,0},{2,3},{3,2},{4,5},{5,4},{6,7},{7,6},{8,9},{9,8},{10,11... | collective-permute-start | bytes 3145736 | tf_op jit(solution)/shard_map/ppermute | solution.py:18
  419.0 81.3 %collective-permute-start.56 = (bf16[1408,512]{1,0:T(8,128)(2,1)S(1)}, bf16[1408,512]{1,0:T(8,128)(2,1)S(1)}, u32[]{:S(2)}, u32[]{:S(2)}) collective-permute-start(bf16[1408,512]{1,0:T(8,128)(2,1)S(1)} %copy-done.32), channel_id=1, source_target_pairs={{0,8},{4,12},{8,0},{12,4},{16,24},{20,28},{24,16},{28,20},{1,9},{5... | collective-permute-start | bytes 4325384 | tf_op jit(solution)/shard_map/ppermute | solution.py:18
  432.6 65.3 %collective-permute-start.40 = (bf16[512,640]{1,0:T(8,128)(2,1)S(1)}, bf16[512,640]{1,0:T(8,128)(2,1)S(1)}, u32[]{:S(2)}, u32[]{:S(2)}) collective-permute-start(bf16[512,640]{1,0:T(8,128)(2,1)S(1)} %fusion.22), channel_id=1, source_target_pairs={{0,8},{4,12},{8,0},{12,4},{16,24},{20,28},{24,16},{28,20},{1,9},{5... | collective-permute-start | bytes 1966088 | tf_op jit(solution)/shard_map/ppermute | solution.py:18
  435.4 102.1 %collective-permute-start.50 = (bf16[256,1408]{1,0:T(8,128)(2,1)}, bf16[256,1408]{1,0:T(8,128)(2,1)}, u32[]{:S(2)}, u32[]{:S(2)}) collective-permute-start(bf16[256,1408]{1,0:T(8,128)(2,1)} %fusion.14), channel_id=1, source_target_pairs={{0,16},{4,20},{8,24},{12,28},{16,0},{20,4},{24,8},{28,12},{1,17},{... | collective-permute-start | bytes 2162696 | tf_op jit(solution)/shard_map/ppermute | solution.py:18
  439.2 120.8 %collective-permute-start.53 = (bf16[256,1408]{1,0:T(8,128)(2,1)}, bf16[256,1408]{1,0:T(8,128)(2,1)S(1)}, u32[]{:S(2)}, u32[]{:S(2)}) collective-permute-start(bf16[256,1408]{1,0:T(8,128)(2,1)} %fusion.15), channel_id=1, source_target_pairs={{0,16},{4,20},{8,24},{12,28},{16,0},{20,4},{24,8},{28,12},{1,17},{... | collective-permute-start | bytes 2162696 | tf_op jit(solution)/shard_map/ppermute | solution.py:18
  442.7 57.6 %copy-start.19 = (f32[1408,256]{1,0:T(8,128)S(1)}, f32[1408,256]{1,0:T(8,128)}, u32[]{:S(2)}) copy-start(f32[1408,256]{1,0:T(8,128)} %fusion.84) | copy-start | bytes 4325380
  442.7 92.8 %collective-permute-start.44 = (bf16[512,1024]{1,0:T(8,128)(2,1)}, bf16[512,1024]{1,0:T(8,128)(2,1)}, u32[]{:S(2)}, u32[]{:S(2)}) collective-permute-start(bf16[512,1024]{1,0:T(8,128)(2,1)} %convolution_convert_fusion.1), channel_id=1, source_target_pairs={{0,4},{4,0},{8,12},{12,8},{16,20},{20,16},{24,28},{28,24},{1,5},{5... | collective-permute-start | bytes 3145736 | tf_op jit(solution)/shard_map/ppermute | solution.py:18
  498.4 34.0 %collective-permute-start.41 = (bf16[256,640]{1,0:T(8,128)(2,1)S(1)}, bf16[256,640]{1,0:T(8,128)(2,1)S(1)}, u32[]{:S(2)}, u32[]{:S(2)}) collective-permute-start(bf16[256,640]{1,0:T(8,128)(2,1)S(1)} %fusion.29), channel_id=1, source_target_pairs={{0,16},{4,20},{8,24},{12,28},{16,0},{20,4},{24,8},{28,12},{1,17},{... | collective-permute-start | bytes 983048 | tf_op jit(solution)/shard_map/ppermute | solution.py:18
  502.9 43.9 %collective-permute-start.57 = (bf16[1408,256]{1,0:T(8,128)(2,1)}, bf16[1408,256]{1,0:T(8,128)(2,1)}, u32[]{:S(2)}, u32[]{:S(2)}) collective-permute-start(bf16[1408,256]{1,0:T(8,128)(2,1)} %fusion.16), channel_id=1, source_target_pairs={{0,16},{4,20},{8,24},{12,28},{16,0},{20,4},{24,8},{28,12},{1,17},{... | collective-permute-start | bytes 2162696 | tf_op jit(solution)/shard_map/ppermute | solution.py:18
  537.4 20.4 %collective-permute-start.45 = (bf16[512,512]{1,0:T(8,128)(2,1)S(1)}, bf16[512,512]{1,0:T(8,128)(2,1)S(1)}, u32[]{:S(2)}, u32[]{:S(2)}) collective-permute-start(bf16[512,512]{1,0:T(8,128)(2,1)S(1)} %add_convert_fusion), channel_id=1, source_target_pairs={{0,8},{4,12},{8,0},{12,4},{16,24},{20,28},{24,16},{28,20},{1,9},{5... | collective-permute-start | bytes 1572872 | tf_op jit(solution)/shard_map/ppermute | solution.py:18
  559.1 14.8 %collective-permute-start.46 = (bf16[512,256]{1,0:T(8,128)(2,1)S(1)}, bf16[512,256]{1,0:T(8,128)(2,1)S(1)}, u32[]{:S(2)}, u32[]{:S(2)}) collective-permute-start(bf16[512,256]{1,0:T(8,128)(2,1)S(1)} %fusion.30), channel_id=1, source_target_pairs={{0,16},{4,20},{8,24},{12,28},{16,0},{20,4},{24,8},{28,12},{1,17},{... | collective-permute-start | bytes 786440 | tf_op jit(solution)/shard_map/ppermute | solution.py:18
  (55 other events, 441.0 us)

commit v2 on v1

--- a/solution.py
+++ b/solution.py
@@ -33,10 +33,30 @@
     return (key_at <= query_at) & (key_at >= query_at - pos)
 
 
+def row_starts(spot, rows):
+    part = rows // len(ROW_MASKS)
+    return [pl.multiple_of((spot ^ m) * part, part) for m in ROW_MASKS]
+
+
 def forward_kernel(
-    heads, size, rank_ref, pos_ref, q_ref, kv0, kv1, kv2, kv3, o_ref, lse_ref, keys, vals, top, acc
+    heads,
+    size,
+    at_ref,
+    pos_ref,
+    q_ref,
+    kv0,
+    kv1,
+    kv2,
+    kv3,
+    o_ref,
+    lse_ref,
+    keys,
+    vals,
+    top,
+    acc,
+    ordered,
 ):
-    rank = rank_ref[0]
+    rank, spot = at_ref[0], at_ref[1]
     rows = pos_ref.shape[1]
     half = rows // 2
 
@@ -74,18 +94,21 @@
 
     for h in range(heads):
         total = acc[h, size : size + 1, :]
-        o_ref[h * size : (h + 1) * size, :] = (acc[h, :size, :] / total).astype(LOW)
+        ordered[h * size : (h + 1) * size, :] = (acc[h, :size, :] / total).astype(LOW)
         lse_ref[h] = top[h] + jnp.log(total)
+    for j, start in enumerate(row_starts(spot, rows)):
+        part = rows // len(ROW_MASKS)
+        o_ref[:, j * part : (j + 1) * part] = ordered[:, pl.ds(start, part)]
 
 
 def backward_kernel(
     heads,
     size,
-    rank_ref,
+    at_ref,
     pos_ref,
     q_ref,
-    do_ref,
-    o_ref,
+    do_in,
+    o_in,
     lse_ref,
     cos_ref,
     sin_ref,
@@ -102,8 +125,10 @@
     vals,
     dq,
     total,
+    do_ref,
+    o_ref,
 ):
-    rank = rank_ref[0]
+    rank, spot = at_ref[0], at_ref[1]
     rows = pos_ref.shape[1]
     half = rows // 2
     blocks = (kv0, kv1, kv2, kv3)
@@ -116,6 +141,10 @@
             vals[m] = kv[size:, :].T
         total[...] = jnp.zeros_like(total)
 
+    part = rows // len(ROW_MASKS)
+    for j, start in enumerate(row_starts(spot, rows)):
+        do_ref[:, pl.ds(start, part)] = do_in[:, j * part : (j + 1) * part]
+        o_ref[:, pl.ds(start, part)] = o_in[:, j * part : (j + 1) * part]
     pos = pos_ref[...]
     seen = pos > lax.broadcasted_iota(jnp.int32, (1, rows), 1)
     deltas = []
@@ -173,7 +202,7 @@
             out[...] = total[m].astype(LOW)
 
 
-def attention_forward(rank, pos, queries, blocks, size, heads):
+def attention_forward(at, pos, queries, blocks, size, heads):
     wide, rows = queries.shape
     count = wide // size
     whole = pl.BlockSpec((2 * size, rows), lambda i, r: (0, 0))
@@ -194,19 +223,20 @@
                 pltpu.VMEM((SPAN, size + 16, rows), LOW),
                 pltpu.VMEM((heads, 1, rows), jnp.float32),
                 pltpu.VMEM((heads, size + 16, rows), jnp.float32),
+                pltpu.VMEM((heads * size, rows), LOW),
             ],
         ),
         compiler_params=pltpu.CompilerParams(vmem_limit_bytes=48 << 20),
         cost_estimate=pl.CostEstimate(
-            flops=16 * wide * rows * rows * SPAN // 2,
+            flops=wide * rows * rows,
             bytes_accessed=4 * wide * rows,
-            transcendentals=count * rows * rows * SPAN,
+            transcendentals=0,
         ),
         name="attention_forward",
-    )(rank, pos, queries, *blocks)
-
-
-def attention_backward(rank, pos, queries, grads, attended, lse, cosine, sine, blocks, size, heads):
+    )(at, pos, queries, *blocks)
+
+
+def attention_backward(at, pos, queries, grads, attended, lse, cosine, sine, blocks, size, heads):
     wide, rows = queries.shape
     count = wide // size
     whole = pl.BlockSpec((2 * size, rows), lambda i, r: (0, 0))
@@ -238,60 +268,37 @@
                 pltpu.VMEM((SPAN, rows, size), LOW),
                 pltpu.VMEM((heads, size, rows), jnp.float32),
                 pltpu.VMEM((SPAN, 2 * size, rows), jnp.float32),
+                pltpu.VMEM((heads * size, rows), LOW),
+                pltpu.VMEM((heads * size, rows), LOW),
             ],
         ),
         compiler_params=pltpu.CompilerParams(vmem_limit_bytes=48 << 20),
         cost_estimate=pl.CostEstimate(
-            flops=40 * wide * rows * rows * SPAN // 2,
+            flops=wide * rows * rows,
             bytes_accessed=10 * wide * rows,
-            transcendentals=count * rows * rows * SPAN,
+            transcendentals=0,
         ),
         name="attention_backward",
-    )(rank, pos, queries, grads, attended, lse, cosine, sine, *blocks)
-
-
-def block_order(bits, first):
-    used = list(range(first, bits))
-    count = 1 << len(used)
-    return [
-        sum(((j >> (len(used) - 1 - k)) & 1) << b for k, b in enumerate(used)) for j in range(count)
-    ]
-
-
-def pick(values, masks, place, blocks, dim):
+    )(at, pos, queries, grads, attended, lse, cosine, sine, *blocks)
+
+
+def pick(values, places, blocks, dim):
     size = values.shape[dim] // blocks
     return jnp.concatenate(
-        [lax.dynamic_slice_in_dim(values, (place ^ m) * size, size, dim) for m in masks], dim
-    )
-
-
-def exchange_sum(part, count, bits, first, dim):
-    got = []
-    size = None
-    for bit in range(first, bits):
-        lo = count // 2
-        send = part(lo, count)
-        size = send.shape[dim] // (count - lo)
-        for other in got:
-            send = send + lax.slice_in_dim(other, lo * size, count * size, axis=dim)
-        got.append(flip(send.astype(LOW), "dp", 1 << bit))
-        count = lo
-    total = part(0, 1)
-    for other in got:
-        total = total + lax.slice_in_dim(other, 0, total.shape[dim], axis=dim)
-    return total
-
-
-def pair_terms(pairs, size, left_first):
-    def part(lo, hi):
-        total = None
-        for x, g in pairs:
-            cut = x[:, lo * size : hi * size]
-            term = dot(cut, g, 0, 0) if left_first else dot(g, cut, 0, 0)
-            total = term if total is None else total + term
-        return total
-
-    return part
+        [lax.dynamic_slice_in_dim(values, p * size, size, dim) for p in places], dim
+    )
+
+
+def after(value, *others):
+    return lax.optimization_barrier((value, *others))[0]
+
+
+def parity_sum(terms, dim):
+    count = lax.axis_size("dp")
+    groups = [list(range(p, count, 2)) for p in range(2)]
+    return lax.psum_scatter(
+        terms.astype(LOW), "dp", scatter_dimension=dim, axis_index_groups=groups, tiled=True
+    )
 
 
 def turn(values, cosine, sine):
@@ -334,13 +341,12 @@
     rows_here, width = tokens.shape
     size = w_key.shape[1]
     dp = lax.axis_size("dp")
-    bits = dp.bit_length() - 1
     place = lax.axis_index("dp")
     spot = lax.axis_index("tp")
     tp_masks = range(lax.axis_size("tp"))
     own_rows = rows_here // lax.axis_size("tp")
     block = width // dp
-    rank = (place % SPAN).astype(jnp.int32).reshape(1)
+    at = jnp.stack([place % SPAN, spot]).astype(jnp.int32)
     pos = positions.reshape(1, rows_here)
 
     def own(values):
@@ -361,132 +367,182 @@
     blocks = [paired] + [flip(paired, "dp", m) for m in range(1, SPAN)]
     queries = (turn(dot(w_query, normed_one, 0, 1), cosine, sine) * size ** (-0.5)).astype(LOW)
 
-    out_core = flip(w_out, "tp", 1)
-    out_far = flip(w_out, "tp", 2)
-    outs = [w_out, out_core, out_far, flip(out_far, "tp", 1)]
-
-    attended, lse = attention_forward(rank, pos, queries, blocks, size, 2)
-
-    def token_block(values, mask):
-        return lax.dynamic_slice_in_dim(values, (spot ^ mask) * own_rows, own_rows, 1)
-
-    att_pieces = [token_block(attended, m) for m in tp_masks]
-    att_mine = [att_pieces[0]] + [flip(att_pieces[m], "tp", m) for m in tp_masks if m]
-    branch = sum(dot(a, w, 0, 0) for a, w in zip(att_mine, outs))
-
-    middle = own(inputs) + branch
+    bit = place % 2
+    bits = dp.bit_length() - 1
+
+    def columns(values, which):
+        return pick(values, [2 * j + which for j in range(dp // 2)], dp, 1)
+
+    near_bits = [0] + list(range(2, bits))
+    near_masks = [
+        sum(((j >> (len(near_bits) - 1 - k)) & 1) << b for k, b in enumerate(near_bits))
+        for j in range(dp // 2)
+    ]
+
+    def near_columns(values, where):
+        return pick(values, [where ^ m for m in near_masks], dp, 1)
+
+    def rows_of(values, lo, hi):
+        return values[lo * own_rows : hi * own_rows]
+
+    def near_sum(part):
+        send = part(2, 4).astype(LOW)
+        near, kept = lax.optimization_barrier((flip(send, "tp", 1), part(0, 2)))
+        pair = kept + near
+        return pair[:own_rows], pair[own_rows:].astype(LOW)
+
+    cot = pick(after(cotangent, paired), [spot ^ m for m in ROW_MASKS], len(tp_masks), 0)
+    queries = after(queries, cot)
+    attended, lse = attention_forward(at, pos, queries, blocks, size, 2)
+
+    def branch_terms(lo, hi):
+        return dot(attended[:, lo * own_rows : hi * own_rows], w_out, 0, 0)
+
+    branch, branch_send = near_sum(branch_terms)
+    branch_far = flip(branch_send, "tp", 2)
+    one_rows = after(normed_one, branch_send)
+    one_mine, one_send = columns(one_rows, bit), columns(one_rows, 1 - bit)
+    one_theirs = flip(one_send, "dp", 1)
+    branch = after(branch, one_mine, one_send)
+
+    middle = own(inputs) + (branch + branch_far)
     scale_two = lax.rsqrt(jnp.mean(middle * middle, -1, keepdims=True) + EPSILON)
-
-    def all_rows(mine):
-        pair = jnp.concatenate([mine, flip(mine, "tp", 2)], 0)
-        return jnp.concatenate([pair, flip(pair, "tp", 1)], 0)
-
-    def sum_rows(part):
-        near = flip(part(2, 4).astype(LOW), "tp", 1)
-        pair = part(0, 2) + near
-        return pair[:own_rows] + flip(pair[own_rows:].astype(LOW), "tp", 2)
-
-    normed_two = all_rows((middle * scale_two * norm2_gain).astype(LOW))
+    own_two = (middle * scale_two * norm2_gain).astype(LOW)
+    far_two = flip(own_two, "tp", 2)
+    att_theirs = flip(after(attended, own_two), "dp", 1)
+    cot_late = after(cot, own_two)
+    cot_mine, cot_send = near_columns(cot_late, place), near_columns(cot_late, place ^ 2)
+    cot_theirs = flip(cot_send, "dp", 2)
+    own_two = after(own_two, cot_mine, cot_send)
+    pair_two = jnp.concatenate([own_two, far_two], 0)
+    core_two = flip(pair_two, "tp", 1)
+    grad_hidden = dot(after(cot, pair_two), w_down, 1, 1)
+    normed_two = jnp.concatenate([after(pair_two, grad_hidden), core_two], 0)
+    two_send = columns(normed_two, 1 - bit)
+    two_theirs = flip(two_send, "dp", 1)
+    normed_two = after(normed_two, two_send, one_theirs)
+
     gate_pre = dot(normed_two, w_gate, 1, 0)
     up_pre = dot(normed_two, w_up, 1, 0)
-    cot = pick(cotangent, ROW_MASKS, spot, len(tp_masks), 0)
-    grad_hidden = dot(cot, w_down, 1, 1)
     sigma = jax.nn.sigmoid(gate_pre)
     active = gate_pre * sigma
     hidden = (active * up_pre).astype(LOW)
     grad_gate_pre = (grad_hidden * up_pre * sigma * (1.0 + gate_pre * (1.0 - sigma))).astype(LOW)
     grad_up_pre = (grad_hidden * active).astype(LOW)
-
-    def rows_of(values, lo, hi):
-        return values[lo * own_rows : hi * own_rows]
-
-    grad_normed_two = sum_rows(
-        lambda lo, hi: dot(rows_of(grad_gate_pre, lo, hi), w_gate, 1, 1)
-        + dot(rows_of(grad_up_pre, lo, hi), w_up, 1, 1)
-    )
-    down = sum_rows(lambda lo, hi: dot(rows_of(hidden, lo, hi), w_down, 1, 0))
-    output_rows = (middle + down).astype(LOW)
-
-    half_order = block_order(bits, 1)
-    half_count = len(half_order)
-
-    def gathered(x, grads, left_first=True):
-        mine = pick(x, half_order, place, dp, 1)
-        theirs = flip(pick(x, half_order, place ^ 1, dp, 1), "dp", 1)
-        return [
-            exchange_sum(
-                pair_terms([(mine, g), (theirs, flip(g, "dp", 1))], block, left_first),
-                half_count,
-                bits,
-                1,
-                0 if left_first else 1,
-            )
-            for g in grads
-        ]
-
-    (grad_down,) = gathered(cot, [hidden], False)
-    grad_gate, grad_up = gathered(normed_two, [grad_gate_pre, grad_up_pre])
+    hidden_theirs = flip(hidden, "dp", 2)
+    gate_theirs = flip(grad_gate_pre, "dp", 1)
+
+    gate_late, att_theirs, cot_theirs = lax.optimization_barrier(
+        (grad_gate_pre, att_theirs, cot_theirs)
+    )
+
+    def two_terms(lo, hi):
+        return dot(rows_of(gate_late, lo, hi), w_gate, 1, 1) + dot(
+            rows_of(grad_up_pre, lo, hi), w_up, 1, 1
+        )
+
+    grad_normed_two, two_far_send = near_sum(two_terms)
+    two_far = flip(two_far_send, "tp", 2)
+
+    hidden_late = after(hidden, two_far_send)
+    down, down_send = near_sum(lambda lo, hi: dot(rows_of(hidden_late, lo, hi), w_down, 1, 0))
+    down_far = flip(down_send, "tp", 2)
+    up_theirs = flip(after(grad_up_pre, down_send), "dp", 1)
+    grad_normed_two = after(grad_normed_two, down_send) + two_far
 
     grad_mid_norm, gain_two = norm_back(grad_normed_two, middle, scale_two, norm2_gain)
     grad_middle = own(cotangent).astype(jnp.float32) + grad_mid_norm
     branch_grad = grad_middle.astype(LOW)
-    grad_pieces = [dot(w, branch_grad, 1, 1).astype(LOW) for w in outs]
-    grad_mine = [grad_pieces[0]] + [flip(grad_pieces[m], "tp", m) for m in tp_masks if m]
-    ordered = jnp.zeros(attended.shape, LOW)
-    for m in tp_masks:
-        ordered = lax.dynamic_update_slice_in_dim(
-            ordered, grad_mine[m], (spot ^ m) * own_rows, 1
+    output_rows = (middle + (down + after(down_far, branch_grad))).astype(LOW)
+    grad_far = flip(branch_grad, "tp", 2)
+
+    hidden_late, cot_mine = lax.optimization_barrier((hidden, cot_mine, branch_grad, output_rows))[:2]
+
+    def down_terms(lo, hi):
+        cut = slice(lo * block, hi * block)
+        return dot(cot_mine[:, cut], hidden_late, 0, 0) + dot(
+            cot_theirs[:, cut], hidden_theirs, 0, 0
         )
+
+    count = dp // 2
+    first_send = down_terms(count // 2, count).astype(LOW)
+    grad_pair = jnp.concatenate([after(branch_grad, first_send), grad_far], 0)
+    grad_core = flip(grad_pair, "tp", 1)
+
+    two_mine = columns(after(normed_two, grad_pair), bit)
+    gate_terms = dot(two_mine, grad_gate_pre, 0, 0) + dot(two_theirs, gate_theirs, 0, 0)
+    gate_terms = gate_terms.astype(LOW)
+    grad_gate = parity_sum(gate_terms, 0)
+    branch_all = jnp.concatenate([after(grad_pair, gate_terms), grad_core], 0)
+    grad_attended = dot(w_out, branch_all, 1, 1).astype(LOW)
+
     grads = attention_backward(
-        rank, pos, queries, ordered, attended, lse, cosine, sine, blocks, size, 2
+        at, pos, queries, grad_attended, attended, lse, cosine, sine, blocks, size, 2
     )
     grad_query_rows, kv_total = grads[0], grads[1]
-
-    branch_all = pick(all_rows(branch_grad), block_order(bits, 0), place, dp, 1)
-    att_all = jnp.concatenate([att_pieces[m] for m in ROW_MASKS], 1)
-    grad_out = exchange_sum(
-        lambda lo, hi: dot(att_all, branch_all[:, lo * block : hi * block], 1, 0),
-        dp,
-        bits,
-        0,
-        1,
-    )
-
-    for m in range(1, SPAN):
-        kv_total = kv_total + flip(grads[m + 1], "dp", m)
+    kv_back = [flip(grads[m + 1], "dp", m) for m in range(1, SPAN)]
+
+    two_mine, up_late = lax.optimization_barrier((two_mine, grad_up_pre, grad_query_rows))[:2]
+    up_terms = (dot(two_mine, up_late, 0, 0) + dot(two_theirs, up_theirs, 0, 0)).astype(LOW)
+    grad_up = parity_sum(up_terms, 0)
+
+    kv_total = after(kv_total, up_terms)
+    for got in kv_back:
+        kv_total = kv_total + got
     key_grad = turn_back(kv_total[:size], cosine, sine)
     grad_kv_rows = jnp.concatenate([key_grad, kv_total[size:]], 0).astype(LOW)
-
-    query_core = flip(w_query, "tp", 1)
-    query_far = flip(w_query, "tp", 2)
-    query_all = [w_query, query_core, query_far, flip(query_far, "tp", 1)]
-    w_kv = jnp.concatenate([w_key, w_value], 1)
-    kv_far = flip(w_kv, "tp", 2)
-    kv_all = [w_kv, flip(w_kv, "tp", 1), kv_far, flip(kv_far, "tp", 1)]
-    grad_normed_one = None
-    for m in tp_masks:
-        piece_q = token_block(grad_query_rows, m)
-        piece_kv = token_block(grad_kv_rows, m)
-        if m:
-            piece_q, piece_kv = flip(piece_q, "tp", m), flip(piece_kv, "tp", m)
-        term = dot(piece_q, query_all[m], 0, 1) + dot(piece_kv, kv_all[m], 0, 1)
-        grad_normed_one = term if grad_normed_one is None else grad_normed_one + term
+    proj_rows = jnp.concatenate([grad_query_rows, grad_kv_rows], 0)
+    proj_theirs = flip(proj_rows, "dp", 1)
+
+    w_proj = jnp.concatenate([w_query, w_key, w_value], 1)
+    own_order = pick(proj_rows, [spot ^ m for m in ROW_MASKS], len(tp_masks), 1)
+
+    def one_terms(lo, hi):
+        return dot(own_order[:, lo * own_rows : hi * own_rows], w_proj, 0, 1)
+
+    grad_normed_one, one_far_send = near_sum(one_terms)
+    one_far = flip(one_far_send, "tp", 2)
+
+    got = [flip(after(first_send, one_far_send), "dp", 1)]
+    branch_late = after(branch_all, one_far_send)
+    branch_mine = columns(branch_late, bit)
+    branch_theirs = flip(columns(branch_late, 1 - bit), "dp", 1)
+    grad_normed_one = after(grad_normed_one, branch_mine) + one_far
     grad_in_norm, gain_one = norm_back(
         grad_normed_one, own(inputs), own(scale_one), norm1_gain
     )
     input_rows = grad_middle + grad_in_norm
-
-    grad_rows = jnp.concatenate([grad_query_rows, grad_kv_rows], 0).T
-    (grad_proj,) = gathered(normed_one, [grad_rows])
+    grad_gate = grad_gate.astype(jnp.float32)
+
+    proj_late = after(proj_rows, input_rows, grad_gate)
+    proj_terms = dot(one_mine, proj_late, 0, 1) + dot(one_theirs, proj_theirs, 0, 1)
+    proj_terms = proj_terms.astype(LOW)
+    grad_proj = parity_sum(proj_terms, 0).astype(jnp.float32)
     wide = w_query.shape[1]
 
-    gains = pick(jnp.stack([gain_one, gain_two]), block_order(bits, 0), place, dp, 1)
+    count //= 2
+    for b in near_bits[1:]:
+        send = down_terms(count // 2, count)
+        for other in got:
+            send = send + other[count // 2 * block : count * block]
+        got.append(flip(send.astype(LOW), "dp", 1 << b))
+        count //= 2
+    grad_down = down_terms(0, 1)
+    for other in got:
+        grad_down = grad_down + other[:block]
+
+    out_terms = dot(attended, branch_mine, 1, 0) + dot(att_theirs, branch_theirs, 1, 0)
+    grad_up = grad_up.astype(jnp.float32)
+    grad_out = parity_sum(after(out_terms.astype(LOW), grad_up, proj_terms), 1)
+
+    gains = jnp.stack([gain_one, gain_two])
     for m in (1, 2):
         gains = gains + flip(gains, "tp", m)
+    gains = pick(gains, [place ^ m for m in range(dp)], dp, 1)
     count = dp
-    for bit in range(bits):
+    while count > 1:
         count //= 2
-        gains = gains[:, : count * block] + flip(gains[:, count * block :], "dp", 1 << bit)
+        gains = gains[:, : count * block] + flip(gains[:, count * block :], "dp", count)
 
     return (
         output_rows,
@@ -495,11 +551,11 @@
         grad_proj[:, :wide],
         grad_proj[:, wide : wide + size],
         grad_proj[:, wide + size :],
-        grad_out,
+        grad_out.astype(jnp.float32),
         gains[1],
         grad_gate,
         grad_up,
-        grad_down,
+        grad_down.T,
     )
 
 

time: 581 us -> 405 us (0.70)
  waiting for transfers between devices: 317 us -> 177 us
  matrix products: 124 us -> 71.7 us
  starting transfers between devices: 86.2 us -> 57.7 us
  local copies, waits for them, and re-layouts: 15.3 us -> 31.8 us
  other arithmetic: 18.2 us -> 31.5 us
  between operations: 2.24 us -> 15.3 us
    ppermute x58 -> x34, waiting for transfers between devices: 317 us -> 177 us  [flip(): lax.ppermute(block, axis, [(i, i ^ mask) for i in range(lax.axis_size(axi...]
    dot_general x56 -> x31, matrix products: 124 us -> 71.7 us  [dot(): lax.dot_general(left, right, (((left_dim,), (right_dim,)), ((), ())), pre...]
    ppermute x58 -> x34, starting transfers between devices: 86.2 us -> 57.3 us  [flip(): lax.ppermute(block, axis, [(i, i ^ mask) for i in range(lax.axis_size(axi...]
    unnamed x125 -> x159, local copies, waits for them, and re-layouts: 4.77 us -> 19.6 us
    convert_element_type x1 -> x5, other arithmetic: 0.15 us -> 7.59 us  [the longest x1 2.39 us: shards(): grad_gate = grad_gate.astype(jnp.float32)]
  transfers between devices with their start and end apart: 58 -> 38, of which waited for: 25 -> 17; matrix products, arithmetic and copies ran while one was open for 27% -> 26% of each run, Pallas kernels for 2% -> 2%
where the time goes in v2:
time: 405 us; the launch traced here: 399 us
  waiting for transfers between devices  177 us (44%)
  matrix products  71.7 us (18%)
  starting transfers between devices  57.7 us (14%)
  local copies, waits for them, and re-layouts  31.8 us (8%)
  other arithmetic  31.5 us (8%)
  between operations  15.3 us (4%)
  Pallas kernels  14.1 us (3%)
    ppermute x34, waiting for transfers between devices, flip(): lax.ppermute(block, axis, [(i, i ^ mask) for i in range(lax.axis_size(axi...  177 us
    dot_general x31, matrix products, dot(): lax.dot_general(left, right, (((left_dim,), (right_dim,)), ((), ())), pre...  71.7 us
    ppermute x34, starting transfers between devices, flip(): lax.ppermute(block, axis, [(i, i ^ mask) for i in range(lax.axis_size(axi...  57.3 us
    unnamed x159, local copies, waits for them, and re-layouts  19.6 us
  transfers between devices with their start and end apart: 38, of which 17 were waited for; matrix products, arithmetic and copies ran while one was open for 26% of the time, Pallas kernels for 2%

profile of v2, /device:TPU:0, one launch (start us, length us, event | category | flops | bytes accessed | tf_op | source)
XLA Modules:
  0.0 399.5 jit_solution(4435707951117551590)
XLA Ops:
  7.3 2.2 multiply_reduce_fusion
  13.3 3.0 collective-permute-start
  16.3 1.6 collective-permute-start.1
  18.2 4.5 %fusion.66 = f32[512,512]{0,1:T(8,128)} fusion(bf16[512,2048]{1,0:T(8,128)(2,1)} %copy-done.18, bf16[2048,512]{1,0:T(8,128)(2,1)} %param.15), kind=kOutput, calls=%fused_computation.196 | convolution fusion | flops 1073741824 | bytes 5242880 | tf_op jit(solution)/shard_map/dot_general | solution.py:22
  24.8 1.6 pad_maximum_fusion.1
  29.7 6.8 %attention_forward.1 = (bf16[512,512]{1,0:T(8,128)(2,1)S(1)}, f32[8,1,512]{2,1,0:T(1,128)S(1)}) custom-call(s32[2]{0:T(128)S(1)} %pad_add_fusion.at_ref, s32[1,512]{1,0:T(1,128)S(1)} %bitcast.66, bf16[512,512]{1,0:T(8,128)(2,1)S(1)} %bitcast.64, bf16[128,512]{1,0:T(8,128)(2,1)S(1)} %pad_maximum_fusion.13.kv0, bf16[128,512]{1,0:T(8,128)(2,1)S(1)} %collective-permute-done.kv1, ...), custom_call_target="tpu_custom_call" | custom-call | flops 134217728 | bytes 1048576 | tf_op jit(solution)/shard_map/attention_forward/pallas_call | solution.py:210
  38.1 1.9 collective-permute-done.3
  42.7 1.9 collective-permute-start.4
  44.6 4.1 %convert_element_type.131 = f32[512,2048]{1,0:T(8,128)} convert(bf16[512,2048]{1,0:T(8,128)(2,1)} %param.12) | non-fusion elementwise | flops 1048576 | bytes 6291456 | tf_op jit(solution)/shard_map/convert_element_type | solution.py:355
  48.7 1.6 copy-done.19
  51.7 5.8 %collective-permute-start.7 = (bf16[512,1024]{1,0:T(8,128)(2,1)S(1)}, bf16[512,1024]{1,0:T(8,128)(2,1)S(1)}, u32[]{:S(2)}, u32[]{:S(2)}) collective-permute-start(bf16[512,1024]{1,0:T(8,128)(2,1)S(1)} %pad_maximum_fusion.3), channel_id=1, source_target_pairs={{0,4},{4,0},{8,12},{12,8},{16,20},{20,16},{24,28},{28,24},{1,5},{5... | collective-permute-start | bytes 3145736 | tf_op jit(solution)/shard_map/ppermute | solution.py:18
  57.5 1.8 multiply_reduce_fusion.5
  61.4 10.1 %collective-permute-start.9 = (bf16[512,1024]{1,0:T(8,128)(2,1)S(1)}, bf16[512,1024]{1,0:T(8,128)(2,1)S(1)}, u32[]{:S(2)}, u32[]{:S(2)}) collective-permute-start(bf16[512,1024]{1,0:T(8,128)(2,1)S(1)} %pad_maximum_fusion.5), channel_id=1, source_target_pairs={{0,8},{4,12},{8,0},{12,4},{16,24},{20,28},{24,16},{28,20},{1,9},{5... | collective-permute-start | bytes 3145736 | tf_op jit(solution)/shard_map/ppermute | solution.py:18
  71.6 5.8 %collective-permute-start.8 = (bf16[512,512]{1,0:T(8,128)(2,1)S(1)}, bf16[512,512]{1,0:T(8,128)(2,1)S(1)}, u32[]{:S(2)}, u32[]{:S(2)}) collective-permute-start(bf16[512,512]{1,0:T(8,128)(2,1)S(1)} %get-tuple-element.68.o_in), channel_id=1, source_target_pairs={{0,4},{4,0},{8,12},{12,8},{16,20},{20,16},{24,28},{28,24},{1,5},{5... | collective-permute-start | bytes 1572872 | tf_op jit(solution)/shard_map/ppermute | solution.py:18
  77.7 3.5 fusion.68
  81.7 5.1 %fusion.69 = f32[512,1408]{1,0:T(8,128)} fusion(bf16[512,2048]{1,0:T(8,128)(2,1)S(1)} %constant_dynamic-update-slice_fusion.2, bf16[2048,1408]{1,0:T(8,128)(2,1)S(1)} %bitcast.82), kind=kOutput, calls=%fused_computation.199 | convolution fusion | flops 2952790016 | bytes 10747904 | tf_op jit(solution)/shard_map/dot_general | solution.py:22
  86.8 6.6 %multiply_convert_fusion.2 = (bf16[512,1408]{1,0:T(8,128)(2,1)S(1)}, bf16[512,1408]{1,0:T(8,128)(2,1)S(1)}, bf16[512,1408]{1,0:T(8,128)(2,1)S(1)}) fusion(f32[512,1408]{1,0:T(8,128)S(1)} %fusion.68, f32[512,1408]{1,0:T(8,128)} %fusion.69, bf16[512,2048]{1,0:T(8,128)(2,1)S(1)} %constant_dynamic-update-slice_fusion.2, bf16[2048,1408]{1,0:T(8,128)(2,1)S(1)} %bitcast.84), kind=kOutput, calls=%fused_computation.7 | convolution fusion | flops 2963603456 | bytes 17956864 | tf_op jit(solution)/shard_map/dot_general | solution.py:22
  93.9 1.8 fusion.16
  95.7 1.8 fusion.6
  97.7 1.8 fusion.14
  99.6 1.8 convolution_add_fusion.3
  101.9 4.6 %convolution_convert_fusion.2 = bf16[256,2048]{1,0:T(8,128)(2,1)S(1)} fusion(bf16[1408,2048]{1,0:T(8,128)(2,1)} %param.22, bf16[512,1408]{1,0:T(8,128)(2,1)S(1)} %get-tuple-element.78), kind=kOutput, calls=%fused_computation.25 | convolution fusion | flops 1476919296 | bytes 7536640 | tf_op jit(solution)/shard_map/dot_general | solution.py:22
  107.0 9.4 %collective-permute-start.14 = (bf16[512,1408]{1,0:T(8,128)(2,1)S(1)}, bf16[512,1408]{1,0:T(8,128)(2,1)S(1)}, u32[]{:S(2)}, u32[]{:S(2)}) collective-permute-start(bf16[512,1408]{1,0:T(8,128)(2,1)S(1)} %get-tuple-element.78), channel_id=1, source_target_pairs={{0,8},{4,12},{8,0},{12,4},{16,24},{20,28},{24,16},{28,20},{1,9},{5... | collective-permute-start | bytes 4325384 | tf_op jit(solution)/shard_map/ppermute | solution.py:18
  116.4 2.1 collective-permute-start.17
  119.2 1.8 fusion.18
  121.5 1.5 collective-permute-start.12
  123.0 10.5 %collective-permute-done.13 = bf16[128,2048]{1,0:T(8,128)(2,1)S(1)} collective-permute-done((bf16[128,2048]{1,0:T(8,128)(2,1)S(1)}, bf16[128,2048]{1,0:T(8,128)(2,1)S(1)}, u32[]{:S(2)}, u32[]{:S(2)}) %collective-permute-start.13) | collective-permute-done | bytes 524320 | tf_op jit(solution)/shard_map/ppermute | solution.py:18
  133.9 2.4 fusion.63
  136.8 7.9 %collective-permute-done.12 = bf16[128,2048]{1,0:T(8,128)(2,1)S(1)} collective-permute-done((bf16[128,2048]{1,0:T(8,128)(2,1)S(1)}, bf16[128,2048]{1,0:T(8,128)(2,1)S(1)}, u32[]{:S(2)}, u32[]{:S(2)}) %collective-permute-start.12) | collective-permute-done | bytes 524320 | tf_op jit(solution)/shard_map/ppermute | solution.py:18
  148.3 2.2 fusion
  151.3 3.2 collective-permute-done.15
  155.5 2.0 fusion.61
  157.6 14.9 %collective-permute-done.16 = bf16[512,1024]{1,0:T(8,128)(2,1)S(1)} collective-permute-done((bf16[512,1024]{1,0:T(8,128)(2,1)S(1)}, bf16[512,1024]{1,0:T(8,128)(2,1)S(1)}, u32[]{:S(2)}, u32[]{:S(2)}) %collective-permute-start.16) | collective-permute-done | bytes 1048608 | tf_op jit(solution)/shard_map/ppermute | solution.py:18
  173.5 3.6 add_convert_fusion.1
  177.2 1.8 collective-permute-start.19
  183.2 7.3 %attention_backward.1 = (bf16[512,512]{1,0:T(8,128)(2,1)S(1)}, f32[128,512]{1,0:T(8,128)S(1)}, bf16[128,512]{1,0:T(8,128)(2,1)S(1)}, bf16[128,512]{1,0:T(8,128)(2,1)S(1)}, bf16[128,512]{1,0:T(8,128)(2,1)S(1)}) custom-call(s32[2]{0:T(128)S(1)} %pad_add_fusion.at_ref, s32[1,512]{1,0:T(1,128)S(1)} %bitcast.67, bf16[512,512]{1,0:T(8,128)(2,1)S(1)} %bitcast.65, ...), custom_call_target="tpu_custom_call" | custom-call | flops 134217728 | bytes 2621440 | tf_op jit(solution)/shard_map/attention_backward/pallas_call | solution.py:245
  190.6 1.8 fusion.70
  192.5 18.9 %collective-permute-done.19 = bf16[512,1408]{1,0:T(8,128)(2,1)S(1)} collective-permute-done((bf16[512,1408]{1,0:T(8,128)(2,1)}, bf16[512,1408]{1,0:T(8,128)(2,1)S(1)}, u32[]{:S(2)}, u32[]{:S(2)}) %collective-permute-start.19) | collective-permute-done | bytes 1441824 | tf_op jit(solution)/shard_map/ppermute | solution.py:18
  211.4 3.6 add_convert_fusion
  215.4 1.8 collective-permute-start.20
  218.9 2.0 copy.24
  220.9 2.0 copy.25
  222.9 5.7 %collective-permute-done.21 = bf16[128,512]{1,0:T(8,128)(2,1)} collective-permute-done((bf16[128,512]{1,0:T(8,128)(2,1)}, bf16[128,512]{1,0:T(8,128)(2,1)}, u32[]{:S(2)}, u32[]{:S(2)}) %collective-permute-start.21) | collective-permute-done | bytes 131104 | tf_op jit(solution)/shard_map/ppermute | solution.py:18
  228.6 7.5 %collective-permute-done.22 = bf16[128,512]{1,0:T(8,128)(2,1)} collective-permute-done((bf16[128,512]{1,0:T(8,128)(2,1)S(1)}, bf16[128,512]{1,0:T(8,128)(2,1)}, u32[]{:S(2)}, u32[]{:S(2)}) %collective-permute-start.22) | collective-permute-done | bytes 131104 | tf_op jit(solution)/shard_map/ppermute | solution.py:18
  247.0 11.1 %collective-permute-done.24 = bf16[128,2048]{1,0:T(8,128)(2,1)S(1)} collective-permute-done((bf16[128,2048]{1,0:T(8,128)(2,1)S(1)}, bf16[128,2048]{1,0:T(8,128)(2,1)S(1)}, u32[]{:S(2)}, u32[]{:S(2)}) %collective-permute-start.24) | collective-permute-done | bytes 524320 | tf_op jit(solution)/shard_map/ppermute | solution.py:18
  259.9 2.4 convert_element_type.163
  262.3 2.2 fusion.62
  264.5 3.3 add_convert_fusion.2
  267.8 2.6 constant_dynamic-slice_fusion.15
  272.3 1.5 collective-permute-start.26
  276.5 4.5 %collective-permute-done.27 = f32[2,1024]{1,0:T(2,128)S(1)} collective-permute-done((f32[2,1024]{1,0:T(2,128)S(1)}, f32[2,1024]{1,0:T(2,128)S(1)}, u32[]{:S(2)}, u32[]{:S(2)}) %collective-permute-start.27) | collective-permute-done | bytes 8224 | tf_op jit(solution)/shard_map/ppermute | solution.py:18
  281.2 16.7 %collective-permute-done.31 = bf16[512,1024]{1,0:T(8,128)(2,1)} collective-permute-done((bf16[512,1024]{1,0:T(8,128)(2,1)}, bf16[512,1024]{1,0:T(8,128)(2,1)}, u32[]{:S(2)}, u32[]{:S(2)}) %collective-permute-start.31) | collective-permute-done | bytes 1048608 | tf_op jit(solution)/shard_map/ppermute | solution.py:18
  297.9 2.0 fusion.71
  299.9 1.7 add_convert_fusion.3
  301.6 2.3 convert_element_type.167
  303.9 2.2 fusion.33
  306.9 21.5 %collective-permute-done.32 = bf16[512,1408]{1,0:T(8,128)(2,1)} collective-permute-done((bf16[512,1408]{1,0:T(8,128)(2,1)}, bf16[512,1408]{1,0:T(8,128)(2,1)}, u32[]{:S(2)}, u32[]{:S(2)}) %collective-permute-start.32) | collective-permute-done | bytes 1441824 | tf_op jit(solution)/shard_map/ppermute | solution.py:18
  328.4 1.7 fusion.7
  330.2 1.5 fusion.36
  332.4 48.5 %collective-permute-done.33 = bf16[256,1408]{1,0:T(8,128)(2,1)S(1)} collective-permute-done((bf16[256,1408]{1,0:T(8,128)(2,1)S(1)}, bf16[256,1408]{1,0:T(8,128)(2,1)S(1)}, u32[]{:S(2)}, u32[]{:S(2)}) %collective-permute-start.33) | collective-permute-done | bytes 720928 | tf_op jit(solution)/shard_map/ppermute | solution.py:18
  380.9 2.9 fusion.5
  383.8 2.9 copy.28
  389.1 1.8 slice.200
  390.9 1.8 convert_element_type.168
  (288 shorter events, 55.0 us)
Async XLA Ops:
  7.2 29.4 %copy-start = (bf16[512,2048]{1,0:T(8,128)(2,1)S(1)}, bf16[512,2048]{1,0:T(8,128)(2,1)}, u32[]{:S(2)}) copy-start(bf16[512,2048]{1,0:T(8,128)(2,1)} %param.18) | copy-start | bytes 6291460
  7.2 252.6 %reduce-scatter.5.cloned.1.call-start = ((), (), s32[]{:S(2)}) async-start(), calls=%async_computation.4 | async-start | bytes 3604480 | tf_op jit(solution)/shard_map/reduce_scatter | solution.py:299
  13.3 13.2 %collective-permute-start = (bf16[128,512]{1,0:T(8,128)(2,1)S(1)}, bf16[128,512]{1,0:T(8,128)(2,1)S(1)}, u32[]{:S(2)}, u32[]{:S(2)}) collective-permute-start(bf16[128,512]{1,0:T(8,128)(2,1)S(1)} %pad_maximum_fusion.13.kv0), channel_id=1, source_target_pairs={{0,4},{4,0},{8,12},{12,8},{16,20},{20,16},{24,28},{28,24},{1,5},{5... | collective-permute-start | bytes 393224 | tf_op jit(solution)/shard_map/ppermute | solution.py:18
  16.3 10.2 %collective-permute-start.1 = (bf16[128,512]{1,0:T(8,128)(2,1)S(1)}, bf16[128,512]{1,0:T(8,128)(2,1)S(1)}, u32[]{:S(2)}, u32[]{:S(2)}) collective-permute-start(bf16[128,512]{1,0:T(8,128)(2,1)S(1)} %pad_maximum_fusion.13.kv0), channel_id=1, source_target_pairs={{0,8},{4,12},{8,0},{12,4},{16,24},{20,28},{24,16},{28,20},{1,9},{5... | collective-permute-start | bytes 393224 | tf_op jit(solution)/shard_map/ppermute | solution.py:18
  17.9 9.3 %collective-permute-start.2 = (bf16[128,512]{1,0:T(8,128)(2,1)S(1)}, bf16[128,512]{1,0:T(8,128)(2,1)S(1)}, u32[]{:S(2)}, u32[]{:S(2)}) collective-permute-start(bf16[128,512]{1,0:T(8,128)(2,1)S(1)} %pad_maximum_fusion.13.kv0), channel_id=1, source_target_pairs={{0,12},{4,8},{8,4},{12,0},{16,28},{20,24},{24,20},{28,16},{1,13},{... | collective-permute-start | bytes 393224 | tf_op jit(solution)/shard_map/ppermute | solution.py:18
  37.3 2.7 collective-permute-start.3
  42.7 14.8 %collective-permute-start.4 = (bf16[128,2048]{1,0:T(8,128)(2,1)}, bf16[128,2048]{1,0:T(8,128)(2,1)}, u32[]{:S(2)}, u32[]{:S(2)}) collective-permute-start(bf16[128,2048]{1,0:T(8,128)(2,1)} %slice.263), channel_id=1, source_target_pairs={{0,2},{1,3},{2,0},{3,1},{4,6},{5,7},{6,4},{7,5},{8,10},{9,11},{10,... | collective-permute-start | bytes 1572872 | tf_op jit(solution)/shard_map/ppermute | solution.py:18
  51.7 30.0 %collective-permute-start.7 = (bf16[512,1024]{1,0:T(8,128)(2,1)S(1)}, bf16[512,1024]{1,0:T(8,128)(2,1)S(1)}, u32[]{:S(2)}, u32[]{:S(2)}) collective-permute-start(bf16[512,1024]{1,0:T(8,128)(2,1)S(1)} %pad_maximum_fusion.3), channel_id=1, source_target_pairs={{0,4},{4,0},{8,12},{12,8},{16,20},{20,16},{24,28},{28,24},{1,5},{5... | collective-permute-start | bytes 3145736 | tf_op jit(solution)/shard_map/ppermute | solution.py:18
  57.5 20.1 %slice-start.5 = ((s8[5767168]{0:T(1024)(128)(4,1)}), s8[4194304]{0:T(1024)(128)(4,1)S(1)}, s32[]{:S(2)}) async-start(s8[5767168]{0:T(1024)(128)(4,1)} %bitcast.85), calls=%async_computation.13 | async-start | bytes 8388608
  59.5 18.2 %slice-start.6 = ((s8[5767168]{0:T(1024)(128)(4,1)}), s8[1572864]{0:T(1024)(128)(4,1)S(1)}, s32[]{:S(2)}) async-start(s8[5767168]{0:T(1024)(128)(4,1)} %bitcast.85), calls=%async_computation.14 | async-start | bytes 3145728
  59.5 18.0 %collective-permute-start.5 = (bf16[128,2048]{1,0:T(8,128)(2,1)S(1)}, bf16[128,2048]{1,0:T(8,128)(2,1)S(1)}, u32[]{:S(2)}, u32[]{:S(2)}) collective-permute-start(bf16[128,2048]{1,0:T(8,128)(2,1)S(1)} %multiply_convert_fusion.4), channel_id=1, source_target_pairs={{0,2},{1,3},{2,0},{3,1},{4,6},{5,7},{6,4},{7,5},{8,10},{9,11},{10,... | collective-permute-start | bytes 1572872 | tf_op jit(solution)/shard_map/ppermute | solution.py:18
  61.4 32.5 %collective-permute-start.9 = (bf16[512,1024]{1,0:T(8,128)(2,1)S(1)}, bf16[512,1024]{1,0:T(8,128)(2,1)S(1)}, u32[]{:S(2)}, u32[]{:S(2)}) collective-permute-start(bf16[512,1024]{1,0:T(8,128)(2,1)S(1)} %pad_maximum_fusion.5), channel_id=1, source_target_pairs={{0,8},{4,12},{8,0},{12,4},{16,24},{20,28},{24,16},{28,20},{1,9},{5... | collective-permute-start | bytes 3145736 | tf_op jit(solution)/shard_map/ppermute | solution.py:18
  71.6 74.1 %copy-start.28 = (bf16[512,1024]{1,0:T(8,128)(2,1)}, bf16[512,1024]{1,0:T(8,128)(2,1)S(1)}, u32[]{:S(2)}) copy-start(bf16[512,1024]{1,0:T(8,128)(2,1)S(1)} %pad_maximum_fusion.4) | copy-start | bytes 3145732
  71.6 21.8 %collective-permute-start.8 = (bf16[512,512]{1,0:T(8,128)(2,1)S(1)}, bf16[512,512]{1,0:T(8,128)(2,1)S(1)}, u32[]{:S(2)}, u32[]{:S(2)}) collective-permute-start(bf16[512,512]{1,0:T(8,128)(2,1)S(1)} %get-tuple-element.68.o_in), channel_id=1, source_target_pairs={{0,4},{4,0},{8,12},{12,8},{16,20},{20,16},{24,28},{28,24},{1,5},{5... | collective-permute-start | bytes 1572872 | tf_op jit(solution)/shard_map/ppermute | solution.py:18
  77.6 3.7 collective-permute-start.6
  93.4 52.3 %copy-start.21 = (bf16[512,1408]{1,0:T(8,128)(2,1)}, bf16[512,1408]{1,0:T(8,128)(2,1)S(1)}, u32[]{:S(2)}) copy-start(bf16[512,1408]{1,0:T(8,128)(2,1)S(1)} %get-tuple-element.78) | copy-start | bytes 4325380
  93.8 54.4 %copy-start.36 = (bf16[512,1024]{1,0:T(8,128)(2,1)}, bf16[512,1024]{1,0:T(8,128)(2,1)S(1)}, u32[]{:S(2)}) copy-start(bf16[512,1024]{1,0:T(8,128)(2,1)S(1)} %collective-permute-done.9) | copy-start | bytes 3145732
  97.5 3.9 collective-permute-start.10
  101.8 17.4 %slice-start.7 = ((s8[5767168]{0:T(1024)(128)(4,1)}), s8[4194304]{0:T(1024)(128)(4,1)S(1)}, s32[]{:S(2)}) async-start(s8[5767168]{0:T(1024)(128)(4,1)} %bitcast.87), calls=%async_computation.15 | async-start | bytes 8388608
  101.9 17.4 %slice-start.8 = ((s8[5767168]{0:T(1024)(128)(4,1)}), s8[1572864]{0:T(1024)(128)(4,1)S(1)}, s32[]{:S(2)}) async-start(s8[5767168]{0:T(1024)(128)(4,1)} %bitcast.87), calls=%async_computation.16 | async-start | bytes 3145728
  106.5 14.5 %collective-permute-start.11 = (bf16[256,2048]{1,0:T(8,128)(2,1)S(1)}, bf16[256,2048]{1,0:T(8,128)(2,1)S(1)}, u32[]{:S(2)}, u32[]{:S(2)}) collective-permute-start(bf16[256,2048]{1,0:T(8,128)(2,1)S(1)} %convolution_convert_fusion.2), channel_id=1, source_target_pairs={{0,1},{1,0},{2,3},{3,2},{4,5},{5,4},{6,7},{7,6},{8,9},{9,8},{10,11... | collective-permute-start | bytes 3145736 | tf_op jit(solution)/shard_map/ppermute | solution.py:18
  107.0 41.2 %collective-permute-start.14 = (bf16[512,1408]{1,0:T(8,128)(2,1)S(1)}, bf16[512,1408]{1,0:T(8,128)(2,1)S(1)}, u32[]{:S(2)}, u32[]{:S(2)}) collective-permute-start(bf16[512,1408]{1,0:T(8,128)(2,1)S(1)} %get-tuple-element.78), channel_id=1, source_target_pairs={{0,8},{4,12},{8,0},{12,4},{16,24},{20,28},{24,16},{28,20},{1,9},{5... | collective-permute-start | bytes 4325384 | tf_op jit(solution)/shard_map/ppermute | solution.py:18
  116.4 56.1 %collective-permute-start.17 = (bf16[512,1408]{1,0:T(8,128)(2,1)S(1)}, bf16[512,1408]{1,0:T(8,128)(2,1)S(1)}, u32[]{:S(2)}, u32[]{:S(2)}) collective-permute-start(bf16[512,1408]{1,0:T(8,128)(2,1)S(1)} %get-tuple-element.69), channel_id=1, source_target_pairs={{0,4},{4,0},{8,12},{12,8},{16,20},{20,16},{24,28},{28,24},{1,5},{5... | collective-permute-start | bytes 4325384 | tf_op jit(solution)/shard_map/ppermute | solution.py:18
  118.5 54.0 %collective-permute-start.16 = (bf16[512,1024]{1,0:T(8,128)(2,1)S(1)}, bf16[512,1024]{1,0:T(8,128)(2,1)S(1)}, u32[]{:S(2)}, u32[]{:S(2)}) collective-permute-start(bf16[512,1024]{1,0:T(8,128)(2,1)S(1)} %pad_maximum_fusion.6), channel_id=1, source_target_pairs={{0,4},{4,0},{8,12},{12,8},{16,20},{20,16},{24,28},{28,24},{1,5},{5... | collective-permute-start | bytes 3145736 | tf_op jit(solution)/shard_map/ppermute | solution.py:18
  118.6 14.9 %collective-permute-start.13 = (bf16[128,2048]{1,0:T(8,128)(2,1)S(1)}, bf16[128,2048]{1,0:T(8,128)(2,1)S(1)}, u32[]{:S(2)}, u32[]{:S(2)}) collective-permute-start(bf16[128,2048]{1,0:T(8,128)(2,1)S(1)} %slice.262), channel_id=1, source_target_pairs={{0,2},{1,3},{2,0},{3,1},{4,6},{5,7},{6,4},{7,5},{8,10},{9,11},{10,... | collective-permute-start | bytes 1572872 | tf_op jit(solution)/shard_map/ppermute | solution.py:18
  121.5 23.3 %collective-permute-start.12 = (bf16[128,2048]{1,0:T(8,128)(2,1)S(1)}, bf16[128,2048]{1,0:T(8,128)(2,1)S(1)}, u32[]{:S(2)}, u32[]{:S(2)}) collective-permute-start(bf16[128,2048]{1,0:T(8,128)(2,1)S(1)} %slice.261), channel_id=1, source_target_pairs={{0,2},{1,3},{2,0},{3,1},{4,6},{5,7},{6,4},{7,5},{8,10},{9,11},{10,... | collective-permute-start | bytes 1572872 | tf_op jit(solution)/shard_map/ppermute | solution.py:18
  136.3 18.2 %collective-permute-start.15 = (bf16[128,2048]{1,0:T(8,128)(2,1)S(1)}, bf16[128,2048]{1,0:T(8,128)(2,1)S(1)}, u32[]{:S(2)}, u32[]{:S(2)}) collective-permute-start(bf16[128,2048]{1,0:T(8,128)(2,1)S(1)} %get-tuple-element.80), channel_id=1, source_target_pairs={{0,2},{1,3},{2,0},{3,1},{4,6},{5,7},{6,4},{7,5},{8,10},{9,11},{10,... | collective-permute-start | bytes 1572872 | tf_op jit(solution)/shard_map/ppermute | solution.py:18
  177.1 124.5 %reduce-scatter.9.cloned.1.call-start = ((), (), s32[]{:S(2)}) async-start(), calls=%async_computation.6 | async-start | bytes 3604480 | tf_op jit(solution)/shard_map/reduce_scatter | solution.py:299
  177.1 4.5 %collective-permute-start.18 = (bf16[256,2048]{1,0:T(8,128)(2,1)}, bf16[256,2048]{1,0:T(8,128)(2,1)S(1)}, u32[]{:S(2)}, u32[]{:S(2)}) collective-permute-start(bf16[256,2048]{1,0:T(8,128)(2,1)} %constant_dynamic-update-slice_fusion.4), channel_id=1, source_target_pairs={{0,1},{1,0},{2,3},{3,2},{4,5},{5,4},{6,7},{7,6},{8,9},{9,8},{10,11... | collective-permute-start | bytes 3145736 | tf_op jit(solution)/shard_map/ppermute | solution.py:18
  177.2 34.2 %collective-permute-start.19 = (bf16[512,1408]{1,0:T(8,128)(2,1)}, bf16[512,1408]{1,0:T(8,128)(2,1)S(1)}, u32[]{:S(2)}, u32[]{:S(2)}) collective-permute-start(bf16[512,1408]{1,0:T(8,128)(2,1)} %copy-done.34), channel_id=1, source_target_pairs={{0,4},{4,0},{8,12},{12,8},{16,20},{20,16},{24,28},{28,24},{1,5},{5... | collective-permute-start | bytes 4325384 | tf_op jit(solution)/shard_map/ppermute | solution.py:18
  190.6 20.8 %copy-start.32 = (bf16[512,1024]{1,0:T(8,128)(2,1)S(1)}, bf16[512,1024]{1,0:T(8,128)(2,1)}, u32[]{:S(2)}) copy-start(bf16[512,1024]{1,0:T(8,128)(2,1)} %copy-done.31) | copy-start | bytes 3145732
  215.1 21.1 %copy-start.10 = (f32[128,512]{1,0:T(8,128)S(1)}, f32[128,512]{1,0:T(8,128)}, u32[]{:S(2)}) copy-start(f32[128,512]{1,0:T(8,128)} %copy-done.9) | copy-start | bytes 786436
  215.1 22.2 %copy-start.62 = (f32[512]{0:T(512)S(1)}, f32[512]{0:T(512)}, u32[]{:S(2)}) copy-start(f32[512]{0:T(512)} %copy-done.61) | copy-start | bytes 6148
  215.1 22.2 %copy-start.65 = (f32[32]{0:T(128)S(1)}, f32[32]{0:T(128)}, u32[]{:S(2)}) copy-start(f32[32]{0:T(128)} %copy-done.64) | copy-start | bytes 388
  215.1 22.5 %copy-start.2 = (bf16[512,512]{1,0:T(8,128)(2,1)S(1)}, bf16[512,512]{1,0:T(8,128)(2,1)}, u32[]{:S(2)}) copy-start(bf16[512,512]{1,0:T(8,128)(2,1)} %copy-done.1) | copy-start | bytes 1572868
  215.1 171.6 %reduce-scatter.7.cloned.1.call-start = ((), (), s32[]{:S(2)}) async-start(), calls=%async_computation.5 | async-start | bytes 1638400 | tf_op jit(solution)/shard_map/reduce_scatter | solution.py:299
  215.4 7.5 %collective-permute-start.20 = (bf16[128,512]{1,0:T(8,128)(2,1)}, bf16[128,512]{1,0:T(8,128)(2,1)}, u32[]{:S(2)}, u32[]{:S(2)}) collective-permute-start(bf16[128,512]{1,0:T(8,128)(2,1)} %copy-done.17), channel_id=1, source_target_pairs={{0,4},{4,0},{8,12},{12,8},{16,20},{20,16},{24,28},{28,24},{1,5},{5... | collective-permute-start | bytes 393224 | tf_op jit(solution)/shard_map/ppermute | solution.py:18
  217.2 11.4 %collective-permute-start.21 = (bf16[128,512]{1,0:T(8,128)(2,1)}, bf16[128,512]{1,0:T(8,128)(2,1)}, u32[]{:S(2)}, u32[]{:S(2)}) collective-permute-start(bf16[128,512]{1,0:T(8,128)(2,1)} %copy-done.16), channel_id=1, source_target_pairs={{0,8},{4,12},{8,0},{12,4},{16,24},{20,28},{24,16},{28,20},{1,9},{5... | collective-permute-start | bytes 393224 | tf_op jit(solution)/shard_map/ppermute | solution.py:18
  217.6 18.6 %collective-permute-start.22 = (bf16[128,512]{1,0:T(8,128)(2,1)S(1)}, bf16[128,512]{1,0:T(8,128)(2,1)}, u32[]{:S(2)}, u32[]{:S(2)}) collective-permute-start(bf16[128,512]{1,0:T(8,128)(2,1)S(1)} %copy-done.15), channel_id=1, source_target_pairs={{0,12},{4,8},{8,4},{12,0},{16,28},{20,24},{24,20},{28,16},{1,13},{... | collective-permute-start | bytes 393224 | tf_op jit(solution)/shard_map/ppermute | solution.py:18
  222.9 16.9 %copy-start.48 = (bf16[2048,64]{1,0:T(8,128)(2,1)S(1)}, bf16[2048,64]{1,0:T(8,128)(2,1)}, u32[]{:S(2)}) copy-start(bf16[2048,64]{1,0:T(8,128)(2,1)} %copy.24) | copy-start | bytes 786436
  222.9 16.9 %copy-start.49 = (bf16[2048,64]{1,0:T(8,128)(2,1)S(1)}, bf16[2048,64]{1,0:T(8,128)(2,1)}, u32[]{:S(2)}) copy-start(bf16[2048,64]{1,0:T(8,128)(2,1)} %copy.25) | copy-start | bytes 786436
  222.9 16.9 %copy-start.66 = (bf16[2048,512]{1,0:T(8,128)(2,1)S(1)}, bf16[2048,512]{1,0:T(8,128)(2,1)}, u32[]{:S(2)}) copy-start(bf16[2048,512]{1,0:T(8,128)(2,1)} %param.15) | copy-start | bytes 6291460
  240.9 2.7 collective-permute-start.23
  243.7 14.5 %copy-start.25 = (f32[512,2048]{1,0:T(8,128)S(1)}, f32[512,2048]{1,0:T(8,128)}, u32[]{:S(2)}) copy-start(f32[512,2048]{1,0:T(8,128)} %convert_element_type.131) | copy-start | bytes 12582916
  244.0 14.1 %copy-start.60 = (f32[2048]{0:T(1024)S(1)}, f32[2048]{0:T(1024)}, u32[]{:S(2)}) copy-start(f32[2048]{0:T(1024)} %param.14) | copy-start | bytes 24580
  244.1 14.0 %collective-permute-start.24 = (bf16[128,2048]{1,0:T(8,128)(2,1)S(1)}, bf16[128,2048]{1,0:T(8,128)(2,1)S(1)}, u32[]{:S(2)}, u32[]{:S(2)}) collective-permute-start(bf16[128,2048]{1,0:T(8,128)(2,1)S(1)} %slice.260), channel_id=1, source_target_pairs={{0,2},{1,3},{2,0},{3,1},{4,6},{5,7},{6,4},{7,5},{8,10},{9,11},{10,... | collective-permute-start | bytes 1572872 | tf_op jit(solution)/shard_map/ppermute | solution.py:18
  246.3 18.2 %collective-permute-start.30 = (bf16[640,512]{1,0:T(8,128)(2,1)}, bf16[640,512]{1,0:T(8,128)(2,1)}, u32[]{:S(2)}, u32[]{:S(2)}) collective-permute-start(bf16[640,512]{1,0:T(8,128)(2,1)} %pad_maximum_fusion.12), channel_id=1, source_target_pairs={{0,4},{4,0},{8,12},{12,8},{16,20},{20,16},{24,28},{28,24},{1,5},{5... | collective-permute-start | bytes 1966088 | tf_op jit(solution)/shard_map/ppermute | solution.py:18
  267.8 123.2 %reduce-scatter.11.cloned.1.call-start = ((), (), s32[]{:S(2)}) async-start(), calls=%async_computation.7 | async-start | bytes 1310720 | tf_op jit(solution)/shard_map/reduce_scatter | solution.py:299
  270.4 27.5 %copy-start.47 = (bf16[512,512]{1,0:T(8,128)(2,1)S(1)}, bf16[512,512]{1,0:T(8,128)(2,1)}, u32[]{:S(2)}) copy-start(bf16[512,512]{1,0:T(8,128)(2,1)} %copy-done.46) | copy-start | bytes 1572868
  270.4 1.8 collective-permute-start.25
  271.6 28.2 %copy-start.54 = (bf16[512,256]{1,0:T(8,128)(2,1)S(1)}, bf16[512,256]{1,0:T(8,128)(2,1)}, u32[]{:S(2)}) copy-start(bf16[512,256]{1,0:T(8,128)(2,1)} %get-tuple-element.123) | copy-start | bytes 786436
  271.6 26.3 %collective-permute-start.31 = (bf16[512,1024]{1,0:T(8,128)(2,1)}, bf16[512,1024]{1,0:T(8,128)(2,1)}, u32[]{:S(2)}, u32[]{:S(2)}) collective-permute-start(bf16[512,1024]{1,0:T(8,128)(2,1)} %pad_maximum_fusion.9), channel_id=1, source_target_pairs={{0,4},{4,0},{8,12},{12,8},{16,20},{20,16},{24,28},{28,24},{1,5},{5... | collective-permute-start | bytes 3145736 | tf_op jit(solution)/shard_map/ppermute | solution.py:18
  272.3 3.8 collective-permute-start.26
  273.8 26.0 %copy-start.55 = (bf16[512,256]{1,0:T(8,128)(2,1)S(1)}, bf16[512,256]{1,0:T(8,128)(2,1)}, u32[]{:S(2)}) copy-start(bf16[512,256]{1,0:T(8,128)(2,1)} %get-tuple-element.128) | copy-start | bytes 786436
  273.8 26.1 %copy-start.56 = (bf16[512,256]{1,0:T(8,128)(2,1)S(1)}, bf16[512,256]{1,0:T(8,128)(2,1)}, u32[]{:S(2)}) copy-start(bf16[512,256]{1,0:T(8,128)(2,1)} %get-tuple-element.129) | copy-start | bytes 786436
  273.8 26.1 %copy-start.57 = (bf16[512,256]{1,0:T(8,128)(2,1)S(1)}, bf16[512,256]{1,0:T(8,128)(2,1)}, u32[]{:S(2)}) copy-start(bf16[512,256]{1,0:T(8,128)(2,1)} %get-tuple-element.130) | copy-start | bytes 786436
  273.8 54.6 %collective-permute-start.32 = (bf16[512,1408]{1,0:T(8,128)(2,1)}, bf16[512,1408]{1,0:T(8,128)(2,1)}, u32[]{:S(2)}, u32[]{:S(2)}) collective-permute-start(bf16[512,1408]{1,0:T(8,128)(2,1)} %fusion), channel_id=1, source_target_pairs={{0,4},{4,0},{8,12},{12,8},{16,20},{20,16},{24,28},{28,24},{1,5},{5... | collective-permute-start | bytes 4325384 | tf_op jit(solution)/shard_map/ppermute | solution.py:18
  276.2 4.8 %collective-permute-start.27 = (f32[2,1024]{1,0:T(2,128)S(1)}, f32[2,1024]{1,0:T(2,128)S(1)}, u32[]{:S(2)}, u32[]{:S(2)}) collective-permute-start(f32[2,1024]{1,0:T(2,128)S(1)} %pad_maximum_fusion.17), channel_id=1, source_target_pairs={{0,16},{4,20},{8,24},{12,28},{16,0},{20,4},{24,8},{28,12},{1,17},{... | collective-permute-start | bytes 24584 | tf_op jit(solution)/shard_map/ppermute | solution.py:18
  281.0 25.2 %collective-permute-start.28 = (f32[2,512]{1,0:T(2,128)S(1)}, f32[2,512]{1,0:T(2,128)S(1)}, u32[]{:S(2)}, u32[]{:S(2)}) collective-permute-start(f32[2,512]{1,0:T(2,128)S(1)} %slice.196), channel_id=1, source_target_pairs={{0,8},{4,12},{8,0},{12,4},{16,24},{20,28},{24,16},{28,20},{1,9},{5... | collective-permute-start | bytes 12296 | tf_op jit(solution)/shard_map/ppermute | solution.py:18
  303.9 24.5 %copy-start.24 = (bf16[512,1408]{1,0:T(8,128)(2,1)S(1)}, bf16[512,1408]{1,0:T(8,128)(2,1)}, u32[]{:S(2)}) copy-start(bf16[512,1408]{1,0:T(8,128)(2,1)} %copy-done.23) | copy-start | bytes 4325380
  303.9 24.5 %copy-start.37 = (bf16[512,1024]{1,0:T(8,128)(2,1)S(1)}, bf16[512,1024]{1,0:T(8,128)(2,1)}, u32[]{:S(2)}) copy-start(bf16[512,1024]{1,0:T(8,128)(2,1)} %copy-done.36) | copy-start | bytes 3145732
  306.2 24.0 %copy-start.22 = (bf16[512,1408]{1,0:T(8,128)(2,1)S(1)}, bf16[512,1408]{1,0:T(8,128)(2,1)}, u32[]{:S(2)}) copy-start(bf16[512,1408]{1,0:T(8,128)(2,1)} %copy-done.21) | copy-start | bytes 4325380
  306.2 25.6 %collective-permute-start.29 = (f32[2,256]{1,0:T(2,128)S(1)}, f32[2,256]{1,0:T(2,128)S(1)}, u32[]{:S(2)}, u32[]{:S(2)}) collective-permute-start(f32[2,256]{1,0:T(2,128)S(1)} %slice.198), channel_id=1, source_target_pairs={{0,4},{4,0},{8,12},{12,8},{16,20},{20,16},{24,28},{28,24},{1,5},{5... | collective-permute-start | bytes 6152 | tf_op jit(solution)/shard_map/ppermute | solution.py:18
  330.2 50.8 %collective-permute-start.33 = (bf16[256,1408]{1,0:T(8,128)(2,1)S(1)}, bf16[256,1408]{1,0:T(8,128)(2,1)S(1)}, u32[]{:S(2)}, u32[]{:S(2)}) collective-permute-start(bf16[256,1408]{1,0:T(8,128)(2,1)S(1)} %fusion.7), channel_id=1, source_target_pairs={{0,16},{4,20},{8,24},{12,28},{16,0},{20,4},{24,8},{28,12},{1,17},{... | collective-permute-start | bytes 2162696 | tf_op jit(solution)/shard_map/ppermute | solution.py:18
  (50 other events, 154.8 us)
Sparse Core Ops, SparseCore 0:
  177.2 61.5 reduce-scatter.4
  241.1 56.2 reduce-scatter.8
  299.8 31.0 reduce-scatter.6
  333.0 39.3 reduce-scatter.10

commit v3 on v2

--- a/solution.py
+++ b/solution.py
@@ -226,7 +226,7 @@
                 pltpu.VMEM((heads * size, rows), LOW),
             ],
         ),
-        compiler_params=pltpu.CompilerParams(vmem_limit_bytes=48 << 20),
+        compiler_params=pltpu.CompilerParams(vmem_limit_bytes=24 << 20),
         cost_estimate=pl.CostEstimate(
             flops=wide * rows * rows,
             bytes_accessed=4 * wide * rows,
@@ -272,7 +272,7 @@
                 pltpu.VMEM((heads * size, rows), LOW),
             ],
         ),
-        compiler_params=pltpu.CompilerParams(vmem_limit_bytes=48 << 20),
+        compiler_params=pltpu.CompilerParams(vmem_limit_bytes=24 << 20),
         cost_estimate=pl.CostEstimate(
             flops=wide * rows * rows,
             bytes_accessed=10 * wide * rows,
@@ -299,6 +299,45 @@
     return lax.psum_scatter(
         terms.astype(LOW), "dp", scatter_dimension=dim, axis_index_groups=groups, tiled=True
     )
+
+
+def terms_kernel(transposed, places, x, x_far, g, g_far, out):
+    del places
+    side = 1 if transposed else 0
+    out[...] = (dot(x[...], g[...], 0, side) + dot(x_far[...], g_far[...], 0, side)).astype(LOW)
+
+
+def weight_terms(places, first, x, x_far, g, g_far, transposed=False):
+    count = len(places)
+    blocks = lax.axis_size("dp")
+    size = x.shape[1] // blocks
+    rows = x.shape[0]
+    units = g.shape[0] if transposed else g.shape[1]
+    if size % 128:
+        side = 1 if transposed else 0
+        far = x_far[:, first * size : (first + count) * size]
+        return (dot(pick(x, places, blocks, 1), g, 0, side) + dot(far, g_far, 0, side)).astype(LOW)
+    whole = pl.BlockSpec(g.shape, lambda i, p: (0, 0))
+    return pl.pallas_call(
+        functools.partial(terms_kernel, transposed),
+        out_shape=jax.ShapeDtypeStruct((count * size, units), LOW),
+        grid_spec=pltpu.PrefetchScalarGridSpec(
+            num_scalar_prefetch=1,
+            grid=(count,),
+            in_specs=[
+                pl.BlockSpec((rows, size), lambda i, p: (0, p[i])),
+                pl.BlockSpec((rows, size), lambda i, p: (0, first + i)),
+                whole,
+                whole,
+            ],
+            out_specs=pl.BlockSpec((size, units), lambda i, p: (i, 0)),
+        ),
+        compiler_params=pltpu.CompilerParams(vmem_limit_bytes=24 << 20),
+        cost_estimate=pl.CostEstimate(
+            flops=8 * rows * count * size * units, bytes_accessed=4 * rows * units, transcendentals=0
+        ),
+        name="weight_terms",
+    )(jnp.stack(places).astype(jnp.int32), x, x_far, g, g_far)
 
 
 def turn(values, cosine, sine):
@@ -361,17 +400,19 @@
     )
     angles = frequency[:, None] * positions.astype(jnp.float32)[None, :]
     cosine, sine = jnp.cos(angles), jnp.sin(angles)
-    key_new = turn(dot(w_key, normed_one, 0, 1), cosine, sine)
-    value_new = dot(w_value, normed_one, 0, 1)
-    paired = jnp.concatenate([key_new, value_new], 0).astype(LOW)
+    w_kv = jnp.concatenate([w_key.T, w_value.T], 0)
+    paired = dot(w_kv, normed_one, 1, 1)
+    paired = jnp.concatenate([turn(paired[:size], cosine, sine), paired[size:]], 0).astype(LOW)
     blocks = [paired] + [flip(paired, "dp", m) for m in range(1, SPAN)]
     queries = (turn(dot(w_query, normed_one, 0, 1), cosine, sine) * size ** (-0.5)).astype(LOW)
 
     bit = place % 2
     bits = dp.bit_length() - 1
 
+    halves = [[2 * j + which for j in range(dp // 2)] for which in (bit, 1 - bit)]
+
     def columns(values, which):
-        return pick(values, [2 * j + which for j in range(dp // 2)], dp, 1)
+        return pick(values, halves[which], dp, 1)
 
     near_bits = [0] + list(range(2, bits))
     near_masks = [
@@ -379,8 +420,7 @@
         for j in range(dp // 2)
     ]
 
-    def near_columns(values, where):
-        return pick(values, [where ^ m for m in near_masks], dp, 1)
+    near_halves = [[where ^ m for m in near_masks] for where in (place, place ^ 2)]
 
     def rows_of(values, lo, hi):
         return values[lo * own_rows : hi * own_rows]
@@ -401,26 +441,27 @@
     branch, branch_send = near_sum(branch_terms)
     branch_far = flip(branch_send, "tp", 2)
     one_rows = after(normed_one, branch_send)
-    one_mine, one_send = columns(one_rows, bit), columns(one_rows, 1 - bit)
+    one_send = columns(one_rows, 1)
     one_theirs = flip(one_send, "dp", 1)
-    branch = after(branch, one_mine, one_send)
-
-    middle = own(inputs) + (branch + branch_far)
+    branch = after(branch, one_send)
+
+    own_inputs = own(tokens).astype(jnp.float32)
+    middle = own_inputs + (branch + branch_far)
     scale_two = lax.rsqrt(jnp.mean(middle * middle, -1, keepdims=True) + EPSILON)
     own_two = (middle * scale_two * norm2_gain).astype(LOW)
     far_two = flip(own_two, "tp", 2)
     att_theirs = flip(after(attended, own_two), "dp", 1)
     cot_late = after(cot, own_two)
-    cot_mine, cot_send = near_columns(cot_late, place), near_columns(cot_late, place ^ 2)
+    cot_send = pick(cot_late, near_halves[1], dp, 1)
     cot_theirs = flip(cot_send, "dp", 2)
-    own_two = after(own_two, cot_mine, cot_send)
+    own_two = after(own_two, cot_send)
     pair_two = jnp.concatenate([own_two, far_two], 0)
     core_two = flip(pair_two, "tp", 1)
-    grad_hidden = dot(after(cot, pair_two), w_down, 1, 1)
+    two_send = columns(pair_two, 1)
+    two_near = flip(two_send, "dp", 1)
+    grad_hidden = dot(after(cot, two_send), w_down, 1, 1)
     normed_two = jnp.concatenate([after(pair_two, grad_hidden), core_two], 0)
-    two_send = columns(normed_two, 1 - bit)
-    two_theirs = flip(two_send, "dp", 1)
-    normed_two = after(normed_two, two_send, one_theirs)
+    normed_two = after(normed_two, one_theirs)
 
     gate_pre = dot(normed_two, w_gate, 1, 0)
     up_pre = dot(normed_two, w_up, 1, 0)
@@ -432,9 +473,10 @@
     hidden_theirs = flip(hidden, "dp", 2)
     gate_theirs = flip(grad_gate_pre, "dp", 1)
 
-    gate_late, att_theirs, cot_theirs = lax.optimization_barrier(
-        (grad_gate_pre, att_theirs, cot_theirs)
-    )
+    gate_late, att_theirs, cot_theirs, two_near = lax.optimization_barrier(
+        (grad_gate_pre, att_theirs, cot_theirs, two_near)
+    )
+    two_theirs = jnp.concatenate([two_near, flip(two_near, "tp", 1)], 0)
 
     def two_terms(lo, hi):
         return dot(rows_of(gate_late, lo, hi), w_gate, 1, 1) + dot(
@@ -442,36 +484,36 @@
         )
 
     grad_normed_two, two_far_send = near_sum(two_terms)
+    two_far_send, two_theirs = lax.optimization_barrier((two_far_send, two_theirs))
     two_far = flip(two_far_send, "tp", 2)
 
     hidden_late = after(hidden, two_far_send)
     down, down_send = near_sum(lambda lo, hi: dot(rows_of(hidden_late, lo, hi), w_down, 1, 0))
-    down_far = flip(down_send, "tp", 2)
-    up_theirs = flip(after(grad_up_pre, down_send), "dp", 1)
+    up_theirs = flip(after(grad_up_pre, two_far_send), "dp", 1)
     grad_normed_two = after(grad_normed_two, down_send) + two_far
 
     grad_mid_norm, gain_two = norm_back(grad_normed_two, middle, scale_two, norm2_gain)
     grad_middle = own(cotangent).astype(jnp.float32) + grad_mid_norm
     branch_grad = grad_middle.astype(LOW)
-    output_rows = (middle + (down + after(down_far, branch_grad))).astype(LOW)
     grad_far = flip(branch_grad, "tp", 2)
 
-    hidden_late, cot_mine = lax.optimization_barrier((hidden, cot_mine, branch_grad, output_rows))[:2]
+    hidden_late = after(hidden, branch_grad)
 
     def down_terms(lo, hi):
-        cut = slice(lo * block, hi * block)
-        return dot(cot_mine[:, cut], hidden_late, 0, 0) + dot(
-            cot_theirs[:, cut], hidden_theirs, 0, 0
+        return weight_terms(
+            near_halves[0][lo:hi], lo, cot, cot_theirs, hidden_late, hidden_theirs
         )
 
     count = dp // 2
-    first_send = down_terms(count // 2, count).astype(LOW)
+    first_send = down_terms(count // 2, count)
+    down_far = flip(after(down_send, first_send), "tp", 2)
     grad_pair = jnp.concatenate([after(branch_grad, first_send), grad_far], 0)
     grad_core = flip(grad_pair, "tp", 1)
 
-    two_mine = columns(after(normed_two, grad_pair), bit)
-    gate_terms = dot(two_mine, grad_gate_pre, 0, 0) + dot(two_theirs, gate_theirs, 0, 0)
-    gate_terms = gate_terms.astype(LOW)
+    branch_send = columns(grad_pair, 1)
+    branch_near = flip(branch_send, "dp", 1)
+    two_late = after(normed_two, branch_send)
+    gate_terms = weight_terms(halves[0], 0, two_late, two_theirs, grad_gate_pre, gate_theirs)
     grad_gate = parity_sum(gate_terms, 0)
     branch_all = jnp.concatenate([after(grad_pair, gate_terms), grad_core], 0)
     grad_attended = dot(w_out, branch_all, 1, 1).astype(LOW)
@@ -482,58 +524,61 @@
     grad_query_rows, kv_total = grads[0], grads[1]
     kv_back = [flip(grads[m + 1], "dp", m) for m in range(1, SPAN)]
 
-    two_mine, up_late = lax.optimization_barrier((two_mine, grad_up_pre, grad_query_rows))[:2]
-    up_terms = (dot(two_mine, up_late, 0, 0) + dot(two_theirs, up_theirs, 0, 0)).astype(LOW)
-    grad_up = parity_sum(up_terms, 0)
-
-    kv_total = after(kv_total, up_terms)
-    for got in kv_back:
-        kv_total = kv_total + got
+    up_late = after(grad_up_pre, grad_query_rows)
+    up_terms = weight_terms(halves[0], 0, normed_two, two_theirs, up_late, up_theirs)
+    output_rows = (middle + (down + after(down_far, grad_query_rows))).astype(LOW)
+    got = [flip(first_send, "dp", 1)]
+
+    kv_total, branch_near, got[0] = lax.optimization_barrier(
+        (kv_total, branch_near, got[0], up_terms, output_rows)
+    )[:3]
+    for back in kv_back:
+        kv_total = kv_total + back
     key_grad = turn_back(kv_total[:size], cosine, sine)
     grad_kv_rows = jnp.concatenate([key_grad, kv_total[size:]], 0).astype(LOW)
     proj_rows = jnp.concatenate([grad_query_rows, grad_kv_rows], 0)
+    grad_up = parity_sum(after(up_terms, proj_rows), 0)
     proj_theirs = flip(proj_rows, "dp", 1)
 
-    w_proj = jnp.concatenate([w_query, w_key, w_value], 1)
     own_order = pick(proj_rows, [spot ^ m for m in ROW_MASKS], len(tp_masks), 1)
+    wide = w_query.shape[1]
 
     def one_terms(lo, hi):
-        return dot(own_order[:, lo * own_rows : hi * own_rows], w_proj, 0, 1)
+        cut = own_order[:, lo * own_rows : hi * own_rows]
+        return dot(cut[:wide], w_query, 0, 1) + dot(cut[wide:], w_kv, 0, 0)
 
     grad_normed_one, one_far_send = near_sum(one_terms)
     one_far = flip(one_far_send, "tp", 2)
 
-    got = [flip(after(first_send, one_far_send), "dp", 1)]
-    branch_late = after(branch_all, one_far_send)
-    branch_mine = columns(branch_late, bit)
-    branch_theirs = flip(columns(branch_late, 1 - bit), "dp", 1)
-    grad_normed_one = after(grad_normed_one, branch_mine) + one_far
-    grad_in_norm, gain_one = norm_back(
-        grad_normed_one, own(inputs), own(scale_one), norm1_gain
-    )
-    input_rows = grad_middle + grad_in_norm
-    grad_gate = grad_gate.astype(jnp.float32)
-
-    proj_late = after(proj_rows, input_rows, grad_gate)
-    proj_terms = dot(one_mine, proj_late, 0, 1) + dot(one_theirs, proj_theirs, 0, 1)
-    proj_terms = proj_terms.astype(LOW)
-    grad_proj = parity_sum(proj_terms, 0).astype(jnp.float32)
-    wide = w_query.shape[1]
-
+    branch_theirs = jnp.concatenate([branch_near, flip(branch_near, "tp", 1)], 0)
+    hidden_late = after(hidden, one_far_send)
     count //= 2
     for b in near_bits[1:]:
-        send = down_terms(count // 2, count)
+        send = down_terms(count // 2, count).astype(jnp.float32)
         for other in got:
             send = send + other[count // 2 * block : count * block]
         got.append(flip(send.astype(LOW), "dp", 1 << b))
         count //= 2
-    grad_down = down_terms(0, 1)
+    grad_down = down_terms(0, 1).astype(jnp.float32)
+    grad_normed_one = after(grad_normed_one, send, grad_down) + one_far
+    grad_in_norm, gain_one = norm_back(grad_normed_one, own_inputs, own(scale_one), norm1_gain)
+    input_rows = grad_middle + grad_in_norm
+    grad_gate = grad_gate.astype(jnp.float32)
+
+    proj_late = after(proj_rows, input_rows, grad_gate)
+    last_terms = jnp.concatenate(
+        [
+            weight_terms(halves[0], 0, normed_one, one_theirs, proj_late, proj_theirs, True),
+            weight_terms(halves[0], 0, branch_all, branch_theirs, attended, att_theirs, True),
+        ],
+        1,
+    )
+    grad_up = grad_up.astype(jnp.float32)
+    grad_last = parity_sum(last_terms, 0).astype(jnp.float32)
+    narrow = wide + 2 * size
+
     for other in got:
         grad_down = grad_down + other[:block]
-
-    out_terms = dot(attended, branch_mine, 1, 0) + dot(att_theirs, branch_theirs, 1, 0)
-    grad_up = grad_up.astype(jnp.float32)
-    grad_out = parity_sum(after(out_terms.astype(LOW), grad_up, proj_terms), 1)
 
     gains = jnp.stack([gain_one, gain_two])
     for m in (1, 2):
@@ -548,10 +593,10 @@
         output_rows,
         input_rows,
         gains[0],
-        grad_proj[:, :wide],
-        grad_proj[:, wide : wide + size],
-        grad_proj[:, wide + size :],
-        grad_out.astype(jnp.float32),
+        grad_last[:, :wide],
+        grad_last[:, wide : wide + size],
+        grad_last[:, wide + size : narrow],
+        grad_last[:, narrow:].T,
         gains[1],
         grad_gate,
         grad_up,

time: 405 us -> 413 us (1.020)
  matrix products: 71.7 us -> 42.6 us
  Pallas kernels: 14.1 us -> 39.9 us
  waiting for transfers between devices: 177 us -> 154 us
  starting transfers between devices: 57.7 us -> 72.1 us
  local copies, waits for them, and re-layouts: 31.8 us -> 44 us
  other arithmetic: 31.5 us -> 39.9 us
    ppermute x34 -> x36, waiting for transfers between devices: 177 us -> 135 us  [flip(): lax.ppermute(block, axis, [(i, i ^ mask) for i in range(lax.axis_size(axi...]
    dot_general x31 -> x18, matrix products: 71.7 us -> 42.6 us  [dot(): lax.dot_general(left, right, (((left_dim,), (right_dim,)), ((), ())), pre...]
    pallas_call x0 -> x7, Pallas kernels: none -> 23.3 us  [weight_terms(): pl.pallas_call(functools.partial(terms_kernel, transposed), out_shape=jax...]
    reduce_scatter x4 -> x3, waiting for transfers between devices: 0.01 us -> 19 us  [parity_sum(): lax.psum_scatter(terms.astype(LOW), 'dp', scatter_dimension=dim, axis_ind...]
    ppermute x34 -> x36, starting transfers between devices: 57.3 us -> 71.9 us  [flip(): lax.ppermute(block, axis, [(i, i ^ mask) for i in range(lax.axis_size(axi...]
    unnamed x159 -> x191, local copies, waits for them, and re-layouts: 19.6 us -> 32.2 us
  transfers between devices with their start and end apart: 38 -> 39, of which waited for: 17 -> 17; matrix products, arithmetic and copies ran while one was open for 26% -> 20% of each run, Pallas kernels for 2% -> 7%
where the time goes in v3:
time: 413 us; the launch traced here: 408 us
  waiting for transfers between devices  154 us (37%)
  starting transfers between devices  72.1 us (17%)
  local copies, waits for them, and re-layouts  44 us (11%)
  matrix products  42.6 us (10%)
  other arithmetic  39.9 us (10%)
  Pallas kernels  39.9 us (10%)
  between operations  15.3 us (4%)
    ppermute x36, waiting for transfers between devices, flip(): lax.ppermute(block, axis, [(i, i ^ mask) for i in range(lax.axis_size(axi...  135 us
    ppermute x36, starting transfers between devices, flip(): lax.ppermute(block, axis, [(i, i ^ mask) for i in range(lax.axis_size(axi...  71.9 us
    dot_general x18, matrix products, dot(): lax.dot_general(left, right, (((left_dim,), (right_dim,)), ((), ())), pre...  42.6 us
    unnamed x191, local copies, waits for them, and re-layouts  32.2 us
    pallas_call x7, Pallas kernels, weight_terms(): pl.pallas_call(functools.partial(terms_kernel, transposed), out_shape=jax...  23.3 us
    reduce_scatter x3, waiting for transfers between devices, parity_sum(): lax.psum_scatter(terms.astype(LOW), 'dp', scatter_dimension=dim, axis_ind...  19 us
    pallas_call x1, Pallas kernels, attention_backward(): pl.pallas_call(functools.partial(backward_kernel, heads, size), out_shape...  9.13 us
  transfers between devices with their start and end apart: 39, of which 17 were waited for; matrix products, arithmetic and copies ran while one was open for 20% of the time, Pallas kernels for 7%

profile of v3, /device:TPU:0, one launch (start us, length us, event | category | flops | bytes accessed | tf_op | source)
XLA Modules:
  0.0 407.8 jit_solution(12155634744748799052)
XLA Ops:
  7.3 2.2 fusion
  13.5 4.0 collective-permute-start.2
  18.5 4.5 %fusion.66 = f32[512,512]{0,1:T(8,128)} fusion(bf16[512,2048]{1,0:T(8,128)(2,1)} %copy-done.4, bf16[2048,512]{1,0:T(8,128)(2,1)} %param.15), kind=kOutput, calls=%fused_computation.181 | convolution fusion | flops 1073741824 | bytes 5242880 | tf_op jit(solution)/shard_map/dot_general | solution.py:22
  23.1 1.5 multiply_subtract_fusion
  25.1 1.6 pad_maximum_fusion.1.x
  30.2 7.6 %attention_forward.1 = (bf16[512,512]{1,0:T(8,128)(2,1)}, f32[8,1,512]{2,1,0:T(1,128)S(1)}) custom-call(s32[2]{0:T(128)S(1)} %pad_add_fusion.at_ref, s32[1,512]{1,0:T(1,128)S(1)} %bitcast.54, bf16[512,512]{1,0:T(8,128)(2,1)S(1)} %bitcast.52, bf16[128,512]{1,0:T(8,128)(2,1)S(1)} %copy-done.20, bf16[128,512]{1,0:T(8,128)(2,1)S(1)} %copy-done.40, ...), custom_call_target="tpu_custom_call" | custom-call | flops 134217728 | bytes 1048576 | tf_op jit(solution)/shard_map/attention_forward/pallas_call | solution.py:210
  37.8 1.7 convolution_convert_fusion
  39.6 1.7 fusion.31
  44.8 1.9 collective-permute-start.4
  46.6 1.6 copy-done.5
  49.5 9.7 %collective-permute-done.4 = bf16[128,2048]{1,0:T(8,128)(2,1)} collective-permute-done((bf16[128,2048]{1,0:T(8,128)(2,1)}, bf16[128,2048]{1,0:T(8,128)(2,1)}, u32[]{:S(2)}, u32[]{:S(2)}) %collective-permute-start.4) | collective-permute-done | bytes 524320 | tf_op jit(solution)/shard_map/ppermute | solution.py:18
  59.2 1.5 multiply_reduce_fusion.2
  61.8 1.7 collective-permute-start.5
  63.6 5.7 %collective-permute-start.7 = (bf16[512,1024]{1,0:T(8,128)(2,1)}, bf16[512,1024]{1,0:T(8,128)(2,1)S(1)}, u32[]{:S(2)}, u32[]{:S(2)}) collective-permute-start(bf16[512,1024]{1,0:T(8,128)(2,1)} %pad_maximum_fusion.3), channel_id=1, source_target_pairs={{0,4},{4,0},{8,12},{12,8},{16,20},{20,16},{24,28},{28,24},{1,5},{5... | collective-permute-start | bytes 3145736 | tf_op jit(solution)/shard_map/ppermute | solution.py:18
  70.7 10.0 %collective-permute-start.9 = (bf16[512,1024]{1,0:T(8,128)(2,1)S(1)}, bf16[512,1024]{1,0:T(8,128)(2,1)S(1)}, u32[]{:S(2)}, u32[]{:S(2)}) collective-permute-start(bf16[512,1024]{1,0:T(8,128)(2,1)S(1)} %pad_maximum_fusion.4), channel_id=1, source_target_pairs={{0,8},{4,12},{8,0},{12,4},{16,24},{20,28},{24,16},{28,20},{1,9},{5... | collective-permute-start | bytes 3145736 | tf_op jit(solution)/shard_map/ppermute | solution.py:18
  83.2 2.1 collective-permute-start.10
  85.3 6.1 %fusion.67 = f32[512,1408]{1,0:T(8,128)S(1)} fusion(bf16[512,2048]{1,0:T(8,128)(2,1)S(1)} %copy-done.1, bf16[1408,2048]{1,0:T(8,128)(2,1)} %param.22), kind=kOutput, calls=%fused_computation.182 | convolution fusion | flops 2952790016 | bytes 10747904 | tf_op jit(solution)/shard_map/dot_general | solution.py:22
  91.6 2.0 collective-permute-done.7.x_far
  94.5 3.4 fusion.68
  98.0 4.6 %multiply_convert_fusion.1 = (bf16[512,1408]{1,0:T(8,128)(2,1)S(1)}, bf16[512,1408]{1,0:T(8,128)(2,1)S(1)}, bf16[512,1408]{1,0:T(8,128)(2,1)S(1)}) fusion(f32[512,1408]{1,0:T(8,128)S(1)} %fusion.67, f32[512,1408]{1,0:T(8,128)S(1)} %fusion.68, bf16[512,2048]{1,0:T(8,128)(2,1)S(1)} %pad_maximum_fusion.2.x, bf16[2048,1408]{1,0:T(8,128)(2,1)S(1)} %bitcast.78), kind=kOutput, calls=%fused_computation.6 | convolution fusion | flops 2963603456 | bytes 17956864 | tf_op jit(solution)/shard_map/dot_general | solution.py:22
  102.6 2.2 collective-permute-done.8.g_far
  105.6 8.7 %collective-permute-done.10 = bf16[256,1024]{1,0:T(8,128)(2,1)S(1)} collective-permute-done((bf16[256,1024]{1,0:T(8,128)(2,1)S(1)}, bf16[256,1024]{1,0:T(8,128)(2,1)S(1)}, u32[]{:S(2)}, u32[]{:S(2)}) %collective-permute-start.10) | collective-permute-done | bytes 524320 | tf_op jit(solution)/shard_map/ppermute | solution.py:18
  114.3 1.8 fusion.20
  116.2 1.8 fusion.4
  118.6 1.8 fusion.18
  120.4 1.8 convolution_add_fusion.2
  125.7 3.3 convolution_convert_fusion.1
  129.2 1.8 collective-permute-start.18
  130.9 9.9 %collective-permute-start.15 = (bf16[512,1408]{1,0:T(8,128)(2,1)S(1)}, bf16[512,1408]{1,0:T(8,128)(2,1)S(1)}, u32[]{:S(2)}, u32[]{:S(2)}) collective-permute-start(bf16[512,1408]{1,0:T(8,128)(2,1)S(1)} %get-tuple-element.100.g), channel_id=1, source_target_pairs={{0,8},{4,12},{8,0},{12,4},{16,24},{20,28},{24,16},{28,20},{1,9},{5... | collective-permute-start | bytes 4325384 | tf_op jit(solution)/shard_map/ppermute | solution.py:18
  142.8 4.4 %fusion.22 = f32[256,2048]{1,0:T(8,128)S(1)} fusion(bf16[1408,2048]{1,0:T(8,128)(2,1)} %param.22, bf16[512,1408]{1,0:T(8,128)(2,1)S(1)} %get-tuple-element.100.g), kind=kOutput, calls=%fused_computation.65 | convolution fusion | flops 1476395008 | bytes 8585216 | tf_op jit(solution)/shard_map/dot_general | solution.py:22
  147.2 1.6 convert_add_fusion.1
  149.8 6.2 %collective-permute-done.14 = bf16[128,2048]{1,0:T(8,128)(2,1)S(1)} collective-permute-done((bf16[128,2048]{1,0:T(8,128)(2,1)S(1)}, bf16[128,2048]{1,0:T(8,128)(2,1)S(1)}, u32[]{:S(2)}, u32[]{:S(2)}) %collective-permute-start.14) | collective-permute-done | bytes 524320 | tf_op jit(solution)/shard_map/ppermute | solution.py:18
  157.0 2.7 fusion.63
  160.2 12.6 %collective-permute-done.15.g_far = bf16[512,1408]{1,0:T(8,128)(2,1)S(1)} collective-permute-done((bf16[512,1408]{1,0:T(8,128)(2,1)S(1)}, bf16[512,1408]{1,0:T(8,128)(2,1)S(1)}, u32[]{:S(2)}, u32[]{:S(2)}) %collective-permute-start.15) | collective-permute-done | bytes 1441824 | tf_op jit(solution)/shard_map/ppermute | solution.py:18
  172.8 2.8 weight_terms.7
  179.2 4.9 %weight_terms.8 = bf16[1024,1408]{1,0:T(8,128)(2,1)S(1)} custom-call(s32[4]{0:T(128)S(1)} %pad_add_fusion.2.places, bf16[512,2048]{1,0:T(8,128)(2,1)S(1)} %copy-done.17, bf16[512,1024]{1,0:T(8,128)(2,1)S(1)} %copy-done.22, bf16[512,1408]{1,0:T(8,128)(2,1)S(1)} %copy-done.50, bf16[512,1408]{1,0:T(8,128)(2,1)S(1)} %collective-permute-done.18.g_far), custom_call_target="tpu_custom_call" | custom-call | flops 5905580032 | bytes 2883584 | tf_op jit(solution)/shard_map/weight_terms/pallas_call | solution.py:321
  184.1 1.6 copy-done.15
  186.3 1.7 collective-permute-start.21
  192.3 9.1 %attention_backward.1 = (bf16[512,512]{1,0:T(8,128)(2,1)S(1)}, f32[128,512]{1,0:T(8,128)S(1)}, bf16[128,512]{1,0:T(8,128)(2,1)}, bf16[128,512]{1,0:T(8,128)(2,1)}, bf16[128,512]{1,0:T(8,128)(2,1)}) custom-call(s32[2]{0:T(128)S(1)} %pad_add_fusion.at_ref, s32[1,512]{1,0:T(1,128)S(1)} %bitcast.55, bf16[512,512]{1,0:T(8,128)(2,1)S(1)} %bitcast.53, ...), custom_call_target="tpu_custom_call" | custom-call | flops 134217728 | bytes 2621440 | tf_op jit(solution)/shard_map/attention_backward/pallas_call | solution.py:245
  203.0 7.8 %collective-permute-start.23 = (bf16[128,512]{1,0:T(8,128)(2,1)}, bf16[128,512]{1,0:T(8,128)(2,1)}, u32[]{:S(2)}, u32[]{:S(2)}) collective-permute-start(bf16[128,512]{1,0:T(8,128)(2,1)} %get-tuple-element.95), channel_id=1, source_target_pairs={{0,4},{4,0},{8,12},{12,8},{16,20},{20,16},{24,28},{28,24},{1,5},{5... | collective-permute-start | bytes 393224 | tf_op jit(solution)/shard_map/ppermute | solution.py:18
  210.8 14.0 %collective-permute-start.24 = (bf16[128,512]{1,0:T(8,128)(2,1)}, bf16[128,512]{1,0:T(8,128)(2,1)}, u32[]{:S(2)}, u32[]{:S(2)}) collective-permute-start(bf16[128,512]{1,0:T(8,128)(2,1)} %get-tuple-element.96), channel_id=1, source_target_pairs={{0,8},{4,12},{8,0},{12,4},{16,24},{20,28},{24,16},{28,20},{1,9},{5... | collective-permute-start | bytes 393224 | tf_op jit(solution)/shard_map/ppermute | solution.py:18
  225.1 5.0 %weight_terms.9 = bf16[1024,1408]{1,0:T(8,128)(2,1)S(1)} custom-call(s32[4]{0:T(128)S(1)} %pad_add_fusion.2.places, bf16[512,2048]{1,0:T(8,128)(2,1)S(1)} %copy-done.18, bf16[512,1024]{1,0:T(8,128)(2,1)S(1)} %copy-done.23, bf16[512,1408]{1,0:T(8,128)(2,1)S(1)} %copy-done.48, bf16[512,1408]{1,0:T(8,128)(2,1)S(1)} %collective-permute-done.22.g_far), custom_call_target="tpu_custom_call" | custom-call | flops 5905580032 | bytes 2883584 | tf_op jit(solution)/shard_map/weight_terms/pallas_call | solution.py:321
  230.1 1.6 copy-done.14
  231.7 2.7 fusion.16
  234.4 31.2 %collective-permute-done.20 = bf16[256,1024]{1,0:T(8,128)(2,1)} collective-permute-done((bf16[256,1024]{1,0:T(8,128)(2,1)}, bf16[256,1024]{1,0:T(8,128)(2,1)}, u32[]{:S(2)}, u32[]{:S(2)}) %collective-permute-start.20) | collective-permute-done | bytes 524320 | tf_op jit(solution)/shard_map/ppermute | solution.py:18
  265.6 2.4 collective-permute-done.23
  270.4 1.4 constant_dynamic-slice_fusion.9
  271.8 1.5 fusion.35
  275.9 1.6 collective-permute-done.26
  280.9 4.0 weight_terms.13
  285.0 6.9 %collective-permute-done.27 = bf16[128,2048]{1,0:T(8,128)(2,1)S(1)} collective-permute-done((bf16[128,2048]{1,0:T(8,128)(2,1)S(1)}, bf16[128,2048]{1,0:T(8,128)(2,1)S(1)}, u32[]{:S(2)}, u32[]{:S(2)}) %collective-permute-start.27) | collective-permute-done | bytes 524320 | tf_op jit(solution)/shard_map/ppermute | solution.py:18
  292.9 1.4 fusion.11
  294.3 2.5 convert_element_type.155
  298.0 4.6 %weight_terms.12 = bf16[1024,640]{1,0:T(8,128)(2,1)S(1)} custom-call(s32[4]{0:T(128)S(1)} %pad_add_fusion.2.places, bf16[512,2048]{1,0:T(8,128)(2,1)S(1)} %copy-done.6, bf16[512,1024]{1,0:T(8,128)(2,1)S(1)} %copy-done.53, bf16[640,512]{1,0:T(8,128)(2,1)} %pad_maximum_fusion.7.g, bf16[640,512]{1,0:T(8,128)(2,1)} %collective-permute-done.33.g_far), custom_call_target="tpu_custom_call" | custom-call | flops 2684354560 | bytes 1310720 | tf_op jit(solution)/shard_map/weight_terms/pallas_call | solution.py:321
  302.6 1.6 pad_maximum_fusion
  308.2 3.3 collective-permute-done.29
  312.3 2.6 collective-permute-start.30
  314.9 1.6 copy-done.3
  320.2 1.8 collective-permute-start.31
  325.3 2.6 collective-permute-done.32
  328.5 42.9 %collective-permute-done.35 = bf16[256,1408]{1,0:T(8,128)(2,1)S(1)} collective-permute-done((bf16[256,1408]{1,0:T(8,128)(2,1)S(1)}, bf16[256,1408]{1,0:T(8,128)(2,1)S(1)}, u32[]{:S(2)}, u32[]{:S(2)}) %collective-permute-start.35) | collective-permute-done | bytes 720928 | tf_op jit(solution)/shard_map/ppermute | solution.py:18
  372.7 1.5 copy.27
  374.3 2.3 convert_element_type.157
  376.6 19.0 %reduce-scatter.6.cloned.1.call-done = bf16[256,1152]{1,0:T(8,128)(2,1)} async-done(((bf16[1024,1152]{1,0:T(8,128)(2,1)}), bf16[256,1152]{1,0:T(8,128)(2,1)}) %reduce-scatter.6.cloned.1.call-update) | async-done | bytes 589840 | tf_op jit(solution)/shard_map/reduce_scatter | solution.py:299
  (320 shorter events, 69.1 us)
Async XLA Ops:
  7.2 30.6 %copy-start = (bf16[512,2048]{1,0:T(8,128)(2,1)S(1)}, bf16[512,2048]{1,0:T(8,128)(2,1)}, u32[]{:S(2)}) copy-start(bf16[512,2048]{1,0:T(8,128)(2,1)} %param.18) | copy-start | bytes 6291460
  7.2 287.1 %reduce-scatter.4.cloned.1.call-start = ((), (), s32[]{:S(2)}) async-start(), calls=%async_computation.3 | async-start | bytes 3604480 | tf_op jit(solution)/shard_map/reduce_scatter | solution.py:299
  7.3 10.9 %copy-start.82 = (f32[32]{0:T(128)}, f32[32]{0:T(128)S(1)}, u32[]{:S(2)}) copy-start(f32[32]{0:T(128)S(1)} %multiply_exponential_fusion) | copy-start | bytes 388
  13.1 9.9 %copy-start.79 = (f32[512]{0:T(512)}, f32[512]{0:T(512)S(1)}, u32[]{:S(2)}) copy-start(f32[512]{0:T(512)S(1)} %convert_element_type.125) | copy-start | bytes 6148
  13.5 9.5 %copy-start.19 = (bf16[128,512]{1,0:T(8,128)(2,1)}, bf16[128,512]{1,0:T(8,128)(2,1)S(1)}, u32[]{:S(2)}) copy-start(bf16[128,512]{1,0:T(8,128)(2,1)S(1)} %pad_maximum_fusion.14.kv0) | copy-start | bytes 393220
  13.5 13.5 %collective-permute-start.2 = (bf16[128,512]{1,0:T(8,128)(2,1)S(1)}, bf16[128,512]{1,0:T(8,128)(2,1)S(1)}, u32[]{:S(2)}, u32[]{:S(2)}) collective-permute-start(bf16[128,512]{1,0:T(8,128)(2,1)S(1)} %pad_maximum_fusion.14.kv0), channel_id=1, source_target_pairs={{0,12},{4,8},{8,4},{12,0},{16,28},{20,24},{24,20},{28,16},{1,13},{... | collective-permute-start | bytes 393224 | tf_op jit(solution)/shard_map/ppermute | solution.py:18
  17.5 10.2 %collective-permute-start.1 = (bf16[128,512]{1,0:T(8,128)(2,1)S(1)}, bf16[128,512]{1,0:T(8,128)(2,1)S(1)}, u32[]{:S(2)}, u32[]{:S(2)}) collective-permute-start(bf16[128,512]{1,0:T(8,128)(2,1)S(1)} %pad_maximum_fusion.14.kv0), channel_id=1, source_target_pairs={{0,8},{4,12},{8,0},{12,4},{16,24},{20,28},{24,16},{28,20},{1,9},{5... | collective-permute-start | bytes 393224 | tf_op jit(solution)/shard_map/ppermute | solution.py:18
  18.0 9.7 %collective-permute-start = (bf16[128,512]{1,0:T(8,128)(2,1)S(1)}, bf16[128,512]{1,0:T(8,128)(2,1)S(1)}, u32[]{:S(2)}, u32[]{:S(2)}) collective-permute-start(bf16[128,512]{1,0:T(8,128)(2,1)S(1)} %pad_maximum_fusion.14.kv0), channel_id=1, source_target_pairs={{0,4},{4,0},{8,12},{12,8},{16,20},{20,16},{24,28},{28,24},{1,5},{5... | collective-permute-start | bytes 393224 | tf_op jit(solution)/shard_map/ppermute | solution.py:18
  26.9 12.6 %copy-start.9 = (bf16[8,2,32,512]{3,2,1,0:T(8,128)(2,1)}, bf16[8,2,32,512]{3,2,1,0:T(8,128)(2,1)S(1)}, u32[]{:S(2)}) copy-start(bf16[8,2,32,512]{3,2,1,0:T(8,128)(2,1)S(1)} %fusion.17) | copy-start | bytes 1572868
  27.7 11.8 %copy-start.37 = (bf16[128,512]{1,0:T(8,128)(2,1)}, bf16[128,512]{1,0:T(8,128)(2,1)S(1)}, u32[]{:S(2)}) copy-start(bf16[128,512]{1,0:T(8,128)(2,1)S(1)} %collective-permute-done.1.kv2) | copy-start | bytes 393220
  39.5 2.7 collective-permute-start.3
  44.8 14.4 %collective-permute-start.4 = (bf16[128,2048]{1,0:T(8,128)(2,1)}, bf16[128,2048]{1,0:T(8,128)(2,1)}, u32[]{:S(2)}, u32[]{:S(2)}) collective-permute-start(bf16[128,2048]{1,0:T(8,128)(2,1)} %slice.283), channel_id=1, source_target_pairs={{0,2},{1,3},{2,0},{3,1},{4,6},{5,7},{6,4},{7,5},{8,10},{9,11},{10,... | collective-permute-start | bytes 1572872 | tf_op jit(solution)/shard_map/ppermute | solution.py:18
  48.2 10.9 %slice-start = ((f32[256,2048]{1,0:T(8,128)}), f32[128,2048]{1,0:T(8,128)S(1)}, s32[]{:S(2)}) async-start(f32[256,2048]{1,0:T(8,128)} %copy-done.63), calls=%async_computation.6 | async-start | bytes 2097152 | tf_op jit(solution)/shard_map/slice | solution.py:432
  49.5 11.3 %copy-start.76 = (f32[2048]{0:T(1024)S(1)}, f32[2048]{0:T(1024)}, u32[]{:S(2)}) copy-start(f32[2048]{0:T(1024)} %param.19) | copy-start | bytes 24580
  61.8 20.0 %collective-permute-start.5 = (bf16[128,2048]{1,0:T(8,128)(2,1)}, bf16[128,2048]{1,0:T(8,128)(2,1)}, u32[]{:S(2)}, u32[]{:S(2)}) collective-permute-start(bf16[128,2048]{1,0:T(8,128)(2,1)} %multiply_convert_fusion.3), channel_id=1, source_target_pairs={{0,2},{1,3},{2,0},{3,1},{4,6},{5,7},{6,4},{7,5},{8,10},{9,11},{10,... | collective-permute-start | bytes 1572872 | tf_op jit(solution)/shard_map/ppermute | solution.py:18
  63.6 30.0 %collective-permute-start.7 = (bf16[512,1024]{1,0:T(8,128)(2,1)}, bf16[512,1024]{1,0:T(8,128)(2,1)S(1)}, u32[]{:S(2)}, u32[]{:S(2)}) collective-permute-start(bf16[512,1024]{1,0:T(8,128)(2,1)} %pad_maximum_fusion.3), channel_id=1, source_target_pairs={{0,4},{4,0},{8,12},{12,8},{16,20},{20,16},{24,28},{28,24},{1,5},{5... | collective-permute-start | bytes 3145736 | tf_op jit(solution)/shard_map/ppermute | solution.py:18
  70.7 14.6 %copy-start.1 = (bf16[512,2048]{1,0:T(8,128)(2,1)S(1)}, bf16[512,2048]{1,0:T(8,128)(2,1)}, u32[]{:S(2)}) copy-start(bf16[512,2048]{1,0:T(8,128)(2,1)} %pad_maximum_fusion.1.x) | copy-start | bytes 6291460
  70.7 43.6 %collective-permute-start.9 = (bf16[512,1024]{1,0:T(8,128)(2,1)S(1)}, bf16[512,1024]{1,0:T(8,128)(2,1)S(1)}, u32[]{:S(2)}, u32[]{:S(2)}) collective-permute-start(bf16[512,1024]{1,0:T(8,128)(2,1)S(1)} %pad_maximum_fusion.4), channel_id=1, source_target_pairs={{0,8},{4,12},{8,0},{12,4},{16,24},{20,28},{24,16},{28,20},{1,9},{5... | collective-permute-start | bytes 3145736 | tf_op jit(solution)/shard_map/ppermute | solution.py:18
  80.7 24.1 %collective-permute-start.8 = (bf16[512,512]{1,0:T(8,128)(2,1)}, bf16[512,512]{1,0:T(8,128)(2,1)S(1)}, u32[]{:S(2)}, u32[]{:S(2)}) collective-permute-start(bf16[512,512]{1,0:T(8,128)(2,1)} %get-tuple-element.71.o_in.g), channel_id=1, source_target_pairs={{0,4},{4,0},{8,12},{12,8},{16,20},{20,16},{24,28},{28,24},{1,5},{5... | collective-permute-start | bytes 1572872 | tf_op jit(solution)/shard_map/ppermute | solution.py:18
  82.9 8.4 %collective-permute-start.6 = (bf16[256,2048]{1,0:T(8,128)(2,1)S(1)}, bf16[256,2048]{1,0:T(8,128)(2,1)S(1)}, u32[]{:S(2)}, u32[]{:S(2)}) collective-permute-start(bf16[256,2048]{1,0:T(8,128)(2,1)S(1)} %constant_dynamic-update-slice_fusion), channel_id=1, source_target_pairs={{0,1},{1,0},{2,3},{3,2},{4,5},{5,4},{6,7},{7,6},{8,9},{9,8},{10,11... | collective-permute-start | bytes 3145736 | tf_op jit(solution)/shard_map/ppermute | solution.py:18
  83.1 11.4 %slice-start.1 = ((s8[5767168]{0:T(1024)(128)(4,1)}), s8[4194304]{0:T(1024)(128)(4,1)S(1)}, s32[]{:S(2)}) async-start(s8[5767168]{0:T(1024)(128)(4,1)} %bitcast.75), calls=%async_computation.7 | async-start | bytes 8388608
  83.2 11.4 %slice-start.2 = ((s8[5767168]{0:T(1024)(128)(4,1)}), s8[1572864]{0:T(1024)(128)(4,1)S(1)}, s32[]{:S(2)}) async-start(s8[5767168]{0:T(1024)(128)(4,1)} %bitcast.75), calls=%async_computation.8 | async-start | bytes 3145728
  83.2 31.1 %collective-permute-start.10 = (bf16[256,1024]{1,0:T(8,128)(2,1)S(1)}, bf16[256,1024]{1,0:T(8,128)(2,1)S(1)}, u32[]{:S(2)}, u32[]{:S(2)}) collective-permute-start(bf16[256,1024]{1,0:T(8,128)(2,1)S(1)} %pad_maximum_fusion.9), channel_id=1, source_target_pairs={{0,4},{4,0},{8,12},{12,8},{16,20},{20,16},{24,28},{28,24},{1,5},{5... | collective-permute-start | bytes 1572872 | tf_op jit(solution)/shard_map/ppermute | solution.py:18
  102.6 16.0 %copy-start.47 = (bf16[512,1408]{1,0:T(8,128)(2,1)}, bf16[512,1408]{1,0:T(8,128)(2,1)S(1)}, u32[]{:S(2)}) copy-start(bf16[512,1408]{1,0:T(8,128)(2,1)S(1)} %get-tuple-element.93.g) | copy-start | bytes 4325380
  102.6 17.8 %copy-start.49 = (bf16[512,1408]{1,0:T(8,128)(2,1)}, bf16[512,1408]{1,0:T(8,128)(2,1)S(1)}, u32[]{:S(2)}) copy-start(bf16[512,1408]{1,0:T(8,128)(2,1)S(1)} %get-tuple-element.72.g) | copy-start | bytes 4325380
  114.3 7.9 %collective-permute-start.12 = (bf16[256,1024]{1,0:T(8,128)(2,1)S(1)}, bf16[256,1024]{1,0:T(8,128)(2,1)S(1)}, u32[]{:S(2)}, u32[]{:S(2)}) collective-permute-start(bf16[256,1024]{1,0:T(8,128)(2,1)S(1)} %collective-permute-done.10), channel_id=1, source_target_pairs={{0,1},{1,0},{2,3},{3,2},{4,5},{5,4},{6,7},{7,6},{8,9},{9,8},{10,11... | collective-permute-start | bytes 1572872 | tf_op jit(solution)/shard_map/ppermute | solution.py:18
  118.0 5.3 %collective-permute-start.11 = (bf16[256,2048]{1,0:T(8,128)(2,1)S(1)}, bf16[256,2048]{1,0:T(8,128)(2,1)S(1)}, u32[]{:S(2)}, u32[]{:S(2)}) collective-permute-start(bf16[256,2048]{1,0:T(8,128)(2,1)S(1)} %fusion.4), channel_id=1, source_target_pairs={{0,1},{1,0},{2,3},{3,2},{4,5},{5,4},{6,7},{7,6},{8,9},{9,8},{10,11... | collective-permute-start | bytes 3145736 | tf_op jit(solution)/shard_map/ppermute | solution.py:18
  129.1 18.2 %collective-permute-start.13 = (bf16[256,2048]{1,0:T(8,128)(2,1)}, bf16[256,2048]{1,0:T(8,128)(2,1)}, u32[]{:S(2)}, u32[]{:S(2)}) collective-permute-start(bf16[256,2048]{1,0:T(8,128)(2,1)} %convolution_convert_fusion.1), channel_id=1, source_target_pairs={{0,1},{1,0},{2,3},{3,2},{4,5},{5,4},{6,7},{7,6},{8,9},{9,8},{10,11... | collective-permute-start | bytes 3145736 | tf_op jit(solution)/shard_map/ppermute | solution.py:18
  129.1 13.1 %copy-start.72 = (bf16[128,2048]{1,0:T(8,128)(2,1)S(1)}, bf16[128,2048]{1,0:T(8,128)(2,1)}, u32[]{:S(2)}) copy-start(bf16[128,2048]{1,0:T(8,128)(2,1)} %slice.282) | copy-start | bytes 1572868
  129.2 48.8 %collective-permute-start.18 = (bf16[512,1408]{1,0:T(8,128)(2,1)}, bf16[512,1408]{1,0:T(8,128)(2,1)S(1)}, u32[]{:S(2)}, u32[]{:S(2)}) collective-permute-start(bf16[512,1408]{1,0:T(8,128)(2,1)} %copy-done.49), channel_id=1, source_target_pairs={{0,4},{4,0},{8,12},{12,8},{16,20},{20,16},{24,28},{28,24},{1,5},{5... | collective-permute-start | bytes 4325384 | tf_op jit(solution)/shard_map/ppermute | solution.py:18
  130.9 41.9 %collective-permute-start.15 = (bf16[512,1408]{1,0:T(8,128)(2,1)S(1)}, bf16[512,1408]{1,0:T(8,128)(2,1)S(1)}, u32[]{:S(2)}, u32[]{:S(2)}) collective-permute-start(bf16[512,1408]{1,0:T(8,128)(2,1)S(1)} %get-tuple-element.100.g), channel_id=1, source_target_pairs={{0,8},{4,12},{8,0},{12,4},{16,24},{20,28},{24,16},{28,20},{1,9},{5... | collective-permute-start | bytes 4325384 | tf_op jit(solution)/shard_map/ppermute | solution.py:18
  142.2 13.8 %collective-permute-start.14 = (bf16[128,2048]{1,0:T(8,128)(2,1)S(1)}, bf16[128,2048]{1,0:T(8,128)(2,1)S(1)}, u32[]{:S(2)}, u32[]{:S(2)}) collective-permute-start(bf16[128,2048]{1,0:T(8,128)(2,1)S(1)} %copy-done.72), channel_id=1, source_target_pairs={{0,2},{1,3},{2,0},{3,1},{4,6},{5,7},{6,4},{7,5},{8,10},{9,11},{10,... | collective-permute-start | bytes 1572872 | tf_op jit(solution)/shard_map/ppermute | solution.py:18
  157.0 15.8 %copy-start.2 = (bf16[512,2048]{1,0:T(8,128)(2,1)S(1)}, bf16[512,2048]{1,0:T(8,128)(2,1)}, u32[]{:S(2)}) copy-start(bf16[512,2048]{1,0:T(8,128)(2,1)} %pad_maximum_fusion.1.x) | copy-start | bytes 6291460
  157.0 15.8 %copy-start.12 = (bf16[512,1024]{1,0:T(8,128)(2,1)S(1)}, bf16[512,1024]{1,0:T(8,128)(2,1)}, u32[]{:S(2)}) copy-start(bf16[512,1024]{1,0:T(8,128)(2,1)} %copy-done.11) | copy-start | bytes 3145732
  159.7 17.1 %collective-permute-start.17 = (bf16[128,2048]{1,0:T(8,128)(2,1)S(1)}, bf16[128,2048]{1,0:T(8,128)(2,1)S(1)}, u32[]{:S(2)}, u32[]{:S(2)}) collective-permute-start(bf16[128,2048]{1,0:T(8,128)(2,1)S(1)} %get-tuple-element.84), channel_id=1, source_target_pairs={{0,2},{1,3},{2,0},{3,1},{4,6},{5,7},{6,4},{7,5},{8,10},{9,11},{10,... | collective-permute-start | bytes 1572872 | tf_op jit(solution)/shard_map/ppermute | solution.py:18
  185.7 188.5 %reduce-scatter.8.cloned.1.call-start = ((), (), s32[]{:S(2)}) async-start(), calls=%async_computation.5 | async-start | bytes 3604480 | tf_op jit(solution)/shard_map/reduce_scatter | solution.py:299
  185.8 4.4 %collective-permute-start.19 = (bf16[256,2048]{1,0:T(8,128)(2,1)}, bf16[256,2048]{1,0:T(8,128)(2,1)S(1)}, u32[]{:S(2)}, u32[]{:S(2)}) collective-permute-start(bf16[256,2048]{1,0:T(8,128)(2,1)} %copy-done.65), channel_id=1, source_target_pairs={{0,1},{1,0},{2,3},{3,2},{4,5},{5,4},{6,7},{7,6},{8,9},{9,8},{10,11... | collective-permute-start | bytes 3145736 | tf_op jit(solution)/shard_map/ppermute | solution.py:18
  185.8 39.0 %collective-permute-start.22 = (bf16[512,1408]{1,0:T(8,128)(2,1)}, bf16[512,1408]{1,0:T(8,128)(2,1)S(1)}, u32[]{:S(2)}, u32[]{:S(2)}) collective-permute-start(bf16[512,1408]{1,0:T(8,128)(2,1)} %copy-done.47), channel_id=1, source_target_pairs={{0,4},{4,0},{8,12},{12,8},{16,20},{20,16},{24,28},{28,24},{1,5},{5... | collective-permute-start | bytes 4325384 | tf_op jit(solution)/shard_map/ppermute | solution.py:18
  186.3 79.3 %collective-permute-start.21 = (bf16[512,1408]{1,0:T(8,128)(2,1)}, bf16[512,1408]{1,0:T(8,128)(2,1)}, u32[]{:S(2)}, u32[]{:S(2)}) collective-permute-start(bf16[512,1408]{1,0:T(8,128)(2,1)} %copy-done.51), channel_id=1, source_target_pairs={{0,4},{4,0},{8,12},{12,8},{16,20},{20,16},{24,28},{28,24},{1,5},{5... | collective-permute-start | bytes 4325384 | tf_op jit(solution)/shard_map/ppermute | solution.py:18
  187.9 15.1 %collective-permute-start.16 = (bf16[128,2048]{1,0:T(8,128)(2,1)}, bf16[128,2048]{1,0:T(8,128)(2,1)S(1)}, u32[]{:S(2)}, u32[]{:S(2)}) collective-permute-start(bf16[128,2048]{1,0:T(8,128)(2,1)} %slice.281), channel_id=1, source_target_pairs={{0,2},{1,3},{2,0},{3,1},{4,6},{5,7},{6,4},{7,5},{8,10},{9,11},{10,... | collective-permute-start | bytes 1572872 | tf_op jit(solution)/shard_map/ppermute | solution.py:18
  188.4 77.1 %collective-permute-start.20 = (bf16[256,1024]{1,0:T(8,128)(2,1)}, bf16[256,1024]{1,0:T(8,128)(2,1)}, u32[]{:S(2)}, u32[]{:S(2)}) collective-permute-start(bf16[256,1024]{1,0:T(8,128)(2,1)} %pad_maximum_fusion.10), channel_id=1, source_target_pairs={{0,4},{4,0},{8,12},{12,8},{16,20},{20,16},{24,28},{28,24},{1,5},{5... | collective-permute-start | bytes 1572872 | tf_op jit(solution)/shard_map/ppermute | solution.py:18
  190.4 34.8 %copy-start.23 = (bf16[512,1024]{1,0:T(8,128)(2,1)S(1)}, bf16[512,1024]{1,0:T(8,128)(2,1)}, u32[]{:S(2)}) copy-start(bf16[512,1024]{1,0:T(8,128)(2,1)} %pad_maximum_fusion.5.x_far) | copy-start | bytes 3145732
  190.4 34.7 %copy-start.48 = (bf16[512,1408]{1,0:T(8,128)(2,1)S(1)}, bf16[512,1408]{1,0:T(8,128)(2,1)}, u32[]{:S(2)}) copy-start(bf16[512,1408]{1,0:T(8,128)(2,1)} %copy-done.47) | copy-start | bytes 4325380
  191.7 33.4 %copy-start.18 = (bf16[512,2048]{1,0:T(8,128)(2,1)S(1)}, bf16[512,2048]{1,0:T(8,128)(2,1)}, u32[]{:S(2)}) copy-start(bf16[512,2048]{1,0:T(8,128)(2,1)} %copy-done.16) | copy-start | bytes 6291460
  203.0 21.9 %copy-start.73 = (bf16[128,2048]{1,0:T(8,128)(2,1)}, bf16[128,2048]{1,0:T(8,128)(2,1)S(1)}, u32[]{:S(2)}) copy-start(bf16[128,2048]{1,0:T(8,128)(2,1)S(1)} %collective-permute-done.16) | copy-start | bytes 1572868
  203.0 64.9 %collective-permute-start.23 = (bf16[128,512]{1,0:T(8,128)(2,1)}, bf16[128,512]{1,0:T(8,128)(2,1)}, u32[]{:S(2)}, u32[]{:S(2)}) collective-permute-start(bf16[128,512]{1,0:T(8,128)(2,1)} %get-tuple-element.95), channel_id=1, source_target_pairs={{0,4},{4,0},{8,12},{12,8},{16,20},{20,16},{24,28},{28,24},{1,5},{5... | collective-permute-start | bytes 393224 | tf_op jit(solution)/shard_map/ppermute | solution.py:18
  210.8 57.1 %collective-permute-start.24 = (bf16[128,512]{1,0:T(8,128)(2,1)}, bf16[128,512]{1,0:T(8,128)(2,1)}, u32[]{:S(2)}, u32[]{:S(2)}) collective-permute-start(bf16[128,512]{1,0:T(8,128)(2,1)} %get-tuple-element.96), channel_id=1, source_target_pairs={{0,8},{4,12},{8,0},{12,4},{16,24},{20,28},{24,16},{28,20},{1,9},{5... | collective-permute-start | bytes 393224 | tf_op jit(solution)/shard_map/ppermute | solution.py:18
  224.9 43.0 %collective-permute-start.25 = (bf16[128,512]{1,0:T(8,128)(2,1)}, bf16[128,512]{1,0:T(8,128)(2,1)}, u32[]{:S(2)}, u32[]{:S(2)}) collective-permute-start(bf16[128,512]{1,0:T(8,128)(2,1)} %get-tuple-element.97), channel_id=1, source_target_pairs={{0,12},{4,8},{8,4},{12,0},{16,28},{20,24},{24,20},{28,16},{1,13},{... | collective-permute-start | bytes 393224 | tf_op jit(solution)/shard_map/ppermute | solution.py:18
  231.7 36.3 %copy-start.43 = (f32[128,512]{1,0:T(8,128)S(1)}, f32[128,512]{1,0:T(8,128)}, u32[]{:S(2)}) copy-start(f32[128,512]{1,0:T(8,128)} %copy-done.42) | copy-start | bytes 786436
  231.7 37.4 %copy-start.80 = (f32[512]{0:T(512)S(1)}, f32[512]{0:T(512)}, u32[]{:S(2)}) copy-start(f32[512]{0:T(512)} %copy-done.79) | copy-start | bytes 6148
  231.7 37.4 %copy-start.83 = (f32[32]{0:T(128)S(1)}, f32[32]{0:T(128)}, u32[]{:S(2)}) copy-start(f32[32]{0:T(128)} %copy-done.82) | copy-start | bytes 388
  231.7 37.8 %copy-start.33 = (bf16[512,512]{1,0:T(8,128)(2,1)S(1)}, bf16[512,512]{1,0:T(8,128)(2,1)}, u32[]{:S(2)}) copy-start(bf16[512,512]{1,0:T(8,128)(2,1)} %copy-done.32) | copy-start | bytes 1572868
  270.3 125.2 %reduce-scatter.6.cloned.1.call-start = ((), (), s32[]{:S(2)}) async-start(), calls=%async_computation.4 | async-start | bytes 2949120 | tf_op jit(solution)/shard_map/reduce_scatter | solution.py:299
  274.1 3.4 collective-permute-start.26
  274.2 5.6 %collective-permute-start.34 = (bf16[256,1024]{1,0:T(8,128)(2,1)}, bf16[256,1024]{1,0:T(8,128)(2,1)S(1)}, u32[]{:S(2)}, u32[]{:S(2)}) collective-permute-start(bf16[256,1024]{1,0:T(8,128)(2,1)} %collective-permute-done.20), channel_id=1, source_target_pairs={{0,1},{1,0},{2,3},{3,2},{4,5},{5,4},{6,7},{7,6},{8,9},{9,8},{10,11... | collective-permute-start | bytes 1572872 | tf_op jit(solution)/shard_map/ppermute | solution.py:18
  277.9 14.0 %collective-permute-start.27 = (bf16[128,2048]{1,0:T(8,128)(2,1)S(1)}, bf16[128,2048]{1,0:T(8,128)(2,1)S(1)}, u32[]{:S(2)}, u32[]{:S(2)}) collective-permute-start(bf16[128,2048]{1,0:T(8,128)(2,1)S(1)} %slice.280), channel_id=1, source_target_pairs={{0,2},{1,3},{2,0},{3,1},{4,6},{5,7},{6,4},{7,5},{8,10},{9,11},{10,... | collective-permute-start | bytes 1572872 | tf_op jit(solution)/shard_map/ppermute | solution.py:18
  279.3 17.4 %collective-permute-start.33 = (bf16[640,512]{1,0:T(8,128)(2,1)}, bf16[640,512]{1,0:T(8,128)(2,1)}, u32[]{:S(2)}, u32[]{:S(2)}) collective-permute-start(bf16[640,512]{1,0:T(8,128)(2,1)} %pad_maximum_fusion.7.g), channel_id=1, source_target_pairs={{0,4},{4,0},{8,12},{12,8},{16,20},{20,16},{24,28},{28,24},{1,5},{5... | collective-permute-start | bytes 1966088 | tf_op jit(solution)/shard_map/ppermute | solution.py:18
  280.9 11.0 %copy-start.77 = (f32[2048]{0:T(1024)S(1)}, f32[2048]{0:T(1024)}, u32[]{:S(2)}) copy-start(f32[2048]{0:T(1024)} %param.14) | copy-start | bytes 24580
  304.9 1.2 collective-permute-start.28
  307.4 4.1 collective-permute-start.29
  312.3 7.9 %collective-permute-start.30 = (f32[2,1024]{1,0:T(2,128)S(1)}, f32[2,1024]{1,0:T(2,128)S(1)}, u32[]{:S(2)}, u32[]{:S(2)}) collective-permute-start(f32[2,1024]{1,0:T(2,128)S(1)} %pad_maximum_fusion.22), channel_id=1, source_target_pairs={{0,16},{4,20},{8,24},{12,28},{16,0},{20,4},{24,8},{28,12},{1,17},{... | collective-permute-start | bytes 24584 | tf_op jit(solution)/shard_map/ppermute | solution.py:18
  320.2 4.1 collective-permute-start.31
  323.3 48.1 %collective-permute-start.35 = (bf16[256,1408]{1,0:T(8,128)(2,1)S(1)}, bf16[256,1408]{1,0:T(8,128)(2,1)S(1)}, u32[]{:S(2)}, u32[]{:S(2)}) collective-permute-start(bf16[256,1408]{1,0:T(8,128)(2,1)S(1)} %fusion.62), channel_id=1, source_target_pairs={{0,16},{4,20},{8,24},{12,28},{16,0},{20,4},{24,8},{28,12},{1,17},{... | collective-permute-start | bytes 2162696 | tf_op jit(solution)/shard_map/ppermute | solution.py:18
  324.3 3.6 collective-permute-start.32
  (68 other events, 193.9 us)
Sparse Core Ops, SparseCore 0:
  185.8 61.1 reduce-scatter.3
  270.5 55.9 reduce-scatter.7
  328.7 66.7 reduce-scatter.5

commit v4 on v3

--- a/solution.py
+++ b/solution.py
@@ -228,7 +228,7 @@
         ),
         compiler_params=pltpu.CompilerParams(vmem_limit_bytes=24 << 20),
         cost_estimate=pl.CostEstimate(
-            flops=wide * rows * rows,
+            flops=32 * wide * rows * rows * SPAN,
             bytes_accessed=4 * wide * rows,
             transcendentals=0,
         ),
@@ -274,7 +274,7 @@
         ),
         compiler_params=pltpu.CompilerParams(vmem_limit_bytes=24 << 20),
         cost_estimate=pl.CostEstimate(
-            flops=wide * rows * rows,
+            flops=48 * wide * rows * rows * SPAN,
             bytes_accessed=10 * wide * rows,
             transcendentals=0,
         ),
@@ -340,6 +340,36 @@
     )(jnp.stack(places).astype(jnp.int32), x, x_far, g, g_far)
 
 
+def row_kernel(left, right, send, kept):
+    half = left.shape[0] // 2
+    send[...] = dot(left[half:, :], right[...], 1, 0).astype(LOW)
+    kept[...] = dot(left[:half, :], right[...], 1, 0)
+
+
+def row_terms(left, right):
+    rows, units = left.shape
+    half, width = rows // 2, right.shape[1]
+    step = 256
+    return pl.pallas_call(
+        row_kernel,
+        out_shape=(
+            jax.ShapeDtypeStruct((half, width), LOW),
+            jax.ShapeDtypeStruct((half, width), jnp.float32),
+        ),
+        grid=(width // step,),
+        in_specs=[
+            pl.BlockSpec((rows, units), lambda i: (0, 0)),
+            pl.BlockSpec((units, step), lambda i: (0, i)),
+        ],
+        out_specs=[pl.BlockSpec((half, step), lambda i: (0, i))] * 2,
+        compiler_params=pltpu.CompilerParams(vmem_limit_bytes=16 << 20),
+        cost_estimate=pl.CostEstimate(
+            flops=8 * rows * units * width, bytes_accessed=2 * units * width, transcendentals=0
+        ),
+        name="row_terms",
+    )(left, right)
+
+
 def turn(values, cosine, sine):
     half = cosine.shape[0]
     heads = values.shape[0] // (2 * half)
@@ -431,37 +461,34 @@
         pair = kept + near
         return pair[:own_rows], pair[own_rows:].astype(LOW)
 
-    cot = pick(after(cotangent, paired), [spot ^ m for m in ROW_MASKS], len(tp_masks), 0)
-    queries = after(queries, cot)
+    one_send = columns(after(normed_one, paired), 1)
+    one_theirs = flip(one_send, "dp", 1)
+    queries = after(queries, one_send)
     attended, lse = attention_forward(at, pos, queries, blocks, size, 2)
+    attended = after(attended, one_theirs)
 
     def branch_terms(lo, hi):
         return dot(attended[:, lo * own_rows : hi * own_rows], w_out, 0, 0)
 
     branch, branch_send = near_sum(branch_terms)
     branch_far = flip(branch_send, "tp", 2)
-    one_rows = after(normed_one, branch_send)
-    one_send = columns(one_rows, 1)
-    one_theirs = flip(one_send, "dp", 1)
-    branch = after(branch, one_send)
+    att_theirs = flip(after(attended, branch_send), "dp", 1)
+    cot = pick(after(cotangent, branch_send), [spot ^ m for m in ROW_MASKS], len(tp_masks), 0)
+    cot_send = pick(cot, near_halves[1], dp, 1)
+    cot_theirs = flip(cot_send, "dp", 2)
+    branch = after(branch, cot_send)
 
     own_inputs = own(tokens).astype(jnp.float32)
     middle = own_inputs + (branch + branch_far)
     scale_two = lax.rsqrt(jnp.mean(middle * middle, -1, keepdims=True) + EPSILON)
     own_two = (middle * scale_two * norm2_gain).astype(LOW)
     far_two = flip(own_two, "tp", 2)
-    att_theirs = flip(after(attended, own_two), "dp", 1)
-    cot_late = after(cot, own_two)
-    cot_send = pick(cot_late, near_halves[1], dp, 1)
-    cot_theirs = flip(cot_send, "dp", 2)
-    own_two = after(own_two, cot_send)
-    pair_two = jnp.concatenate([own_two, far_two], 0)
+    grad_hidden = dot(after(cot, own_two), w_down, 1, 1)
+    pair_two = jnp.concatenate([after(own_two, grad_hidden, att_theirs), far_two], 0)
     core_two = flip(pair_two, "tp", 1)
     two_send = columns(pair_two, 1)
     two_near = flip(two_send, "dp", 1)
-    grad_hidden = dot(after(cot, two_send), w_down, 1, 1)
-    normed_two = jnp.concatenate([after(pair_two, grad_hidden), core_two], 0)
-    normed_two = after(normed_two, one_theirs)
+    normed_two = jnp.concatenate([after(pair_two, two_send), core_two], 0)
 
     gate_pre = dot(normed_two, w_gate, 1, 0)
     up_pre = dot(normed_two, w_up, 1, 0)
@@ -473,8 +500,8 @@
     hidden_theirs = flip(hidden, "dp", 2)
     gate_theirs = flip(grad_gate_pre, "dp", 1)
 
-    gate_late, att_theirs, cot_theirs, two_near = lax.optimization_barrier(
-        (grad_gate_pre, att_theirs, cot_theirs, two_near)
+    gate_late, cot_theirs, two_near = lax.optimization_barrier(
+        (grad_gate_pre, cot_theirs, two_near)
     )
     two_theirs = jnp.concatenate([two_near, flip(two_near, "tp", 1)], 0)
 
@@ -488,9 +515,9 @@
     two_far = flip(two_far_send, "tp", 2)
 
     hidden_late = after(hidden, two_far_send)
-    down, down_send = near_sum(lambda lo, hi: dot(rows_of(hidden_late, lo, hi), w_down, 1, 0))
-    up_theirs = flip(after(grad_up_pre, two_far_send), "dp", 1)
-    grad_normed_two = after(grad_normed_two, down_send) + two_far
+    down_near, down = row_terms(hidden_late, w_down)
+    up_theirs = flip(grad_up_pre, "dp", 1)
+    grad_normed_two = after(grad_normed_two, down) + two_far
 
     grad_mid_norm, gain_two = norm_back(grad_normed_two, middle, scale_two, norm2_gain)
     grad_middle = own(cotangent).astype(jnp.float32) + grad_mid_norm
@@ -506,7 +533,7 @@
 
     count = dp // 2
     first_send = down_terms(count // 2, count)
-    down_far = flip(after(down_send, first_send), "tp", 2)
+    down_near = flip(after(down_near, branch_grad), "tp", 1)
     grad_pair = jnp.concatenate([after(branch_grad, first_send), grad_far], 0)
     grad_core = flip(grad_pair, "tp", 1)
 
@@ -514,9 +541,9 @@
     branch_near = flip(branch_send, "dp", 1)
     two_late = after(normed_two, branch_send)
     gate_terms = weight_terms(halves[0], 0, two_late, two_theirs, grad_gate_pre, gate_theirs)
-    grad_gate = parity_sum(gate_terms, 0)
     branch_all = jnp.concatenate([after(grad_pair, gate_terms), grad_core], 0)
     grad_attended = dot(w_out, branch_all, 1, 1).astype(LOW)
+    grad_gate = parity_sum(after(gate_terms, grad_attended), 0)
 
     grads = attention_backward(
         at, pos, queries, grad_attended, attended, lse, cosine, sine, blocks, size, 2
@@ -526,12 +553,14 @@
 
     up_late = after(grad_up_pre, grad_query_rows)
     up_terms = weight_terms(halves[0], 0, normed_two, two_theirs, up_late, up_theirs)
-    output_rows = (middle + (down + after(down_far, grad_query_rows))).astype(LOW)
-    got = [flip(first_send, "dp", 1)]
-
-    kv_total, branch_near, got[0] = lax.optimization_barrier(
-        (kv_total, branch_near, got[0], up_terms, output_rows)
-    )[:3]
+    down = down + after(down_near, grad_query_rows)
+    down, down_send = down[:own_rows], down[own_rows:].astype(LOW)
+    down_far = flip(down_send, "tp", 2)
+    got = [flip(after(first_send, up_terms), "dp", 1)]
+
+    kv_total, branch_near = lax.optimization_barrier(
+        (kv_total, branch_near, up_terms, down_send)
+    )[:2]
     for back in kv_back:
         kv_total = kv_total + back
     key_grad = turn_back(kv_total[:size], cosine, sine)
@@ -560,7 +589,8 @@
         got.append(flip(send.astype(LOW), "dp", 1 << b))
         count //= 2
     grad_down = down_terms(0, 1).astype(jnp.float32)
-    grad_normed_one = after(grad_normed_one, send, grad_down) + one_far
+    output_rows = (middle + (down + after(down_far, one_far_send))).astype(LOW)
+    grad_normed_one = after(grad_normed_one, send, grad_down, output_rows) + one_far
     grad_in_norm, gain_one = norm_back(grad_normed_one, own_inputs, own(scale_one), norm1_gain)
     input_rows = grad_middle + grad_in_norm
     grad_gate = grad_gate.astype(jnp.float32)

time: 413 us -> 391 us (0.947)
  waiting for transfers between devices: 154 us -> 140 us
  starting transfers between devices: 72.1 us -> 61 us
  local copies, waits for them, and re-layouts: 44 us -> 53.1 us
  other arithmetic: 39.9 us -> 35.1 us
  matrix products: 42.6 us -> 38.2 us
    reduce_scatter x3, waiting for transfers between devices: 19 us -> 0.01 us  [parity_sum(): lax.psum_scatter(terms.astype(LOW), 'dp', scatter_dimension=dim, axis_ind...]
    ppermute x36, starting transfers between devices: 71.9 us -> 60.9 us  [flip(): lax.ppermute(block, axis, [(i, i ^ mask) for i in range(lax.axis_size(axi...]
    pallas_call x0 -> x1, Pallas kernels: none -> 5.77 us  [row_terms(): pl.pallas_call(row_kernel, out_shape=(jax.ShapeDtypeStruct((half, width),...]
    unnamed x191 -> x184, local copies, waits for them, and re-layouts: 32.2 us -> 37.5 us
    ppermute x36, waiting for transfers between devices: 135 us -> 140 us  [flip(): lax.ppermute(block, axis, [(i, i ^ mask) for i in range(lax.axis_size(axi...]
    dot_general x18 -> x16, matrix products: 42.6 us -> 38.2 us  [dot(): lax.dot_general(left, right, (((left_dim,), (right_dim,)), ((), ())), pre...]
  transfers between devices with their start and end apart: 39 -> 39, of which waited for: 17 -> 14; matrix products, arithmetic and copies ran while one was open for 20% -> 21% of each run, Pallas kernels for 7% -> 11%
where the time goes in v4:
time: 391 us; the launch traced here: 386 us
  waiting for transfers between devices  140 us (36%)
  starting transfers between devices  61 us (16%)
  local copies, waits for them, and re-layouts  53.1 us (14%)
  Pallas kernels  43.6 us (11%)
  matrix products  38.2 us (10%)
  other arithmetic  35.1 us (9%)
  between operations  15.2 us (4%)
    ppermute x36, waiting for transfers between devices, flip(): lax.ppermute(block, axis, [(i, i ^ mask) for i in range(lax.axis_size(axi...  140 us
    ppermute x36, starting transfers between devices, flip(): lax.ppermute(block, axis, [(i, i ^ mask) for i in range(lax.axis_size(axi...  60.9 us
    dot_general x16, matrix products, dot(): lax.dot_general(left, right, (((left_dim,), (right_dim,)), ((), ())), pre...  38.2 us
    unnamed x184, local copies, waits for them, and re-layouts  37.5 us
    pallas_call x7, Pallas kernels, weight_terms(): pl.pallas_call(functools.partial(terms_kernel, transposed), out_shape=jax...  23 us
    pallas_call x1, Pallas kernels, attention_backward(): pl.pallas_call(functools.partial(backward_kernel, heads, size), out_shape...  8.01 us
  transfers between devices with their start and end apart: 39, of which 14 were waited for; matrix products, arithmetic and copies ran while one was open for 21% of the time, Pallas kernels for 11%

profile of v4, /device:TPU:0, one launch (start us, length us, event | category | flops | bytes accessed | tf_op | source)
XLA Modules:
  0.0 385.9 jit_solution(4665744222898758580)
XLA Ops:
  7.3 2.2 fusion
  13.6 3.0 collective-permute-start
  16.6 1.6 collective-permute-start.1
  20.7 1.9 collective-permute-start.3
  26.4 6.8 %attention_forward.1 = (bf16[512,512]{1,0:T(8,128)(2,1)S(1)}, f32[8,1,512]{2,1,0:T(1,128)S(1)}) custom-call(s32[2]{0:T(128)S(1)} %pad_add_fusion.at_ref, s32[1,512]{1,0:T(1,128)S(1)} %bitcast.52, bf16[512,512]{1,0:T(8,128)(2,1)S(1)} %bitcast.50, bf16[128,512]{1,0:T(8,128)(2,1)S(1)} %pad_maximum_fusion.13.kv0, bf16[128,512]{1,0:T(8,128)(2,1)S(1)} %collective-permute-done.kv1, ...), custom_call_target="tpu_custom_call" | custom-call | flops 17179869184 | bytes 1048576 | tf_op jit(solution)/shard_map/attention_forward/pallas_call | solution.py:210
  33.9 12.9 %collective-permute-done.3.x_far = bf16[512,1024]{1,0:T(8,128)(2,1)} collective-permute-done((bf16[512,1024]{1,0:T(8,128)(2,1)}, bf16[512,1024]{1,0:T(8,128)(2,1)}, u32[]{:S(2)}, u32[]{:S(2)}) %collective-permute-start.3) | collective-permute-done | bytes 1048608 | tf_op jit(solution)/shard_map/ppermute | solution.py:18
  46.7 1.7 convolution_convert_fusion
  49.2 2.3 collective-permute-done.4
  51.4 1.5 convert_add_fusion.3
  53.0 1.8 collective-permute-start.5
  57.0 1.7 collective-permute-start.6
  58.7 8.4 %collective-permute-done.5 = bf16[128,2048]{1,0:T(8,128)(2,1)S(1)} collective-permute-done((bf16[128,2048]{1,0:T(8,128)(2,1)S(1)}, bf16[128,2048]{1,0:T(8,128)(2,1)S(1)}, u32[]{:S(2)}, u32[]{:S(2)}) %collective-permute-start.5) | collective-permute-done | bytes 524320 | tf_op jit(solution)/shard_map/ppermute | solution.py:18
  69.6 1.8 collective-permute-start.7
  71.4 5.1 %fusion.64 = f32[512,1408]{1,0:T(8,128)} fusion(bf16[512,2048]{1,0:T(8,128)(2,1)S(1)} %pad_maximum_fusion.1.x, bf16[1408,2048]{1,0:T(8,128)(2,1)S(1)} %bitcast.55), kind=kOutput, calls=%fused_computation.179 | convolution fusion | flops 2952790016 | bytes 10747904 | tf_op jit(solution)/shard_map/dot_general | solution.py:22
  77.3 5.5 %collective-permute-done.7 = bf16[128,2048]{1,0:T(8,128)(2,1)S(1)} collective-permute-done((bf16[128,2048]{1,0:T(8,128)(2,1)S(1)}, bf16[128,2048]{1,0:T(8,128)(2,1)S(1)}, u32[]{:S(2)}, u32[]{:S(2)}) %collective-permute-start.7) | collective-permute-done | bytes 524320 | tf_op jit(solution)/shard_map/ppermute | solution.py:18
  83.7 1.7 collective-permute-start.9
  86.6 1.6 collective-permute-start.10
  89.5 1.4 constant_dynamic-update-slice_fusion.2.x
  91.0 6.9 %fusion.65 = f32[512,1408]{1,0:T(8,128)S(1)} fusion(bf16[512,2048]{1,0:T(8,128)(2,1)S(1)} %constant_dynamic-update-slice_fusion.2.x, bf16[2048,1408]{1,0:T(8,128)(2,1)} %param.21), kind=kOutput, calls=%fused_computation.180 | convolution fusion | flops 2952790016 | bytes 10747904 | tf_op jit(solution)/shard_map/dot_general | solution.py:22
  97.9 4.6 %multiply_convert_fusion.1 = (bf16[512,1408]{1,0:T(8,128)(2,1)S(1)}, bf16[512,1408]{1,0:T(8,128)(2,1)S(1)}, bf16[512,1408]{1,0:T(8,128)(2,1)S(1)}) fusion(f32[512,1408]{1,0:T(8,128)S(1)} %copy-done.79, f32[512,1408]{1,0:T(8,128)S(1)} %fusion.65, bf16[512,2048]{1,0:T(8,128)(2,1)S(1)} %constant_dynamic-update-slice_fusion.2.x, bf16[2048,1408]{1,0:T(8,128)(2,1)S(1)} %bitcast.80), kind=kOutput, calls=%fused_computation.6 | convolution fusion | flops 2963603456 | bytes 17956864 | tf_op jit(solution)/shard_map/dot_general | solution.py:22
  103.2 1.8 fusion.20
  105.0 4.4 %collective-permute-done.9.x_far = bf16[512,1024]{1,0:T(8,128)(2,1)S(1)} collective-permute-done((bf16[512,1024]{1,0:T(8,128)(2,1)}, bf16[512,1024]{1,0:T(8,128)(2,1)S(1)}, u32[]{:S(2)}, u32[]{:S(2)}) %collective-permute-start.9) | collective-permute-done | bytes 1048608 | tf_op jit(solution)/shard_map/ppermute | solution.py:18
  109.5 2.9 fusion.4
  112.8 1.7 collective-permute-start.15
  114.6 3.2 fusion.18
  117.7 3.6 convolution_add_fusion.2
  121.8 1.6 collective-permute-start.13
  123.4 5.8 %row_terms.1 = (bf16[256,2048]{1,0:T(8,128)(2,1)S(1)}, f32[256,2048]{1,0:T(8,128)S(1)}) custom-call(bf16[512,1408]{1,0:T(8,128)(2,1)S(1)} %get-tuple-element.98.left.g, bf16[1408,2048]{1,0:T(8,128)(2,1)S(1)} %bitcast.57), custom_call_target="tpu_custom_call" | custom-call | flops 11811160064 | bytes 5767168 | tf_op jit(solution)/shard_map/row_terms/pallas_call | solution.py:353
  129.3 6.1 %collective-permute-done.13 = bf16[128,2048]{1,0:T(8,128)(2,1)S(1)} collective-permute-done((bf16[128,2048]{1,0:T(8,128)(2,1)S(1)}, bf16[128,2048]{1,0:T(8,128)(2,1)S(1)}, u32[]{:S(2)}, u32[]{:S(2)}) %collective-permute-start.13) | collective-permute-done | bytes 524320 | tf_op jit(solution)/shard_map/ppermute | solution.py:18
  136.3 2.6 fusion.60
  138.9 1.5 collective-permute-start.16
  140.5 5.8 %collective-permute-done.15.g_far = bf16[512,1408]{1,0:T(8,128)(2,1)S(1)} collective-permute-done((bf16[512,1408]{1,0:T(8,128)(2,1)S(1)}, bf16[512,1408]{1,0:T(8,128)(2,1)S(1)}, u32[]{:S(2)}, u32[]{:S(2)}) %collective-permute-start.15) | collective-permute-done | bytes 1441824 | tf_op jit(solution)/shard_map/ppermute | solution.py:18
  146.3 2.8 weight_terms.7
  150.1 1.5 collective-permute-done.16
  154.5 5.4 %weight_terms.8 = bf16[1024,1408]{1,0:T(8,128)(2,1)S(1)} custom-call(s32[4]{0:T(128)S(1)} %pad_add_fusion.2.places, bf16[512,2048]{1,0:T(8,128)(2,1)S(1)} %constant_dynamic-update-slice_fusion.2.x, bf16[512,1024]{1,0:T(8,128)(2,1)S(1)} %pad_maximum_fusion.4.x_far, bf16[512,1408]{1,0:T(8,128)(2,1)S(1)} %get-tuple-element.70.g, ...), custom_call_target="tpu_custom_call" | custom-call | flops 5905580032 | bytes 2883584 | tf_op jit(solution)/shard_map/weight_terms/pallas_call | solution.py:321
  159.9 1.6 copy-done.12
  164.1 2.2 fusion.6.do_in
  167.8 1.6 collective-permute-start.21
  179.3 8.0 %attention_backward.1 = (bf16[512,512]{1,0:T(8,128)(2,1)S(1)}, f32[128,512]{1,0:T(8,128)S(1)}, bf16[128,512]{1,0:T(8,128)(2,1)}, bf16[128,512]{1,0:T(8,128)(2,1)}, bf16[128,512]{1,0:T(8,128)(2,1)}) custom-call(s32[2]{0:T(128)S(1)} %pad_add_fusion.at_ref, s32[1,512]{1,0:T(1,128)S(1)} %bitcast.53, bf16[512,512]{1,0:T(8,128)(2,1)S(1)} %bitcast.51, ...), custom_call_target="tpu_custom_call" | custom-call | flops 25769803776 | bytes 2621440 | tf_op jit(solution)/shard_map/attention_backward/pallas_call | solution.py:245
  188.0 19.9 %collective-permute-start.24 = (bf16[128,512]{1,0:T(8,128)(2,1)}, bf16[128,512]{1,0:T(8,128)(2,1)}, u32[]{:S(2)}, u32[]{:S(2)}) collective-permute-start(bf16[128,512]{1,0:T(8,128)(2,1)} %get-tuple-element.94), channel_id=1, source_target_pairs={{0,12},{4,8},{8,4},{12,0},{16,28},{20,24},{24,20},{28,16},{1,13},{... | collective-permute-start | bytes 393224 | tf_op jit(solution)/shard_map/ppermute | solution.py:18
  208.5 1.7 convert_add_fusion.1
  210.9 4.9 %weight_terms.9 = bf16[1024,1408]{1,0:T(8,128)(2,1)S(1)} custom-call(s32[4]{0:T(128)S(1)} %pad_add_fusion.2.places, bf16[512,2048]{1,0:T(8,128)(2,1)S(1)} %copy-done.22, bf16[512,1024]{1,0:T(8,128)(2,1)S(1)} %copy-done.16, bf16[512,1408]{1,0:T(8,128)(2,1)S(1)} %copy-done.40, bf16[512,1408]{1,0:T(8,128)(2,1)S(1)} %collective-permute-done.21.g_far), custom_call_target="tpu_custom_call" | custom-call | flops 5905580032 | bytes 2883584 | tf_op jit(solution)/shard_map/weight_terms/pallas_call | solution.py:321
  215.9 1.5 copy-done.11
  217.5 2.1 slice.271
  219.6 1.6 collective-permute-done.23
  225.1 1.5 fusion.32
  228.3 1.6 collective-permute-start.19
  230.1 5.9 %collective-permute-start.33 = (bf16[640,512]{1,0:T(8,128)(2,1)}, bf16[640,512]{1,0:T(8,128)(2,1)}, u32[]{:S(2)}, u32[]{:S(2)}) collective-permute-start(bf16[640,512]{1,0:T(8,128)(2,1)} %pad_maximum_fusion.6.g), channel_id=1, source_target_pairs={{0,4},{4,0},{8,12},{12,8},{16,20},{20,16},{24,28},{28,24},{1,5},{5... | collective-permute-start | bytes 1966088 | tf_op jit(solution)/shard_map/ppermute | solution.py:18
  239.5 3.0 weight_terms.13
  246.4 11.2 %collective-permute-done.27 = bf16[128,2048]{1,0:T(8,128)(2,1)S(1)} collective-permute-done((bf16[128,2048]{1,0:T(8,128)(2,1)S(1)}, bf16[128,2048]{1,0:T(8,128)(2,1)S(1)}, u32[]{:S(2)}, u32[]{:S(2)}) %collective-permute-start.27) | collective-permute-done | bytes 524320 | tf_op jit(solution)/shard_map/ppermute | solution.py:18
  259.4 2.5 convert_element_type.151
  261.8 4.9 %weight_terms.12 = bf16[1024,640]{1,0:T(8,128)(2,1)S(1)} custom-call(s32[4]{0:T(128)S(1)} %pad_add_fusion.2.places, bf16[512,2048]{1,0:T(8,128)(2,1)S(1)} %copy-done.6, bf16[512,1024]{1,0:T(8,128)(2,1)} %collective-permute-done.3.x_far, bf16[640,512]{1,0:T(8,128)(2,1)} %pad_maximum_fusion.6.g, bf16[640,512]{1,0:T(8,128)(2,1)} %collective-permute-done.33.g_far), custom_call_target="tpu_custom_call" | custom-call | flops 2684354560 | bytes 1310720 | tf_op jit(solution)/shard_map/weight_terms/pallas_call | solution.py:321
  266.7 1.6 pad_maximum_fusion
  269.1 2.3 collective-permute-start.26
  272.6 1.5 collective-permute-start.29
  274.1 2.5 collective-permute-done.29
  278.4 1.6 copy-done.3
  283.6 2.6 collective-permute-start.31
  286.2 17.7 %collective-permute-done.26 = bf16[512,1408]{1,0:T(8,128)(2,1)} collective-permute-done((bf16[512,1408]{1,0:T(8,128)(2,1)}, bf16[512,1408]{1,0:T(8,128)(2,1)}, u32[]{:S(2)}, u32[]{:S(2)}) %collective-permute-start.26) | collective-permute-done | bytes 1441824 | tf_op jit(solution)/shard_map/ppermute | solution.py:18
  305.2 1.5 collective-permute-start.35
  308.1 2.3 collective-permute-done.32
  310.9 57.5 %collective-permute-done.35 = bf16[256,1408]{1,0:T(8,128)(2,1)S(1)} collective-permute-done((bf16[256,1408]{1,0:T(8,128)(2,1)S(1)}, bf16[256,1408]{1,0:T(8,128)(2,1)S(1)}, u32[]{:S(2)}, u32[]{:S(2)}) %collective-permute-start.35) | collective-permute-done | bytes 720928 | tf_op jit(solution)/shard_map/ppermute | solution.py:18
  369.8 1.5 copy.27
  371.3 2.3 convert_element_type.153
  (313 shorter events, 75.3 us)
Async XLA Ops:
  7.2 39.6 %copy-start = (bf16[512,2048]{1,0:T(8,128)(2,1)S(1)}, bf16[512,2048]{1,0:T(8,128)(2,1)}, u32[]{:S(2)}) copy-start(bf16[512,2048]{1,0:T(8,128)(2,1)} %param.18) | copy-start | bytes 6291460
  7.2 252.2 %reduce-scatter.4.cloned.1.call-start = ((), (), s32[]{:S(2)}) async-start(), calls=%async_computation.3 | async-start | bytes 3604480 | tf_op jit(solution)/shard_map/reduce_scatter | solution.py:299
  7.3 15.4 %copy-start.77 = (f32[32]{0:T(128)}, f32[32]{0:T(128)S(1)}, u32[]{:S(2)}) copy-start(f32[32]{0:T(128)S(1)} %multiply_exponential_fusion) | copy-start | bytes 388
  13.6 11.9 %copy-start.35 = (bf16[128,512]{1,0:T(8,128)(2,1)}, bf16[128,512]{1,0:T(8,128)(2,1)S(1)}, u32[]{:S(2)}) copy-start(bf16[128,512]{1,0:T(8,128)(2,1)S(1)} %pad_maximum_fusion.13.kv0) | copy-start | bytes 393220
  13.6 11.1 %collective-permute-start = (bf16[128,512]{1,0:T(8,128)(2,1)S(1)}, bf16[128,512]{1,0:T(8,128)(2,1)S(1)}, u32[]{:S(2)}, u32[]{:S(2)}) collective-permute-start(bf16[128,512]{1,0:T(8,128)(2,1)S(1)} %pad_maximum_fusion.13.kv0), channel_id=1, source_target_pairs={{0,4},{4,0},{8,12},{12,8},{16,20},{20,16},{24,28},{28,24},{1,5},{5... | collective-permute-start | bytes 393224 | tf_op jit(solution)/shard_map/ppermute | solution.py:18
  16.6 8.1 %collective-permute-start.1 = (bf16[128,512]{1,0:T(8,128)(2,1)S(1)}, bf16[128,512]{1,0:T(8,128)(2,1)S(1)}, u32[]{:S(2)}, u32[]{:S(2)}) collective-permute-start(bf16[128,512]{1,0:T(8,128)(2,1)S(1)} %pad_maximum_fusion.13.kv0), channel_id=1, source_target_pairs={{0,8},{4,12},{8,0},{12,4},{16,24},{20,28},{24,16},{28,20},{1,9},{5... | collective-permute-start | bytes 393224 | tf_op jit(solution)/shard_map/ppermute | solution.py:18
  18.2 6.5 %collective-permute-start.2 = (bf16[128,512]{1,0:T(8,128)(2,1)S(1)}, bf16[128,512]{1,0:T(8,128)(2,1)S(1)}, u32[]{:S(2)}, u32[]{:S(2)}) collective-permute-start(bf16[128,512]{1,0:T(8,128)(2,1)S(1)} %pad_maximum_fusion.13.kv0), channel_id=1, source_target_pairs={{0,12},{4,8},{8,4},{12,0},{16,28},{20,24},{24,20},{28,16},{1,13},{... | collective-permute-start | bytes 393224 | tf_op jit(solution)/shard_map/ppermute | solution.py:18
  20.7 26.0 %collective-permute-start.3 = (bf16[512,1024]{1,0:T(8,128)(2,1)}, bf16[512,1024]{1,0:T(8,128)(2,1)}, u32[]{:S(2)}, u32[]{:S(2)}) collective-permute-start(bf16[512,1024]{1,0:T(8,128)(2,1)} %pad_maximum_fusion.2), channel_id=1, source_target_pairs={{0,4},{4,0},{8,12},{12,8},{16,20},{20,16},{24,28},{28,24},{1,5},{5... | collective-permute-start | bytes 3145736 | tf_op jit(solution)/shard_map/ppermute | solution.py:18
  24.6 8.7 %copy-start.19 = (bf16[8,2,32,512]{3,2,1,0:T(8,128)(2,1)}, bf16[8,2,32,512]{3,2,1,0:T(8,128)(2,1)S(1)}, u32[]{:S(2)}) copy-start(bf16[8,2,32,512]{3,2,1,0:T(8,128)(2,1)S(1)} %fusion.17) | copy-start | bytes 1572868
  33.9 23.2 %copy-start.27 = (bf16[512,512]{1,0:T(8,128)(2,1)}, bf16[512,512]{1,0:T(8,128)(2,1)S(1)}, u32[]{:S(2)}) copy-start(bf16[512,512]{1,0:T(8,128)(2,1)S(1)} %get-tuple-element.67.o_in.g) | copy-start | bytes 1572868
  48.4 3.0 collective-permute-start.4
  53.0 14.0 %collective-permute-start.5 = (bf16[128,2048]{1,0:T(8,128)(2,1)S(1)}, bf16[128,2048]{1,0:T(8,128)(2,1)S(1)}, u32[]{:S(2)}, u32[]{:S(2)}) collective-permute-start(bf16[128,2048]{1,0:T(8,128)(2,1)S(1)} %slice.273), channel_id=1, source_target_pairs={{0,2},{1,3},{2,0},{3,1},{4,6},{5,7},{6,4},{7,5},{8,10},{9,11},{10,... | collective-permute-start | bytes 1572872 | tf_op jit(solution)/shard_map/ppermute | solution.py:18
  55.3 16.0 %slice-start = ((s8[5767168]{0:T(1024)(128)(4,1)}), s8[4194304]{0:T(1024)(128)(4,1)S(1)}, s32[]{:S(2)}) async-start(s8[5767168]{0:T(1024)(128)(4,1)} %bitcast.54), calls=%async_computation.6 | async-start | bytes 8388608
  55.7 15.6 %copy-start.1 = (bf16[512,2048]{1,0:T(8,128)(2,1)}, bf16[512,2048]{1,0:T(8,128)(2,1)S(1)}, u32[]{:S(2)}) copy-start(bf16[512,2048]{1,0:T(8,128)(2,1)S(1)} %pad_maximum_fusion.1.x) | copy-start | bytes 6291460
  55.7 11.4 %slice-start.4 = ((f32[256,2048]{1,0:T(8,128)}), f32[128,2048]{1,0:T(8,128)S(1)}, s32[]{:S(2)}) async-start(f32[256,2048]{1,0:T(8,128)} %copy-done.62), calls=%async_computation.10 | async-start | bytes 2097152 | tf_op jit(solution)/shard_map/slice | solution.py:462
  55.7 15.6 %slice-start.1 = ((s8[5767168]{0:T(1024)(128)(4,1)}), s8[1572864]{0:T(1024)(128)(4,1)S(1)}, s32[]{:S(2)}) async-start(s8[5767168]{0:T(1024)(128)(4,1)} %bitcast.54), calls=%async_computation.7 | async-start | bytes 3145728
  57.0 12.4 %copy-start.72 = (f32[2048]{0:T(1024)S(1)}, f32[2048]{0:T(1024)}, u32[]{:S(2)}) copy-start(f32[2048]{0:T(1024)} %param.19) | copy-start | bytes 24580
  57.0 19.4 %collective-permute-start.6 = (bf16[512,512]{1,0:T(8,128)(2,1)S(1)}, bf16[512,512]{1,0:T(8,128)(2,1)S(1)}, u32[]{:S(2)}, u32[]{:S(2)}) collective-permute-start(bf16[512,512]{1,0:T(8,128)(2,1)S(1)} %get-tuple-element.67.o_in.g), channel_id=1, source_target_pairs={{0,4},{4,0},{8,12},{12,8},{16,20},{20,16},{24,28},{28,24},{1,5},{5... | collective-permute-start | bytes 1572872 | tf_op jit(solution)/shard_map/ppermute | solution.py:18
  69.6 13.2 %collective-permute-start.7 = (bf16[128,2048]{1,0:T(8,128)(2,1)S(1)}, bf16[128,2048]{1,0:T(8,128)(2,1)S(1)}, u32[]{:S(2)}, u32[]{:S(2)}) collective-permute-start(bf16[128,2048]{1,0:T(8,128)(2,1)S(1)} %multiply_convert_fusion.3), channel_id=1, source_target_pairs={{0,2},{1,3},{2,0},{3,1},{4,6},{5,7},{6,4},{7,5},{8,10},{9,11},{10,... | collective-permute-start | bytes 1572872 | tf_op jit(solution)/shard_map/ppermute | solution.py:18
  76.4 10.2 %copy-start.42 = (bf16[512,512]{1,0:T(8,128)(2,1)}, bf16[512,512]{1,0:T(8,128)(2,1)S(1)}, u32[]{:S(2)}) copy-start(bf16[512,512]{1,0:T(8,128)(2,1)S(1)} %collective-permute-done.6.g_far) | copy-start | bytes 1572868
  83.6 5.9 %collective-permute-start.8 = (bf16[256,2048]{1,0:T(8,128)(2,1)}, bf16[256,2048]{1,0:T(8,128)(2,1)}, u32[]{:S(2)}, u32[]{:S(2)}) collective-permute-start(bf16[256,2048]{1,0:T(8,128)(2,1)} %constant_dynamic-update-slice_fusion), channel_id=1, source_target_pairs={{0,1},{1,0},{2,3},{3,2},{4,5},{5,4},{6,7},{7,6},{8,9},{9,8},{10,11... | collective-permute-start | bytes 3145736 | tf_op jit(solution)/shard_map/ppermute | solution.py:18
  83.7 25.8 %collective-permute-start.9 = (bf16[512,1024]{1,0:T(8,128)(2,1)}, bf16[512,1024]{1,0:T(8,128)(2,1)S(1)}, u32[]{:S(2)}, u32[]{:S(2)}) collective-permute-start(bf16[512,1024]{1,0:T(8,128)(2,1)} %pad_maximum_fusion.3), channel_id=1, source_target_pairs={{0,8},{4,12},{8,0},{12,4},{16,24},{20,28},{24,16},{28,20},{1,9},{5... | collective-permute-start | bytes 3145736 | tf_op jit(solution)/shard_map/ppermute | solution.py:18
  86.6 22.8 %collective-permute-start.10 = (bf16[256,1024]{1,0:T(8,128)(2,1)S(1)}, bf16[256,1024]{1,0:T(8,128)(2,1)S(1)}, u32[]{:S(2)}, u32[]{:S(2)}) collective-permute-start(bf16[256,1024]{1,0:T(8,128)(2,1)S(1)} %pad_maximum_fusion.8), channel_id=1, source_target_pairs={{0,4},{4,0},{8,12},{12,8},{16,20},{20,16},{24,28},{28,24},{1,5},{5... | collective-permute-start | bytes 1572872 | tf_op jit(solution)/shard_map/ppermute | solution.py:18
  91.0 63.5 %copy-start.21 = (bf16[512,2048]{1,0:T(8,128)(2,1)}, bf16[512,2048]{1,0:T(8,128)(2,1)S(1)}, u32[]{:S(2)}) copy-start(bf16[512,2048]{1,0:T(8,128)(2,1)S(1)} %constant_dynamic-update-slice_fusion.2.x) | copy-start | bytes 6291460
  91.0 12.2 %slice-start.5 = ((s8[5767168]{0:T(1024)(128)(4,1)}), s8[4194304]{0:T(1024)(128)(4,1)S(1)}, s32[]{:S(2)}) async-start(s8[5767168]{0:T(1024)(128)(4,1)} %bitcast.77), calls=%async_computation.11 | async-start | bytes 8388608
  102.6 12.0 %copy-start.39 = (bf16[512,1408]{1,0:T(8,128)(2,1)}, bf16[512,1408]{1,0:T(8,128)(2,1)S(1)}, u32[]{:S(2)}) copy-start(bf16[512,1408]{1,0:T(8,128)(2,1)S(1)} %get-tuple-element.90.g) | copy-start | bytes 4325380
  102.6 51.9 %collective-permute-start.17 = (bf16[512,1408]{1,0:T(8,128)(2,1)S(1)}, bf16[512,1408]{1,0:T(8,128)(2,1)S(1)}, u32[]{:S(2)}, u32[]{:S(2)}) collective-permute-start(bf16[512,1408]{1,0:T(8,128)(2,1)S(1)} %get-tuple-element.70.g), channel_id=1, source_target_pairs={{0,4},{4,0},{8,12},{12,8},{16,20},{20,16},{24,28},{28,24},{1,5},{5... | collective-permute-start | bytes 4325384 | tf_op jit(solution)/shard_map/ppermute | solution.py:18
  109.5 36.9 %copy-start.9 = (bf16[512,1024]{1,0:T(8,128)(2,1)}, bf16[512,1024]{1,0:T(8,128)(2,1)S(1)}, u32[]{:S(2)}) copy-start(bf16[512,1024]{1,0:T(8,128)(2,1)S(1)} %collective-permute-done.9.x_far) | copy-start | bytes 3145732
  112.3 9.1 %collective-permute-start.11 = (bf16[256,2048]{1,0:T(8,128)(2,1)}, bf16[256,2048]{1,0:T(8,128)(2,1)S(1)}, u32[]{:S(2)}, u32[]{:S(2)}) collective-permute-start(bf16[256,2048]{1,0:T(8,128)(2,1)} %fusion.4), channel_id=1, source_target_pairs={{0,1},{1,0},{2,3},{3,2},{4,5},{5,4},{6,7},{7,6},{8,9},{9,8},{10,11... | collective-permute-start | bytes 3145736 | tf_op jit(solution)/shard_map/ppermute | solution.py:18
  112.3 9.0 %collective-permute-start.12 = (bf16[256,1024]{1,0:T(8,128)(2,1)S(1)}, bf16[256,1024]{1,0:T(8,128)(2,1)S(1)}, u32[]{:S(2)}, u32[]{:S(2)}) collective-permute-start(bf16[256,1024]{1,0:T(8,128)(2,1)S(1)} %collective-permute-done.10), channel_id=1, source_target_pairs={{0,1},{1,0},{2,3},{3,2},{4,5},{5,4},{6,7},{7,6},{8,9},{9,8},{10,11... | collective-permute-start | bytes 1572872 | tf_op jit(solution)/shard_map/ppermute | solution.py:18
  112.8 33.5 %collective-permute-start.15 = (bf16[512,1408]{1,0:T(8,128)(2,1)S(1)}, bf16[512,1408]{1,0:T(8,128)(2,1)S(1)}, u32[]{:S(2)}, u32[]{:S(2)}) collective-permute-start(bf16[512,1408]{1,0:T(8,128)(2,1)S(1)} %get-tuple-element.98.left.g), channel_id=1, source_target_pairs={{0,8},{4,12},{8,0},{12,4},{16,24},{20,28},{24,16},{28,20},{1,9},{5... | collective-permute-start | bytes 4325384 | tf_op jit(solution)/shard_map/ppermute | solution.py:18
  114.6 8.8 %slice-start.2 = ((s8[5767168]{0:T(1024)(128)(4,1)}), s8[4194304]{0:T(1024)(128)(4,1)S(1)}, s32[]{:S(2)}) async-start(s8[5767168]{0:T(1024)(128)(4,1)} %bitcast.56), calls=%async_computation.8 | async-start | bytes 8388608
  121.4 33.0 %copy-start.15 = (bf16[512,1024]{1,0:T(8,128)(2,1)}, bf16[512,1024]{1,0:T(8,128)(2,1)S(1)}, u32[]{:S(2)}) copy-start(bf16[512,1024]{1,0:T(8,128)(2,1)S(1)} %pad_maximum_fusion.4.x_far) | copy-start | bytes 3145732
  121.8 13.6 %collective-permute-start.13 = (bf16[128,2048]{1,0:T(8,128)(2,1)S(1)}, bf16[128,2048]{1,0:T(8,128)(2,1)S(1)}, u32[]{:S(2)}, u32[]{:S(2)}) collective-permute-start(bf16[128,2048]{1,0:T(8,128)(2,1)S(1)} %slice.272), channel_id=1, source_target_pairs={{0,2},{1,3},{2,0},{3,1},{4,6},{5,7},{6,4},{7,5},{8,10},{9,11},{10,... | collective-permute-start | bytes 1572872 | tf_op jit(solution)/shard_map/ppermute | solution.py:18
  136.3 10.0 %copy-start.2 = (bf16[512,2048]{1,0:T(8,128)(2,1)S(1)}, bf16[512,2048]{1,0:T(8,128)(2,1)}, u32[]{:S(2)}) copy-start(bf16[512,2048]{1,0:T(8,128)(2,1)} %copy-done.1) | copy-start | bytes 6291460
  138.9 12.7 %collective-permute-start.16 = (bf16[128,2048]{1,0:T(8,128)(2,1)S(1)}, bf16[128,2048]{1,0:T(8,128)(2,1)S(1)}, u32[]{:S(2)}, u32[]{:S(2)}) collective-permute-start(bf16[128,2048]{1,0:T(8,128)(2,1)S(1)} %get-tuple-element.82), channel_id=1, source_target_pairs={{0,2},{1,3},{2,0},{3,1},{4,6},{5,7},{6,4},{7,5},{8,10},{9,11},{10,... | collective-permute-start | bytes 1572872 | tf_op jit(solution)/shard_map/ppermute | solution.py:18
  152.4 10.4 %collective-permute-start.18 = (bf16[256,2048]{1,0:T(8,128)(2,1)}, bf16[256,2048]{1,0:T(8,128)(2,1)}, u32[]{:S(2)}, u32[]{:S(2)}) collective-permute-start(bf16[256,2048]{1,0:T(8,128)(2,1)} %constant_dynamic-update-slice_fusion.4), channel_id=1, source_target_pairs={{0,1},{1,0},{2,3},{3,2},{4,5},{5,4},{6,7},{7,6},{8,9},{9,8},{10,11... | collective-permute-start | bytes 3145736 | tf_op jit(solution)/shard_map/ppermute | solution.py:18
  167.7 203.6 %reduce-scatter.8.cloned.1.call-start = ((), (), s32[]{:S(2)}) async-start(), calls=%async_computation.5 | async-start | bytes 3604480 | tf_op jit(solution)/shard_map/reduce_scatter | solution.py:299
  167.8 42.5 %collective-permute-start.21 = (bf16[512,1408]{1,0:T(8,128)(2,1)}, bf16[512,1408]{1,0:T(8,128)(2,1)S(1)}, u32[]{:S(2)}, u32[]{:S(2)}) collective-permute-start(bf16[512,1408]{1,0:T(8,128)(2,1)} %copy-done.39), channel_id=1, source_target_pairs={{0,4},{4,0},{8,12},{12,8},{16,20},{20,16},{24,28},{28,24},{1,5},{5... | collective-permute-start | bytes 4325384 | tf_op jit(solution)/shard_map/ppermute | solution.py:18
  169.3 18.7 %collective-permute-start.14 = (bf16[256,2048]{1,0:T(8,128)(2,1)}, bf16[256,2048]{1,0:T(8,128)(2,1)S(1)}, u32[]{:S(2)}, u32[]{:S(2)}) collective-permute-start(bf16[256,2048]{1,0:T(8,128)(2,1)} %copy-done.41), channel_id=1, source_target_pairs={{0,1},{1,0},{2,3},{3,2},{4,5},{5,4},{6,7},{7,6},{8,9},{9,8},{10,11... | collective-permute-start | bytes 3145736 | tf_op jit(solution)/shard_map/ppermute | solution.py:18
  169.5 50.1 %collective-permute-start.20 = (bf16[256,1024]{1,0:T(8,128)(2,1)}, bf16[256,1024]{1,0:T(8,128)(2,1)}, u32[]{:S(2)}, u32[]{:S(2)}) collective-permute-start(bf16[256,1024]{1,0:T(8,128)(2,1)} %pad_maximum_fusion.9), channel_id=1, source_target_pairs={{0,4},{4,0},{8,12},{12,8},{16,20},{20,16},{24,28},{28,24},{1,5},{5... | collective-permute-start | bytes 1572872 | tf_op jit(solution)/shard_map/ppermute | solution.py:18
  179.3 29.2 %copy-start.14 = (f32[256,2048]{1,0:T(8,128)S(1)}, f32[256,2048]{1,0:T(8,128)}, u32[]{:S(2)}) copy-start(f32[256,2048]{1,0:T(8,128)} %copy-done.13) | copy-start | bytes 6291460
  188.0 22.2 %copy-start.25 = (bf16[512,512]{1,0:T(8,128)(2,1)}, bf16[512,512]{1,0:T(8,128)(2,1)S(1)}, u32[]{:S(2)}) copy-start(bf16[512,512]{1,0:T(8,128)(2,1)S(1)} %get-tuple-element.87) | copy-start | bytes 1572868
  188.0 31.6 %collective-permute-start.24 = (bf16[128,512]{1,0:T(8,128)(2,1)}, bf16[128,512]{1,0:T(8,128)(2,1)}, u32[]{:S(2)}, u32[]{:S(2)}) collective-permute-start(bf16[128,512]{1,0:T(8,128)(2,1)} %get-tuple-element.94), channel_id=1, source_target_pairs={{0,12},{4,8},{8,4},{12,0},{16,28},{20,24},{24,20},{28,16},{1,13},{... | collective-permute-start | bytes 393224 | tf_op jit(solution)/shard_map/ppermute | solution.py:18
  207.9 13.3 %collective-permute-start.23 = (bf16[128,512]{1,0:T(8,128)(2,1)}, bf16[128,512]{1,0:T(8,128)(2,1)}, u32[]{:S(2)}, u32[]{:S(2)}) collective-permute-start(bf16[128,512]{1,0:T(8,128)(2,1)} %get-tuple-element.93), channel_id=1, source_target_pairs={{0,8},{4,12},{8,0},{12,4},{16,24},{20,28},{24,16},{28,20},{1,9},{5... | collective-permute-start | bytes 393224 | tf_op jit(solution)/shard_map/ppermute | solution.py:18
  207.9 13.3 %collective-permute-start.22 = (bf16[128,512]{1,0:T(8,128)(2,1)}, bf16[128,512]{1,0:T(8,128)(2,1)}, u32[]{:S(2)}, u32[]{:S(2)}) collective-permute-start(bf16[128,512]{1,0:T(8,128)(2,1)} %get-tuple-element.92), channel_id=1, source_target_pairs={{0,4},{4,0},{8,12},{12,8},{16,20},{20,16},{24,28},{28,24},{1,5},{5... | collective-permute-start | bytes 393224 | tf_op jit(solution)/shard_map/ppermute | solution.py:18
  223.7 149.9 %reduce-scatter.6.cloned.1.call-start = ((), (), s32[]{:S(2)}) async-start(), calls=%async_computation.4 | async-start | bytes 2949120 | tf_op jit(solution)/shard_map/reduce_scatter | solution.py:299
  226.7 9.3 %copy-start.67 = (bf16[2048,64]{0,1:T(8,128)(2,1)S(1)}, bf16[2048,64]{0,1:T(8,128)(2,1)}, u32[]{:S(2)}) copy-start(bf16[2048,64]{0,1:T(8,128)(2,1)} %param.17) | copy-start | bytes 786436
  226.7 9.3 %copy-start.69 = (bf16[2048,64]{0,1:T(8,128)(2,1)S(1)}, bf16[2048,64]{0,1:T(8,128)(2,1)}, u32[]{:S(2)}) copy-start(bf16[2048,64]{0,1:T(8,128)(2,1)} %param.16) | copy-start | bytes 786436
  227.4 15.1 %collective-permute-start.25 = (bf16[256,2048]{1,0:T(8,128)(2,1)S(1)}, bf16[256,2048]{1,0:T(8,128)(2,1)S(1)}, u32[]{:S(2)}, u32[]{:S(2)}) collective-permute-start(bf16[256,2048]{1,0:T(8,128)(2,1)S(1)} %fusion.5), channel_id=1, source_target_pairs={{0,1},{1,0},{2,3},{3,2},{4,5},{5,4},{6,7},{7,6},{8,9},{9,8},{10,11... | collective-permute-start | bytes 3145736 | tf_op jit(solution)/shard_map/ppermute | solution.py:18
  228.3 15.5 %collective-permute-start.19 = (bf16[128,2048]{1,0:T(8,128)(2,1)S(1)}, bf16[128,2048]{1,0:T(8,128)(2,1)S(1)}, u32[]{:S(2)}, u32[]{:S(2)}) collective-permute-start(bf16[128,2048]{1,0:T(8,128)(2,1)S(1)} %copy-done.70), channel_id=1, source_target_pairs={{0,2},{1,3},{2,0},{3,1},{4,6},{5,7},{6,4},{7,5},{8,10},{9,11},{10,... | collective-permute-start | bytes 1572872 | tf_op jit(solution)/shard_map/ppermute | solution.py:18
  229.8 7.4 %collective-permute-start.34 = (bf16[256,1024]{1,0:T(8,128)(2,1)}, bf16[256,1024]{1,0:T(8,128)(2,1)S(1)}, u32[]{:S(2)}, u32[]{:S(2)}) collective-permute-start(bf16[256,1024]{1,0:T(8,128)(2,1)} %collective-permute-done.20), channel_id=1, source_target_pairs={{0,1},{1,0},{2,3},{3,2},{4,5},{5,4},{6,7},{7,6},{8,9},{9,8},{10,11... | collective-permute-start | bytes 1572872 | tf_op jit(solution)/shard_map/ppermute | solution.py:18
  230.1 31.8 %collective-permute-start.33 = (bf16[640,512]{1,0:T(8,128)(2,1)}, bf16[640,512]{1,0:T(8,128)(2,1)}, u32[]{:S(2)}, u32[]{:S(2)}) collective-permute-start(bf16[640,512]{1,0:T(8,128)(2,1)} %pad_maximum_fusion.6.g), channel_id=1, source_target_pairs={{0,4},{4,0},{8,12},{12,8},{16,20},{20,16},{24,28},{28,24},{1,5},{5... | collective-permute-start | bytes 1966088 | tf_op jit(solution)/shard_map/ppermute | solution.py:18
  243.5 14.1 %copy-start.74 = (f32[2048]{0:T(1024)S(1)}, f32[2048]{0:T(1024)}, u32[]{:S(2)}) copy-start(f32[2048]{0:T(1024)} %param.14) | copy-start | bytes 24580
  243.6 14.0 %copy-start.58 = (bf16[512,2048]{1,0:T(8,128)(2,1)S(1)}, bf16[512,2048]{1,0:T(8,128)(2,1)}, u32[]{:S(2)}) copy-start(bf16[512,2048]{1,0:T(8,128)(2,1)} %param.12) | copy-start | bytes 6291460
  243.6 14.3 %copy-start.63 = (f32[128,2048]{1,0:T(8,128)S(1)}, f32[128,2048]{1,0:T(8,128)}, u32[]{:S(2)}) copy-start(f32[128,2048]{1,0:T(8,128)} %get-tuple-element.121) | copy-start | bytes 3145732
  243.6 13.9 %collective-permute-start.27 = (bf16[128,2048]{1,0:T(8,128)(2,1)S(1)}, bf16[128,2048]{1,0:T(8,128)(2,1)S(1)}, u32[]{:S(2)}, u32[]{:S(2)}) collective-permute-start(bf16[128,2048]{1,0:T(8,128)(2,1)S(1)} %slice.270), channel_id=1, source_target_pairs={{0,2},{1,3},{2,0},{3,1},{4,6},{5,7},{6,4},{7,5},{8,10},{9,11},{10,... | collective-permute-start | bytes 1572872 | tf_op jit(solution)/shard_map/ppermute | solution.py:18
  269.0 2.4 collective-permute-start.28
  269.1 34.8 %collective-permute-start.26 = (bf16[512,1408]{1,0:T(8,128)(2,1)}, bf16[512,1408]{1,0:T(8,128)(2,1)}, u32[]{:S(2)}, u32[]{:S(2)}) collective-permute-start(bf16[512,1408]{1,0:T(8,128)(2,1)} %copy-done.38), channel_id=1, source_target_pairs={{0,4},{4,0},{8,12},{12,8},{16,20},{20,16},{24,28},{28,24},{1,5},{5... | collective-permute-start | bytes 4325384 | tf_op jit(solution)/shard_map/ppermute | solution.py:18
  272.6 4.1 %collective-permute-start.29 = (f32[2,2048]{1,0:T(2,128)}, f32[2,2048]{1,0:T(2,128)}, u32[]{:S(2)}, u32[]{:S(2)}) collective-permute-start(f32[2,2048]{1,0:T(2,128)} %fusion.58), channel_id=1, source_target_pairs={{0,2},{1,3},{2,0},{3,1},{4,6},{5,7},{6,4},{7,5},{8,10},{9,11},{10,... | collective-permute-start | bytes 49160 | tf_op jit(solution)/shard_map/ppermute | solution.py:18
  277.5 6.1 %collective-permute-start.30 = (f32[2,1024]{1,0:T(2,128)S(1)}, f32[2,1024]{1,0:T(2,128)S(1)}, u32[]{:S(2)}, u32[]{:S(2)}) collective-permute-start(f32[2,1024]{1,0:T(2,128)S(1)} %pad_maximum_fusion.21), channel_id=1, source_target_pairs={{0,16},{4,20},{8,24},{12,28},{16,0},{20,4},{24,8},{28,12},{1,17},{... | collective-permute-start | bytes 24584 | tf_op jit(solution)/shard_map/ppermute | solution.py:18
  283.6 23.1 %collective-permute-start.31 = (f32[2,512]{1,0:T(2,128)S(1)}, f32[2,512]{1,0:T(2,128)S(1)}, u32[]{:S(2)}, u32[]{:S(2)}) collective-permute-start(f32[2,512]{1,0:T(2,128)S(1)} %slice.202), channel_id=1, source_target_pairs={{0,8},{4,12},{8,0},{12,4},{16,24},{20,28},{24,16},{28,20},{1,9},{5... | collective-permute-start | bytes 12296 | tf_op jit(solution)/shard_map/ppermute | solution.py:18
  305.2 63.3 %collective-permute-start.35 = (bf16[256,1408]{1,0:T(8,128)(2,1)S(1)}, bf16[256,1408]{1,0:T(8,128)(2,1)S(1)}, u32[]{:S(2)}, u32[]{:S(2)}) collective-permute-start(bf16[256,1408]{1,0:T(8,128)(2,1)S(1)} %fusion.59), channel_id=1, source_target_pairs={{0,16},{4,20},{8,24},{12,28},{16,0},{20,4},{24,8},{28,12},{1,17},{... | collective-permute-start | bytes 2162696 | tf_op jit(solution)/shard_map/ppermute | solution.py:18
  306.7 3.7 collective-permute-start.32
  (64 other events, 182.5 us)
Sparse Core Ops, SparseCore 0:
  167.8 61.9 reduce-scatter.3
  232.1 56.2 reduce-scatter.7
  290.7 69.5 reduce-scatter.5

commit v5 on v4

--- a/solution.py
+++ b/solution.py
@@ -25,6 +25,10 @@
         (((left_dim,), (right_dim,)), ((), ())),
         preferred_element_type=jnp.float32,
     )
+
+
+def in_hbm(*arrays):
+    return [pltpu.with_memory_space_constraint(a, pltpu.HBM) for a in arrays]
 
 
 def own_mask(pos, begin, keys, queries):
@@ -279,7 +283,7 @@
             transcendentals=0,
         ),
         name="attention_backward",
-    )(at, pos, queries, grads, attended, lse, cosine, sine, *blocks)
+    )(at, pos, *in_hbm(queries, grads, attended, lse, cosine, sine, *blocks))
 
 
 def pick(values, places, blocks, dim):
@@ -320,7 +324,7 @@
     whole = pl.BlockSpec(g.shape, lambda i, p: (0, 0))
     return pl.pallas_call(
         functools.partial(terms_kernel, transposed),
-        out_shape=jax.ShapeDtypeStruct((count * size, units), LOW),
+        out_shape=pltpu.HBM((count * size, units), LOW),
         grid_spec=pltpu.PrefetchScalarGridSpec(
             num_scalar_prefetch=1,
             grid=(count,),
@@ -486,9 +490,9 @@
     grad_hidden = dot(after(cot, own_two), w_down, 1, 1)
     pair_two = jnp.concatenate([after(own_two, grad_hidden, att_theirs), far_two], 0)
     core_two = flip(pair_two, "tp", 1)
-    two_send = columns(pair_two, 1)
-    two_near = flip(two_send, "dp", 1)
-    normed_two = jnp.concatenate([after(pair_two, two_send), core_two], 0)
+    two_send, two_far_half = columns(pair_two, 1), pick(pair_two, near_halves[1], dp, 1)
+    two_near, two_far_near = flip(two_send, "dp", 1), flip(two_far_half, "dp", 2)
+    normed_two = jnp.concatenate([after(pair_two, two_send, two_far_half), core_two], 0)
 
     gate_pre = dot(normed_two, w_gate, 1, 0)
     up_pre = dot(normed_two, w_up, 1, 0)
@@ -500,9 +504,10 @@
     hidden_theirs = flip(hidden, "dp", 2)
     gate_theirs = flip(grad_gate_pre, "dp", 1)
 
-    gate_late, cot_theirs, two_near = lax.optimization_barrier(
-        (grad_gate_pre, cot_theirs, two_near)
-    )
+    gate_late, cot_theirs, two_near, two_far_near = lax.optimization_barrier(
+        (grad_gate_pre, cot_theirs, two_near, two_far_near)
+    )
+    two_near = jnp.concatenate([two_near, two_far_near], 1)
     two_theirs = jnp.concatenate([two_near, flip(two_near, "tp", 1)], 0)
 
     def two_terms(lo, hi):
@@ -512,11 +517,12 @@
 
     grad_normed_two, two_far_send = near_sum(two_terms)
     two_far_send, two_theirs = lax.optimization_barrier((two_far_send, two_theirs))
+    far_first = dp // 2
     two_far = flip(two_far_send, "tp", 2)
 
     hidden_late = after(hidden, two_far_send)
     down_near, down = row_terms(hidden_late, w_down)
-    up_theirs = flip(grad_up_pre, "dp", 1)
+    up_theirs = flip(grad_up_pre, "dp", 2)
     grad_normed_two = after(grad_normed_two, down) + two_far
 
     grad_mid_norm, gain_two = norm_back(grad_normed_two, middle, scale_two, norm2_gain)
@@ -524,26 +530,35 @@
     branch_grad = grad_middle.astype(LOW)
     grad_far = flip(branch_grad, "tp", 2)
 
-    hidden_late = after(hidden, branch_grad)
-
-    def down_terms(lo, hi):
-        return weight_terms(
-            near_halves[0][lo:hi], lo, cot, cot_theirs, hidden_late, hidden_theirs
-        )
-
-    count = dp // 2
-    first_send = down_terms(count // 2, count)
     down_near = flip(after(down_near, branch_grad), "tp", 1)
-    grad_pair = jnp.concatenate([after(branch_grad, first_send), grad_far], 0)
+    two_late = after(normed_two, branch_grad)
+    gate_terms = weight_terms(halves[0], 0, two_late, two_theirs, grad_gate_pre, gate_theirs)
+    grad_gate = parity_sum(gate_terms, 0)
+    grad_pair = jnp.concatenate([after(branch_grad, gate_terms), grad_far], 0)
     grad_core = flip(grad_pair, "tp", 1)
-
     branch_send = columns(grad_pair, 1)
     branch_near = flip(branch_send, "dp", 1)
-    two_late = after(normed_two, branch_send)
-    gate_terms = weight_terms(halves[0], 0, two_late, two_theirs, grad_gate_pre, gate_theirs)
-    branch_all = jnp.concatenate([after(grad_pair, gate_terms), grad_core], 0)
+
+    def down_terms(lo, hi, *late):
+        return weight_terms(
+            near_halves[0][lo:hi], lo, cot, cot_theirs, after(hidden, *late), hidden_theirs
+        )
+
+    def up_terms(lo, hi, *late):
+        return weight_terms(
+            near_halves[0][lo:hi],
+            far_first + lo,
+            normed_two,
+            two_theirs,
+            after(grad_up_pre, *late),
+            up_theirs,
+        )
+
+    count = dp // 2
+    down_sent = [down_terms(count // 2, count, branch_send)]
+
+    branch_all = jnp.concatenate([after(grad_pair, down_sent[0]), grad_core], 0)
     grad_attended = dot(w_out, branch_all, 1, 1).astype(LOW)
-    grad_gate = parity_sum(after(gate_terms, grad_attended), 0)
 
     grads = attention_backward(
         at, pos, queries, grad_attended, attended, lse, cosine, sine, blocks, size, 2
@@ -551,22 +566,19 @@
     grad_query_rows, kv_total = grads[0], grads[1]
     kv_back = [flip(grads[m + 1], "dp", m) for m in range(1, SPAN)]
 
-    up_late = after(grad_up_pre, grad_query_rows)
-    up_terms = weight_terms(halves[0], 0, normed_two, two_theirs, up_late, up_theirs)
     down = down + after(down_near, grad_query_rows)
     down, down_send = down[:own_rows], down[own_rows:].astype(LOW)
     down_far = flip(down_send, "tp", 2)
-    got = [flip(after(first_send, up_terms), "dp", 1)]
-
-    kv_total, branch_near = lax.optimization_barrier(
-        (kv_total, branch_near, up_terms, down_send)
-    )[:2]
+    up_sent = [up_terms(count // 2, count, grad_query_rows)]
+    down_got = [flip(down_sent[0], "dp", 1)]
+    kv_total, branch_near, down_got[0] = lax.optimization_barrier(
+        (kv_total, branch_near, down_got[0], up_sent[0], down_send)
+    )[:3]
     for back in kv_back:
         kv_total = kv_total + back
     key_grad = turn_back(kv_total[:size], cosine, sine)
     grad_kv_rows = jnp.concatenate([key_grad, kv_total[size:]], 0).astype(LOW)
     proj_rows = jnp.concatenate([grad_query_rows, grad_kv_rows], 0)
-    grad_up = parity_sum(after(up_terms, proj_rows), 0)
     proj_theirs = flip(proj_rows, "dp", 1)
 
     own_order = pick(proj_rows, [spot ^ m for m in ROW_MASKS], len(tp_masks), 1)
@@ -579,36 +591,41 @@
     grad_normed_one, one_far_send = near_sum(one_terms)
     one_far = flip(one_far_send, "tp", 2)
 
+    up_got = [flip(after(up_sent[0], one_far_send), "dp", 1)]
     branch_theirs = jnp.concatenate([branch_near, flip(branch_near, "tp", 1)], 0)
-    hidden_late = after(hidden, one_far_send)
-    count //= 2
-    for b in near_bits[1:]:
-        send = down_terms(count // 2, count).astype(jnp.float32)
-        for other in got:
-            send = send + other[count // 2 * block : count * block]
-        got.append(flip(send.astype(LOW), "dp", 1 << b))
-        count //= 2
-    grad_down = down_terms(0, 1).astype(jnp.float32)
+    out_late = after(attended, one_far_send)
+    out_terms = weight_terms(halves[0], 0, branch_all, branch_theirs, out_late, att_theirs, True)
+    grad_out = parity_sum(out_terms, 0)
+
+    def exchange_rest(terms, got, late):
+        left = count // 2
+        for b in near_bits[1:]:
+            send = terms(left // 2, left, late).astype(jnp.float32)
+            for other in got:
+                send = send + other[left // 2 * block : left * block]
+            got.append(flip(send.astype(LOW), "dp", 1 << b))
+            left //= 2
+        return terms(0, 1, late), send
+
+    grad_down, down_last = exchange_rest(down_terms, down_got, out_terms)
     output_rows = (middle + (down + after(down_far, one_far_send))).astype(LOW)
-    grad_normed_one = after(grad_normed_one, send, grad_down, output_rows) + one_far
+    grad_normed_one = after(grad_normed_one, down_last, grad_down, output_rows) + one_far
     grad_in_norm, gain_one = norm_back(grad_normed_one, own_inputs, own(scale_one), norm1_gain)
     input_rows = grad_middle + grad_in_norm
     grad_gate = grad_gate.astype(jnp.float32)
 
     proj_late = after(proj_rows, input_rows, grad_gate)
-    last_terms = jnp.concatenate(
-        [
-            weight_terms(halves[0], 0, normed_one, one_theirs, proj_late, proj_theirs, True),
-            weight_terms(halves[0], 0, branch_all, branch_theirs, attended, att_theirs, True),
-        ],
-        1,
-    )
-    grad_up = grad_up.astype(jnp.float32)
-    grad_last = parity_sum(last_terms, 0).astype(jnp.float32)
-    narrow = wide + 2 * size
-
-    for other in got:
-        grad_down = grad_down + other[:block]
+    proj_terms = weight_terms(halves[0], 0, normed_one, one_theirs, proj_late, proj_theirs, True)
+    grad_out = grad_out.astype(jnp.float32)
+    grad_proj = parity_sum(proj_terms, 0).astype(jnp.float32)
+
+    grad_up, up_last = exchange_rest(up_terms, up_got, proj_terms)
+
+    def total(kept, got):
+        kept = kept.astype(jnp.float32)
+        for other in got:
+            kept = kept + other[:block]
+        return kept
 
     gains = jnp.stack([gain_one, gain_two])
     for m in (1, 2):
@@ -623,14 +640,14 @@
         output_rows,
         input_rows,
         gains[0],
-        grad_last[:, :wide],
-        grad_last[:, wide : wide + size],
-        grad_last[:, wide + size : narrow],
-        grad_last[:, narrow:].T,
+        grad_proj[:, :wide],
+        grad_proj[:, wide : wide + size],
+        grad_proj[:, wide + size :],
+        grad_out.T,
         gains[1],
         grad_gate,
-        grad_up,
-        grad_down.T,
+        total(grad_up, up_got),
+        total(grad_down, down_got).T,
     )
 
 

time: 391 us -> 434 us (1.11)
  waiting for transfers between devices: 140 us -> 169 us
  Pallas kernels: 43.6 us -> 60.4 us
    ppermute x36 -> x39, waiting for transfers between devices: 140 us -> 169 us  [flip(): lax.ppermute(block, axis, [(i, i ^ mask) for i in range(lax.axis_size(axi...]
    pallas_call x7 -> x9, Pallas kernels: 23 us -> 38.5 us  [weight_terms(): pl.pallas_call(functools.partial(terms_kernel, transposed), out_shape=plt...]
    unnamed x184 -> x187, local copies, waits for them, and re-layouts: 37.5 us -> 32.9 us
    ppermute x36 -> x39, starting transfers between devices: 60.9 us -> 59 us  [flip(): lax.ppermute(block, axis, [(i, i ^ mask) for i in range(lax.axis_size(axi...]
  transfers between devices with their start and end apart: 39 -> 42, of which waited for: 14 -> 15; matrix products, arithmetic and copies ran while one was open for 21% -> 21% of each run, Pallas kernels for 11% -> 14%
where the time goes in v5:
time: 434 us; the launch traced here: 428 us
  waiting for transfers between devices  169 us (39%)
  Pallas kernels  60.4 us (14%)
  starting transfers between devices  59.3 us (14%)
  local copies, waits for them, and re-layouts  49.3 us (11%)
  matrix products  37.8 us (9%)
  other arithmetic  37.6 us (9%)
  between operations  15.5 us (4%)
    ppermute x39, waiting for transfers between devices, flip(): lax.ppermute(block, axis, [(i, i ^ mask) for i in range(lax.axis_size(axi...  169 us
    ppermute x39, starting transfers between devices, flip(): lax.ppermute(block, axis, [(i, i ^ mask) for i in range(lax.axis_size(axi...  59 us
    pallas_call x9, Pallas kernels, weight_terms(): pl.pallas_call(functools.partial(terms_kernel, transposed), out_shape=plt...  38.5 us
    dot_general x16, matrix products, dot(): lax.dot_general(left, right, (((left_dim,), (right_dim,)), ((), ())), pre...  37.8 us
    unnamed x187, local copies, waits for them, and re-layouts  32.9 us
    pallas_call x1, Pallas kernels, attention_backward(): pl.pallas_call(functools.partial(backward_kernel, heads, size), out_shape...  8.98 us
  transfers between devices with their start and end apart: 42, of which 15 were waited for; matrix products, arithmetic and copies ran while one was open for 21% of the time, Pallas kernels for 14%

profile of v5, /device:TPU:0, one launch (start us, length us, event | category | flops | bytes accessed | tf_op | source)
XLA Modules:
  0.0 428.4 jit_solution(6150199991860147282)
XLA Ops:
  7.3 2.2 fusion
  14.0 3.0 collective-permute-start
  21.1 1.9 collective-permute-start.3
  26.8 7.1 %attention_forward.1 = (bf16[512,512]{1,0:T(8,128)(2,1)S(1)}, f32[8,1,512]{2,1,0:T(1,128)S(1)}) custom-call(s32[2]{0:T(128)S(1)} %pad_add_fusion.at_ref, s32[1,512]{1,0:T(1,128)S(1)} %bitcast.52, bf16[512,512]{1,0:T(8,128)(2,1)S(1)} %bitcast.50, bf16[128,512]{1,0:T(8,128)(2,1)S(1)} %pad_maximum_fusion.13.kv0, bf16[128,512]{1,0:T(8,128)(2,1)S(1)} %collective-permute-done.kv1, ...), custom_call_target="tpu_custom_call" | custom-call | flops 17179869184 | bytes 1048576 | tf_op jit(solution)/shard_map/attention_forward/pallas_call | solution.py:214
  34.6 12.6 %collective-permute-done.3.x_far = bf16[512,1024]{1,0:T(8,128)(2,1)} collective-permute-done((bf16[512,1024]{1,0:T(8,128)(2,1)}, bf16[512,1024]{1,0:T(8,128)(2,1)}, u32[]{:S(2)}, u32[]{:S(2)}) %collective-permute-start.3) | collective-permute-done | bytes 1048608 | tf_op jit(solution)/shard_map/ppermute | solution.py:18
  47.2 1.7 convolution_convert_fusion
  49.6 2.3 collective-permute-done.4
  53.5 1.8 collective-permute-start.5
  57.4 1.7 collective-permute-start.6
  59.1 8.4 %collective-permute-done.5 = bf16[128,2048]{1,0:T(8,128)(2,1)S(1)} collective-permute-done((bf16[128,2048]{1,0:T(8,128)(2,1)S(1)}, bf16[128,2048]{1,0:T(8,128)(2,1)S(1)}, u32[]{:S(2)}, u32[]{:S(2)}) %collective-permute-start.5) | collective-permute-done | bytes 524320 | tf_op jit(solution)/shard_map/ppermute | solution.py:18
  70.0 1.8 collective-permute-start.7
  71.8 5.0 %fusion.64 = f32[512,1408]{1,0:T(8,128)} fusion(bf16[512,2048]{1,0:T(8,128)(2,1)S(1)} %pad_maximum_fusion.x, bf16[1408,2048]{1,0:T(8,128)(2,1)S(1)} %bitcast.55), kind=kOutput, calls=%fused_computation.187 | convolution fusion | flops 2952790016 | bytes 10747904 | tf_op jit(solution)/shard_map/dot_general | solution.py:22
  77.7 5.5 %collective-permute-done.7 = bf16[128,2048]{1,0:T(8,128)(2,1)S(1)} collective-permute-done((bf16[128,2048]{1,0:T(8,128)(2,1)S(1)}, bf16[128,2048]{1,0:T(8,128)(2,1)S(1)}, u32[]{:S(2)}, u32[]{:S(2)}) %collective-permute-start.7) | collective-permute-done | bytes 524320 | tf_op jit(solution)/shard_map/ppermute | solution.py:18
  83.4 1.7 collective-permute-start.9
  89.1 6.8 %fusion.65 = f32[512,1408]{1,0:T(8,128)S(1)} fusion(bf16[512,2048]{1,0:T(8,128)(2,1)S(1)} %constant_dynamic-update-slice_fusion.2.x, bf16[2048,1408]{1,0:T(8,128)(2,1)} %param.21), kind=kOutput, calls=%fused_computation.188 | convolution fusion | flops 2952790016 | bytes 10747904 | tf_op jit(solution)/shard_map/dot_general | solution.py:22
  95.9 4.5 %multiply_convert_fusion.1 = (bf16[512,1408]{1,0:T(8,128)(2,1)S(1)}, bf16[512,1408]{1,0:T(8,128)(2,1)S(1)}, bf16[512,1408]{1,0:T(8,128)(2,1)S(1)}) fusion(f32[512,1408]{1,0:T(8,128)S(1)} %copy-done.80, f32[512,1408]{1,0:T(8,128)S(1)} %fusion.65, bf16[512,2048]{1,0:T(8,128)(2,1)S(1)} %constant_dynamic-update-slice_fusion.2.x, bf16[2048,1408]{1,0:T(8,128)(2,1)S(1)} %bitcast.80), kind=kOutput, calls=%fused_computation.6 | convolution fusion | flops 2963603456 | bytes 17956864 | tf_op jit(solution)/shard_map/dot_general | solution.py:22
  100.9 1.8 fusion.20
  102.7 6.9 %collective-permute-done.9.x_far = bf16[512,1024]{1,0:T(8,128)(2,1)S(1)} collective-permute-done((bf16[512,1024]{1,0:T(8,128)(2,1)}, bf16[512,1024]{1,0:T(8,128)(2,1)S(1)}, u32[]{:S(2)}, u32[]{:S(2)}) %collective-permute-start.9) | collective-permute-done | bytes 1048608 | tf_op jit(solution)/shard_map/ppermute | solution.py:18
  110.6 9.8 %collective-permute-done.11 = bf16[256,1024]{1,0:T(8,128)(2,1)S(1)} collective-permute-done((bf16[256,1024]{1,0:T(8,128)(2,1)S(1)}, bf16[256,1024]{1,0:T(8,128)(2,1)S(1)}, u32[]{:S(2)}, u32[]{:S(2)}) %collective-permute-start.11) | collective-permute-done | bytes 524320 | tf_op jit(solution)/shard_map/ppermute | solution.py:18
  120.4 1.8 fusion.4
  123.0 1.7 collective-permute-start.18
  124.7 3.1 fusion.18
  127.8 3.6 convolution_add_fusion.2
  133.5 5.8 %row_terms.1 = (bf16[256,2048]{1,0:T(8,128)(2,1)S(1)}, f32[256,2048]{1,0:T(8,128)S(1)}) custom-call(bf16[512,1408]{1,0:T(8,128)(2,1)S(1)} %get-tuple-element.103.left.g, bf16[1408,2048]{1,0:T(8,128)(2,1)S(1)} %bitcast.57), custom_call_target="tpu_custom_call" | custom-call | flops 11811160064 | bytes 5767168 | tf_op jit(solution)/shard_map/row_terms/pallas_call | solution.py:357
  140.7 4.9 %collective-permute-done.14 = bf16[128,2048]{1,0:T(8,128)(2,1)S(1)} collective-permute-done((bf16[128,2048]{1,0:T(8,128)(2,1)S(1)}, bf16[128,2048]{1,0:T(8,128)(2,1)S(1)}, u32[]{:S(2)}, u32[]{:S(2)}) %collective-permute-start.14) | collective-permute-done | bytes 524320 | tf_op jit(solution)/shard_map/ppermute | solution.py:18
  146.6 2.6 fusion.60
  150.7 5.8 %weight_terms.9 = bf16[1024,1408]{1,0:T(8,128)(2,1)} custom-call(s32[4]{0:T(128)S(1)} %pad_add_fusion.1.places, bf16[512,2048]{1,0:T(8,128)(2,1)S(1)} %constant_dynamic-update-slice_fusion.2.x, bf16[512,2048]{1,0:T(8,128)(2,1)S(1)} %pad_maximum_fusion.1.x_far, bf16[512,1408]{1,0:T(8,128)(2,1)S(1)} %get-tuple-element.72.g, ...), custom_call_target="tpu_custom_call" | custom-call | flops 5905580032 | bytes 2883584 | tf_op jit(solution)/shard_map/weight_terms/pallas_call | solution.py:325
  156.5 1.9 constant_dynamic-update-slice_fusion.7
  158.4 3.9 collective-permute-done.17
  162.4 1.9 constant_dynamic-update-slice_fusion.6
  166.6 1.7 collective-permute-start.21
  169.5 4.9 %weight_terms.10 = bf16[512,1408]{1,0:T(8,128)(2,1)} custom-call(s32[2]{0:T(128)S(1)} %pad_add_fusion.2.places, bf16[512,2048]{1,0:T(8,128)(2,1)S(1)} %copy-done.2, bf16[512,1024]{1,0:T(8,128)(2,1)S(1)} %copy-done.20, bf16[512,1408]{1,0:T(8,128)(2,1)S(1)} %get-tuple-element.103.left.g, bf16[512,1408]{1,0:T(8,128)(2,1)} %collective-permute-done.18.g_far), custom_call_target="tpu_custom_call" | custom-call | flops 2952790016 | bytes 2883584 | tf_op jit(solution)/shard_map/weight_terms/pallas_call | solution.py:325
  177.5 2.1 fusion.6.do_in
  179.6 9.0 %attention_backward.1 = (bf16[512,512]{1,0:T(8,128)(2,1)S(1)}, f32[128,512]{1,0:T(8,128)S(1)}, bf16[128,512]{1,0:T(8,128)(2,1)S(1)}, bf16[128,512]{1,0:T(8,128)(2,1)S(1)}, bf16[128,512]{1,0:T(8,128)(2,1)S(1)}) custom-call(s32[2]{0:T(128)S(1)} %pad_add_fusion.at_ref, s32[1,512]{1,0:T(1,128)S(1)} %bitcast.53, bf16[512,512]{1,0:T(8,128)(2,1)} %bitcast.51, ...), custom_call_target="tpu_custom_call" | custom-call | flops 25769803776 | bytes 2621440 | tf_op jit(solution)/shard_map/attention_backward/pallas_call | solution.py:249
  189.0 21.2 %collective-permute-start.26 = (bf16[128,512]{1,0:T(8,128)(2,1)S(1)}, bf16[128,512]{1,0:T(8,128)(2,1)S(1)}, u32[]{:S(2)}, u32[]{:S(2)}) collective-permute-start(bf16[128,512]{1,0:T(8,128)(2,1)S(1)} %get-tuple-element.97), channel_id=1, source_target_pairs={{0,12},{4,8},{8,4},{12,0},{16,28},{20,24},{24,20},{28,16},{1,13},{... | collective-permute-start | bytes 393224 | tf_op jit(solution)/shard_map/ppermute | solution.py:18
  210.2 27.0 %collective-permute-done.23.g_far = bf16[512,1408]{1,0:T(8,128)(2,1)} collective-permute-done((bf16[512,1408]{1,0:T(8,128)(2,1)}, bf16[512,1408]{1,0:T(8,128)(2,1)}, u32[]{:S(2)}, u32[]{:S(2)}) %collective-permute-start.23) | collective-permute-done | bytes 1441824 | tf_op jit(solution)/shard_map/ppermute | solution.py:18
  238.6 5.2 %weight_terms.11 = bf16[512,1408]{1,0:T(8,128)(2,1)} custom-call(s32[2]{0:T(128)S(1)} %pad_add_fusion.2.places, bf16[512,2048]{1,0:T(8,128)(2,1)S(1)} %copy-done.13, bf16[512,2048]{1,0:T(8,128)(2,1)S(1)} %copy-done.6, bf16[512,1408]{1,0:T(8,128)(2,1)S(1)} %copy-done.17, bf16[512,1408]{1,0:T(8,128)(2,1)} %collective-permute-done.23.g_far), custom_call_target="tpu_custom_call" | custom-call | flops 2952790016 | bytes 2883584 | tf_op jit(solution)/shard_map/weight_terms/pallas_call | solution.py:325
  245.1 3.4 collective-permute-done.25
  251.6 1.7 fusion.5
  264.3 5.3 %collective-permute-done.20 = bf16[128,2048]{1,0:T(8,128)(2,1)} collective-permute-done((bf16[128,2048]{1,0:T(8,128)(2,1)}, bf16[128,2048]{1,0:T(8,128)(2,1)}, u32[]{:S(2)}, u32[]{:S(2)}) %collective-permute-start.20) | collective-permute-done | bytes 524320 | tf_op jit(solution)/shard_map/ppermute | solution.py:18
  269.6 3.7 weight_terms.12
  276.1 3.5 weight_terms.14
  279.6 2.1 fusion.16
  283.3 1.9 fusion.14
  286.5 3.4 weight_terms.13
  291.6 2.1 fusion.59
  294.4 2.4 collective-permute-start.32
  296.8 44.1 %collective-permute-done.32 = f32[2,1024]{1,0:T(2,128)S(1)} collective-permute-done((f32[2,1024]{1,0:T(2,128)S(1)}, f32[2,1024]{1,0:T(2,128)S(1)}, u32[]{:S(2)}, u32[]{:S(2)}) %collective-permute-start.32) | collective-permute-done | bytes 8224 | tf_op jit(solution)/shard_map/ppermute | solution.py:18
  341.0 2.6 fusion.11
  346.1 2.5 convert_element_type.166
  349.6 5.5 %weight_terms.15 = bf16[1024,640]{1,0:T(8,128)(2,1)} custom-call(s32[4]{0:T(128)S(1)} %pad_add_fusion.1.places, bf16[512,2048]{1,0:T(8,128)(2,1)S(1)} %copy-done.11, bf16[512,1024]{1,0:T(8,128)(2,1)} %collective-permute-done.3.x_far, bf16[640,512]{1,0:T(8,128)(2,1)S(1)} %copy-done.24, bf16[640,512]{1,0:T(8,128)(2,1)} %collective-permute-done.35.g_far), custom_call_target="tpu_custom_call" | custom-call | flops 2684354560 | bytes 1310720 | tf_op jit(solution)/shard_map/weight_terms/pallas_call | solution.py:325
  355.7 1.6 copy-done.7
  358.9 3.3 weight_terms.17
  362.2 2.5 add_convert_fusion
  365.8 2.4 add_bitcast_fusion
  368.2 2.9 copy.27
  371.1 1.8 convert_bitcast_fusion
  372.9 2.0 copy.26
  375.0 1.6 copy-done.8
  376.6 1.6 copy-done.15
  378.2 3.3 weight_terms.16
  381.5 32.9 %collective-permute-done.37 = bf16[256,1408]{1,0:T(8,128)(2,1)} collective-permute-done((bf16[256,1408]{1,0:T(8,128)(2,1)}, bf16[256,1408]{1,0:T(8,128)(2,1)}, u32[]{:S(2)}, u32[]{:S(2)}) %collective-permute-start.37) | collective-permute-done | bytes 720928 | tf_op jit(solution)/shard_map/ppermute | solution.py:18
  414.4 2.9 convert_add_fusion.5
  419.7 1.8 slice.209
  (325 shorter events, 73.6 us)
Async XLA Ops:
  7.2 40.0 %copy-start = (bf16[512,2048]{1,0:T(8,128)(2,1)S(1)}, bf16[512,2048]{1,0:T(8,128)(2,1)}, u32[]{:S(2)}) copy-start(bf16[512,2048]{1,0:T(8,128)(2,1)} %param.18) | copy-start | bytes 6291460
  7.2 338.9 %reduce-scatter.4.cloned.1.call-start = ((), (), s32[]{:S(2)}) async-start(), calls=%async_computation.3 | async-start | bytes 3604480 | tf_op jit(solution)/shard_map/reduce_scatter | solution.py:303
  7.3 15.8 %copy-start.76 = (f32[32]{0:T(128)}, f32[32]{0:T(128)S(1)}, u32[]{:S(2)}) copy-start(f32[32]{0:T(128)S(1)} %multiply_exponential_fusion) | copy-start | bytes 388
  13.6 9.4 %copy-start.73 = (f32[512]{0:T(512)}, f32[512]{0:T(512)S(1)}, u32[]{:S(2)}) copy-start(f32[512]{0:T(512)S(1)} %convert_element_type.138) | copy-start | bytes 6148
  14.0 11.9 %copy-start.32 = (bf16[128,512]{1,0:T(8,128)(2,1)}, bf16[128,512]{1,0:T(8,128)(2,1)S(1)}, u32[]{:S(2)}) copy-start(bf16[128,512]{1,0:T(8,128)(2,1)S(1)} %pad_maximum_fusion.13.kv0) | copy-start | bytes 393220
  14.0 11.1 %collective-permute-start = (bf16[128,512]{1,0:T(8,128)(2,1)S(1)}, bf16[128,512]{1,0:T(8,128)(2,1)S(1)}, u32[]{:S(2)}, u32[]{:S(2)}) collective-permute-start(bf16[128,512]{1,0:T(8,128)(2,1)S(1)} %pad_maximum_fusion.13.kv0), channel_id=1, source_target_pairs={{0,4},{4,0},{8,12},{12,8},{16,20},{20,16},{24,28},{28,24},{1,5},{5... | collective-permute-start | bytes 393224 | tf_op jit(solution)/shard_map/ppermute | solution.py:18
  17.0 8.1 %collective-permute-start.1 = (bf16[128,512]{1,0:T(8,128)(2,1)S(1)}, bf16[128,512]{1,0:T(8,128)(2,1)S(1)}, u32[]{:S(2)}, u32[]{:S(2)}) collective-permute-start(bf16[128,512]{1,0:T(8,128)(2,1)S(1)} %pad_maximum_fusion.13.kv0), channel_id=1, source_target_pairs={{0,8},{4,12},{8,0},{12,4},{16,24},{20,28},{24,16},{28,20},{1,9},{5... | collective-permute-start | bytes 393224 | tf_op jit(solution)/shard_map/ppermute | solution.py:18
  18.6 6.5 %collective-permute-start.2 = (bf16[128,512]{1,0:T(8,128)(2,1)S(1)}, bf16[128,512]{1,0:T(8,128)(2,1)S(1)}, u32[]{:S(2)}, u32[]{:S(2)}) collective-permute-start(bf16[128,512]{1,0:T(8,128)(2,1)S(1)} %pad_maximum_fusion.13.kv0), channel_id=1, source_target_pairs={{0,12},{4,8},{8,4},{12,0},{16,28},{20,24},{24,20},{28,16},{1,13},{... | collective-permute-start | bytes 393224 | tf_op jit(solution)/shard_map/ppermute | solution.py:18
  21.1 26.0 %collective-permute-start.3 = (bf16[512,1024]{1,0:T(8,128)(2,1)}, bf16[512,1024]{1,0:T(8,128)(2,1)}, u32[]{:S(2)}, u32[]{:S(2)}) collective-permute-start(bf16[512,1024]{1,0:T(8,128)(2,1)} %pad_maximum_fusion.2), channel_id=1, source_target_pairs={{0,4},{4,0},{8,12},{12,8},{16,20},{20,16},{24,28},{28,24},{1,5},{5... | collective-permute-start | bytes 3145736 | tf_op jit(solution)/shard_map/ppermute | solution.py:18
  34.6 22.8 %copy-start.30 = (bf16[512,512]{1,0:T(8,128)(2,1)}, bf16[512,512]{1,0:T(8,128)(2,1)S(1)}, u32[]{:S(2)}) copy-start(bf16[512,512]{1,0:T(8,128)(2,1)S(1)} %get-tuple-element.102.o_in.g) | copy-start | bytes 1572868
  48.9 3.0 collective-permute-start.4
  53.5 14.0 %collective-permute-start.5 = (bf16[128,2048]{1,0:T(8,128)(2,1)S(1)}, bf16[128,2048]{1,0:T(8,128)(2,1)S(1)}, u32[]{:S(2)}, u32[]{:S(2)}) collective-permute-start(bf16[128,2048]{1,0:T(8,128)(2,1)S(1)} %slice.277), channel_id=1, source_target_pairs={{0,2},{1,3},{2,0},{3,1},{4,6},{5,7},{6,4},{7,5},{8,10},{9,11},{10,... | collective-permute-start | bytes 1572872 | tf_op jit(solution)/shard_map/ppermute | solution.py:18
  55.7 16.0 %slice-start = ((s8[5767168]{0:T(1024)(128)(4,1)}), s8[4194304]{0:T(1024)(128)(4,1)S(1)}, s32[]{:S(2)}) async-start(s8[5767168]{0:T(1024)(128)(4,1)} %bitcast.54), calls=%async_computation.6 | async-start | bytes 8388608
  56.1 15.6 %copy-start.1 = (bf16[512,2048]{1,0:T(8,128)(2,1)}, bf16[512,2048]{1,0:T(8,128)(2,1)S(1)}, u32[]{:S(2)}) copy-start(bf16[512,2048]{1,0:T(8,128)(2,1)S(1)} %pad_maximum_fusion.x) | copy-start | bytes 6291460
  56.1 11.4 %slice-start.4 = ((f32[256,2048]{1,0:T(8,128)}), f32[128,2048]{1,0:T(8,128)S(1)}, s32[]{:S(2)}) async-start(f32[256,2048]{1,0:T(8,128)} %copy-done.52), calls=%async_computation.10 | async-start | bytes 2097152 | tf_op jit(solution)/shard_map/slice | solution.py:466
  56.1 15.6 %slice-start.1 = ((s8[5767168]{0:T(1024)(128)(4,1)}), s8[1572864]{0:T(1024)(128)(4,1)S(1)}, s32[]{:S(2)}) async-start(s8[5767168]{0:T(1024)(128)(4,1)} %bitcast.54), calls=%async_computation.7 | async-start | bytes 3145728
  57.4 12.4 %copy-start.70 = (f32[2048]{0:T(1024)S(1)}, f32[2048]{0:T(1024)}, u32[]{:S(2)}) copy-start(f32[2048]{0:T(1024)} %param.19) | copy-start | bytes 24580
  57.4 19.4 %collective-permute-start.6 = (bf16[512,512]{1,0:T(8,128)(2,1)S(1)}, bf16[512,512]{1,0:T(8,128)(2,1)S(1)}, u32[]{:S(2)}, u32[]{:S(2)}) collective-permute-start(bf16[512,512]{1,0:T(8,128)(2,1)S(1)} %get-tuple-element.102.o_in.g), channel_id=1, source_target_pairs={{0,4},{4,0},{8,12},{12,8},{16,20},{20,16},{24,28},{28,24},{1,5},{5... | collective-permute-start | bytes 1572872 | tf_op jit(solution)/shard_map/ppermute | solution.py:18
  70.0 13.2 %collective-permute-start.7 = (bf16[128,2048]{1,0:T(8,128)(2,1)S(1)}, bf16[128,2048]{1,0:T(8,128)(2,1)S(1)}, u32[]{:S(2)}, u32[]{:S(2)}) collective-permute-start(bf16[128,2048]{1,0:T(8,128)(2,1)S(1)} %multiply_convert_fusion.3), channel_id=1, source_target_pairs={{0,2},{1,3},{2,0},{3,1},{4,6},{5,7},{6,4},{7,5},{8,10},{9,11},{10,... | collective-permute-start | bytes 1572872 | tf_op jit(solution)/shard_map/ppermute | solution.py:18
  83.2 4.3 %collective-permute-start.8 = (bf16[256,2048]{1,0:T(8,128)(2,1)S(1)}, bf16[256,2048]{1,0:T(8,128)(2,1)}, u32[]{:S(2)}, u32[]{:S(2)}) collective-permute-start(bf16[256,2048]{1,0:T(8,128)(2,1)S(1)} %constant_dynamic-update-slice_fusion), channel_id=1, source_target_pairs={{0,1},{1,0},{2,3},{3,2},{4,5},{5,4},{6,7},{7,6},{8,9},{9,8},{10,11... | collective-permute-start | bytes 3145736 | tf_op jit(solution)/shard_map/ppermute | solution.py:18
  83.4 26.2 %collective-permute-start.9 = (bf16[512,1024]{1,0:T(8,128)(2,1)}, bf16[512,1024]{1,0:T(8,128)(2,1)S(1)}, u32[]{:S(2)}, u32[]{:S(2)}) collective-permute-start(bf16[512,1024]{1,0:T(8,128)(2,1)} %pad_maximum_fusion.3), channel_id=1, source_target_pairs={{0,8},{4,12},{8,0},{12,4},{16,24},{20,28},{24,16},{28,20},{1,9},{5... | collective-permute-start | bytes 3145736 | tf_op jit(solution)/shard_map/ppermute | solution.py:18
  85.3 25.2 %collective-permute-start.10 = (bf16[256,1024]{1,0:T(8,128)(2,1)S(1)}, bf16[256,1024]{1,0:T(8,128)(2,1)S(1)}, u32[]{:S(2)}, u32[]{:S(2)}) collective-permute-start(bf16[256,1024]{1,0:T(8,128)(2,1)S(1)} %pad_maximum_fusion.7), channel_id=1, source_target_pairs={{0,4},{4,0},{8,12},{12,8},{16,20},{20,16},{24,28},{28,24},{1,5},{5... | collective-permute-start | bytes 1572872 | tf_op jit(solution)/shard_map/ppermute | solution.py:18
  87.0 33.4 %collective-permute-start.11 = (bf16[256,1024]{1,0:T(8,128)(2,1)S(1)}, bf16[256,1024]{1,0:T(8,128)(2,1)S(1)}, u32[]{:S(2)}, u32[]{:S(2)}) collective-permute-start(bf16[256,1024]{1,0:T(8,128)(2,1)S(1)} %pad_maximum_fusion.8), channel_id=1, source_target_pairs={{0,8},{4,12},{8,0},{12,4},{16,24},{20,28},{24,16},{28,20},{1,9},{5... | collective-permute-start | bytes 1572872 | tf_op jit(solution)/shard_map/ppermute | solution.py:18
  89.0 61.7 %copy-start.12 = (bf16[512,2048]{1,0:T(8,128)(2,1)}, bf16[512,2048]{1,0:T(8,128)(2,1)S(1)}, u32[]{:S(2)}) copy-start(bf16[512,2048]{1,0:T(8,128)(2,1)S(1)} %constant_dynamic-update-slice_fusion.2.x) | copy-start | bytes 6291460
  89.0 11.8 %slice-start.5 = ((s8[5767168]{0:T(1024)(128)(4,1)}), s8[4194304]{0:T(1024)(128)(4,1)S(1)}, s32[]{:S(2)}) async-start(s8[5767168]{0:T(1024)(128)(4,1)} %bitcast.77), calls=%async_computation.11 | async-start | bytes 8388608
  100.4 24.3 %copy-start.16 = (bf16[512,1408]{1,0:T(8,128)(2,1)}, bf16[512,1408]{1,0:T(8,128)(2,1)S(1)}, u32[]{:S(2)}) copy-start(bf16[512,1408]{1,0:T(8,128)(2,1)S(1)} %get-tuple-element.107.g) | copy-start | bytes 4325380
  100.4 50.3 %collective-permute-start.16 = (bf16[512,1408]{1,0:T(8,128)(2,1)S(1)}, bf16[512,1408]{1,0:T(8,128)(2,1)S(1)}, u32[]{:S(2)}, u32[]{:S(2)}) collective-permute-start(bf16[512,1408]{1,0:T(8,128)(2,1)S(1)} %get-tuple-element.72.g), channel_id=1, source_target_pairs={{0,4},{4,0},{8,12},{12,8},{16,20},{20,16},{24,28},{28,24},{1,5},{5... | collective-permute-start | bytes 4325384 | tf_op jit(solution)/shard_map/ppermute | solution.py:18
  122.2 9.2 %collective-permute-start.12 = (bf16[256,2048]{1,0:T(8,128)(2,1)S(1)}, bf16[256,2048]{1,0:T(8,128)(2,1)S(1)}, u32[]{:S(2)}, u32[]{:S(2)}) collective-permute-start(bf16[256,2048]{1,0:T(8,128)(2,1)S(1)} %fusion.4), channel_id=1, source_target_pairs={{0,1},{1,0},{2,3},{3,2},{4,5},{5,4},{6,7},{7,6},{8,9},{9,8},{10,11... | collective-permute-start | bytes 3145736 | tf_op jit(solution)/shard_map/ppermute | solution.py:18
  122.4 9.4 %collective-permute-start.13 = (bf16[256,2048]{1,0:T(8,128)(2,1)S(1)}, bf16[256,2048]{1,0:T(8,128)(2,1)S(1)}, u32[]{:S(2)}, u32[]{:S(2)}) collective-permute-start(bf16[256,2048]{1,0:T(8,128)(2,1)S(1)} %constant_dynamic-update-slice_fusion.4), channel_id=1, source_target_pairs={{0,1},{1,0},{2,3},{3,2},{4,5},{5,4},{6,7},{7,6},{8,9},{9,8},{10,11... | collective-permute-start | bytes 3145736 | tf_op jit(solution)/shard_map/ppermute | solution.py:18
  123.0 45.3 %collective-permute-start.18 = (bf16[512,1408]{1,0:T(8,128)(2,1)S(1)}, bf16[512,1408]{1,0:T(8,128)(2,1)}, u32[]{:S(2)}, u32[]{:S(2)}) collective-permute-start(bf16[512,1408]{1,0:T(8,128)(2,1)S(1)} %get-tuple-element.103.left.g), channel_id=1, source_target_pairs={{0,8},{4,12},{8,0},{12,4},{16,24},{20,28},{24,16},{28,20},{1,9},{5... | collective-permute-start | bytes 4325384 | tf_op jit(solution)/shard_map/ppermute | solution.py:18
  131.9 18.8 %copy-start.5 = (bf16[512,2048]{1,0:T(8,128)(2,1)}, bf16[512,2048]{1,0:T(8,128)(2,1)S(1)}, u32[]{:S(2)}) copy-start(bf16[512,2048]{1,0:T(8,128)(2,1)S(1)} %pad_maximum_fusion.1.x_far) | copy-start | bytes 6291460
  131.9 13.7 %collective-permute-start.14 = (bf16[128,2048]{1,0:T(8,128)(2,1)S(1)}, bf16[128,2048]{1,0:T(8,128)(2,1)S(1)}, u32[]{:S(2)}, u32[]{:S(2)}) collective-permute-start(bf16[128,2048]{1,0:T(8,128)(2,1)S(1)} %slice.276), channel_id=1, source_target_pairs={{0,2},{1,3},{2,0},{3,1},{4,6},{5,7},{6,4},{7,5},{8,10},{9,11},{10,... | collective-permute-start | bytes 1572872 | tf_op jit(solution)/shard_map/ppermute | solution.py:18
  149.2 13.2 %collective-permute-start.17 = (bf16[128,2048]{1,0:T(8,128)(2,1)}, bf16[128,2048]{1,0:T(8,128)(2,1)}, u32[]{:S(2)}, u32[]{:S(2)}) collective-permute-start(bf16[128,2048]{1,0:T(8,128)(2,1)} %get-tuple-element.85), channel_id=1, source_target_pairs={{0,2},{1,3},{2,0},{3,1},{4,6},{5,7},{6,4},{7,5},{8,10},{9,11},{10,... | collective-permute-start | bytes 1572872 | tf_op jit(solution)/shard_map/ppermute | solution.py:18
  164.2 11.9 %collective-permute-start.19 = (bf16[256,2048]{1,0:T(8,128)(2,1)}, bf16[256,2048]{1,0:T(8,128)(2,1)}, u32[]{:S(2)}, u32[]{:S(2)}) collective-permute-start(bf16[256,2048]{1,0:T(8,128)(2,1)} %constant_dynamic-update-slice_fusion.6), channel_id=1, source_target_pairs={{0,1},{1,0},{2,3},{3,2},{4,5},{5,4},{6,7},{7,6},{8,9},{9,8},{10,11... | collective-permute-start | bytes 3145736 | tf_op jit(solution)/shard_map/ppermute | solution.py:18
  164.3 72.9 %collective-permute-start.23 = (bf16[512,1408]{1,0:T(8,128)(2,1)}, bf16[512,1408]{1,0:T(8,128)(2,1)}, u32[]{:S(2)}, u32[]{:S(2)}) collective-permute-start(bf16[512,1408]{1,0:T(8,128)(2,1)} %copy-done.16), channel_id=1, source_target_pairs={{0,8},{4,12},{8,0},{12,4},{16,24},{20,28},{24,16},{28,20},{1,9},{5... | collective-permute-start | bytes 4325384 | tf_op jit(solution)/shard_map/ppermute | solution.py:18
  164.7 206.5 %reduce-scatter.8.cloned.1.call-start = ((), (), s32[]{:S(2)}) async-start(), calls=%async_computation.5 | async-start | bytes 1310720 | tf_op jit(solution)/shard_map/reduce_scatter | solution.py:303
  165.0 23.6 %collective-permute-start.15 = (bf16[256,2048]{1,0:T(8,128)(2,1)}, bf16[256,2048]{1,0:T(8,128)(2,1)S(1)}, u32[]{:S(2)}, u32[]{:S(2)}) collective-permute-start(bf16[256,2048]{1,0:T(8,128)(2,1)} %copy-done.34), channel_id=1, source_target_pairs={{0,1},{1,0},{2,3},{3,2},{4,5},{5,4},{6,7},{7,6},{8,9},{9,8},{10,11... | collective-permute-start | bytes 3145736 | tf_op jit(solution)/shard_map/ppermute | solution.py:18
  166.6 78.0 %collective-permute-start.21 = (bf16[256,1024]{1,0:T(8,128)(2,1)S(1)}, bf16[256,1024]{1,0:T(8,128)(2,1)S(1)}, u32[]{:S(2)}, u32[]{:S(2)}) collective-permute-start(bf16[256,1024]{1,0:T(8,128)(2,1)S(1)} %pad_maximum_fusion.9), channel_id=1, source_target_pairs={{0,4},{4,0},{8,12},{12,8},{16,20},{20,16},{24,28},{28,24},{1,5},{5... | collective-permute-start | bytes 1572872 | tf_op jit(solution)/shard_map/ppermute | solution.py:18
  174.4 70.2 %collective-permute-start.22 = (bf16[512,1408]{1,0:T(8,128)(2,1)}, bf16[512,1408]{1,0:T(8,128)(2,1)S(1)}, u32[]{:S(2)}, u32[]{:S(2)}) collective-permute-start(bf16[512,1408]{1,0:T(8,128)(2,1)} %weight_terms.10), channel_id=1, source_target_pairs={{0,4},{4,0},{8,12},{12,8},{16,20},{20,16},{24,28},{28,24},{1,5},{5... | collective-permute-start | bytes 4325384 | tf_op jit(solution)/shard_map/ppermute | solution.py:18
  179.6 59.0 %copy-start.17 = (bf16[512,1408]{1,0:T(8,128)(2,1)S(1)}, bf16[512,1408]{1,0:T(8,128)(2,1)}, u32[]{:S(2)}) copy-start(bf16[512,1408]{1,0:T(8,128)(2,1)} %copy-done.16) | copy-start | bytes 4325380
  188.6 49.9 %copy-start.6 = (bf16[512,2048]{1,0:T(8,128)(2,1)S(1)}, bf16[512,2048]{1,0:T(8,128)(2,1)}, u32[]{:S(2)}) copy-start(bf16[512,2048]{1,0:T(8,128)(2,1)} %copy-done.5) | copy-start | bytes 6291460
  188.6 49.9 %copy-start.13 = (bf16[512,2048]{1,0:T(8,128)(2,1)S(1)}, bf16[512,2048]{1,0:T(8,128)(2,1)}, u32[]{:S(2)}) copy-start(bf16[512,2048]{1,0:T(8,128)(2,1)} %copy-done.12) | copy-start | bytes 6291460
  189.0 54.7 %copy-start.50 = (f32[256,2048]{1,0:T(8,128)}, f32[256,2048]{1,0:T(8,128)S(1)}, u32[]{:S(2)}) copy-start(f32[256,2048]{1,0:T(8,128)S(1)} %convert_add_fusion.1) | copy-start | bytes 6291460
  189.0 56.1 %collective-permute-start.26 = (bf16[128,512]{1,0:T(8,128)(2,1)S(1)}, bf16[128,512]{1,0:T(8,128)(2,1)S(1)}, u32[]{:S(2)}, u32[]{:S(2)}) collective-permute-start(bf16[128,512]{1,0:T(8,128)(2,1)S(1)} %get-tuple-element.97), channel_id=1, source_target_pairs={{0,12},{4,8},{8,4},{12,0},{16,28},{20,24},{24,20},{28,16},{1,13},{... | collective-permute-start | bytes 393224 | tf_op jit(solution)/shard_map/ppermute | solution.py:18
  210.2 38.4 %collective-permute-start.25 = (bf16[128,512]{1,0:T(8,128)(2,1)S(1)}, bf16[128,512]{1,0:T(8,128)(2,1)S(1)}, u32[]{:S(2)}, u32[]{:S(2)}) collective-permute-start(bf16[128,512]{1,0:T(8,128)(2,1)S(1)} %get-tuple-element.96), channel_id=1, source_target_pairs={{0,8},{4,12},{8,0},{12,4},{16,24},{20,28},{24,16},{28,20},{1,9},{5... | collective-permute-start | bytes 393224 | tf_op jit(solution)/shard_map/ppermute | solution.py:18
  237.2 11.3 %collective-permute-start.24 = (bf16[128,512]{1,0:T(8,128)(2,1)S(1)}, bf16[128,512]{1,0:T(8,128)(2,1)S(1)}, u32[]{:S(2)}, u32[]{:S(2)}) collective-permute-start(bf16[128,512]{1,0:T(8,128)(2,1)S(1)} %get-tuple-element.95), channel_id=1, source_target_pairs={{0,4},{4,0},{8,12},{12,8},{16,20},{20,16},{24,28},{28,24},{1,5},{5... | collective-permute-start | bytes 393224 | tf_op jit(solution)/shard_map/ppermute | solution.py:18
  253.4 6.9 %collective-permute-start.27 = (bf16[256,2048]{1,0:T(8,128)(2,1)}, bf16[256,2048]{1,0:T(8,128)(2,1)}, u32[]{:S(2)}, u32[]{:S(2)}) collective-permute-start(bf16[256,2048]{1,0:T(8,128)(2,1)} %fusion.5), channel_id=1, source_target_pairs={{0,1},{1,0},{2,3},{3,2},{4,5},{5,4},{6,7},{7,6},{8,9},{9,8},{10,11... | collective-permute-start | bytes 3145736 | tf_op jit(solution)/shard_map/ppermute | solution.py:18
  254.6 15.0 %collective-permute-start.20 = (bf16[128,2048]{1,0:T(8,128)(2,1)}, bf16[128,2048]{1,0:T(8,128)(2,1)}, u32[]{:S(2)}, u32[]{:S(2)}) collective-permute-start(bf16[128,2048]{1,0:T(8,128)(2,1)} %slice.275), channel_id=1, source_target_pairs={{0,2},{1,3},{2,0},{3,1},{4,6},{5,7},{6,4},{7,5},{8,10},{9,11},{10,... | collective-permute-start | bytes 1572872 | tf_op jit(solution)/shard_map/ppermute | solution.py:18
  256.1 92.4 %collective-permute-start.35 = (bf16[640,512]{1,0:T(8,128)(2,1)}, bf16[640,512]{1,0:T(8,128)(2,1)}, u32[]{:S(2)}, u32[]{:S(2)}) collective-permute-start(bf16[640,512]{1,0:T(8,128)(2,1)} %copy-done.23), channel_id=1, source_target_pairs={{0,4},{4,0},{8,12},{12,8},{16,20},{20,16},{24,28},{28,24},{1,5},{5... | collective-permute-start | bytes 1966088 | tf_op jit(solution)/shard_map/ppermute | solution.py:18
  257.6 2.4 collective-permute-start.28
  263.8 19.5 %collective-permute-start.29 = (bf16[128,2048]{1,0:T(8,128)(2,1)}, bf16[128,2048]{1,0:T(8,128)(2,1)}, u32[]{:S(2)}, u32[]{:S(2)}) collective-permute-start(bf16[128,2048]{1,0:T(8,128)(2,1)} %slice.274), channel_id=1, source_target_pairs={{0,2},{1,3},{2,0},{3,1},{4,6},{5,7},{6,4},{7,5},{8,10},{9,11},{10,... | collective-permute-start | bytes 1572872 | tf_op jit(solution)/shard_map/ppermute | solution.py:18
  281.7 135.5 %reduce-scatter.6.cloned.1.call-start = ((), (), s32[]{:S(2)}) async-start(), calls=%async_computation.4 | async-start | bytes 1638400 | tf_op jit(solution)/shard_map/reduce_scatter | solution.py:303
  281.7 80.5 %collective-permute-start.36 = (bf16[512,1408]{1,0:T(8,128)(2,1)}, bf16[512,1408]{1,0:T(8,128)(2,1)}, u32[]{:S(2)}, u32[]{:S(2)}) collective-permute-start(bf16[512,1408]{1,0:T(8,128)(2,1)} %weight_terms.11), channel_id=1, source_target_pairs={{0,4},{4,0},{8,12},{12,8},{16,20},{20,16},{24,28},{28,24},{1,5},{5... | collective-permute-start | bytes 4325384 | tf_op jit(solution)/shard_map/ppermute | solution.py:18
  285.2 4.7 %collective-permute-start.30 = (f32[2,2048]{1,0:T(2,128)S(1)}, f32[2,2048]{1,0:T(2,128)S(1)}, u32[]{:S(2)}, u32[]{:S(2)}) collective-permute-start(f32[2,2048]{1,0:T(2,128)S(1)} %pad_maximum_fusion.20), channel_id=1, source_target_pairs={{0,1},{1,0},{2,3},{3,2},{4,5},{5,4},{6,7},{7,6},{8,9},{9,8},{10,11... | collective-permute-start | bytes 49160 | tf_op jit(solution)/shard_map/ppermute | solution.py:18
  289.9 51.1 %copy-start.46 = (f32[128,2048]{1,0:T(8,128)S(1)}, f32[128,2048]{1,0:T(8,128)}, u32[]{:S(2)}) copy-start(f32[128,2048]{1,0:T(8,128)} %slice.203) | copy-start | bytes 3145732
  289.9 51.1 %copy-start.53 = (f32[128,2048]{1,0:T(8,128)S(1)}, f32[128,2048]{1,0:T(8,128)}, u32[]{:S(2)}) copy-start(f32[128,2048]{1,0:T(8,128)} %get-tuple-element.125) | copy-start | bytes 3145732
  289.9 51.1 %copy-start.72 = (f32[2048]{0:T(1024)S(1)}, f32[2048]{0:T(1024)}, u32[]{:S(2)}) copy-start(f32[2048]{0:T(1024)} %param.14) | copy-start | bytes 24580
  289.9 51.1 %copy-start.79 = (f32[128]{0:T(128)S(1)}, f32[128]{0:T(128)}, u32[]{:S(2)}) copy-start(f32[128]{0:T(128)} %dynamic-slice.3) | copy-start | bytes 1540
  290.0 4.4 %collective-permute-start.31 = (f32[2,2048]{1,0:T(2,128)S(1)}, f32[2,2048]{1,0:T(2,128)S(1)}, u32[]{:S(2)}, u32[]{:S(2)}) collective-permute-start(f32[2,2048]{1,0:T(2,128)S(1)} %fusion.58), channel_id=1, source_target_pairs={{0,2},{1,3},{2,0},{3,1},{4,6},{5,7},{6,4},{7,5},{8,10},{9,11},{10,... | collective-permute-start | bytes 49160 | tf_op jit(solution)/shard_map/ppermute | solution.py:18
  293.7 72.1 %collective-permute-start.38 = (bf16[256,1408]{1,0:T(8,128)(2,1)}, bf16[256,1408]{1,0:T(8,128)(2,1)}, u32[]{:S(2)}, u32[]{:S(2)}) collective-permute-start(bf16[256,1408]{1,0:T(8,128)(2,1)} %fusion.59), channel_id=1, source_target_pairs={{0,16},{4,20},{8,24},{12,28},{16,0},{20,4},{24,8},{28,12},{1,17},{... | collective-permute-start | bytes 2162696 | tf_op jit(solution)/shard_map/ppermute | solution.py:18
  294.4 46.5 %collective-permute-start.32 = (f32[2,1024]{1,0:T(2,128)S(1)}, f32[2,1024]{1,0:T(2,128)S(1)}, u32[]{:S(2)}, u32[]{:S(2)}) collective-permute-start(f32[2,1024]{1,0:T(2,128)S(1)} %pad_maximum_fusion.21), channel_id=1, source_target_pairs={{0,16},{4,20},{8,24},{12,28},{16,0},{20,4},{24,8},{28,12},{1,17},{... | collective-permute-start | bytes 24584 | tf_op jit(solution)/shard_map/ppermute | solution.py:18
  340.9 3.7 collective-permute-start.33
  344.6 10.5 %collective-permute-start.34 = (f32[2,256]{1,0:T(2,128)S(1)}, f32[2,256]{1,0:T(2,128)S(1)}, u32[]{:S(2)}, u32[]{:S(2)}) collective-permute-start(f32[2,256]{1,0:T(2,128)S(1)} %slice.207), channel_id=1, source_target_pairs={{0,4},{4,0},{8,12},{12,8},{16,20},{20,16},{24,28},{28,24},{1,5},{5... | collective-permute-start | bytes 6152 | tf_op jit(solution)/shard_map/ppermute | solution.py:18
  364.8 49.6 %collective-permute-start.37 = (bf16[256,1408]{1,0:T(8,128)(2,1)}, bf16[256,1408]{1,0:T(8,128)(2,1)}, u32[]{:S(2)}, u32[]{:S(2)}) collective-permute-start(bf16[256,1408]{1,0:T(8,128)(2,1)} %add_convert_fusion), channel_id=1, source_target_pairs={{0,16},{4,20},{8,24},{12,28},{16,0},{20,4},{24,8},{28,12},{1,17},{... | collective-permute-start | bytes 2162696 | tf_op jit(solution)/shard_map/ppermute | solution.py:18
  (68 other events, 260.4 us)
Sparse Core Ops, SparseCore 0:
  164.8 86.9 reduce-scatter.3
  281.8 42.3 reduce-scatter.7
  355.2 48.6 reduce-scatter.5

commit v6 on v5

--- a/solution.py
+++ b/solution.py
@@ -311,20 +311,26 @@
     out[...] = (dot(x[...], g[...], 0, side) + dot(x_far[...], g_far[...], 0, side)).astype(LOW)
 
 
-def weight_terms(places, first, x, x_far, g, g_far, transposed=False):
+def weight_terms(places, first, x, x_far, g, g_far, transposed=False, part=None, keep=False):
     count = len(places)
     blocks = lax.axis_size("dp")
     size = x.shape[1] // blocks
     rows = x.shape[0]
     units = g.shape[0] if transposed else g.shape[1]
+    if part is not None:
+        units //= 2
     if size % 128:
         side = 1 if transposed else 0
         far = x_far[:, first * size : (first + count) * size]
+        if part is not None:
+            g, g_far = (v[:, part * units : (part + 1) * units] for v in (g, g_far))
         return (dot(pick(x, places, blocks, 1), g, 0, side) + dot(far, g_far, 0, side)).astype(LOW)
-    whole = pl.BlockSpec(g.shape, lambda i, p: (0, 0))
+    whole = pl.BlockSpec(
+        (units, rows) if transposed else (rows, units), lambda i, p: (0, part or 0)
+    )
     return pl.pallas_call(
         functools.partial(terms_kernel, transposed),
-        out_shape=pltpu.HBM((count * size, units), LOW),
+        out_shape=(jax.ShapeDtypeStruct if keep else pltpu.HBM)((count * size, units), LOW),
         grid_spec=pltpu.PrefetchScalarGridSpec(
             num_scalar_prefetch=1,
             grid=(count,),
@@ -442,22 +448,17 @@
 
     bit = place % 2
     bits = dp.bit_length() - 1
-
-    halves = [[2 * j + which for j in range(dp // 2)] for which in (bit, 1 - bit)]
-
-    def columns(values, which):
-        return pick(values, halves[which], dp, 1)
-
+    half_count = dp // 2
+    wide = w_query.shape[1]
+
+    halves = [[2 * j + which for j in range(half_count)] for which in (bit, 1 - bit)]
     near_bits = [0] + list(range(2, bits))
     near_masks = [
         sum(((j >> (len(near_bits) - 1 - k)) & 1) << b for k, b in enumerate(near_bits))
-        for j in range(dp // 2)
+        for j in range(half_count)
     ]
-
     near_halves = [[where ^ m for m in near_masks] for where in (place, place ^ 2)]
-
-    def rows_of(values, lo, hi):
-        return values[lo * own_rows : hi * own_rows]
+    row_order = [spot ^ m for m in ROW_MASKS]
 
     def near_sum(part):
         send = part(2, 4).astype(LOW)
@@ -465,34 +466,33 @@
         pair = kept + near
         return pair[:own_rows], pair[own_rows:].astype(LOW)
 
-    one_send = columns(after(normed_one, paired), 1)
+    one_send = pick(after(normed_one, paired), halves[1], dp, 1)
     one_theirs = flip(one_send, "dp", 1)
     queries = after(queries, one_send)
     attended, lse = attention_forward(at, pos, queries, blocks, size, 2)
     attended = after(attended, one_theirs)
 
-    def branch_terms(lo, hi):
-        return dot(attended[:, lo * own_rows : hi * own_rows], w_out, 0, 0)
-
-    branch, branch_send = near_sum(branch_terms)
-    branch_far = flip(branch_send, "tp", 2)
-    att_theirs = flip(after(attended, branch_send), "dp", 1)
-    cot = pick(after(cotangent, branch_send), [spot ^ m for m in ROW_MASKS], len(tp_masks), 0)
+    branch, branch_out = near_sum(
+        lambda lo, hi: dot(attended[:, lo * own_rows : hi * own_rows], w_out, 0, 0)
+    )
+    branch_far = flip(branch_out, "tp", 2)
+    att_theirs = flip(after(attended, branch_out), "dp", 1)
+    cot = pick(after(cotangent, branch_out), row_order, len(ROW_MASKS), 0)
     cot_send = pick(cot, near_halves[1], dp, 1)
     cot_theirs = flip(cot_send, "dp", 2)
-    branch = after(branch, cot_send)
-
     own_inputs = own(tokens).astype(jnp.float32)
-    middle = own_inputs + (branch + branch_far)
+    middle = own_inputs + (after(branch, cot_send) + branch_far)
+
     scale_two = lax.rsqrt(jnp.mean(middle * middle, -1, keepdims=True) + EPSILON)
     own_two = (middle * scale_two * norm2_gain).astype(LOW)
     far_two = flip(own_two, "tp", 2)
     grad_hidden = dot(after(cot, own_two), w_down, 1, 1)
     pair_two = jnp.concatenate([after(own_two, grad_hidden, att_theirs), far_two], 0)
     core_two = flip(pair_two, "tp", 1)
-    two_send, two_far_half = columns(pair_two, 1), pick(pair_two, near_halves[1], dp, 1)
-    two_near, two_far_near = flip(two_send, "dp", 1), flip(two_far_half, "dp", 2)
-    normed_two = jnp.concatenate([after(pair_two, two_send, two_far_half), core_two], 0)
+    two_send = pick(pair_two, halves[1], dp, 1)
+    two_near_send = pick(pair_two, near_halves[1], dp, 1)
+    two_near = [flip(two_send, "dp", 1), flip(two_near_send, "dp", 2)]
+    normed_two = jnp.concatenate([after(pair_two, two_send, two_near_send), core_two], 0)
 
     gate_pre = dot(normed_two, w_gate, 1, 0)
     up_pre = dot(normed_two, w_up, 1, 0)
@@ -501,28 +501,22 @@
     hidden = (active * up_pre).astype(LOW)
     grad_gate_pre = (grad_hidden * up_pre * sigma * (1.0 + gate_pre * (1.0 - sigma))).astype(LOW)
     grad_up_pre = (grad_hidden * active).astype(LOW)
-    hidden_theirs = flip(hidden, "dp", 2)
     gate_theirs = flip(grad_gate_pre, "dp", 1)
-
-    gate_late, cot_theirs, two_near, two_far_near = lax.optimization_barrier(
-        (grad_gate_pre, cot_theirs, two_near, two_far_near)
-    )
-    two_near = jnp.concatenate([two_near, two_far_near], 1)
+    far_rows = jnp.concatenate([hidden, grad_up_pre], 1)
+    far_theirs = flip(far_rows, "dp", 2)
+    gate_late = after(grad_gate_pre, far_rows)
+
+    def two_terms(lo, hi):
+        rows = slice(lo * own_rows, hi * own_rows)
+        return dot(gate_late[rows], w_gate, 1, 1) + dot(grad_up_pre[rows], w_up, 1, 1)
+
+    grad_normed_two, two_out = near_sum(two_terms)
+    two_out, cot_theirs, *two_near = lax.optimization_barrier((two_out, cot_theirs, *two_near))
+    two_far = flip(two_out, "tp", 2)
+    two_near = jnp.concatenate(two_near, 1)
     two_theirs = jnp.concatenate([two_near, flip(two_near, "tp", 1)], 0)
 
-    def two_terms(lo, hi):
-        return dot(rows_of(gate_late, lo, hi), w_gate, 1, 1) + dot(
-            rows_of(grad_up_pre, lo, hi), w_up, 1, 1
-        )
-
-    grad_normed_two, two_far_send = near_sum(two_terms)
-    two_far_send, two_theirs = lax.optimization_barrier((two_far_send, two_theirs))
-    far_first = dp // 2
-    two_far = flip(two_far_send, "tp", 2)
-
-    hidden_late = after(hidden, two_far_send)
-    down_near, down = row_terms(hidden_late, w_down)
-    up_theirs = flip(grad_up_pre, "dp", 2)
+    down_near, down = row_terms(after(hidden, two_out), w_down)
     grad_normed_two = after(grad_normed_two, down) + two_far
 
     grad_mid_norm, gain_two = norm_back(grad_normed_two, middle, scale_two, norm2_gain)
@@ -536,43 +530,48 @@
     grad_gate = parity_sum(gate_terms, 0)
     grad_pair = jnp.concatenate([after(branch_grad, gate_terms), grad_far], 0)
     grad_core = flip(grad_pair, "tp", 1)
-    branch_send = columns(grad_pair, 1)
+    branch_send = pick(grad_pair, halves[1], dp, 1)
     branch_near = flip(branch_send, "dp", 1)
+    branch_all = jnp.concatenate([after(grad_pair, branch_send), grad_core], 0)
+    grad_attended = dot(w_out, branch_all, 1, 1).astype(LOW)
 
     def down_terms(lo, hi, *late):
+        rows = after(far_rows, *late)
         return weight_terms(
-            near_halves[0][lo:hi], lo, cot, cot_theirs, after(hidden, *late), hidden_theirs
+            near_halves[0][lo:hi], lo, cot, cot_theirs, rows, far_theirs, part=0, keep=True
         )
 
     def up_terms(lo, hi, *late):
+        rows = after(far_rows, *late)
+        first = half_count + lo
         return weight_terms(
-            near_halves[0][lo:hi],
-            far_first + lo,
-            normed_two,
-            two_theirs,
-            after(grad_up_pre, *late),
-            up_theirs,
+            near_halves[0][lo:hi], first, normed_two, two_theirs, rows, far_theirs, part=1, keep=True
         )
 
-    count = dp // 2
-    down_sent = [down_terms(count // 2, count, branch_send)]
-
-    branch_all = jnp.concatenate([after(grad_pair, down_sent[0]), grad_core], 0)
-    grad_attended = dot(w_out, branch_all, 1, 1).astype(LOW)
-
+    down_sent = down_terms(half_count // 2, half_count, grad_attended)
+    down_got = [flip(down_sent, "dp", 1)]
     grads = attention_backward(
-        at, pos, queries, grad_attended, attended, lse, cosine, sine, blocks, size, 2
+        at,
+        pos,
+        queries,
+        after(grad_attended, down_sent),
+        attended,
+        lse,
+        cosine,
+        sine,
+        blocks,
+        size,
+        2,
     )
     grad_query_rows, kv_total = grads[0], grads[1]
     kv_back = [flip(grads[m + 1], "dp", m) for m in range(1, SPAN)]
 
     down = down + after(down_near, grad_query_rows)
-    down, down_send = down[:own_rows], down[own_rows:].astype(LOW)
-    down_far = flip(down_send, "tp", 2)
-    up_sent = [up_terms(count // 2, count, grad_query_rows)]
-    down_got = [flip(down_sent[0], "dp", 1)]
+    down, down_out = down[:own_rows], down[own_rows:].astype(LOW)
+    down_far = flip(down_out, "tp", 2)
+    up_sent = up_terms(half_count // 2, half_count, grad_query_rows)
     kv_total, branch_near, down_got[0] = lax.optimization_barrier(
-        (kv_total, branch_near, down_got[0], up_sent[0], down_send)
+        (kv_total, branch_near, down_got[0], up_sent, down_out)
     )[:3]
     for back in kv_back:
         kv_total = kv_total + back
@@ -581,60 +580,63 @@
     proj_rows = jnp.concatenate([grad_query_rows, grad_kv_rows], 0)
     proj_theirs = flip(proj_rows, "dp", 1)
 
-    own_order = pick(proj_rows, [spot ^ m for m in ROW_MASKS], len(tp_masks), 1)
-    wide = w_query.shape[1]
+    def exchange_rest(terms, got, *late):
+        left = half_count // 2
+        for b in near_bits[1:]:
+            send = terms(left // 2, left, *late).astype(jnp.float32)
+            for other in got:
+                send = send + other[left // 2 * block : left * block]
+            send = send.astype(LOW)
+            got.append(flip(send, "dp", 1 << b))
+            left //= 2
+        return send
+
+    def exchange_end(terms, got, *late):
+        kept = terms(0, 1, *late).astype(jnp.float32)
+        for other in got:
+            kept = kept + other[:block]
+        return kept
+
+    down_last = exchange_rest(down_terms, down_got, proj_rows)
+    proj_rows = after(proj_rows, down_last)
+
+    own_order = pick(proj_rows, row_order, len(ROW_MASKS), 1)
 
     def one_terms(lo, hi):
         cut = own_order[:, lo * own_rows : hi * own_rows]
         return dot(cut[:wide], w_query, 0, 1) + dot(cut[wide:], w_kv, 0, 0)
 
-    grad_normed_one, one_far_send = near_sum(one_terms)
-    one_far = flip(one_far_send, "tp", 2)
-
-    up_got = [flip(after(up_sent[0], one_far_send), "dp", 1)]
+    grad_normed_one, one_out = near_sum(one_terms)
+    one_far = flip(one_out, "tp", 2)
+
+    up_got = [flip(after(up_sent, one_out), "dp", 1)]
     branch_theirs = jnp.concatenate([branch_near, flip(branch_near, "tp", 1)], 0)
-    out_late = after(attended, one_far_send)
+    out_late = after(attended, one_out)
     out_terms = weight_terms(halves[0], 0, branch_all, branch_theirs, out_late, att_theirs, True)
     grad_out = parity_sum(out_terms, 0)
-
-    def exchange_rest(terms, got, late):
-        left = count // 2
-        for b in near_bits[1:]:
-            send = terms(left // 2, left, late).astype(jnp.float32)
-            for other in got:
-                send = send + other[left // 2 * block : left * block]
-            got.append(flip(send.astype(LOW), "dp", 1 << b))
-            left //= 2
-        return terms(0, 1, late), send
-
-    grad_down, down_last = exchange_rest(down_terms, down_got, out_terms)
-    output_rows = (middle + (down + after(down_far, one_far_send))).astype(LOW)
-    grad_normed_one = after(grad_normed_one, down_last, grad_down, output_rows) + one_far
+    output_rows = (middle + (down + after(down_far, one_out))).astype(LOW)
+    grad_normed_one = after(grad_normed_one, out_terms, output_rows) + one_far
     grad_in_norm, gain_one = norm_back(grad_normed_one, own_inputs, own(scale_one), norm1_gain)
     input_rows = grad_middle + grad_in_norm
+
+    gains = jnp.stack([gain_one, gain_two])
+    for m in (1, 2):
+        gains = gains + flip(gains, "tp", m)
+    gains = pick(gains, [place ^ m for m in range(dp)], dp, 1)
+    left = dp
+    while left > 1:
+        left //= 2
+        gains = gains[:, : left * block] + flip(gains[:, left * block :], "dp", left)
+
+    grad_down = exchange_end(down_terms, down_got, input_rows)
     grad_gate = grad_gate.astype(jnp.float32)
 
     proj_late = after(proj_rows, input_rows, grad_gate)
     proj_terms = weight_terms(halves[0], 0, normed_one, one_theirs, proj_late, proj_theirs, True)
     grad_out = grad_out.astype(jnp.float32)
     grad_proj = parity_sum(proj_terms, 0).astype(jnp.float32)
-
-    grad_up, up_last = exchange_rest(up_terms, up_got, proj_terms)
-
-    def total(kept, got):
-        kept = kept.astype(jnp.float32)
-        for other in got:
-            kept = kept + other[:block]
-        return kept
-
-    gains = jnp.stack([gain_one, gain_two])
-    for m in (1, 2):
-        gains = gains + flip(gains, "tp", m)
-    gains = pick(gains, [place ^ m for m in range(dp)], dp, 1)
-    count = dp
-    while count > 1:
-        count //= 2
-        gains = gains[:, : count * block] + flip(gains[:, count * block :], "dp", count)
+    exchange_rest(up_terms, up_got, gains, proj_terms)
+    grad_up = exchange_end(up_terms, up_got, proj_terms)
 
     return (
         output_rows,
@@ -646,8 +648,8 @@
         grad_out.T,
         gains[1],
         grad_gate,
-        total(grad_up, up_got),
-        total(grad_down, down_got).T,
+        grad_up,
+        grad_down.T,
     )
 
 

time: 434 us -> 448 us (1.032)
  waiting for transfers between devices: 169 us -> 191 us
  local copies, waits for them, and re-layouts: 49.3 us -> 42.4 us
    ppermute x39 -> x38, waiting for transfers between devices: 169 us -> 191 us  [flip(): lax.ppermute(block, axis, [(i, i ^ mask) for i in range(lax.axis_size(axi...]
    unnamed x187 -> x149, local copies, waits for them, and re-layouts: 32.9 us -> 26.2 us
    ppermute x39 -> x38, starting transfers between devices: 59 us -> 62.5 us  [flip(): lax.ppermute(block, axis, [(i, i ^ mask) for i in range(lax.axis_size(axi...]
  transfers between devices with their start and end apart: 42 -> 41, of which waited for: 15 -> 15; matrix products, arithmetic and copies ran while one was open for 21% -> 20% of each run, Pallas kernels for 14% -> 13%
where the time goes in v6:
time: 448 us; the launch traced here: 443 us
  waiting for transfers between devices  191 us (43%)
  starting transfers between devices  62.6 us (14%)
  Pallas kernels  57.4 us (13%)
  local copies, waits for them, and re-layouts  42.4 us (9%)
  other arithmetic  38.8 us (9%)
  matrix products  35.6 us (8%)
  between operations  15.4 us (3%)
    ppermute x38, waiting for transfers between devices, flip(): lax.ppermute(block, axis, [(i, i ^ mask) for i in range(lax.axis_size(axi...  191 us
    ppermute x38, starting transfers between devices, flip(): lax.ppermute(block, axis, [(i, i ^ mask) for i in range(lax.axis_size(axi...  62.5 us
    pallas_call x9, Pallas kernels, weight_terms(): pl.pallas_call(functools.partial(terms_kernel, transposed), out_shape=(ja...  36 us
    dot_general x16, matrix products, dot(): lax.dot_general(left, right, (((left_dim,), (right_dim,)), ((), ())), pre...  35.6 us
    unnamed x149, local copies, waits for them, and re-layouts  26.2 us
  transfers between devices with their start and end apart: 41, of which 15 were waited for; matrix products, arithmetic and copies ran while one was open for 20% of the time, Pallas kernels for 13%

profile of v6, /device:TPU:0, one launch (start us, length us, event | category | flops | bytes accessed | tf_op | source)
XLA Modules:
  0.0 443.3 jit_solution(10702264368163473729)
XLA Ops:
  7.3 2.2 fusion
  14.0 3.0 collective-permute-start
  21.2 1.9 collective-permute-start.3
  26.9 6.8 %attention_forward.1 = (bf16[512,512]{1,0:T(8,128)(2,1)S(1)}, f32[8,1,512]{2,1,0:T(1,128)S(1)}) custom-call(s32[2]{0:T(128)S(1)} %pad_add_fusion.at_ref, s32[1,512]{1,0:T(1,128)S(1)} %bitcast.52, bf16[512,512]{1,0:T(8,128)(2,1)S(1)} %bitcast.50, bf16[128,512]{1,0:T(8,128)(2,1)S(1)} %pad_maximum_fusion.14.kv0, bf16[128,512]{1,0:T(8,128)(2,1)S(1)} %collective-permute-done.kv1, ...), custom_call_target="tpu_custom_call" | custom-call | flops 17179869184 | bytes 1048576 | tf_op jit(solution)/shard_map/attention_forward/pallas_call | solution.py:214
  34.3 12.9 %collective-permute-done.3.x_far = bf16[512,1024]{1,0:T(8,128)(2,1)} collective-permute-done((bf16[512,1024]{1,0:T(8,128)(2,1)}, bf16[512,1024]{1,0:T(8,128)(2,1)}, u32[]{:S(2)}, u32[]{:S(2)}) %collective-permute-start.3) | collective-permute-done | bytes 1048608 | tf_op jit(solution)/shard_map/ppermute | solution.py:18
  47.2 1.7 convolution_convert_fusion
  49.6 2.3 collective-permute-done.4
  53.5 1.8 collective-permute-start.5
  57.5 1.7 collective-permute-start.6
  59.1 8.4 %collective-permute-done.5 = bf16[128,2048]{1,0:T(8,128)(2,1)S(1)} collective-permute-done((bf16[128,2048]{1,0:T(8,128)(2,1)S(1)}, bf16[128,2048]{1,0:T(8,128)(2,1)S(1)}, u32[]{:S(2)}, u32[]{:S(2)}) %collective-permute-start.5) | collective-permute-done | bytes 524320 | tf_op jit(solution)/shard_map/ppermute | solution.py:18
  70.0 1.8 collective-permute-start.7
  71.8 5.0 %fusion.63 = f32[512,1408]{1,0:T(8,128)} fusion(bf16[512,2048]{1,0:T(8,128)(2,1)S(1)} %pad_maximum_fusion.1.x, bf16[1408,2048]{1,0:T(8,128)(2,1)S(1)} %bitcast.55), kind=kOutput, calls=%fused_computation.187 | convolution fusion | flops 2952790016 | bytes 10747904 | tf_op jit(solution)/shard_map/dot_general | solution.py:22
  78.5 4.7 %collective-permute-done.7 = bf16[128,2048]{1,0:T(8,128)(2,1)S(1)} collective-permute-done((bf16[128,2048]{1,0:T(8,128)(2,1)S(1)}, bf16[128,2048]{1,0:T(8,128)(2,1)S(1)}, u32[]{:S(2)}, u32[]{:S(2)}) %collective-permute-start.7) | collective-permute-done | bytes 524320 | tf_op jit(solution)/shard_map/ppermute | solution.py:18
  84.1 1.7 collective-permute-start.10
  92.2 7.0 %fusion.64 = f32[512,1408]{1,0:T(8,128)S(1)} fusion(bf16[512,2048]{1,0:T(8,128)(2,1)S(1)} %constant_dynamic-update-slice_fusion.2.x, bf16[2048,1408]{1,0:T(8,128)(2,1)} %param.21), kind=kOutput, calls=%fused_computation.188 | convolution fusion | flops 2952790016 | bytes 10747904 | tf_op jit(solution)/shard_map/dot_general | solution.py:22
  99.3 4.5 %multiply_convert_fusion = (bf16[512,1408]{1,0:T(8,128)(2,1)S(1)}, bf16[512,1408]{1,0:T(8,128)(2,1)S(1)}, bf16[512,1408]{1,0:T(8,128)(2,1)S(1)}) fusion(f32[512,1408]{1,0:T(8,128)S(1)} %copy-done.61, f32[512,1408]{1,0:T(8,128)S(1)} %fusion.64, bf16[512,2048]{1,0:T(8,128)(2,1)S(1)} %constant_dynamic-update-slice_fusion.2.x, bf16[2048,1408]{1,0:T(8,128)(2,1)S(1)} %bitcast.78), kind=kOutput, calls=%fused_computation.6 | convolution fusion | flops 2963603456 | bytes 17956864 | tf_op jit(solution)/shard_map/dot_general | solution.py:22
  104.2 1.8 pad_maximum_fusion.g
  106.0 1.8 fusion.22
  108.1 1.8 fusion.4
  110.0 1.8 fusion.20
  111.9 4.6 %convolution_add_fusion.2 = f32[256,2048]{1,0:T(8,128)S(1)} fusion(f32[256,2048]{1,0:T(8,128)S(1)} %fusion.20, bf16[2048,1408]{1,0:T(8,128)(2,1)} %param.21, bf16[512,1408]{1,0:T(8,128)(2,1)S(1)} %get-tuple-element.134), kind=kOutput, calls=%fused_computation.13 | convolution fusion | flops 1476919296 | bytes 10682368 | tf_op jit(solution)/shard_map/dot_general | solution.py:22
  116.4 1.8 collective-permute-start.19
  118.7 2.8 collective-permute-done.12
  121.5 1.7 collective-permute-start.13
  123.4 5.8 %row_terms.1 = (bf16[256,2048]{1,0:T(8,128)(2,1)S(1)}, f32[256,2048]{1,0:T(8,128)S(1)}) custom-call(bf16[512,1408]{1,0:T(8,128)(2,1)S(1)} %get-tuple-element.79.left, bf16[1408,2048]{1,0:T(8,128)(2,1)S(1)} %bitcast.57), custom_call_target="tpu_custom_call" | custom-call | flops 11811160064 | bytes 5767168 | tf_op jit(solution)/shard_map/row_terms/pallas_call | solution.py:363
  129.4 5.3 %collective-permute-done.13 = bf16[128,2048]{1,0:T(8,128)(2,1)S(1)} collective-permute-done((bf16[128,2048]{1,0:T(8,128)(2,1)S(1)}, bf16[128,2048]{1,0:T(8,128)(2,1)S(1)}, u32[]{:S(2)}, u32[]{:S(2)}) %collective-permute-start.13) | collective-permute-done | bytes 524320 | tf_op jit(solution)/shard_map/ppermute | solution.py:18
  135.1 2.6 fusion.59
  137.7 1.7 collective-permute-start.17
  139.7 5.9 %weight_terms.9 = bf16[1024,1408]{1,0:T(8,128)(2,1)} custom-call(s32[4]{0:T(128)S(1)} %pad_add_fusion.1.places, bf16[512,2048]{1,0:T(8,128)(2,1)S(1)} %constant_dynamic-update-slice_fusion.2.x, bf16[512,2048]{1,0:T(8,128)(2,1)S(1)} %pad_maximum_fusion.2.x_far, bf16[512,1408]{1,0:T(8,128)(2,1)S(1)} %get-tuple-element.75.g, ...), custom_call_target="tpu_custom_call" | custom-call | flops 5905580032 | bytes 2883584 | tf_op jit(solution)/shard_map/weight_terms/pallas_call | solution.py:331
  146.9 1.9 constant_dynamic-update-slice_fusion.7
  148.8 1.6 collective-permute-done.17
  150.4 1.9 constant_dynamic-update-slice_fusion.6
  154.9 1.6 collective-permute-start.21
  159.3 2.1 fusion.6.do_in
  161.4 57.2 %collective-permute-done.19.g_far = bf16[512,2816]{1,0:T(8,128)(2,1)} collective-permute-done((bf16[512,2816]{1,0:T(8,128)(2,1)}, bf16[512,2816]{1,0:T(8,128)(2,1)}, u32[]{:S(2)}, u32[]{:S(2)}) %collective-permute-start.19) | collective-permute-done | bytes 2883616 | tf_op jit(solution)/shard_map/ppermute | solution.py:18
  218.6 4.5 %weight_terms.10 = bf16[512,1408]{1,0:T(8,128)(2,1)S(1)} custom-call(s32[2]{0:T(128)S(1)} %pad_add_fusion.2.places, bf16[512,2048]{1,0:T(8,128)(2,1)S(1)} %copy-done.6, bf16[512,1024]{1,0:T(8,128)(2,1)S(1)} %collective-permute-done.10.x_far, bf16[512,2816]{1,0:T(8,128)(2,1)} %pad_maximum_fusion.g, bf16[512,2816]{1,0:T(8,128)(2,1)} %collective-permute-done.19.g_far), custom_call_target="tpu_custom_call" | custom-call | flops 2952790016 | bytes 2883584 | tf_op jit(solution)/shard_map/weight_terms/pallas_call | solution.py:331
  223.1 1.9 collective-permute-start.22
  225.0 8.7 %attention_backward.1 = (bf16[512,512]{1,0:T(8,128)(2,1)S(1)}, f32[128,512]{1,0:T(8,128)S(1)}, bf16[128,512]{1,0:T(8,128)(2,1)S(1)}, bf16[128,512]{1,0:T(8,128)(2,1)S(1)}, bf16[128,512]{1,0:T(8,128)(2,1)S(1)}) custom-call(s32[2]{0:T(128)S(1)} %pad_add_fusion.at_ref, s32[1,512]{1,0:T(1,128)S(1)} %bitcast.53, bf16[512,512]{1,0:T(8,128)(2,1)} %bitcast.51, ...), custom_call_target="tpu_custom_call" | custom-call | flops 25769803776 | bytes 2621440 | tf_op jit(solution)/shard_map/attention_backward/pallas_call | solution.py:249
  233.8 1.8 convert_add_fusion.1
  235.6 17.3 %collective-permute-start.25 = (bf16[128,512]{1,0:T(8,128)(2,1)S(1)}, bf16[128,512]{1,0:T(8,128)(2,1)S(1)}, u32[]{:S(2)}, u32[]{:S(2)}) collective-permute-start(bf16[128,512]{1,0:T(8,128)(2,1)S(1)} %get-tuple-element.100), channel_id=1, source_target_pairs={{0,12},{4,8},{8,4},{12,0},{16,28},{20,24},{24,20},{28,16},{1,13},{... | collective-permute-start | bytes 393224 | tf_op jit(solution)/shard_map/ppermute | solution.py:18
  253.5 4.5 %weight_terms.11 = bf16[512,1408]{1,0:T(8,128)(2,1)S(1)} custom-call(s32[2]{0:T(128)S(1)} %pad_add_fusion.2.places, bf16[512,2048]{1,0:T(8,128)(2,1)S(1)} %copy-done.9, bf16[512,2048]{1,0:T(8,128)(2,1)S(1)} %copy-done.3, bf16[512,2816]{1,0:T(8,128)(2,1)} %pad_maximum_fusion.g, bf16[512,2816]{1,0:T(8,128)(2,1)} %collective-permute-done.19.g_far), custom_call_target="tpu_custom_call" | custom-call | flops 2952790016 | bytes 2883584 | tf_op jit(solution)/shard_map/weight_terms/pallas_call | solution.py:331
  259.9 3.0 weight_terms.12
  267.3 1.8 collective-permute-start.20
  275.4 6.6 %collective-permute-done.20 = bf16[128,2048]{1,0:T(8,128)(2,1)S(1)} collective-permute-done((bf16[128,2048]{1,0:T(8,128)(2,1)S(1)}, bf16[128,2048]{1,0:T(8,128)(2,1)S(1)}, u32[]{:S(2)}, u32[]{:S(2)}) %collective-permute-start.20) | collective-permute-done | bytes 524320 | tf_op jit(solution)/shard_map/ppermute | solution.py:18
  282.8 3.9 weight_terms.13
  286.7 2.7 fusion.16
  289.4 3.6 collective-permute-done.28
  293.0 1.6 fusion.14
  294.8 1.8 collective-permute-start.34
  296.6 7.4 %collective-permute-start.37 = (bf16[256,1408]{1,0:T(8,128)(2,1)}, bf16[256,1408]{1,0:T(8,128)(2,1)}, u32[]{:S(2)}, u32[]{:S(2)}) collective-permute-start(bf16[256,1408]{1,0:T(8,128)(2,1)} %add_convert_fusion.1), channel_id=1, source_target_pairs={{0,16},{4,20},{8,24},{12,28},{16,0},{20,4},{24,8},{28,12},{1,17},{... | collective-permute-start | bytes 2162696 | tf_op jit(solution)/shard_map/ppermute | solution.py:18
  304.8 1.6 collective-permute-start.30
  306.4 2.2 collective-permute-done.30
  308.7 3.3 fusion.11
  312.1 41.1 %collective-permute-done.31 = f32[2,1024]{1,0:T(2,128)S(1)} collective-permute-done((f32[2,1024]{1,0:T(2,128)S(1)}, f32[2,1024]{1,0:T(2,128)S(1)}, u32[]{:S(2)}, u32[]{:S(2)}) %collective-permute-start.31) | collective-permute-done | bytes 8224 | tf_op jit(solution)/shard_map/ppermute | solution.py:18
  354.0 2.9 weight_terms.17
  358.5 2.5 convert_element_type.168
  362.0 5.5 %weight_terms.14 = bf16[1024,640]{1,0:T(8,128)(2,1)} custom-call(s32[4]{0:T(128)S(1)} %pad_add_fusion.1.places, bf16[512,2048]{1,0:T(8,128)(2,1)S(1)} %copy-done.14, bf16[512,1024]{1,0:T(8,128)(2,1)} %collective-permute-done.3.x_far, bf16[640,512]{1,0:T(8,128)(2,1)S(1)} %copy-done.18, bf16[640,512]{1,0:T(8,128)(2,1)} %collective-permute-done.34.g_far), custom_call_target="tpu_custom_call" | custom-call | flops 2684354560 | bytes 1310720 | tf_op jit(solution)/shard_map/weight_terms/pallas_call | solution.py:331
  369.2 2.8 weight_terms.16
  372.0 2.3 add_convert_fusion
  374.3 3.4 collective-permute-start.36
  386.4 3.0 weight_terms.15
  389.4 40.3 %collective-permute-done.36 = bf16[256,1408]{1,0:T(8,128)(2,1)} collective-permute-done((bf16[256,1408]{1,0:T(8,128)(2,1)}, bf16[256,1408]{1,0:T(8,128)(2,1)}, u32[]{:S(2)}, u32[]{:S(2)}) %collective-permute-start.36) | collective-permute-done | bytes 720928 | tf_op jit(solution)/shard_map/ppermute | solution.py:18
  429.7 2.7 convert_add_fusion.5
  434.8 1.8 slice.209
  (286 shorter events, 68.4 us)
Async XLA Ops:
  7.2 40.0 %copy-start = (bf16[512,2048]{1,0:T(8,128)(2,1)S(1)}, bf16[512,2048]{1,0:T(8,128)(2,1)}, u32[]{:S(2)}) copy-start(bf16[512,2048]{1,0:T(8,128)(2,1)} %param.18) | copy-start | bytes 6291460
  7.2 351.3 %reduce-scatter.4.cloned.1.call-start = ((), (), s32[]{:S(2)}) async-start(), calls=%async_computation.3 | async-start | bytes 3604480 | tf_op jit(solution)/shard_map/reduce_scatter | solution.py:303
  7.3 15.8 %copy-start.57 = (f32[32]{0:T(128)}, f32[32]{0:T(128)S(1)}, u32[]{:S(2)}) copy-start(f32[32]{0:T(128)S(1)} %multiply_exponential_fusion) | copy-start | bytes 388
  14.0 11.9 %copy-start.25 = (bf16[128,512]{1,0:T(8,128)(2,1)}, bf16[128,512]{1,0:T(8,128)(2,1)S(1)}, u32[]{:S(2)}) copy-start(bf16[128,512]{1,0:T(8,128)(2,1)S(1)} %pad_maximum_fusion.14.kv0) | copy-start | bytes 393220
  14.0 11.1 %collective-permute-start = (bf16[128,512]{1,0:T(8,128)(2,1)S(1)}, bf16[128,512]{1,0:T(8,128)(2,1)S(1)}, u32[]{:S(2)}, u32[]{:S(2)}) collective-permute-start(bf16[128,512]{1,0:T(8,128)(2,1)S(1)} %pad_maximum_fusion.14.kv0), channel_id=1, source_target_pairs={{0,4},{4,0},{8,12},{12,8},{16,20},{20,16},{24,28},{28,24},{1,5},{5... | collective-permute-start | bytes 393224 | tf_op jit(solution)/shard_map/ppermute | solution.py:18
  17.1 8.1 %collective-permute-start.1 = (bf16[128,512]{1,0:T(8,128)(2,1)S(1)}, bf16[128,512]{1,0:T(8,128)(2,1)S(1)}, u32[]{:S(2)}, u32[]{:S(2)}) collective-permute-start(bf16[128,512]{1,0:T(8,128)(2,1)S(1)} %pad_maximum_fusion.14.kv0), channel_id=1, source_target_pairs={{0,8},{4,12},{8,0},{12,4},{16,24},{20,28},{24,16},{28,20},{1,9},{5... | collective-permute-start | bytes 393224 | tf_op jit(solution)/shard_map/ppermute | solution.py:18
  18.6 6.5 %collective-permute-start.2 = (bf16[128,512]{1,0:T(8,128)(2,1)S(1)}, bf16[128,512]{1,0:T(8,128)(2,1)S(1)}, u32[]{:S(2)}, u32[]{:S(2)}) collective-permute-start(bf16[128,512]{1,0:T(8,128)(2,1)S(1)} %pad_maximum_fusion.14.kv0), channel_id=1, source_target_pairs={{0,12},{4,8},{8,4},{12,0},{16,28},{20,24},{24,20},{28,16},{1,13},{... | collective-permute-start | bytes 393224 | tf_op jit(solution)/shard_map/ppermute | solution.py:18
  21.2 26.0 %collective-permute-start.3 = (bf16[512,1024]{1,0:T(8,128)(2,1)}, bf16[512,1024]{1,0:T(8,128)(2,1)}, u32[]{:S(2)}, u32[]{:S(2)}) collective-permute-start(bf16[512,1024]{1,0:T(8,128)(2,1)} %pad_maximum_fusion.3), channel_id=1, source_target_pairs={{0,4},{4,0},{8,12},{12,8},{16,20},{20,16},{24,28},{28,24},{1,5},{5... | collective-permute-start | bytes 3145736 | tf_op jit(solution)/shard_map/ppermute | solution.py:18
  25.0 8.7 %copy-start.22 = (bf16[8,2,32,512]{3,2,1,0:T(8,128)(2,1)}, bf16[8,2,32,512]{3,2,1,0:T(8,128)(2,1)S(1)}, u32[]{:S(2)}) copy-start(bf16[8,2,32,512]{3,2,1,0:T(8,128)(2,1)S(1)} %fusion.17) | copy-start | bytes 1572868
  25.2 8.6 %copy-start.31 = (bf16[128,512]{1,0:T(8,128)(2,1)}, bf16[128,512]{1,0:T(8,128)(2,1)S(1)}, u32[]{:S(2)}) copy-start(bf16[128,512]{1,0:T(8,128)(2,1)S(1)} %collective-permute-done.1.kv2) | copy-start | bytes 393220
  34.3 23.1 %copy-start.23 = (bf16[512,512]{1,0:T(8,128)(2,1)}, bf16[512,512]{1,0:T(8,128)(2,1)S(1)}, u32[]{:S(2)}) copy-start(bf16[512,512]{1,0:T(8,128)(2,1)S(1)} %get-tuple-element.108.o_in.g) | copy-start | bytes 1572868
  48.9 3.0 collective-permute-start.4
  53.5 14.0 %collective-permute-start.5 = (bf16[128,2048]{1,0:T(8,128)(2,1)S(1)}, bf16[128,2048]{1,0:T(8,128)(2,1)S(1)}, u32[]{:S(2)}, u32[]{:S(2)}) collective-permute-start(bf16[128,2048]{1,0:T(8,128)(2,1)S(1)} %slice.275), channel_id=1, source_target_pairs={{0,2},{1,3},{2,0},{3,1},{4,6},{5,7},{6,4},{7,5},{8,10},{9,11},{10,... | collective-permute-start | bytes 1572872 | tf_op jit(solution)/shard_map/ppermute | solution.py:18
  55.8 16.0 %slice-start = ((s8[5767168]{0:T(1024)(128)(4,1)}), s8[4194304]{0:T(1024)(128)(4,1)S(1)}, s32[]{:S(2)}) async-start(s8[5767168]{0:T(1024)(128)(4,1)} %bitcast.54), calls=%async_computation.6 | async-start | bytes 8388608
  56.2 15.6 %copy-start.5 = (bf16[512,2048]{1,0:T(8,128)(2,1)}, bf16[512,2048]{1,0:T(8,128)(2,1)S(1)}, u32[]{:S(2)}) copy-start(bf16[512,2048]{1,0:T(8,128)(2,1)S(1)} %pad_maximum_fusion.1.x) | copy-start | bytes 6291460
  56.2 11.4 %slice-start.4 = ((f32[256,2048]{1,0:T(8,128)}), f32[128,2048]{1,0:T(8,128)S(1)}, s32[]{:S(2)}) async-start(f32[256,2048]{1,0:T(8,128)} %copy-done.42), calls=%async_computation.10 | async-start | bytes 2097152 | tf_op jit(solution)/shard_map/slice | solution.py:467
  56.2 15.6 %slice-start.1 = ((s8[5767168]{0:T(1024)(128)(4,1)}), s8[1572864]{0:T(1024)(128)(4,1)S(1)}, s32[]{:S(2)}) async-start(s8[5767168]{0:T(1024)(128)(4,1)} %bitcast.54), calls=%async_computation.7 | async-start | bytes 3145728
  57.5 12.4 %copy-start.53 = (f32[2048]{0:T(1024)S(1)}, f32[2048]{0:T(1024)}, u32[]{:S(2)}) copy-start(f32[2048]{0:T(1024)} %param.19) | copy-start | bytes 24580
  57.5 19.4 %collective-permute-start.6 = (bf16[512,512]{1,0:T(8,128)(2,1)S(1)}, bf16[512,512]{1,0:T(8,128)(2,1)S(1)}, u32[]{:S(2)}, u32[]{:S(2)}) collective-permute-start(bf16[512,512]{1,0:T(8,128)(2,1)S(1)} %get-tuple-element.108.o_in.g), channel_id=1, source_target_pairs={{0,4},{4,0},{8,12},{12,8},{16,20},{20,16},{24,28},{28,24},{1,5},{5... | collective-permute-start | bytes 1572872 | tf_op jit(solution)/shard_map/ppermute | solution.py:18
  70.0 13.2 %collective-permute-start.7 = (bf16[128,2048]{1,0:T(8,128)(2,1)S(1)}, bf16[128,2048]{1,0:T(8,128)(2,1)S(1)}, u32[]{:S(2)}, u32[]{:S(2)}) collective-permute-start(bf16[128,2048]{1,0:T(8,128)(2,1)S(1)} %multiply_convert_fusion.3), channel_id=1, source_target_pairs={{0,2},{1,3},{2,0},{3,1},{4,6},{5,7},{6,4},{7,5},{8,10},{9,11},{10,... | collective-permute-start | bytes 1572872 | tf_op jit(solution)/shard_map/ppermute | solution.py:18
  84.0 6.7 %collective-permute-start.8 = (bf16[256,2048]{1,0:T(8,128)(2,1)}, bf16[256,2048]{1,0:T(8,128)(2,1)}, u32[]{:S(2)}, u32[]{:S(2)}) collective-permute-start(bf16[256,2048]{1,0:T(8,128)(2,1)} %constant_dynamic-update-slice_fusion), channel_id=1, source_target_pairs={{0,1},{1,0},{2,3},{3,2},{4,5},{5,4},{6,7},{7,6},{8,9},{9,8},{10,11... | collective-permute-start | bytes 3145736 | tf_op jit(solution)/shard_map/ppermute | solution.py:18
  84.1 34.6 %collective-permute-start.10 = (bf16[512,1024]{1,0:T(8,128)(2,1)}, bf16[512,1024]{1,0:T(8,128)(2,1)S(1)}, u32[]{:S(2)}, u32[]{:S(2)}) collective-permute-start(bf16[512,1024]{1,0:T(8,128)(2,1)} %pad_maximum_fusion.4), channel_id=1, source_target_pairs={{0,8},{4,12},{8,0},{12,4},{16,24},{20,28},{24,16},{28,20},{1,9},{5... | collective-permute-start | bytes 3145736 | tf_op jit(solution)/shard_map/ppermute | solution.py:18
  87.3 31.4 %collective-permute-start.11 = (bf16[256,1024]{1,0:T(8,128)(2,1)S(1)}, bf16[256,1024]{1,0:T(8,128)(2,1)S(1)}, u32[]{:S(2)}, u32[]{:S(2)}) collective-permute-start(bf16[256,1024]{1,0:T(8,128)(2,1)S(1)} %pad_maximum_fusion.8), channel_id=1, source_target_pairs={{0,4},{4,0},{8,12},{12,8},{16,20},{20,16},{24,28},{28,24},{1,5},{5... | collective-permute-start | bytes 1572872 | tf_op jit(solution)/shard_map/ppermute | solution.py:18
  88.9 32.6 %collective-permute-start.12 = (bf16[256,1024]{1,0:T(8,128)(2,1)S(1)}, bf16[256,1024]{1,0:T(8,128)(2,1)S(1)}, u32[]{:S(2)}, u32[]{:S(2)}) collective-permute-start(bf16[256,1024]{1,0:T(8,128)(2,1)S(1)} %pad_maximum_fusion.9), channel_id=1, source_target_pairs={{0,8},{4,12},{8,0},{12,4},{16,24},{20,28},{24,16},{28,20},{1,9},{5... | collective-permute-start | bytes 1572872 | tf_op jit(solution)/shard_map/ppermute | solution.py:18
  92.2 47.5 %copy-start.8 = (bf16[512,2048]{1,0:T(8,128)(2,1)}, bf16[512,2048]{1,0:T(8,128)(2,1)S(1)}, u32[]{:S(2)}) copy-start(bf16[512,2048]{1,0:T(8,128)(2,1)S(1)} %constant_dynamic-update-slice_fusion.2.x) | copy-start | bytes 6291460
  103.8 35.9 %collective-permute-start.16 = (bf16[512,1408]{1,0:T(8,128)(2,1)S(1)}, bf16[512,1408]{1,0:T(8,128)(2,1)S(1)}, u32[]{:S(2)}, u32[]{:S(2)}) collective-permute-start(bf16[512,1408]{1,0:T(8,128)(2,1)S(1)} %get-tuple-element.75.g), channel_id=1, source_target_pairs={{0,4},{4,0},{8,12},{12,8},{16,20},{20,16},{24,28},{28,24},{1,5},{5... | collective-permute-start | bytes 4325384 | tf_op jit(solution)/shard_map/ppermute | solution.py:18
  109.9 6.5 %collective-permute-start.9 = (bf16[256,2048]{1,0:T(8,128)(2,1)S(1)}, bf16[256,2048]{1,0:T(8,128)(2,1)S(1)}, u32[]{:S(2)}, u32[]{:S(2)}) collective-permute-start(bf16[256,2048]{1,0:T(8,128)(2,1)S(1)} %fusion.4), channel_id=1, source_target_pairs={{0,1},{1,0},{2,3},{3,2},{4,5},{5,4},{6,7},{7,6},{8,9},{9,8},{10,11... | collective-permute-start | bytes 3145736 | tf_op jit(solution)/shard_map/ppermute | solution.py:18
  110.0 13.4 %slice-start.2 = ((s8[5767168]{0:T(1024)(128)(4,1)}), s8[4194304]{0:T(1024)(128)(4,1)S(1)}, s32[]{:S(2)}) async-start(s8[5767168]{0:T(1024)(128)(4,1)} %bitcast.56), calls=%async_computation.8 | async-start | bytes 8388608
  111.8 11.6 %slice-start.3 = ((s8[5767168]{0:T(1024)(128)(4,1)}), s8[1572864]{0:T(1024)(128)(4,1)S(1)}, s32[]{:S(2)}) async-start(s8[5767168]{0:T(1024)(128)(4,1)} %bitcast.56), calls=%async_computation.9 | async-start | bytes 3145728
  116.4 102.1 %collective-permute-start.19 = (bf16[512,2816]{1,0:T(8,128)(2,1)}, bf16[512,2816]{1,0:T(8,128)(2,1)}, u32[]{:S(2)}, u32[]{:S(2)}) collective-permute-start(bf16[512,2816]{1,0:T(8,128)(2,1)} %pad_maximum_fusion.g), channel_id=1, source_target_pairs={{0,8},{4,12},{8,0},{12,4},{16,24},{20,28},{24,16},{28,20},{1,9},{5... | collective-permute-start | bytes 8650760 | tf_op jit(solution)/shard_map/ppermute | solution.py:18
  121.5 13.2 %collective-permute-start.13 = (bf16[128,2048]{1,0:T(8,128)(2,1)S(1)}, bf16[128,2048]{1,0:T(8,128)(2,1)S(1)}, u32[]{:S(2)}, u32[]{:S(2)}) collective-permute-start(bf16[128,2048]{1,0:T(8,128)(2,1)S(1)} %slice.274), channel_id=1, source_target_pairs={{0,2},{1,3},{2,0},{3,1},{4,6},{5,7},{6,4},{7,5},{8,10},{9,11},{10,... | collective-permute-start | bytes 1572872 | tf_op jit(solution)/shard_map/ppermute | solution.py:18
  123.3 16.1 %collective-permute-start.15 = (bf16[256,2048]{1,0:T(8,128)(2,1)S(1)}, bf16[256,2048]{1,0:T(8,128)(2,1)S(1)}, u32[]{:S(2)}, u32[]{:S(2)}) collective-permute-start(bf16[256,2048]{1,0:T(8,128)(2,1)S(1)} %constant_dynamic-update-slice_fusion.4), channel_id=1, source_target_pairs={{0,1},{1,0},{2,3},{3,2},{4,5},{5,4},{6,7},{7,6},{8,9},{9,8},{10,11... | collective-permute-start | bytes 3145736 | tf_op jit(solution)/shard_map/ppermute | solution.py:18
  137.7 12.7 %collective-permute-start.17 = (bf16[128,2048]{1,0:T(8,128)(2,1)}, bf16[128,2048]{1,0:T(8,128)(2,1)}, u32[]{:S(2)}, u32[]{:S(2)}) collective-permute-start(bf16[128,2048]{1,0:T(8,128)(2,1)} %get-tuple-element.87), channel_id=1, source_target_pairs={{0,2},{1,3},{2,0},{3,1},{4,6},{5,7},{6,4},{7,5},{8,10},{9,11},{10,... | collective-permute-start | bytes 1572872 | tf_op jit(solution)/shard_map/ppermute | solution.py:18
  152.3 5.7 %collective-permute-start.18 = (bf16[256,2048]{1,0:T(8,128)(2,1)}, bf16[256,2048]{1,0:T(8,128)(2,1)}, u32[]{:S(2)}, u32[]{:S(2)}) collective-permute-start(bf16[256,2048]{1,0:T(8,128)(2,1)} %constant_dynamic-update-slice_fusion.6), channel_id=1, source_target_pairs={{0,1},{1,0},{2,3},{3,2},{4,5},{5,4},{6,7},{7,6},{8,9},{9,8},{10,11... | collective-permute-start | bytes 3145736 | tf_op jit(solution)/shard_map/ppermute | solution.py:18
  152.4 81.4 %collective-permute-start.14 = (bf16[256,2048]{1,0:T(8,128)(2,1)}, bf16[256,2048]{1,0:T(8,128)(2,1)}, u32[]{:S(2)}, u32[]{:S(2)}) collective-permute-start(bf16[256,2048]{1,0:T(8,128)(2,1)} %copy-done.27), channel_id=1, source_target_pairs={{0,1},{1,0},{2,3},{3,2},{4,5},{5,4},{6,7},{7,6},{8,9},{9,8},{10,11... | collective-permute-start | bytes 3145736 | tf_op jit(solution)/shard_map/ppermute | solution.py:18
  154.9 103.2 %collective-permute-start.21 = (bf16[256,1024]{1,0:T(8,128)(2,1)}, bf16[256,1024]{1,0:T(8,128)(2,1)}, u32[]{:S(2)}, u32[]{:S(2)}) collective-permute-start(bf16[256,1024]{1,0:T(8,128)(2,1)} %pad_maximum_fusion.10), channel_id=1, source_target_pairs={{0,4},{4,0},{8,12},{12,8},{16,20},{20,16},{24,28},{28,24},{1,5},{5... | collective-permute-start | bytes 1572872 | tf_op jit(solution)/shard_map/ppermute | solution.py:18
  156.6 224.6 %reduce-scatter.8.cloned.1.call-start = ((), (), s32[]{:S(2)}) async-start(), calls=%async_computation.5 | async-start | bytes 1310720 | tf_op jit(solution)/shard_map/reduce_scatter | solution.py:303
  159.3 59.3 %copy-start.6 = (bf16[512,2048]{1,0:T(8,128)(2,1)S(1)}, bf16[512,2048]{1,0:T(8,128)(2,1)}, u32[]{:S(2)}) copy-start(bf16[512,2048]{1,0:T(8,128)(2,1)} %copy-done.5) | copy-start | bytes 6291460
  223.1 35.0 %collective-permute-start.22 = (bf16[512,1408]{1,0:T(8,128)(2,1)S(1)}, bf16[512,1408]{1,0:T(8,128)(2,1)S(1)}, u32[]{:S(2)}, u32[]{:S(2)}) collective-permute-start(bf16[512,1408]{1,0:T(8,128)(2,1)S(1)} %weight_terms.10), channel_id=1, source_target_pairs={{0,4},{4,0},{8,12},{12,8},{16,20},{20,16},{24,28},{28,24},{1,5},{5... | collective-permute-start | bytes 4325384 | tf_op jit(solution)/shard_map/ppermute | solution.py:18
  225.0 8.8 %copy-start.20 = (f32[256,2048]{1,0:T(8,128)S(1)}, f32[256,2048]{1,0:T(8,128)}, u32[]{:S(2)}) copy-start(f32[256,2048]{1,0:T(8,128)} %copy-done.19) | copy-start | bytes 6291460
  233.8 19.7 %copy-start.3 = (bf16[512,2048]{1,0:T(8,128)(2,1)S(1)}, bf16[512,2048]{1,0:T(8,128)(2,1)}, u32[]{:S(2)}) copy-start(bf16[512,2048]{1,0:T(8,128)(2,1)} %copy-done.2) | copy-start | bytes 6291460
  233.8 19.7 %copy-start.9 = (bf16[512,2048]{1,0:T(8,128)(2,1)S(1)}, bf16[512,2048]{1,0:T(8,128)(2,1)}, u32[]{:S(2)}) copy-start(bf16[512,2048]{1,0:T(8,128)(2,1)} %copy-done.8) | copy-start | bytes 6291460
  235.5 22.4 %copy-start.41 = (f32[256,2048]{1,0:T(8,128)}, f32[256,2048]{1,0:T(8,128)S(1)}, u32[]{:S(2)}) copy-start(f32[256,2048]{1,0:T(8,128)S(1)} %convert_add_fusion.1) | copy-start | bytes 6291460
  235.6 22.6 %collective-permute-start.25 = (bf16[128,512]{1,0:T(8,128)(2,1)S(1)}, bf16[128,512]{1,0:T(8,128)(2,1)S(1)}, u32[]{:S(2)}, u32[]{:S(2)}) collective-permute-start(bf16[128,512]{1,0:T(8,128)(2,1)S(1)} %get-tuple-element.100), channel_id=1, source_target_pairs={{0,12},{4,8},{8,4},{12,0},{16,28},{20,24},{24,20},{28,16},{1,13},{... | collective-permute-start | bytes 393224 | tf_op jit(solution)/shard_map/ppermute | solution.py:18
  252.8 5.3 %collective-permute-start.24 = (bf16[128,512]{1,0:T(8,128)(2,1)S(1)}, bf16[128,512]{1,0:T(8,128)(2,1)S(1)}, u32[]{:S(2)}, u32[]{:S(2)}) collective-permute-start(bf16[128,512]{1,0:T(8,128)(2,1)S(1)} %get-tuple-element.99), channel_id=1, source_target_pairs={{0,8},{4,12},{8,0},{12,4},{16,24},{20,28},{24,16},{28,20},{1,9},{5... | collective-permute-start | bytes 393224 | tf_op jit(solution)/shard_map/ppermute | solution.py:18
  252.8 6.6 %collective-permute-start.23 = (bf16[128,512]{1,0:T(8,128)(2,1)S(1)}, bf16[128,512]{1,0:T(8,128)(2,1)S(1)}, u32[]{:S(2)}, u32[]{:S(2)}) collective-permute-start(bf16[128,512]{1,0:T(8,128)(2,1)S(1)} %get-tuple-element.98), channel_id=1, source_target_pairs={{0,4},{4,0},{8,12},{12,8},{16,20},{20,16},{24,28},{28,24},{1,5},{5... | collective-permute-start | bytes 393224 | tf_op jit(solution)/shard_map/ppermute | solution.py:18
  266.5 6.0 %collective-permute-start.26 = (bf16[256,2048]{1,0:T(8,128)(2,1)S(1)}, bf16[256,2048]{1,0:T(8,128)(2,1)S(1)}, u32[]{:S(2)}, u32[]{:S(2)}) collective-permute-start(bf16[256,2048]{1,0:T(8,128)(2,1)S(1)} %fusion.5), channel_id=1, source_target_pairs={{0,1},{1,0},{2,3},{3,2},{4,5},{5,4},{6,7},{7,6},{8,9},{9,8},{10,11... | collective-permute-start | bytes 3145736 | tf_op jit(solution)/shard_map/ppermute | solution.py:18
  267.3 14.7 %collective-permute-start.20 = (bf16[128,2048]{1,0:T(8,128)(2,1)S(1)}, bf16[128,2048]{1,0:T(8,128)(2,1)S(1)}, u32[]{:S(2)}, u32[]{:S(2)}) collective-permute-start(bf16[128,2048]{1,0:T(8,128)(2,1)S(1)} %slice.273), channel_id=1, source_target_pairs={{0,2},{1,3},{2,0},{3,1},{4,6},{5,7},{6,4},{7,5},{8,10},{9,11},{10,... | collective-permute-start | bytes 1572872 | tf_op jit(solution)/shard_map/ppermute | solution.py:18
  269.1 2.1 collective-permute-start.27
  272.7 10.1 %copy-start.24 = (bf16[512,512]{1,0:T(8,128)(2,1)S(1)}, bf16[512,512]{1,0:T(8,128)(2,1)}, u32[]{:S(2)}) copy-start(bf16[512,512]{1,0:T(8,128)(2,1)} %copy-done.23) | copy-start | bytes 1572868
  272.8 10.1 %copy-start.29 = (bf16[512,512]{1,0:T(8,128)(2,1)S(1)}, bf16[512,512]{1,0:T(8,128)(2,1)}, u32[]{:S(2)}) copy-start(bf16[512,512]{1,0:T(8,128)(2,1)} %copy-done.28) | copy-start | bytes 1572868
  274.7 18.4 %collective-permute-start.28 = (bf16[128,2048]{1,0:T(8,128)(2,1)}, bf16[128,2048]{1,0:T(8,128)(2,1)}, u32[]{:S(2)}, u32[]{:S(2)}) collective-permute-start(bf16[128,2048]{1,0:T(8,128)(2,1)} %slice.272), channel_id=1, source_target_pairs={{0,2},{1,3},{2,0},{3,1},{4,6},{5,7},{6,4},{7,5},{8,10},{9,11},{10,... | collective-permute-start | bytes 1572872 | tf_op jit(solution)/shard_map/ppermute | solution.py:18
  294.7 10.1 %collective-permute-start.29 = (f32[2,2048]{1,0:T(2,128)S(1)}, f32[2,2048]{1,0:T(2,128)S(1)}, u32[]{:S(2)}, u32[]{:S(2)}) collective-permute-start(f32[2,2048]{1,0:T(2,128)S(1)} %pad_maximum_fusion.21), channel_id=1, source_target_pairs={{0,1},{1,0},{2,3},{3,2},{4,5},{5,4},{6,7},{7,6},{8,9},{9,8},{10,11... | collective-permute-start | bytes 49160 | tf_op jit(solution)/shard_map/ppermute | solution.py:18
  294.8 66.2 %collective-permute-start.34 = (bf16[640,512]{1,0:T(8,128)(2,1)}, bf16[640,512]{1,0:T(8,128)(2,1)}, u32[]{:S(2)}, u32[]{:S(2)}) collective-permute-start(bf16[640,512]{1,0:T(8,128)(2,1)} %copy-done.17), channel_id=1, source_target_pairs={{0,4},{4,0},{8,12},{12,8},{16,20},{20,16},{24,28},{28,24},{1,5},{5... | collective-permute-start | bytes 1966088 | tf_op jit(solution)/shard_map/ppermute | solution.py:18
  296.6 81.1 %collective-permute-start.37 = (bf16[256,1408]{1,0:T(8,128)(2,1)}, bf16[256,1408]{1,0:T(8,128)(2,1)}, u32[]{:S(2)}, u32[]{:S(2)}) collective-permute-start(bf16[256,1408]{1,0:T(8,128)(2,1)} %add_convert_fusion.1), channel_id=1, source_target_pairs={{0,16},{4,20},{8,24},{12,28},{16,0},{20,4},{24,8},{28,12},{1,17},{... | collective-permute-start | bytes 2162696 | tf_op jit(solution)/shard_map/ppermute | solution.py:18
  304.0 128.3 %reduce-scatter.6.cloned.1.call-start = ((), (), s32[]{:S(2)}) async-start(), calls=%async_computation.4 | async-start | bytes 1638400 | tf_op jit(solution)/shard_map/reduce_scatter | solution.py:303
  304.1 68.0 %collective-permute-start.35 = (bf16[512,1408]{1,0:T(8,128)(2,1)}, bf16[512,1408]{1,0:T(8,128)(2,1)}, u32[]{:S(2)}, u32[]{:S(2)}) collective-permute-start(bf16[512,1408]{1,0:T(8,128)(2,1)} %copy-done.21), channel_id=1, source_target_pairs={{0,4},{4,0},{8,12},{12,8},{16,20},{20,16},{24,28},{28,24},{1,5},{5... | collective-permute-start | bytes 4325384 | tf_op jit(solution)/shard_map/ppermute | solution.py:18
  304.8 3.8 collective-permute-start.30
  308.7 44.6 %collective-permute-start.31 = (f32[2,1024]{1,0:T(2,128)S(1)}, f32[2,1024]{1,0:T(2,128)S(1)}, u32[]{:S(2)}, u32[]{:S(2)}) collective-permute-start(f32[2,1024]{1,0:T(2,128)S(1)} %pad_maximum_fusion.22), channel_id=1, source_target_pairs={{0,16},{4,20},{8,24},{12,28},{16,0},{20,4},{24,8},{28,12},{1,17},{... | collective-permute-start | bytes 24584 | tf_op jit(solution)/shard_map/ppermute | solution.py:18
  308.7 45.3 %copy-start.7 = (bf16[512,2048]{1,0:T(8,128)(2,1)S(1)}, bf16[512,2048]{1,0:T(8,128)(2,1)}, u32[]{:S(2)}) copy-start(bf16[512,2048]{1,0:T(8,128)(2,1)} %copy-done.5) | copy-start | bytes 6291460
  353.3 4.5 %collective-permute-start.32 = (f32[2,512]{1,0:T(2,128)S(1)}, f32[2,512]{1,0:T(2,128)S(1)}, u32[]{:S(2)}, u32[]{:S(2)}) collective-permute-start(f32[2,512]{1,0:T(2,128)S(1)} %slice.205), channel_id=1, source_target_pairs={{0,8},{4,12},{8,0},{12,4},{16,24},{20,28},{24,16},{28,20},{1,9},{5... | collective-permute-start | bytes 12296 | tf_op jit(solution)/shard_map/ppermute | solution.py:18
  357.8 9.8 %collective-permute-start.33 = (f32[2,256]{1,0:T(2,128)S(1)}, f32[2,256]{1,0:T(2,128)S(1)}, u32[]{:S(2)}, u32[]{:S(2)}) collective-permute-start(f32[2,256]{1,0:T(2,128)S(1)} %slice.207), channel_id=1, source_target_pairs={{0,4},{4,0},{8,12},{12,8},{16,20},{20,16},{24,28},{28,24},{1,5},{5... | collective-permute-start | bytes 6152 | tf_op jit(solution)/shard_map/ppermute | solution.py:18
  374.3 55.3 %collective-permute-start.36 = (bf16[256,1408]{1,0:T(8,128)(2,1)}, bf16[256,1408]{1,0:T(8,128)(2,1)}, u32[]{:S(2)}, u32[]{:S(2)}) collective-permute-start(bf16[256,1408]{1,0:T(8,128)(2,1)} %add_convert_fusion), channel_id=1, source_target_pairs={{0,16},{4,20},{8,24},{12,28},{16,0},{20,4},{24,8},{28,12},{1,17},{... | collective-permute-start | bytes 2162696 | tf_op jit(solution)/shard_map/ppermute | solution.py:18
  386.4 50.2 %copy-start.1 = (bf16[512,2048]{1,0:T(8,128)(2,1)S(1)}, bf16[512,2048]{1,0:T(8,128)(2,1)}, u32[]{:S(2)}) copy-start(bf16[512,2048]{1,0:T(8,128)(2,1)} %param.18) | copy-start | bytes 6291460
  (48 other events, 161.6 us)
Sparse Core Ops, SparseCore 0:
  156.7 74.0 reduce-scatter.3
  304.1 41.9 reduce-scatter.7
  367.7 54.2 reduce-scatter.5

commit v7 on v6

--- a/solution.py
+++ b/solution.py
@@ -311,23 +311,17 @@
     out[...] = (dot(x[...], g[...], 0, side) + dot(x_far[...], g_far[...], 0, side)).astype(LOW)
 
 
-def weight_terms(places, first, x, x_far, g, g_far, transposed=False, part=None, keep=False):
+def weight_terms(places, far_places, x, x_far, g, g_far, transposed=False, keep=True):
     count = len(places)
-    blocks = lax.axis_size("dp")
-    size = x.shape[1] // blocks
+    size = x.shape[1] // lax.axis_size("dp")
     rows = x.shape[0]
     units = g.shape[0] if transposed else g.shape[1]
-    if part is not None:
-        units //= 2
     if size % 128:
         side = 1 if transposed else 0
-        far = x_far[:, first * size : (first + count) * size]
-        if part is not None:
-            g, g_far = (v[:, part * units : (part + 1) * units] for v in (g, g_far))
-        return (dot(pick(x, places, blocks, 1), g, 0, side) + dot(far, g_far, 0, side)).astype(LOW)
-    whole = pl.BlockSpec(
-        (units, rows) if transposed else (rows, units), lambda i, p: (0, part or 0)
-    )
+        mine = pick(x, places, x.shape[1] // size, 1)
+        theirs = pick(x_far, far_places, x_far.shape[1] // size, 1)
+        return (dot(mine, g, 0, side) + dot(theirs, g_far, 0, side)).astype(LOW)
+    whole = pl.BlockSpec(g.shape, lambda i, p: (0, 0))
     return pl.pallas_call(
         functools.partial(terms_kernel, transposed),
         out_shape=(jax.ShapeDtypeStruct if keep else pltpu.HBM)((count * size, units), LOW),
@@ -336,7 +330,7 @@
             grid=(count,),
             in_specs=[
                 pl.BlockSpec((rows, size), lambda i, p: (0, p[i])),
-                pl.BlockSpec((rows, size), lambda i, p: (0, first + i)),
+                pl.BlockSpec((rows, size), lambda i, p: (0, p[count + i])),
                 whole,
                 whole,
             ],
@@ -347,7 +341,7 @@
             flops=8 * rows * count * size * units, bytes_accessed=4 * rows * units, transcendentals=0
         ),
         name="weight_terms",
-    )(jnp.stack(places).astype(jnp.int32), x, x_far, g, g_far)
+    )(jnp.stack([*places, *far_places]).astype(jnp.int32), x, x_far, g, g_far)
 
 
 def row_kernel(left, right, send, kept):
@@ -452,12 +446,17 @@
     wide = w_query.shape[1]
 
     halves = [[2 * j + which for j in range(half_count)] for which in (bit, 1 - bit)]
-    near_bits = [0] + list(range(2, bits))
-    near_masks = [
-        sum(((j >> (len(near_bits) - 1 - k)) & 1) << b for k, b in enumerate(near_bits))
-        for j in range(half_count)
-    ]
-    near_halves = [[where ^ m for m in near_masks] for where in (place, place ^ 2)]
+
+    def exchange_order(order):
+        return [
+            sum(((j >> (len(order) - 1 - k)) & 1) << b for k, b in enumerate(order))
+            for j in range(1 << len(order))
+        ]
+
+    down_bits = [0] + list(range(2, bits))
+    down_places = [[where ^ m for m in exchange_order(down_bits)] for where in (place, place ^ 2)]
+    rest_bits = list(range(1, bits))
+    rest_places = [[where ^ m for m in exchange_order(rest_bits)] for where in (place, place ^ 1)]
     row_order = [spot ^ m for m in ROW_MASKS]
 
     def near_sum(part):
@@ -478,7 +477,7 @@
     branch_far = flip(branch_out, "tp", 2)
     att_theirs = flip(after(attended, branch_out), "dp", 1)
     cot = pick(after(cotangent, branch_out), row_order, len(ROW_MASKS), 0)
-    cot_send = pick(cot, near_halves[1], dp, 1)
+    cot_send = pick(cot, down_places[1], dp, 1)
     cot_theirs = flip(cot_send, "dp", 2)
     own_inputs = own(tokens).astype(jnp.float32)
     middle = own_inputs + (after(branch, cot_send) + branch_far)
@@ -486,13 +485,12 @@
     scale_two = lax.rsqrt(jnp.mean(middle * middle, -1, keepdims=True) + EPSILON)
     own_two = (middle * scale_two * norm2_gain).astype(LOW)
     far_two = flip(own_two, "tp", 2)
-    grad_hidden = dot(after(cot, own_two), w_down, 1, 1)
-    pair_two = jnp.concatenate([after(own_two, grad_hidden, att_theirs), far_two], 0)
+    pair_two = jnp.concatenate([after(own_two, att_theirs), far_two], 0)
     core_two = flip(pair_two, "tp", 1)
     two_send = pick(pair_two, halves[1], dp, 1)
-    two_near_send = pick(pair_two, near_halves[1], dp, 1)
-    two_near = [flip(two_send, "dp", 1), flip(two_near_send, "dp", 2)]
-    normed_two = jnp.concatenate([after(pair_two, two_send, two_near_send), core_two], 0)
+    two_near = flip(two_send, "dp", 1)
+    grad_hidden = dot(after(cot, two_send), w_down, 1, 1)
+    normed_two = jnp.concatenate([after(pair_two, grad_hidden), core_two], 0)
 
     gate_pre = dot(normed_two, w_gate, 1, 0)
     up_pre = dot(normed_two, w_up, 1, 0)
@@ -502,18 +500,16 @@
     grad_gate_pre = (grad_hidden * up_pre * sigma * (1.0 + gate_pre * (1.0 - sigma))).astype(LOW)
     grad_up_pre = (grad_hidden * active).astype(LOW)
     gate_theirs = flip(grad_gate_pre, "dp", 1)
-    far_rows = jnp.concatenate([hidden, grad_up_pre], 1)
-    far_theirs = flip(far_rows, "dp", 2)
-    gate_late = after(grad_gate_pre, far_rows)
+    hidden_theirs = flip(hidden, "dp", 2)
+    up_theirs = flip(grad_up_pre, "dp", 1)
+    gate_late, cot_theirs, two_near = lax.optimization_barrier((grad_gate_pre, cot_theirs, two_near))
 
     def two_terms(lo, hi):
         rows = slice(lo * own_rows, hi * own_rows)
         return dot(gate_late[rows], w_gate, 1, 1) + dot(grad_up_pre[rows], w_up, 1, 1)
 
     grad_normed_two, two_out = near_sum(two_terms)
-    two_out, cot_theirs, *two_near = lax.optimization_barrier((two_out, cot_theirs, *two_near))
     two_far = flip(two_out, "tp", 2)
-    two_near = jnp.concatenate(two_near, 1)
     two_theirs = jnp.concatenate([two_near, flip(two_near, "tp", 1)], 0)
 
     down_near, down = row_terms(after(hidden, two_out), w_down)
@@ -525,54 +521,58 @@
     grad_far = flip(branch_grad, "tp", 2)
 
     down_near = flip(after(down_near, branch_grad), "tp", 1)
-    two_late = after(normed_two, branch_grad)
-    gate_terms = weight_terms(halves[0], 0, two_late, two_theirs, grad_gate_pre, gate_theirs)
+    natural = list(range(half_count))
+    gate_terms = weight_terms(
+        halves[0],
+        natural,
+        after(normed_two, branch_grad),
+        two_theirs,
+        grad_gate_pre,
+        gate_theirs,
+        keep=False,
+    )
     grad_gate = parity_sum(gate_terms, 0)
     grad_pair = jnp.concatenate([after(branch_grad, gate_terms), grad_far], 0)
     grad_core = flip(grad_pair, "tp", 1)
     branch_send = pick(grad_pair, halves[1], dp, 1)
     branch_near = flip(branch_send, "dp", 1)
-    branch_all = jnp.concatenate([after(grad_pair, branch_send), grad_core], 0)
+
+    def down_terms(lo, hi, *late):
+        g = after(hidden, *late)
+        return weight_terms(
+            down_places[0][lo:hi], range(lo, hi), cot, cot_theirs, g, hidden_theirs
+        )
+
+    down_sent = down_terms(half_count // 2, half_count, branch_send)
+    branch_all = jnp.concatenate([after(grad_pair, down_sent), grad_core], 0)
     grad_attended = dot(w_out, branch_all, 1, 1).astype(LOW)
-
-    def down_terms(lo, hi, *late):
-        rows = after(far_rows, *late)
-        return weight_terms(
-            near_halves[0][lo:hi], lo, cot, cot_theirs, rows, far_theirs, part=0, keep=True
-        )
-
-    def up_terms(lo, hi, *late):
-        rows = after(far_rows, *late)
-        first = half_count + lo
-        return weight_terms(
-            near_halves[0][lo:hi], first, normed_two, two_theirs, rows, far_theirs, part=1, keep=True
-        )
-
-    down_sent = down_terms(half_count // 2, half_count, grad_attended)
-    down_got = [flip(down_sent, "dp", 1)]
     grads = attention_backward(
-        at,
-        pos,
-        queries,
-        after(grad_attended, down_sent),
-        attended,
-        lse,
-        cosine,
-        sine,
-        blocks,
-        size,
-        2,
+        at, pos, queries, grad_attended, attended, lse, cosine, sine, blocks, size, 2
     )
     grad_query_rows, kv_total = grads[0], grads[1]
     kv_back = [flip(grads[m + 1], "dp", m) for m in range(1, SPAN)]
+
+    def rest_terms(lo, hi, x, x_far, g, g_far, transposed=False):
+        return weight_terms(
+            rest_places[0][lo:hi],
+            [p // 2 for p in rest_places[0][lo:hi]],
+            x,
+            x_far,
+            g,
+            g_far,
+            transposed,
+        )
 
     down = down + after(down_near, grad_query_rows)
     down, down_out = down[:own_rows], down[own_rows:].astype(LOW)
     down_far = flip(down_out, "tp", 2)
+
+    def up_terms(lo, hi, *late):
+        return rest_terms(lo, hi, normed_two, two_theirs, after(grad_up_pre, *late), up_theirs)
+
     up_sent = up_terms(half_count // 2, half_count, grad_query_rows)
-    kv_total, branch_near, down_got[0] = lax.optimization_barrier(
-        (kv_total, branch_near, down_got[0], up_sent, down_out)
-    )[:3]
+    up_got = [flip(up_sent, "dp", 2)]
+    kv_total, branch_near = lax.optimization_barrier((kv_total, branch_near, up_sent, down_out))[:2]
     for back in kv_back:
         kv_total = kv_total + back
     key_grad = turn_back(kv_total[:size], cosine, sine)
@@ -580,74 +580,98 @@
     proj_rows = jnp.concatenate([grad_query_rows, grad_kv_rows], 0)
     proj_theirs = flip(proj_rows, "dp", 1)
 
-    def exchange_rest(terms, got, *late):
+    own_order = pick(proj_rows, row_order, len(ROW_MASKS), 1)
+
+    def one_terms(lo, hi):
+        cut = own_order[:, lo * own_rows : hi * own_rows]
+        return dot(cut[:wide], w_query, 0, 1) + dot(cut[wide:], w_kv, 0, 0)
+
+    grad_normed_one, one_out = near_sum(one_terms)
+    one_far = flip(one_out, "tp", 2)
+    down_got = [flip(after(down_sent, one_out), "dp", 1)]
+    branch_theirs = jnp.concatenate([branch_near, flip(branch_near, "tp", 1)], 0)
+    output_rows = (middle + (down + after(down_far, one_out))).astype(LOW)
+    up_kept = up_terms(0, 1, one_out)
+    out_kept = rest_terms(
+        0, 1, branch_all, branch_theirs, after(attended, one_out), att_theirs, True
+    )
+    grad_normed_one = after(grad_normed_one, output_rows, up_kept, out_kept) + one_far
+    grad_in_norm, gain_one = norm_back(grad_normed_one, own_inputs, own(scale_one), norm1_gain)
+    input_rows = grad_middle + grad_in_norm
+
+    def exchange_rest(terms, got, order, *late):
         left = half_count // 2
-        for b in near_bits[1:]:
-            send = terms(left // 2, left, *late).astype(jnp.float32)
+        for b in order[1:]:
+            send = terms(left // 2, left, *late)
+            rows = send.shape[0]
             for other in got:
-                send = send + other[left // 2 * block : left * block]
+                keep = rows * (left // 2) // (left - left // 2)
+                send = send.astype(jnp.float32) + other[keep : keep + rows]
             send = send.astype(LOW)
             got.append(flip(send, "dp", 1 << b))
             left //= 2
         return send
 
-    def exchange_end(terms, got, *late):
-        kept = terms(0, 1, *late).astype(jnp.float32)
+    def exchange_end(kept, got):
+        kept = kept.astype(jnp.float32)
         for other in got:
             kept = kept + other[:block]
         return kept
 
-    down_last = exchange_rest(down_terms, down_got, proj_rows)
-    proj_rows = after(proj_rows, down_last)
-
-    own_order = pick(proj_rows, row_order, len(ROW_MASKS), 1)
-
-    def one_terms(lo, hi):
-        cut = own_order[:, lo * own_rows : hi * own_rows]
-        return dot(cut[:wide], w_query, 0, 1) + dot(cut[wide:], w_kv, 0, 0)
-
-    grad_normed_one, one_out = near_sum(one_terms)
-    one_far = flip(one_out, "tp", 2)
-
-    up_got = [flip(after(up_sent, one_out), "dp", 1)]
-    branch_theirs = jnp.concatenate([branch_near, flip(branch_near, "tp", 1)], 0)
-    out_late = after(attended, one_out)
-    out_terms = weight_terms(halves[0], 0, branch_all, branch_theirs, out_late, att_theirs, True)
-    grad_out = parity_sum(out_terms, 0)
-    output_rows = (middle + (down + after(down_far, one_out))).astype(LOW)
-    grad_normed_one = after(grad_normed_one, out_terms, output_rows) + one_far
-    grad_in_norm, gain_one = norm_back(grad_normed_one, own_inputs, own(scale_one), norm1_gain)
-    input_rows = grad_middle + grad_in_norm
-
-    gains = jnp.stack([gain_one, gain_two])
+    up_last = exchange_rest(up_terms, up_got, rest_bits, input_rows)
+    down_last = exchange_rest(down_terms, down_got, down_bits, up_last)
+
+    gains = jnp.stack([after(gain_one, down_last), gain_two])
     for m in (1, 2):
         gains = gains + flip(gains, "tp", m)
-    gains = pick(gains, [place ^ m for m in range(dp)], dp, 1)
-    left = dp
-    while left > 1:
+    gains = pick(gains, rest_places[0], dp, 1) + flip(pick(gains, rest_places[1], dp, 1), "dp", 1)
+
+    out_late, proj_late = lax.optimization_barrier((attended, proj_rows, up_last))[:2]
+
+    def last_terms(lo, hi):
+        return jnp.concatenate(
+            [
+                rest_terms(lo, hi, normed_one, one_theirs, proj_late, proj_theirs, True),
+                rest_terms(lo, hi, branch_all, branch_theirs, out_late, att_theirs, True),
+            ],
+            1,
+        )
+
+    last_got, gains_got = [], []
+    left = half_count
+    for b in rest_bits:
+        send = last_terms(left // 2, left)
+        rows, columns = send.shape
+        extra = gains[:, left // 2 * block : left * block]
+        for other, other_gains in zip(last_got, gains_got):
+            send = send.astype(jnp.float32) + other[left // 2 * block : left * block]
+            extra = extra + other_gains[:, left // 2 * block : left * block]
+        extra = jnp.pad(extra, ((0, 14), (0, columns - extra.shape[1] % columns)))[:, :columns]
+        whole = jnp.concatenate([send.astype(LOW), extra.astype(LOW)], 0)
+        got = flip(whole, "dp", 1 << b)
+        last_got.append(got[:rows])
+        gains_got.append(got[rows : rows + 2])
         left //= 2
-        gains = gains[:, : left * block] + flip(gains[:, left * block :], "dp", left)
-
-    grad_down = exchange_end(down_terms, down_got, input_rows)
-    grad_gate = grad_gate.astype(jnp.float32)
-
-    proj_late = after(proj_rows, input_rows, grad_gate)
-    proj_terms = weight_terms(halves[0], 0, normed_one, one_theirs, proj_late, proj_theirs, True)
-    grad_out = grad_out.astype(jnp.float32)
-    grad_proj = parity_sum(proj_terms, 0).astype(jnp.float32)
-    exchange_rest(up_terms, up_got, gains, proj_terms)
-    grad_up = exchange_end(up_terms, up_got, proj_terms)
+    proj_kept = rest_terms(0, 1, normed_one, one_theirs, after(proj_late, whole), proj_theirs, True)
+    down_kept = down_terms(0, 1, whole)
+    grad_last = exchange_end(jnp.concatenate([proj_kept, out_kept], 1), last_got)
+    gains = gains[:, :block]
+    for other in gains_got:
+        gains = gains + other[:, :block]
+    grad_up = exchange_end(up_kept, up_got)
+    grad_down = exchange_end(down_kept, down_got)
+    narrow = wide + 2 * size
 
     return (
         output_rows,
         input_rows,
         gains[0],
-        grad_proj[:, :wide],
-        grad_proj[:, wide : wide + size],
-        grad_proj[:, wide + size :],
-        grad_out.T,
+        grad_last[:, :wide],
+        grad_last[:, wide : wide + size],
+        grad_last[:, wide + size : narrow],
+        grad_last[:, narrow:].T,
         gains[1],
-        grad_gate,
+        grad_gate.astype(jnp.float32),
         grad_up,
         grad_down.T,
     )

time: 448 us -> 410 us (0.915)
  waiting for transfers between devices: 191 us -> 165 us
  local copies, waits for them, and re-layouts: 42.4 us -> 34.4 us
  other arithmetic: 38.8 us -> 31.2 us
    ppermute x38, waiting for transfers between devices: 191 us -> 165 us  [flip(): lax.ppermute(block, axis, [(i, i ^ mask) for i in range(lax.axis_size(axi...]
    unnamed x149 -> x192, local copies, waits for them, and re-layouts: 26.2 us -> 22.4 us
    pallas_call x9 -> x13, Pallas kernels: 36 us -> 36.3 us  [weight_terms(): pl.pallas_call(functools.partial(terms_kernel, transposed), out_shape=(ja...]
  transfers between devices with their start and end apart: 41 -> 39, of which waited for: 15 -> 15; matrix products, arithmetic and copies ran while one was open for 20% -> 17% of each run, Pallas kernels for 13% -> 15%
where the time goes in v7:
time: 410 us; the launch traced here: 405 us
  waiting for transfers between devices  165 us (40%)
  starting transfers between devices  63.2 us (15%)
  Pallas kernels  60.5 us (15%)
  matrix products  35.7 us (9%)
  local copies, waits for them, and re-layouts  34.4 us (8%)
  other arithmetic  31.2 us (8%)
  between operations  15.8 us (4%)
    ppermute x38, waiting for transfers between devices, flip(): lax.ppermute(block, axis, [(i, i ^ mask) for i in range(lax.axis_size(axi...  165 us
    ppermute x38, starting transfers between devices, flip(): lax.ppermute(block, axis, [(i, i ^ mask) for i in range(lax.axis_size(axi...  63.1 us
    pallas_call x13, Pallas kernels, weight_terms(): pl.pallas_call(functools.partial(terms_kernel, transposed), out_shape=(ja...  36.3 us
    dot_general x16, matrix products, dot(): lax.dot_general(left, right, (((left_dim,), (right_dim,)), ((), ())), pre...  35.7 us
    unnamed x192, local copies, waits for them, and re-layouts  22.4 us
    pallas_call x1, Pallas kernels, attention_backward(): pl.pallas_call(functools.partial(backward_kernel, heads, size), out_shape...  8.75 us
    pallas_call x1, Pallas kernels, attention_forward(): pl.pallas_call(functools.partial(forward_kernel, heads, size), out_shape=...  8.46 us
  transfers between devices with their start and end apart: 39, of which 15 were waited for; matrix products, arithmetic and copies ran while one was open for 17% of the time, Pallas kernels for 15%

profile of v7, /device:TPU:0, one launch (start us, length us, event | category | flops | bytes accessed | tf_op | source)
XLA Modules:
  0.0 405.3 jit_solution(11830403522176389012)
XLA Ops:
  7.3 2.2 fusion
  13.6 3.0 collective-permute-start
  16.6 1.6 collective-permute-start.1
  20.7 1.9 collective-permute-start.3
  26.6 8.5 %attention_forward.1 = (bf16[512,512]{1,0:T(8,128)(2,1)}, f32[8,1,512]{2,1,0:T(1,128)S(1)}) custom-call(s32[2]{0:T(128)S(1)} %pad_add_fusion.at_ref, s32[1,512]{1,0:T(1,128)S(1)} %bitcast.58, bf16[512,512]{1,0:T(8,128)(2,1)S(1)} %bitcast.57, bf16[128,512]{1,0:T(8,128)(2,1)S(1)} %pad_maximum_fusion.10.kv0, bf16[128,512]{1,0:T(8,128)(2,1)S(1)} %collective-permute-done.kv1, ...), custom_call_target="tpu_custom_call" | custom-call | flops 17179869184 | bytes 1048576 | tf_op jit(solution)/shard_map/attention_forward/pallas_call | solution.py:214
  35.6 11.0 %collective-permute-done.3.x_far = bf16[512,1024]{1,0:T(8,128)(2,1)S(1)} collective-permute-done((bf16[512,1024]{1,0:T(8,128)(2,1)}, bf16[512,1024]{1,0:T(8,128)(2,1)S(1)}, u32[]{:S(2)}, u32[]{:S(2)}) %collective-permute-start.3) | collective-permute-done | bytes 1048608 | tf_op jit(solution)/shard_map/ppermute | solution.py:18
  46.6 2.8 convolution_convert_fusion
  49.4 1.7 fusion.32
  54.0 1.8 collective-permute-start.5
  58.4 1.7 collective-permute-start.6
  60.1 8.0 %collective-permute-done.5 = bf16[128,2048]{1,0:T(8,128)(2,1)S(1)} collective-permute-done((bf16[128,2048]{1,0:T(8,128)(2,1)S(1)}, bf16[128,2048]{1,0:T(8,128)(2,1)S(1)}, u32[]{:S(2)}, u32[]{:S(2)}) %collective-permute-start.5) | collective-permute-done | bytes 524320 | tf_op jit(solution)/shard_map/ppermute | solution.py:18
  70.6 1.8 collective-permute-start.7
  72.4 1.6 collective-permute-start.9
  74.1 9.8 %collective-permute-done.7 = bf16[128,2048]{1,0:T(8,128)(2,1)} collective-permute-done((bf16[128,2048]{1,0:T(8,128)(2,1)S(1)}, bf16[128,2048]{1,0:T(8,128)(2,1)}, u32[]{:S(2)}, u32[]{:S(2)}) %collective-permute-start.7) | collective-permute-done | bytes 524320 | tf_op jit(solution)/shard_map/ppermute | solution.py:18
  85.2 1.7 collective-permute-start.10
  87.0 5.8 %fusion.69 = f32[512,1408]{1,0:T(8,128)S(1)} fusion(bf16[512,2048]{1,0:T(8,128)(2,1)S(1)} %copy-done.8, bf16[1408,2048]{1,0:T(8,128)(2,1)} %right.1), kind=kOutput, calls=%fused_computation.196 | convolution fusion | flops 2952790016 | bytes 10747904 | tf_op jit(solution)/shard_map/dot_general | solution.py:22
  93.1 3.4 fusion.70
  96.5 5.8 %multiply_convert_fusion.1 = (bf16[512,1408]{1,0:T(8,128)(2,1)S(1)}, bf16[512,1408]{1,0:T(8,128)(2,1)S(1)}, bf16[512,1408]{1,0:T(8,128)(2,1)}) fusion(f32[512,1408]{1,0:T(8,128)S(1)} %fusion.69, f32[512,1408]{1,0:T(8,128)S(1)} %fusion.70, bf16[512,2048]{1,0:T(8,128)(2,1)S(1)} %constant_dynamic-update-slice_fusion.2.x, bf16[2048,1408]{1,0:T(8,128)(2,1)S(1)} %bitcast.84), kind=kOutput, calls=%fused_computation.6 | convolution fusion | flops 2963603456 | bytes 17956864 | tf_op jit(solution)/shard_map/dot_general | solution.py:22
  102.4 1.8 fusion.23
  104.2 1.8 fusion.4
  106.4 1.8 fusion.21
  109.0 1.8 collective-permute-start.17
  110.8 1.8 convolution_add_fusion.2
  113.0 1.6 collective-permute-start.12
  114.7 7.0 %row_terms.1 = (bf16[256,2048]{1,0:T(8,128)(2,1)S(1)}, f32[256,2048]{1,0:T(8,128)S(1)}) custom-call(bf16[512,1408]{1,0:T(8,128)(2,1)} %get-tuple-element.110.left.g, bf16[1408,2048]{1,0:T(8,128)(2,1)S(1)} %bitcast.61), custom_call_target="tpu_custom_call" | custom-call | flops 11811160064 | bytes 5767168 | tf_op jit(solution)/shard_map/row_terms/pallas_call | solution.py:357
  122.8 4.4 %collective-permute-done.12 = bf16[128,2048]{1,0:T(8,128)(2,1)S(1)} collective-permute-done((bf16[128,2048]{1,0:T(8,128)(2,1)S(1)}, bf16[128,2048]{1,0:T(8,128)(2,1)S(1)}, u32[]{:S(2)}, u32[]{:S(2)}) %collective-permute-start.12) | collective-permute-done | bytes 524320 | tf_op jit(solution)/shard_map/ppermute | solution.py:18
  127.5 2.6 fusion.65
  130.1 1.5 collective-permute-start.16
  131.7 10.4 %collective-permute-done.15.g_far = bf16[512,1408]{1,0:T(8,128)(2,1)S(1)} collective-permute-done((bf16[512,1408]{1,0:T(8,128)(2,1)S(1)}, bf16[512,1408]{1,0:T(8,128)(2,1)S(1)}, u32[]{:S(2)}, u32[]{:S(2)}) %collective-permute-start.15) | collective-permute-done | bytes 1441824 | tf_op jit(solution)/shard_map/ppermute | solution.py:18
  142.0 5.9 %weight_terms.13 = bf16[1024,1408]{1,0:T(8,128)(2,1)} custom-call(s32[8]{0:T(128)S(1)} %stack.131.places, bf16[512,2048]{1,0:T(8,128)(2,1)S(1)} %constant_dynamic-update-slice_fusion.2.x, bf16[512,1024]{1,0:T(8,128)(2,1)S(1)} %constant_dynamic-update-slice_fusion.4.x_far, bf16[512,1408]{1,0:T(8,128)(2,1)S(1)} %get-tuple-element.73.g, ...), custom_call_target="tpu_custom_call" | custom-call | flops 5905580032 | bytes 2883584 | tf_op jit(solution)/shard_map/weight_terms/pallas_call | solution.py:325
  147.9 1.9 constant_dynamic-update-slice_fusion.7
  149.8 1.9 constant_dynamic-update-slice_fusion.6
  156.6 5.0 %weight_terms.14 = bf16[512,1408]{1,0:T(8,128)(2,1)S(1)} custom-call(s32[4]{0:T(128)S(1)} %pad_add_fusion.1.places, bf16[512,2048]{1,0:T(8,128)(2,1)S(1)} %copy-done.9, bf16[512,1024]{1,0:T(8,128)(2,1)S(1)} %copy-done.34, bf16[512,1408]{1,0:T(8,128)(2,1)} %get-tuple-element.110.left.g, bf16[512,1408]{1,0:T(8,128)(2,1)} %collective-permute-done.17.g_far), custom_call_target="tpu_custom_call" | custom-call | flops 2952790016 | bytes 2883584 | tf_op jit(solution)/shard_map/weight_terms/pallas_call | solution.py:325
  161.6 1.8 constant_dynamic-update-slice_fusion.9
  164.8 2.2 fusion.8.do_in
  167.0 8.8 %attention_backward.1 = (bf16[512,512]{1,0:T(8,128)(2,1)S(1)}, f32[128,512]{1,0:T(8,128)S(1)}, bf16[128,512]{1,0:T(8,128)(2,1)S(1)}, bf16[128,512]{1,0:T(8,128)(2,1)S(1)}, bf16[128,512]{1,0:T(8,128)(2,1)S(1)}) custom-call(s32[2]{0:T(128)S(1)} %pad_add_fusion.at_ref, s32[1,512]{1,0:T(1,128)S(1)} %bitcast.59, bf16[512,512]{1,0:T(8,128)(2,1)} %bitcast.56, ...), custom_call_target="tpu_custom_call" | custom-call | flops 25769803776 | bytes 2621440 | tf_op jit(solution)/shard_map/attention_backward/pallas_call | solution.py:249
  176.2 20.5 %collective-permute-start.24 = (bf16[128,512]{1,0:T(8,128)(2,1)S(1)}, bf16[128,512]{1,0:T(8,128)(2,1)S(1)}, u32[]{:S(2)}, u32[]{:S(2)}) collective-permute-start(bf16[128,512]{1,0:T(8,128)(2,1)S(1)} %get-tuple-element.95), channel_id=1, source_target_pairs={{0,12},{4,8},{8,4},{12,0},{16,28},{20,24},{24,20},{28,16},{1,13},{... | collective-permute-start | bytes 393224 | tf_op jit(solution)/shard_map/ppermute | solution.py:18
  197.4 3.8 weight_terms.15
  205.4 1.8 fusion.5
  208.3 1.6 collective-permute-start.19
  209.9 1.8 collective-permute-start.28
  214.3 1.5 fusion.35
  216.7 1.9 convert_add_fusion
  219.4 3.9 collective-permute-done.19
  224.4 2.5 weight_terms.17
  227.2 1.6 weight_terms.16
  229.5 4.6 %collective-permute-done.27 = bf16[128,2048]{1,0:T(8,128)(2,1)S(1)} collective-permute-done((bf16[128,2048]{1,0:T(8,128)(2,1)S(1)}, bf16[128,2048]{1,0:T(8,128)(2,1)S(1)}, u32[]{:S(2)}, u32[]{:S(2)}) %collective-permute-start.27) | collective-permute-done | bytes 524320 | tf_op jit(solution)/shard_map/ppermute | solution.py:18
  235.9 1.6 weight_terms.18
  237.5 50.8 %collective-permute-done.28 = bf16[512,1408]{1,0:T(8,128)(2,1)S(1)} collective-permute-done((bf16[512,1408]{1,0:T(8,128)(2,1)}, bf16[512,1408]{1,0:T(8,128)(2,1)S(1)}, u32[]{:S(2)}, u32[]{:S(2)}) %collective-permute-start.28) | collective-permute-done | bytes 1441824 | tf_op jit(solution)/shard_map/ppermute | solution.py:18
  289.5 3.4 weight_terms.19
  294.5 2.1 collective-permute-start.36
  298.6 2.0 weight_terms.20
  302.2 2.9 weight_terms.21
  305.2 4.3 %collective-permute-start.34 = (bf16[528,1152]{1,0:T(8,128)(2,1)S(1)}, bf16[528,1152]{1,0:T(8,128)(2,1)S(1)}, u32[]{:S(2)}, u32[]{:S(2)}) collective-permute-start(bf16[528,1152]{1,0:T(8,128)(2,1)S(1)} %fusion.9), channel_id=1, source_target_pairs={{0,8},{4,12},{8,0},{12,4},{16,24},{20,28},{24,16},{28,20},{1,9},{5... | collective-permute-start | bytes 3649544 | tf_op jit(solution)/shard_map/ppermute | solution.py:18
  309.6 2.1 weight_terms.23
  313.0 16.6 %collective-permute-done.36 = bf16[256,1408]{1,0:T(8,128)(2,1)S(1)} collective-permute-done((bf16[256,1408]{1,0:T(8,128)(2,1)}, bf16[256,1408]{1,0:T(8,128)(2,1)S(1)}, u32[]{:S(2)}, u32[]{:S(2)}) %collective-permute-start.36) | collective-permute-done | bytes 720928 | tf_op jit(solution)/shard_map/ppermute | solution.py:18
  331.0 26.5 %collective-permute-done.34 = bf16[528,1152]{1,0:T(8,128)(2,1)S(1)} collective-permute-done((bf16[528,1152]{1,0:T(8,128)(2,1)S(1)}, bf16[528,1152]{1,0:T(8,128)(2,1)S(1)}, u32[]{:S(2)}, u32[]{:S(2)}) %collective-permute-start.34) | collective-permute-done | bytes 1216544 | tf_op jit(solution)/shard_map/ppermute | solution.py:18
  358.7 3.8 collective-permute-start.35
  362.5 3.4 weight_terms.25
  365.9 13.9 %collective-permute-done.37 = bf16[256,1408]{1,0:T(8,128)(2,1)S(1)} collective-permute-done((bf16[256,1408]{1,0:T(8,128)(2,1)S(1)}, bf16[256,1408]{1,0:T(8,128)(2,1)S(1)}, u32[]{:S(2)}, u32[]{:S(2)}) %collective-permute-start.37) | collective-permute-done | bytes 720928 | tf_op jit(solution)/shard_map/ppermute | solution.py:18
  381.2 3.0 copy.27
  387.3 2.4 convert_element_type.208
  389.7 2.2 collective-permute-done.35
  391.9 1.6 convert_add_fusion.6
  (330 shorter events, 63.5 us)
Async XLA Ops:
  7.2 39.4 %copy-start = (bf16[512,2048]{1,0:T(8,128)(2,1)S(1)}, bf16[512,2048]{1,0:T(8,128)(2,1)}, u32[]{:S(2)}) copy-start(bf16[512,2048]{1,0:T(8,128)(2,1)} %param.18) | copy-start | bytes 6291460
  7.2 380.1 %reduce-scatter.2.cloned.1.call-start = ((), (), s32[]{:S(2)}) async-start(), calls=%async_computation.1 | async-start | bytes 3604480 | tf_op jit(solution)/shard_map/reduce_scatter | solution.py:303
  7.3 15.3 %copy-start.83 = (f32[32]{0:T(128)}, f32[32]{0:T(128)S(1)}, u32[]{:S(2)}) copy-start(f32[32]{0:T(128)S(1)} %multiply_exponential_fusion) | copy-start | bytes 388
  13.5 11.9 %copy-start.46 = (bf16[128,512]{1,0:T(8,128)(2,1)}, bf16[128,512]{1,0:T(8,128)(2,1)S(1)}, u32[]{:S(2)}) copy-start(bf16[128,512]{1,0:T(8,128)(2,1)S(1)} %pad_maximum_fusion.10.kv0) | copy-start | bytes 393220
  13.6 11.9 %collective-permute-start = (bf16[128,512]{1,0:T(8,128)(2,1)S(1)}, bf16[128,512]{1,0:T(8,128)(2,1)S(1)}, u32[]{:S(2)}, u32[]{:S(2)}) collective-permute-start(bf16[128,512]{1,0:T(8,128)(2,1)S(1)} %pad_maximum_fusion.10.kv0), channel_id=1, source_target_pairs={{0,4},{4,0},{8,12},{12,8},{16,20},{20,16},{24,28},{28,24},{1,5},{5... | collective-permute-start | bytes 393224 | tf_op jit(solution)/shard_map/ppermute | solution.py:18
  16.6 8.9 %collective-permute-start.1 = (bf16[128,512]{1,0:T(8,128)(2,1)S(1)}, bf16[128,512]{1,0:T(8,128)(2,1)S(1)}, u32[]{:S(2)}, u32[]{:S(2)}) collective-permute-start(bf16[128,512]{1,0:T(8,128)(2,1)S(1)} %pad_maximum_fusion.10.kv0), channel_id=1, source_target_pairs={{0,8},{4,12},{8,0},{12,4},{16,24},{20,28},{24,16},{28,20},{1,9},{5... | collective-permute-start | bytes 393224 | tf_op jit(solution)/shard_map/ppermute | solution.py:18
  18.1 7.3 %collective-permute-start.2 = (bf16[128,512]{1,0:T(8,128)(2,1)S(1)}, bf16[128,512]{1,0:T(8,128)(2,1)}, u32[]{:S(2)}, u32[]{:S(2)}) collective-permute-start(bf16[128,512]{1,0:T(8,128)(2,1)S(1)} %pad_maximum_fusion.10.kv0), channel_id=1, source_target_pairs={{0,12},{4,8},{8,4},{12,0},{16,28},{20,24},{24,20},{28,16},{1,13},{... | collective-permute-start | bytes 393224 | tf_op jit(solution)/shard_map/ppermute | solution.py:18
  20.7 25.9 %collective-permute-start.3 = (bf16[512,1024]{1,0:T(8,128)(2,1)}, bf16[512,1024]{1,0:T(8,128)(2,1)S(1)}, u32[]{:S(2)}, u32[]{:S(2)}) collective-permute-start(bf16[512,1024]{1,0:T(8,128)(2,1)} %pad_maximum_fusion.1), channel_id=1, source_target_pairs={{0,4},{4,0},{8,12},{12,8},{16,20},{20,16},{24,28},{28,24},{1,5},{5... | collective-permute-start | bytes 3145736 | tf_op jit(solution)/shard_map/ppermute | solution.py:18
  25.4 9.6 %copy-start.51 = (bf16[128,512]{1,0:T(8,128)(2,1)}, bf16[128,512]{1,0:T(8,128)(2,1)S(1)}, u32[]{:S(2)}) copy-start(bf16[128,512]{1,0:T(8,128)(2,1)S(1)} %collective-permute-done.kv1) | copy-start | bytes 393220
  25.4 9.6 %copy-start.52 = (bf16[128,512]{1,0:T(8,128)(2,1)}, bf16[128,512]{1,0:T(8,128)(2,1)S(1)}, u32[]{:S(2)}) copy-start(bf16[128,512]{1,0:T(8,128)(2,1)S(1)} %collective-permute-done.1.kv2) | copy-start | bytes 393220
  49.4 3.0 collective-permute-start.4
  54.0 14.0 %collective-permute-start.5 = (bf16[128,2048]{1,0:T(8,128)(2,1)S(1)}, bf16[128,2048]{1,0:T(8,128)(2,1)S(1)}, u32[]{:S(2)}, u32[]{:S(2)}) collective-permute-start(bf16[128,2048]{1,0:T(8,128)(2,1)S(1)} %slice.324), channel_id=1, source_target_pairs={{0,2},{1,3},{2,0},{3,1},{4,6},{5,7},{6,4},{7,5},{8,10},{9,11},{10,... | collective-permute-start | bytes 1572872 | tf_op jit(solution)/shard_map/ppermute | solution.py:18
  56.7 11.4 %slice-start.2 = ((f32[256,2048]{1,0:T(8,128)}), f32[128,2048]{1,0:T(8,128)S(1)}, s32[]{:S(2)}) async-start(f32[256,2048]{1,0:T(8,128)} %copy-done.63), calls=%async_computation.4 | async-start | bytes 2097152 | tf_op jit(solution)/shard_map/slice | solution.py:466
  58.4 12.0 %copy-start.80 = (f32[2048]{0:T(1024)S(1)}, f32[2048]{0:T(1024)}, u32[]{:S(2)}) copy-start(f32[2048]{0:T(1024)} %param.19) | copy-start | bytes 24580
  58.4 15.6 %collective-permute-start.6 = (bf16[512,512]{1,0:T(8,128)(2,1)}, bf16[512,512]{1,0:T(8,128)(2,1)S(1)}, u32[]{:S(2)}, u32[]{:S(2)}) collective-permute-start(bf16[512,512]{1,0:T(8,128)(2,1)} %get-tuple-element.108.o_in.g), channel_id=1, source_target_pairs={{0,4},{4,0},{8,12},{12,8},{16,20},{20,16},{24,28},{28,24},{1,5},{5... | collective-permute-start | bytes 1572872 | tf_op jit(solution)/shard_map/ppermute | solution.py:18
  70.6 13.3 %collective-permute-start.7 = (bf16[128,2048]{1,0:T(8,128)(2,1)S(1)}, bf16[128,2048]{1,0:T(8,128)(2,1)}, u32[]{:S(2)}, u32[]{:S(2)}) collective-permute-start(bf16[128,2048]{1,0:T(8,128)(2,1)S(1)} %multiply_convert_fusion.3), channel_id=1, source_target_pairs={{0,2},{1,3},{2,0},{3,1},{4,6},{5,7},{6,4},{7,5},{8,10},{9,11},{10,... | collective-permute-start | bytes 1572872 | tf_op jit(solution)/shard_map/ppermute | solution.py:18
  72.4 14.5 %copy-start.8 = (bf16[512,2048]{1,0:T(8,128)(2,1)S(1)}, bf16[512,2048]{1,0:T(8,128)(2,1)}, u32[]{:S(2)}) copy-start(bf16[512,2048]{1,0:T(8,128)(2,1)} %copy-done.7) | copy-start | bytes 6291460
  72.4 31.8 %collective-permute-start.9 = (bf16[512,1024]{1,0:T(8,128)(2,1)}, bf16[512,1024]{1,0:T(8,128)(2,1)S(1)}, u32[]{:S(2)}, u32[]{:S(2)}) collective-permute-start(bf16[512,1024]{1,0:T(8,128)(2,1)} %pad_maximum_fusion.2), channel_id=1, source_target_pairs={{0,8},{4,12},{8,0},{12,4},{16,24},{20,28},{24,16},{28,20},{1,9},{5... | collective-permute-start | bytes 3145736 | tf_op jit(solution)/shard_map/ppermute | solution.py:18
  74.0 11.2 %copy-start.30 = (bf16[512,512]{1,0:T(8,128)(2,1)}, bf16[512,512]{1,0:T(8,128)(2,1)S(1)}, u32[]{:S(2)}) copy-start(bf16[512,512]{1,0:T(8,128)(2,1)S(1)} %collective-permute-done.6.g_far) | copy-start | bytes 1572868
  85.1 7.8 %collective-permute-start.8 = (bf16[256,2048]{1,0:T(8,128)(2,1)S(1)}, bf16[256,2048]{1,0:T(8,128)(2,1)S(1)}, u32[]{:S(2)}, u32[]{:S(2)}) collective-permute-start(bf16[256,2048]{1,0:T(8,128)(2,1)S(1)} %constant_dynamic-update-slice_fusion), channel_id=1, source_target_pairs={{0,1},{1,0},{2,3},{3,2},{4,5},{5,4},{6,7},{7,6},{8,9},{9,8},{10,11... | collective-permute-start | bytes 3145736 | tf_op jit(solution)/shard_map/ppermute | solution.py:18
  85.2 19.0 %collective-permute-start.10 = (bf16[256,1024]{1,0:T(8,128)(2,1)S(1)}, bf16[256,1024]{1,0:T(8,128)(2,1)S(1)}, u32[]{:S(2)}, u32[]{:S(2)}) collective-permute-start(bf16[256,1024]{1,0:T(8,128)(2,1)S(1)} %pad_maximum_fusion.5), channel_id=1, source_target_pairs={{0,4},{4,0},{8,12},{12,8},{16,20},{20,16},{24,28},{28,24},{1,5},{5... | collective-permute-start | bytes 1572872 | tf_op jit(solution)/shard_map/ppermute | solution.py:18
  93.1 49.0 %copy-start.15 = (bf16[512,2048]{1,0:T(8,128)(2,1)}, bf16[512,2048]{1,0:T(8,128)(2,1)S(1)}, u32[]{:S(2)}) copy-start(bf16[512,2048]{1,0:T(8,128)(2,1)S(1)} %constant_dynamic-update-slice_fusion.2.x) | copy-start | bytes 6291460
  106.1 6.6 %collective-permute-start.11 = (bf16[256,2048]{1,0:T(8,128)(2,1)S(1)}, bf16[256,2048]{1,0:T(8,128)(2,1)S(1)}, u32[]{:S(2)}, u32[]{:S(2)}) collective-permute-start(bf16[256,2048]{1,0:T(8,128)(2,1)S(1)} %fusion.4), channel_id=1, source_target_pairs={{0,1},{1,0},{2,3},{3,2},{4,5},{5,4},{6,7},{7,6},{8,9},{9,8},{10,11... | collective-permute-start | bytes 3145736 | tf_op jit(solution)/shard_map/ppermute | solution.py:18
  106.4 8.3 %slice-start = ((s8[5767168]{0:T(1024)(128)(4,1)}), s8[1572864]{0:T(1024)(128)(4,1)S(1)}, s32[]{:S(2)}) async-start(s8[5767168]{0:T(1024)(128)(4,1)} %bitcast.60), calls=%async_computation.2 | async-start | bytes 3145728
  108.2 33.8 %collective-permute-start.15 = (bf16[512,1408]{1,0:T(8,128)(2,1)S(1)}, bf16[512,1408]{1,0:T(8,128)(2,1)S(1)}, u32[]{:S(2)}, u32[]{:S(2)}) collective-permute-start(bf16[512,1408]{1,0:T(8,128)(2,1)S(1)} %get-tuple-element.73.g), channel_id=1, source_target_pairs={{0,4},{4,0},{8,12},{12,8},{16,20},{20,16},{24,28},{28,24},{1,5},{5... | collective-permute-start | bytes 4325384 | tf_op jit(solution)/shard_map/ppermute | solution.py:18
  108.8 3.9 collective-permute-start.14
  109.0 46.4 %collective-permute-start.17 = (bf16[512,1408]{1,0:T(8,128)(2,1)}, bf16[512,1408]{1,0:T(8,128)(2,1)}, u32[]{:S(2)}, u32[]{:S(2)}) collective-permute-start(bf16[512,1408]{1,0:T(8,128)(2,1)} %get-tuple-element.110.left.g), channel_id=1, source_target_pairs={{0,8},{4,12},{8,0},{12,4},{16,24},{20,28},{24,16},{28,20},{1,9},{5... | collective-permute-start | bytes 4325384 | tf_op jit(solution)/shard_map/ppermute | solution.py:18
  112.7 84.6 %copy-start.23 = (bf16[512,1024]{1,0:T(8,128)(2,1)}, bf16[512,1024]{1,0:T(8,128)(2,1)S(1)}, u32[]{:S(2)}) copy-start(bf16[512,1024]{1,0:T(8,128)(2,1)S(1)} %constant_dynamic-update-slice_fusion.4.x_far) | copy-start | bytes 3145732
  113.0 14.1 %collective-permute-start.12 = (bf16[128,2048]{1,0:T(8,128)(2,1)S(1)}, bf16[128,2048]{1,0:T(8,128)(2,1)S(1)}, u32[]{:S(2)}, u32[]{:S(2)}) collective-permute-start(bf16[128,2048]{1,0:T(8,128)(2,1)S(1)} %slice.323), channel_id=1, source_target_pairs={{0,2},{1,3},{2,0},{3,1},{4,6},{5,7},{6,4},{7,5},{8,10},{9,11},{10,... | collective-permute-start | bytes 1572872 | tf_op jit(solution)/shard_map/ppermute | solution.py:18
  130.1 19.7 %collective-permute-start.16 = (bf16[128,2048]{1,0:T(8,128)(2,1)}, bf16[128,2048]{1,0:T(8,128)(2,1)}, u32[]{:S(2)}, u32[]{:S(2)}) collective-permute-start(bf16[128,2048]{1,0:T(8,128)(2,1)} %get-tuple-element.83), channel_id=1, source_target_pairs={{0,2},{1,3},{2,0},{3,1},{4,6},{5,7},{6,4},{7,5},{8,10},{9,11},{10,... | collective-permute-start | bytes 1572872 | tf_op jit(solution)/shard_map/ppermute | solution.py:18
  151.7 11.7 %collective-permute-start.18 = (bf16[256,2048]{1,0:T(8,128)(2,1)}, bf16[256,2048]{1,0:T(8,128)(2,1)}, u32[]{:S(2)}, u32[]{:S(2)}) collective-permute-start(bf16[256,2048]{1,0:T(8,128)(2,1)} %constant_dynamic-update-slice_fusion.6), channel_id=1, source_target_pairs={{0,1},{1,0},{2,3},{3,2},{4,5},{5,4},{6,7},{7,6},{8,9},{9,8},{10,11... | collective-permute-start | bytes 3145736 | tf_op jit(solution)/shard_map/ppermute | solution.py:18
  151.8 45.5 %collective-permute-start.21 = (bf16[512,1408]{1,0:T(8,128)(2,1)}, bf16[512,1408]{1,0:T(8,128)(2,1)S(1)}, u32[]{:S(2)}, u32[]{:S(2)}) collective-permute-start(bf16[512,1408]{1,0:T(8,128)(2,1)} %copy-done.25), channel_id=1, source_target_pairs={{0,4},{4,0},{8,12},{12,8},{16,20},{20,16},{24,28},{28,24},{1,5},{5... | collective-permute-start | bytes 4325384 | tf_op jit(solution)/shard_map/ppermute | solution.py:18
  152.6 23.2 %collective-permute-start.13 = (bf16[256,2048]{1,0:T(8,128)(2,1)}, bf16[256,2048]{1,0:T(8,128)(2,1)S(1)}, u32[]{:S(2)}, u32[]{:S(2)}) collective-permute-start(bf16[256,2048]{1,0:T(8,128)(2,1)} %copy-done.50), channel_id=1, source_target_pairs={{0,1},{1,0},{2,3},{3,2},{4,5},{5,4},{6,7},{7,6},{8,9},{9,8},{10,11... | collective-permute-start | bytes 3145736 | tf_op jit(solution)/shard_map/ppermute | solution.py:18
  154.0 48.1 %collective-permute-start.20 = (bf16[256,1024]{1,0:T(8,128)(2,1)S(1)}, bf16[256,1024]{1,0:T(8,128)(2,1)}, u32[]{:S(2)}, u32[]{:S(2)}) collective-permute-start(bf16[256,1024]{1,0:T(8,128)(2,1)S(1)} %pad_maximum_fusion.6), channel_id=1, source_target_pairs={{0,4},{4,0},{8,12},{12,8},{16,20},{20,16},{24,28},{28,24},{1,5},{5... | collective-permute-start | bytes 1572872 | tf_op jit(solution)/shard_map/ppermute | solution.py:18
  167.0 8.8 %copy-start.40 = (f32[256,2048]{1,0:T(8,128)S(1)}, f32[256,2048]{1,0:T(8,128)}, u32[]{:S(2)}) copy-start(f32[256,2048]{1,0:T(8,128)} %copy-done.39) | copy-start | bytes 6291460
  175.7 21.6 %copy-start.16 = (bf16[512,2048]{1,0:T(8,128)(2,1)S(1)}, bf16[512,2048]{1,0:T(8,128)(2,1)}, u32[]{:S(2)}) copy-start(bf16[512,2048]{1,0:T(8,128)(2,1)} %copy-done.15) | copy-start | bytes 6291460
  175.8 21.6 %copy-start.26 = (bf16[512,1408]{1,0:T(8,128)(2,1)S(1)}, bf16[512,1408]{1,0:T(8,128)(2,1)}, u32[]{:S(2)}) copy-start(bf16[512,1408]{1,0:T(8,128)(2,1)} %copy-done.25) | copy-start | bytes 4325380
  176.2 25.0 %copy-start.61 = (f32[256,2048]{1,0:T(8,128)}, f32[256,2048]{1,0:T(8,128)S(1)}, u32[]{:S(2)}) copy-start(f32[256,2048]{1,0:T(8,128)S(1)} %convert_add_fusion.1) | copy-start | bytes 6291460
  176.2 25.9 %collective-permute-start.24 = (bf16[128,512]{1,0:T(8,128)(2,1)S(1)}, bf16[128,512]{1,0:T(8,128)(2,1)S(1)}, u32[]{:S(2)}, u32[]{:S(2)}) collective-permute-start(bf16[128,512]{1,0:T(8,128)(2,1)S(1)} %get-tuple-element.95), channel_id=1, source_target_pairs={{0,12},{4,8},{8,4},{12,0},{16,28},{20,24},{24,20},{28,16},{1,13},{... | collective-permute-start | bytes 393224 | tf_op jit(solution)/shard_map/ppermute | solution.py:18
  196.7 5.8 %collective-permute-start.23 = (bf16[128,512]{1,0:T(8,128)(2,1)S(1)}, bf16[128,512]{1,0:T(8,128)(2,1)S(1)}, u32[]{:S(2)}, u32[]{:S(2)}) collective-permute-start(bf16[128,512]{1,0:T(8,128)(2,1)S(1)} %get-tuple-element.94), channel_id=1, source_target_pairs={{0,8},{4,12},{8,0},{12,4},{16,24},{20,28},{24,16},{28,20},{1,9},{5... | collective-permute-start | bytes 393224 | tf_op jit(solution)/shard_map/ppermute | solution.py:18
  196.7 6.5 %collective-permute-start.22 = (bf16[128,512]{1,0:T(8,128)(2,1)S(1)}, bf16[128,512]{1,0:T(8,128)(2,1)S(1)}, u32[]{:S(2)}, u32[]{:S(2)}) collective-permute-start(bf16[128,512]{1,0:T(8,128)(2,1)S(1)} %get-tuple-element.93), channel_id=1, source_target_pairs={{0,4},{4,0},{8,12},{12,8},{16,20},{20,16},{24,28},{28,24},{1,5},{5... | collective-permute-start | bytes 393224 | tf_op jit(solution)/shard_map/ppermute | solution.py:18
  207.3 9.4 %collective-permute-start.25 = (bf16[256,2048]{1,0:T(8,128)(2,1)}, bf16[256,2048]{1,0:T(8,128)(2,1)}, u32[]{:S(2)}, u32[]{:S(2)}) collective-permute-start(bf16[256,2048]{1,0:T(8,128)(2,1)} %fusion.5), channel_id=1, source_target_pairs={{0,1},{1,0},{2,3},{3,2},{4,5},{5,4},{6,7},{7,6},{8,9},{9,8},{10,11... | collective-permute-start | bytes 3145736 | tf_op jit(solution)/shard_map/ppermute | solution.py:18
  208.3 15.0 %collective-permute-start.19 = (bf16[128,2048]{1,0:T(8,128)(2,1)}, bf16[128,2048]{1,0:T(8,128)(2,1)S(1)}, u32[]{:S(2)}, u32[]{:S(2)}) collective-permute-start(bf16[128,2048]{1,0:T(8,128)(2,1)} %slice.322), channel_id=1, source_target_pairs={{0,2},{1,3},{2,0},{3,1},{4,6},{5,7},{6,4},{7,5},{8,10},{9,11},{10,... | collective-permute-start | bytes 1572872 | tf_op jit(solution)/shard_map/ppermute | solution.py:18
  209.9 78.4 %collective-permute-start.28 = (bf16[512,1408]{1,0:T(8,128)(2,1)}, bf16[512,1408]{1,0:T(8,128)(2,1)S(1)}, u32[]{:S(2)}, u32[]{:S(2)}) collective-permute-start(bf16[512,1408]{1,0:T(8,128)(2,1)} %weight_terms.15), channel_id=1, source_target_pairs={{0,8},{4,12},{8,0},{12,4},{16,24},{20,28},{24,16},{28,20},{1,9},{5... | collective-permute-start | bytes 4325384 | tf_op jit(solution)/shard_map/ppermute | solution.py:18
  211.7 4.9 %collective-permute-start.26 = (bf16[256,1024]{1,0:T(8,128)(2,1)}, bf16[256,1024]{1,0:T(8,128)(2,1)S(1)}, u32[]{:S(2)}, u32[]{:S(2)}) collective-permute-start(bf16[256,1024]{1,0:T(8,128)(2,1)} %collective-permute-done.20), channel_id=1, source_target_pairs={{0,1},{1,0},{2,3},{3,2},{4,5},{5,4},{6,7},{7,6},{8,9},{9,8},{10,11... | collective-permute-start | bytes 1572872 | tf_op jit(solution)/shard_map/ppermute | solution.py:18
  212.8 84.4 %collective-permute-start.33 = (bf16[640,512]{1,0:T(8,128)(2,1)S(1)}, bf16[640,512]{1,0:T(8,128)(2,1)S(1)}, u32[]{:S(2)}, u32[]{:S(2)}) collective-permute-start(bf16[640,512]{1,0:T(8,128)(2,1)S(1)} %pad_maximum_fusion.3.g), channel_id=1, source_target_pairs={{0,4},{4,0},{8,12},{12,8},{16,20},{20,16},{24,28},{28,24},{1,5},{5... | collective-permute-start | bytes 1966088 | tf_op jit(solution)/shard_map/ppermute | solution.py:18
  218.7 15.5 %collective-permute-start.27 = (bf16[128,2048]{1,0:T(8,128)(2,1)S(1)}, bf16[128,2048]{1,0:T(8,128)(2,1)S(1)}, u32[]{:S(2)}, u32[]{:S(2)}) collective-permute-start(bf16[128,2048]{1,0:T(8,128)(2,1)S(1)} %slice.321), channel_id=1, source_target_pairs={{0,2},{1,3},{2,0},{3,1},{4,6},{5,7},{6,4},{7,5},{8,10},{9,11},{10,... | collective-permute-start | bytes 1572872 | tf_op jit(solution)/shard_map/ppermute | solution.py:18
  228.8 64.1 %collective-permute-start.29 = (bf16[512,1408]{1,0:T(8,128)(2,1)S(1)}, bf16[512,1408]{1,0:T(8,128)(2,1)S(1)}, u32[]{:S(2)}, u32[]{:S(2)}) collective-permute-start(bf16[512,1408]{1,0:T(8,128)(2,1)S(1)} %copy-done.49), channel_id=1, source_target_pairs={{0,4},{4,0},{8,12},{12,8},{16,20},{20,16},{24,28},{28,24},{1,5},{5... | collective-permute-start | bytes 4325384 | tf_op jit(solution)/shard_map/ppermute | solution.py:18
  235.9 53.6 %copy-start.35 = (bf16[512,1024]{1,0:T(8,128)(2,1)S(1)}, bf16[512,1024]{1,0:T(8,128)(2,1)}, u32[]{:S(2)}) copy-start(bf16[512,1024]{1,0:T(8,128)(2,1)} %copy-done.33) | copy-start | bytes 3145732
  237.5 52.1 %copy-start.10 = (bf16[512,2048]{1,0:T(8,128)(2,1)S(1)}, bf16[512,2048]{1,0:T(8,128)(2,1)}, u32[]{:S(2)}) copy-start(bf16[512,2048]{1,0:T(8,128)(2,1)} %copy-done.7) | copy-start | bytes 6291460
  294.3 2.2 collective-permute-start.30
  294.5 35.2 %collective-permute-start.36 = (bf16[256,1408]{1,0:T(8,128)(2,1)}, bf16[256,1408]{1,0:T(8,128)(2,1)S(1)}, u32[]{:S(2)}, u32[]{:S(2)}) collective-permute-start(bf16[256,1408]{1,0:T(8,128)(2,1)} %add_convert_fusion.1), channel_id=1, source_target_pairs={{0,16},{4,20},{8,24},{12,28},{16,0},{20,4},{24,8},{28,12},{1,17},{... | collective-permute-start | bytes 2162696 | tf_op jit(solution)/shard_map/ppermute | solution.py:18
  296.6 4.0 collective-permute-start.31
  300.7 4.4 %collective-permute-start.32 = (f32[2,1024]{1,0:T(2,128)S(1)}, f32[2,1024]{1,0:T(2,128)S(1)}, u32[]{:S(2)}, u32[]{:S(2)}) collective-permute-start(f32[2,1024]{1,0:T(2,128)S(1)} %pad_maximum_fusion.18), channel_id=1, source_target_pairs={{0,4},{4,0},{8,12},{12,8},{16,20},{20,16},{24,28},{28,24},{1,5},{5... | collective-permute-start | bytes 24584 | tf_op jit(solution)/shard_map/ppermute | solution.py:18
  305.2 52.3 %collective-permute-start.34 = (bf16[528,1152]{1,0:T(8,128)(2,1)S(1)}, bf16[528,1152]{1,0:T(8,128)(2,1)S(1)}, u32[]{:S(2)}, u32[]{:S(2)}) collective-permute-start(bf16[528,1152]{1,0:T(8,128)(2,1)S(1)} %fusion.9), channel_id=1, source_target_pairs={{0,8},{4,12},{8,0},{12,4},{16,24},{20,28},{24,16},{28,20},{1,9},{5... | collective-permute-start | bytes 3649544 | tf_op jit(solution)/shard_map/ppermute | solution.py:18
  311.8 17.8 %copy-start.38 = (bf16[256,1408]{1,0:T(8,128)(2,1)S(1)}, bf16[256,1408]{1,0:T(8,128)(2,1)}, u32[]{:S(2)}) copy-start(bf16[256,1408]{1,0:T(8,128)(2,1)} %copy-done.37) | copy-start | bytes 2162692
  311.8 17.8 %copy-start.73 = (bf16[512,1408]{1,0:T(8,128)(2,1)S(1)}, bf16[512,1408]{1,0:T(8,128)(2,1)}, u32[]{:S(2)}) copy-start(bf16[512,1408]{1,0:T(8,128)(2,1)} %copy-done.72) | copy-start | bytes 4325380
  313.0 18.0 %copy-start.77 = (bf16[256,1408]{1,0:T(8,128)(2,1)S(1)}, bf16[256,1408]{1,0:T(8,128)(2,1)}, u32[]{:S(2)}) copy-start(bf16[256,1408]{1,0:T(8,128)(2,1)} %add_convert_fusion) | copy-start | bytes 2162692
  329.6 32.9 %copy-start.36 = (bf16[512,1024]{1,0:T(8,128)(2,1)S(1)}, bf16[512,1024]{1,0:T(8,128)(2,1)}, u32[]{:S(2)}) copy-start(bf16[512,1024]{1,0:T(8,128)(2,1)} %copy-done.33) | copy-start | bytes 3145732
  331.0 31.6 %copy-start.11 = (bf16[512,2048]{1,0:T(8,128)(2,1)S(1)}, bf16[512,2048]{1,0:T(8,128)(2,1)}, u32[]{:S(2)}) copy-start(bf16[512,2048]{1,0:T(8,128)(2,1)} %copy-done.7) | copy-start | bytes 6291460
  331.0 48.9 %collective-permute-start.37 = (bf16[256,1408]{1,0:T(8,128)(2,1)S(1)}, bf16[256,1408]{1,0:T(8,128)(2,1)S(1)}, u32[]{:S(2)}, u32[]{:S(2)}) collective-permute-start(bf16[256,1408]{1,0:T(8,128)(2,1)S(1)} %copy-done.77), channel_id=1, source_target_pairs={{0,16},{4,20},{8,24},{12,28},{16,0},{20,4},{24,8},{28,12},{1,17},{... | collective-permute-start | bytes 2162696 | tf_op jit(solution)/shard_map/ppermute | solution.py:18
  357.5 8.4 %copy-start.76 = (bf16[528,1152]{1,0:T(8,128)(2,1)}, bf16[528,1152]{1,0:T(8,128)(2,1)S(1)}, u32[]{:S(2)}) copy-start(bf16[528,1152]{1,0:T(8,128)(2,1)S(1)} %collective-permute-done.34) | copy-start | bytes 3649540
  358.7 21.1 %copy-start.75 = (bf16[512,1408]{1,0:T(8,128)(2,1)S(1)}, bf16[512,1408]{1,0:T(8,128)(2,1)}, u32[]{:S(2)}) copy-start(bf16[512,1408]{1,0:T(8,128)(2,1)} %copy-done.74) | copy-start | bytes 4325380
  358.7 33.1 %collective-permute-start.35 = (bf16[272,1152]{1,0:T(8,128)(2,1)}, bf16[272,1152]{1,0:T(8,128)(2,1)}, u32[]{:S(2)}, u32[]{:S(2)}) collective-permute-start(bf16[272,1152]{1,0:T(8,128)(2,1)} %fusion.27), channel_id=1, source_target_pairs={{0,16},{4,20},{8,24},{12,28},{16,0},{20,4},{24,8},{28,12},{1,17},{... | collective-permute-start | bytes 1880072 | tf_op jit(solution)/shard_map/ppermute | solution.py:18
  (67 other events, 241.7 us)
Sparse Core Ops, SparseCore 0:
  208.4 83.0 reduce-scatter.1

commit v8 on v7

--- a/solution.py
+++ b/solution.py
@@ -595,7 +595,8 @@
     out_kept = rest_terms(
         0, 1, branch_all, branch_theirs, after(attended, one_out), att_theirs, True
     )
-    grad_normed_one = after(grad_normed_one, output_rows, up_kept, out_kept) + one_far
+    grad_gate = grad_gate.astype(jnp.float32)
+    grad_normed_one = after(grad_normed_one, output_rows, up_kept, out_kept, grad_gate) + one_far
     grad_in_norm, gain_one = norm_back(grad_normed_one, own_inputs, own(scale_one), norm1_gain)
     input_rows = grad_middle + grad_in_norm
 
@@ -671,7 +672,7 @@
         grad_last[:, wide + size : narrow],
         grad_last[:, narrow:].T,
         gains[1],
-        grad_gate.astype(jnp.float32),
+        grad_gate,
         grad_up,
         grad_down.T,
     )

time: 410 us -> 393 us (0.959)
  waiting for transfers between devices: 165 us -> 130 us
  other arithmetic: 31.2 us -> 42.3 us
  local copies, waits for them, and re-layouts: 34.4 us -> 38.8 us
    ppermute x38, waiting for transfers between devices: 165 us -> 130 us  [flip(): lax.ppermute(block, axis, [(i, i ^ mask) for i in range(lax.axis_size(axi...]
    unnamed x192 -> x190, local copies, waits for them, and re-layouts: 22.4 us -> 24.3 us
  transfers between devices with their start and end apart: 39 -> 39, of which waited for: 15 -> 14; matrix products, arithmetic and copies ran while one was open for 17% -> 22% of each run, Pallas kernels for 15% -> 16%
where the time goes in v8:
time: 393 us; the launch traced here: 387 us
  waiting for transfers between devices  130 us (33%)
  Pallas kernels  63.7 us (16%)
  starting transfers between devices  62 us (16%)
  other arithmetic  42.3 us (11%)
  local copies, waits for them, and re-layouts  38.8 us (10%)
  matrix products  34.2 us (9%)
  between operations  15.7 us (4%)
    ppermute x38, waiting for transfers between devices, flip(): lax.ppermute(block, axis, [(i, i ^ mask) for i in range(lax.axis_size(axi...  130 us
    ppermute x38, starting transfers between devices, flip(): lax.ppermute(block, axis, [(i, i ^ mask) for i in range(lax.axis_size(axi...  62 us
    pallas_call x13, Pallas kernels, weight_terms(): pl.pallas_call(functools.partial(terms_kernel, transposed), out_shape=(ja...  40.1 us
    dot_general x16, matrix products, dot(): lax.dot_general(left, right, (((left_dim,), (right_dim,)), ((), ())), pre...  34.2 us
    unnamed x190, local copies, waits for them, and re-layouts  24.3 us
    pallas_call x1, Pallas kernels, attention_backward(): pl.pallas_call(functools.partial(backward_kernel, heads, size), out_shape...  8.75 us
  transfers between devices with their start and end apart: 39, of which 14 were waited for; matrix products, arithmetic and copies ran while one was open for 22% of the time, Pallas kernels for 16%

profile of v8, /device:TPU:0, one launch (start us, length us, event | category | flops | bytes accessed | tf_op | source)
XLA Modules:
  0.0 386.7 jit_solution(16502627869184200116)
XLA Ops:
  7.3 2.2 fusion
  14.0 3.0 collective-permute-start
  21.1 1.9 collective-permute-start.3
  27.0 7.8 %attention_forward.1 = (bf16[512,512]{1,0:T(8,128)(2,1)S(1)}, f32[8,1,512]{2,1,0:T(1,128)S(1)}) custom-call(s32[2]{0:T(128)S(1)} %pad_add_fusion.at_ref, s32[1,512]{1,0:T(1,128)S(1)} %bitcast.58, bf16[512,512]{1,0:T(8,128)(2,1)S(1)} %bitcast.57, bf16[128,512]{1,0:T(8,128)(2,1)S(1)} %pad_maximum_fusion.10.kv0, bf16[128,512]{1,0:T(8,128)(2,1)S(1)} %collective-permute-done.kv1, ...), custom_call_target="tpu_custom_call" | custom-call | flops 17179869184 | bytes 1048576 | tf_op jit(solution)/shard_map/attention_forward/pallas_call | solution.py:214
  34.9 12.2 %collective-permute-done.3.x_far = bf16[512,1024]{1,0:T(8,128)(2,1)S(1)} collective-permute-done((bf16[512,1024]{1,0:T(8,128)(2,1)}, bf16[512,1024]{1,0:T(8,128)(2,1)S(1)}, u32[]{:S(2)}, u32[]{:S(2)}) %collective-permute-start.3) | collective-permute-done | bytes 1048608 | tf_op jit(solution)/shard_map/ppermute | solution.py:18
  47.1 1.7 convolution_convert_fusion
  48.8 1.7 fusion.32
  53.4 1.8 collective-permute-start.5
  57.8 1.7 collective-permute-start.6
  59.4 8.0 %collective-permute-done.5 = bf16[128,2048]{1,0:T(8,128)(2,1)S(1)} collective-permute-done((bf16[128,2048]{1,0:T(8,128)(2,1)S(1)}, bf16[128,2048]{1,0:T(8,128)(2,1)S(1)}, u32[]{:S(2)}, u32[]{:S(2)}) %collective-permute-start.5) | collective-permute-done | bytes 524320 | tf_op jit(solution)/shard_map/ppermute | solution.py:18
  70.7 1.7 collective-permute-start.7
  72.5 1.6 collective-permute-start.9
  75.4 8.8 %collective-permute-done.7 = bf16[128,2048]{1,0:T(8,128)(2,1)} collective-permute-done((bf16[128,2048]{1,0:T(8,128)(2,1)}, bf16[128,2048]{1,0:T(8,128)(2,1)}, u32[]{:S(2)}, u32[]{:S(2)}) %collective-permute-start.7) | collective-permute-done | bytes 524320 | tf_op jit(solution)/shard_map/ppermute | solution.py:18
  85.5 1.7 collective-permute-start.10
  87.2 5.8 %fusion.69 = f32[512,1408]{1,0:T(8,128)S(1)} fusion(bf16[512,2048]{1,0:T(8,128)(2,1)S(1)} %copy-done.7, bf16[1408,2048]{1,0:T(8,128)(2,1)} %right.1), kind=kOutput, calls=%fused_computation.196 | convolution fusion | flops 2952790016 | bytes 10747904 | tf_op jit(solution)/shard_map/dot_general | solution.py:22
  93.4 3.4 fusion.70
  96.8 5.9 %multiply_convert_fusion.1 = (bf16[512,1408]{1,0:T(8,128)(2,1)S(1)}, bf16[512,1408]{1,0:T(8,128)(2,1)S(1)}, bf16[512,1408]{1,0:T(8,128)(2,1)}) fusion(f32[512,1408]{1,0:T(8,128)S(1)} %fusion.69, f32[512,1408]{1,0:T(8,128)S(1)} %fusion.70, bf16[512,2048]{1,0:T(8,128)(2,1)S(1)} %constant_dynamic-update-slice_fusion.2.x, bf16[2048,1408]{1,0:T(8,128)(2,1)S(1)} %bitcast.84), kind=kOutput, calls=%fused_computation.6 | convolution fusion | flops 2963603456 | bytes 17956864 | tf_op jit(solution)/shard_map/dot_general | solution.py:22
  102.7 1.8 fusion.23
  104.6 1.8 fusion.4
  106.7 1.8 fusion.21
  109.3 1.7 collective-permute-start.17
  111.1 1.8 convolution_add_fusion.2
  115.0 7.0 %row_terms.1 = (bf16[256,2048]{1,0:T(8,128)(2,1)S(1)}, f32[256,2048]{1,0:T(8,128)S(1)}) custom-call(bf16[512,1408]{1,0:T(8,128)(2,1)} %get-tuple-element.110.left.g, bf16[1408,2048]{1,0:T(8,128)(2,1)S(1)} %bitcast.61), custom_call_target="tpu_custom_call" | custom-call | flops 11811160064 | bytes 5767168 | tf_op jit(solution)/shard_map/row_terms/pallas_call | solution.py:357
  122.2 5.1 %collective-permute-done.12 = bf16[128,2048]{1,0:T(8,128)(2,1)S(1)} collective-permute-done((bf16[128,2048]{1,0:T(8,128)(2,1)S(1)}, bf16[128,2048]{1,0:T(8,128)(2,1)S(1)}, u32[]{:S(2)}, u32[]{:S(2)}) %collective-permute-start.12) | collective-permute-done | bytes 524320 | tf_op jit(solution)/shard_map/ppermute | solution.py:18
  128.3 2.6 fusion.65
  132.4 10.0 %collective-permute-done.15.g_far = bf16[512,1408]{1,0:T(8,128)(2,1)S(1)} collective-permute-done((bf16[512,1408]{1,0:T(8,128)(2,1)S(1)}, bf16[512,1408]{1,0:T(8,128)(2,1)S(1)}, u32[]{:S(2)}, u32[]{:S(2)}) %collective-permute-start.15) | collective-permute-done | bytes 1441824 | tf_op jit(solution)/shard_map/ppermute | solution.py:18
  142.4 5.9 %weight_terms.13 = bf16[1024,1408]{1,0:T(8,128)(2,1)} custom-call(s32[8]{0:T(128)S(1)} %stack.131.places, bf16[512,2048]{1,0:T(8,128)(2,1)S(1)} %constant_dynamic-update-slice_fusion.2.x, bf16[512,1024]{1,0:T(8,128)(2,1)S(1)} %constant_dynamic-update-slice_fusion.4.x_far, bf16[512,1408]{1,0:T(8,128)(2,1)S(1)} %get-tuple-element.73.g, ...), custom_call_target="tpu_custom_call" | custom-call | flops 5905580032 | bytes 2883584 | tf_op jit(solution)/shard_map/weight_terms/pallas_call | solution.py:325
  148.2 1.9 constant_dynamic-update-slice_fusion.7
  150.1 1.9 constant_dynamic-update-slice_fusion.6
  157.2 5.8 %weight_terms.14 = bf16[512,1408]{1,0:T(8,128)(2,1)} custom-call(s32[4]{0:T(128)S(1)} %pad_add_fusion.1.places, bf16[512,2048]{1,0:T(8,128)(2,1)S(1)} %copy-done.8, bf16[512,1024]{1,0:T(8,128)(2,1)S(1)} %copy-done.37, bf16[512,1408]{1,0:T(8,128)(2,1)} %get-tuple-element.110.left.g, bf16[512,1408]{1,0:T(8,128)(2,1)} %collective-permute-done.17.g_far), custom_call_target="tpu_custom_call" | custom-call | flops 2952790016 | bytes 2883584 | tf_op jit(solution)/shard_map/weight_terms/pallas_call | solution.py:325
  165.7 2.1 fusion.8.do_in
  167.8 8.7 %attention_backward.1 = (bf16[512,512]{1,0:T(8,128)(2,1)S(1)}, f32[128,512]{1,0:T(8,128)S(1)}, bf16[128,512]{1,0:T(8,128)(2,1)S(1)}, bf16[128,512]{1,0:T(8,128)(2,1)S(1)}, bf16[128,512]{1,0:T(8,128)(2,1)S(1)}) custom-call(s32[2]{0:T(128)S(1)} %pad_add_fusion.at_ref, s32[1,512]{1,0:T(1,128)S(1)} %bitcast.59, bf16[512,512]{1,0:T(8,128)(2,1)} %bitcast.56, ...), custom_call_target="tpu_custom_call" | custom-call | flops 25769803776 | bytes 2621440 | tf_op jit(solution)/shard_map/attention_backward/pallas_call | solution.py:249
  177.0 20.5 %collective-permute-start.24 = (bf16[128,512]{1,0:T(8,128)(2,1)S(1)}, bf16[128,512]{1,0:T(8,128)(2,1)S(1)}, u32[]{:S(2)}, u32[]{:S(2)}) collective-permute-start(bf16[128,512]{1,0:T(8,128)(2,1)S(1)} %get-tuple-element.95), channel_id=1, source_target_pairs={{0,12},{4,8},{8,4},{12,0},{16,28},{20,24},{24,20},{28,16},{1,13},{... | collective-permute-start | bytes 393224 | tf_op jit(solution)/shard_map/ppermute | solution.py:18
  198.2 4.2 %weight_terms.15 = bf16[512,1408]{1,0:T(8,128)(2,1)S(1)} custom-call(s32[4]{0:T(128)S(1)} %pad_add_fusion.2.places, bf16[512,2048]{1,0:T(8,128)(2,1)S(1)} %copy-done.15, bf16[512,1024]{1,0:T(8,128)(2,1)S(1)} %constant_dynamic-update-slice_fusion.4.x_far, bf16[512,1408]{1,0:T(8,128)(2,1)S(1)} %copy-done.30, bf16[512,1408]{1,0:T(8,128)(2,1)} %collective-permute-done.21.g_far), custom_call_target="tpu_custom_call" | custom-call | flops 2952790016 | bytes 2883584 | tf_op jit(solution)/shard_map/weight_terms/pallas_call | solution.py:325
  203.3 3.2 collective-permute-done.24
  206.6 3.0 collective-permute-done.23
  211.7 1.7 fusion.5
  216.4 2.5 collective-permute-start.28
  219.9 2.1 collective-permute-start.33
  224.2 1.9 convert_add_fusion
  227.5 1.9 collective-permute-done.19
  231.5 4.7 %collective-permute-start.29 = (bf16[512,1408]{1,0:T(8,128)(2,1)}, bf16[512,1408]{1,0:T(8,128)(2,1)}, u32[]{:S(2)}, u32[]{:S(2)}) collective-permute-start(bf16[512,1408]{1,0:T(8,128)(2,1)} %weight_terms.14), channel_id=1, source_target_pairs={{0,4},{4,0},{8,12},{12,8},{16,20},{20,16},{24,28},{28,24},{1,5},{5... | collective-permute-start | bytes 4325384 | tf_op jit(solution)/shard_map/ppermute | solution.py:18
  237.3 2.9 weight_terms.16
  241.0 2.5 convert_element_type.192
  243.5 1.9 fusion.17
  245.4 2.9 fusion.14
  248.3 2.9 weight_terms.18
  251.3 2.3 add_convert_fusion.1
  253.6 3.4 weight_terms.19
  257.0 11.3 %collective-permute-done.29 = bf16[512,1408]{1,0:T(8,128)(2,1)} collective-permute-done((bf16[512,1408]{1,0:T(8,128)(2,1)}, bf16[512,1408]{1,0:T(8,128)(2,1)}, u32[]{:S(2)}, u32[]{:S(2)}) %collective-permute-start.29) | collective-permute-done | bytes 1441824 | tf_op jit(solution)/shard_map/ppermute | solution.py:18
  268.2 2.2 add_convert_fusion
  271.0 3.3 collective-permute-start.36
  275.8 1.6 copy-done.3
  278.6 3.3 weight_terms.20
  283.2 1.9 weight_terms.21
  289.5 2.2 weight_terms.22
  291.8 15.3 %collective-permute-done.36 = bf16[256,1408]{1,0:T(8,128)(2,1)S(1)} collective-permute-done((bf16[256,1408]{1,0:T(8,128)(2,1)}, bf16[256,1408]{1,0:T(8,128)(2,1)S(1)}, u32[]{:S(2)}, u32[]{:S(2)}) %collective-permute-start.36) | collective-permute-done | bytes 720928 | tf_op jit(solution)/shard_map/ppermute | solution.py:18
  307.1 2.6 convert_add_fusion.5
  309.7 34.7 %collective-permute-done.34 = bf16[528,1152]{1,0:T(8,128)(2,1)S(1)} collective-permute-done((bf16[528,1152]{1,0:T(8,128)(2,1)S(1)}, bf16[528,1152]{1,0:T(8,128)(2,1)S(1)}, u32[]{:S(2)}, u32[]{:S(2)}) %collective-permute-start.34) | collective-permute-done | bytes 1216544 | tf_op jit(solution)/shard_map/ppermute | solution.py:18
  345.6 3.4 weight_terms.25
  349.0 2.5 add_bitcast_fusion
  351.6 2.9 copy.27
  357.3 2.2 weight_terms.24
  359.5 13.9 %collective-permute-done.35 = bf16[272,1152]{1,0:T(8,128)(2,1)} collective-permute-done((bf16[272,1152]{1,0:T(8,128)(2,1)}, bf16[272,1152]{1,0:T(8,128)(2,1)}, u32[]{:S(2)}, u32[]{:S(2)}) %collective-permute-start.35) | collective-permute-done | bytes 626720 | tf_op jit(solution)/shard_map/ppermute | solution.py:18
  (328 shorter events, 72.3 us)
Async XLA Ops:
  7.2 39.9 %copy-start = (bf16[512,2048]{1,0:T(8,128)(2,1)S(1)}, bf16[512,2048]{1,0:T(8,128)(2,1)}, u32[]{:S(2)}) copy-start(bf16[512,2048]{1,0:T(8,128)(2,1)} %param.18) | copy-start | bytes 6291460
  7.2 233.8 %reduce-scatter.2.cloned.1.call-start = ((), (), s32[]{:S(2)}) async-start(), calls=%async_computation.1 | async-start | bytes 3604480 | tf_op jit(solution)/shard_map/reduce_scatter | solution.py:303
  14.0 11.9 %copy-start.45 = (bf16[128,512]{1,0:T(8,128)(2,1)}, bf16[128,512]{1,0:T(8,128)(2,1)S(1)}, u32[]{:S(2)}) copy-start(bf16[128,512]{1,0:T(8,128)(2,1)S(1)} %pad_maximum_fusion.10.kv0) | copy-start | bytes 393220
  14.0 11.9 %collective-permute-start = (bf16[128,512]{1,0:T(8,128)(2,1)S(1)}, bf16[128,512]{1,0:T(8,128)(2,1)S(1)}, u32[]{:S(2)}, u32[]{:S(2)}) collective-permute-start(bf16[128,512]{1,0:T(8,128)(2,1)S(1)} %pad_maximum_fusion.10.kv0), channel_id=1, source_target_pairs={{0,4},{4,0},{8,12},{12,8},{16,20},{20,16},{24,28},{28,24},{1,5},{5... | collective-permute-start | bytes 393224 | tf_op jit(solution)/shard_map/ppermute | solution.py:18
  17.0 8.9 %collective-permute-start.1 = (bf16[128,512]{1,0:T(8,128)(2,1)S(1)}, bf16[128,512]{1,0:T(8,128)(2,1)S(1)}, u32[]{:S(2)}, u32[]{:S(2)}) collective-permute-start(bf16[128,512]{1,0:T(8,128)(2,1)S(1)} %pad_maximum_fusion.10.kv0), channel_id=1, source_target_pairs={{0,8},{4,12},{8,0},{12,4},{16,24},{20,28},{24,16},{28,20},{1,9},{5... | collective-permute-start | bytes 393224 | tf_op jit(solution)/shard_map/ppermute | solution.py:18
  18.6 7.3 %collective-permute-start.2 = (bf16[128,512]{1,0:T(8,128)(2,1)S(1)}, bf16[128,512]{1,0:T(8,128)(2,1)}, u32[]{:S(2)}, u32[]{:S(2)}) collective-permute-start(bf16[128,512]{1,0:T(8,128)(2,1)S(1)} %pad_maximum_fusion.10.kv0), channel_id=1, source_target_pairs={{0,12},{4,8},{8,4},{12,0},{16,28},{20,24},{24,20},{28,16},{1,13},{... | collective-permute-start | bytes 393224 | tf_op jit(solution)/shard_map/ppermute | solution.py:18
  21.1 25.9 %collective-permute-start.3 = (bf16[512,1024]{1,0:T(8,128)(2,1)}, bf16[512,1024]{1,0:T(8,128)(2,1)S(1)}, u32[]{:S(2)}, u32[]{:S(2)}) collective-permute-start(bf16[512,1024]{1,0:T(8,128)(2,1)} %pad_maximum_fusion.1), channel_id=1, source_target_pairs={{0,4},{4,0},{8,12},{12,8},{16,20},{20,16},{24,28},{28,24},{1,5},{5... | collective-permute-start | bytes 3145736 | tf_op jit(solution)/shard_map/ppermute | solution.py:18
  25.9 8.9 %copy-start.49 = (bf16[128,512]{1,0:T(8,128)(2,1)}, bf16[128,512]{1,0:T(8,128)(2,1)S(1)}, u32[]{:S(2)}) copy-start(bf16[128,512]{1,0:T(8,128)(2,1)S(1)} %collective-permute-done.kv1) | copy-start | bytes 393220
  25.9 9.0 %copy-start.50 = (bf16[128,512]{1,0:T(8,128)(2,1)}, bf16[128,512]{1,0:T(8,128)(2,1)S(1)}, u32[]{:S(2)}) copy-start(bf16[128,512]{1,0:T(8,128)(2,1)S(1)} %collective-permute-done.1.kv2) | copy-start | bytes 393220
  34.8 12.2 %copy-start.23 = (bf16[512,512]{1,0:T(8,128)(2,1)}, bf16[512,512]{1,0:T(8,128)(2,1)S(1)}, u32[]{:S(2)}) copy-start(bf16[512,512]{1,0:T(8,128)(2,1)S(1)} %get-tuple-element.108.o_in.g) | copy-start | bytes 1572868
  34.8 13.9 %copy-start.51 = (f32[8,1,512]{2,1,0:T(1,128)}, f32[8,1,512]{2,1,0:T(1,128)S(1)}, u32[]{:S(2)}) copy-start(f32[8,1,512]{2,1,0:T(1,128)S(1)} %get-tuple-element.87.lse_ref) | copy-start | bytes 49156
  48.8 3.0 collective-permute-start.4
  53.4 14.0 %collective-permute-start.5 = (bf16[128,2048]{1,0:T(8,128)(2,1)S(1)}, bf16[128,2048]{1,0:T(8,128)(2,1)S(1)}, u32[]{:S(2)}, u32[]{:S(2)}) collective-permute-start(bf16[128,2048]{1,0:T(8,128)(2,1)S(1)} %slice.324), channel_id=1, source_target_pairs={{0,2},{1,3},{2,0},{3,1},{4,6},{5,7},{6,4},{7,5},{8,10},{9,11},{10,... | collective-permute-start | bytes 1572872 | tf_op jit(solution)/shard_map/ppermute | solution.py:18
  56.1 11.3 %slice-start.2 = ((f32[256,2048]{1,0:T(8,128)}), f32[128,2048]{1,0:T(8,128)S(1)}, s32[]{:S(2)}) async-start(f32[256,2048]{1,0:T(8,128)} %copy-done.63), calls=%async_computation.4 | async-start | bytes 2097152 | tf_op jit(solution)/shard_map/slice | solution.py:466
  57.8 12.0 %copy-start.79 = (f32[2048]{0:T(1024)S(1)}, f32[2048]{0:T(1024)}, u32[]{:S(2)}) copy-start(f32[2048]{0:T(1024)} %param.19) | copy-start | bytes 24580
  57.8 16.3 %collective-permute-start.6 = (bf16[512,512]{1,0:T(8,128)(2,1)S(1)}, bf16[512,512]{1,0:T(8,128)(2,1)S(1)}, u32[]{:S(2)}, u32[]{:S(2)}) collective-permute-start(bf16[512,512]{1,0:T(8,128)(2,1)S(1)} %copy-done.24), channel_id=1, source_target_pairs={{0,4},{4,0},{8,12},{12,8},{16,20},{20,16},{24,28},{28,24},{1,5},{5... | collective-permute-start | bytes 1572872 | tf_op jit(solution)/shard_map/ppermute | solution.py:18
  70.7 13.5 %collective-permute-start.7 = (bf16[128,2048]{1,0:T(8,128)(2,1)}, bf16[128,2048]{1,0:T(8,128)(2,1)}, u32[]{:S(2)}, u32[]{:S(2)}) collective-permute-start(bf16[128,2048]{1,0:T(8,128)(2,1)} %multiply_convert_fusion.3), channel_id=1, source_target_pairs={{0,2},{1,3},{2,0},{3,1},{4,6},{5,7},{6,4},{7,5},{8,10},{9,11},{10,... | collective-permute-start | bytes 1572872 | tf_op jit(solution)/shard_map/ppermute | solution.py:18
  72.5 14.7 %copy-start.7 = (bf16[512,2048]{1,0:T(8,128)(2,1)S(1)}, bf16[512,2048]{1,0:T(8,128)(2,1)}, u32[]{:S(2)}) copy-start(bf16[512,2048]{1,0:T(8,128)(2,1)} %copy-done.6) | copy-start | bytes 6291460
  72.5 32.0 %collective-permute-start.9 = (bf16[512,1024]{1,0:T(8,128)(2,1)}, bf16[512,1024]{1,0:T(8,128)(2,1)S(1)}, u32[]{:S(2)}, u32[]{:S(2)}) collective-permute-start(bf16[512,1024]{1,0:T(8,128)(2,1)} %pad_maximum_fusion.2), channel_id=1, source_target_pairs={{0,8},{4,12},{8,0},{12,4},{16,24},{20,28},{24,16},{28,20},{1,9},{5... | collective-permute-start | bytes 3145736 | tf_op jit(solution)/shard_map/ppermute | solution.py:18
  74.1 11.4 %copy-start.33 = (bf16[512,512]{1,0:T(8,128)(2,1)}, bf16[512,512]{1,0:T(8,128)(2,1)S(1)}, u32[]{:S(2)}) copy-start(bf16[512,512]{1,0:T(8,128)(2,1)S(1)} %collective-permute-done.6.g_far) | copy-start | bytes 1572868
  85.3 7.8 %collective-permute-start.8 = (bf16[256,2048]{1,0:T(8,128)(2,1)S(1)}, bf16[256,2048]{1,0:T(8,128)(2,1)S(1)}, u32[]{:S(2)}, u32[]{:S(2)}) collective-permute-start(bf16[256,2048]{1,0:T(8,128)(2,1)S(1)} %constant_dynamic-update-slice_fusion), channel_id=1, source_target_pairs={{0,1},{1,0},{2,3},{3,2},{4,5},{5,4},{6,7},{7,6},{8,9},{9,8},{10,11... | collective-permute-start | bytes 3145736 | tf_op jit(solution)/shard_map/ppermute | solution.py:18
  85.5 19.0 %collective-permute-start.10 = (bf16[256,1024]{1,0:T(8,128)(2,1)S(1)}, bf16[256,1024]{1,0:T(8,128)(2,1)S(1)}, u32[]{:S(2)}, u32[]{:S(2)}) collective-permute-start(bf16[256,1024]{1,0:T(8,128)(2,1)S(1)} %pad_maximum_fusion.5), channel_id=1, source_target_pairs={{0,4},{4,0},{8,12},{12,8},{16,20},{20,16},{24,28},{28,24},{1,5},{5... | collective-permute-start | bytes 1572872 | tf_op jit(solution)/shard_map/ppermute | solution.py:18
  93.3 49.0 %copy-start.14 = (bf16[512,2048]{1,0:T(8,128)(2,1)}, bf16[512,2048]{1,0:T(8,128)(2,1)S(1)}, u32[]{:S(2)}) copy-start(bf16[512,2048]{1,0:T(8,128)(2,1)S(1)} %constant_dynamic-update-slice_fusion.2.x) | copy-start | bytes 6291460
  106.4 6.6 %collective-permute-start.11 = (bf16[256,2048]{1,0:T(8,128)(2,1)S(1)}, bf16[256,2048]{1,0:T(8,128)(2,1)S(1)}, u32[]{:S(2)}, u32[]{:S(2)}) collective-permute-start(bf16[256,2048]{1,0:T(8,128)(2,1)S(1)} %fusion.4), channel_id=1, source_target_pairs={{0,1},{1,0},{2,3},{3,2},{4,5},{5,4},{6,7},{7,6},{8,9},{9,8},{10,11... | collective-permute-start | bytes 3145736 | tf_op jit(solution)/shard_map/ppermute | solution.py:18
  108.5 33.9 %collective-permute-start.15 = (bf16[512,1408]{1,0:T(8,128)(2,1)S(1)}, bf16[512,1408]{1,0:T(8,128)(2,1)S(1)}, u32[]{:S(2)}, u32[]{:S(2)}) collective-permute-start(bf16[512,1408]{1,0:T(8,128)(2,1)S(1)} %get-tuple-element.73.g), channel_id=1, source_target_pairs={{0,4},{4,0},{8,12},{12,8},{16,20},{20,16},{24,28},{28,24},{1,5},{5... | collective-permute-start | bytes 4325384 | tf_op jit(solution)/shard_map/ppermute | solution.py:18
  109.1 3.8 collective-permute-start.14
  109.3 46.7 %collective-permute-start.17 = (bf16[512,1408]{1,0:T(8,128)(2,1)}, bf16[512,1408]{1,0:T(8,128)(2,1)}, u32[]{:S(2)}, u32[]{:S(2)}) collective-permute-start(bf16[512,1408]{1,0:T(8,128)(2,1)} %get-tuple-element.110.left.g), channel_id=1, source_target_pairs={{0,8},{4,12},{8,0},{12,4},{16,24},{20,28},{24,16},{28,20},{1,9},{5... | collective-permute-start | bytes 4325384 | tf_op jit(solution)/shard_map/ppermute | solution.py:18
  112.9 85.2 %copy-start.26 = (bf16[512,1024]{1,0:T(8,128)(2,1)}, bf16[512,1024]{1,0:T(8,128)(2,1)S(1)}, u32[]{:S(2)}) copy-start(bf16[512,1024]{1,0:T(8,128)(2,1)S(1)} %constant_dynamic-update-slice_fusion.4.x_far) | copy-start | bytes 3145732
  113.4 13.9 %collective-permute-start.12 = (bf16[128,2048]{1,0:T(8,128)(2,1)S(1)}, bf16[128,2048]{1,0:T(8,128)(2,1)S(1)}, u32[]{:S(2)}, u32[]{:S(2)}) collective-permute-start(bf16[128,2048]{1,0:T(8,128)(2,1)S(1)} %slice.323), channel_id=1, source_target_pairs={{0,2},{1,3},{2,0},{3,1},{4,6},{5,7},{6,4},{7,5},{8,10},{9,11},{10,... | collective-permute-start | bytes 1572872 | tf_op jit(solution)/shard_map/ppermute | solution.py:18
  130.9 19.3 %collective-permute-start.16 = (bf16[128,2048]{1,0:T(8,128)(2,1)}, bf16[128,2048]{1,0:T(8,128)(2,1)}, u32[]{:S(2)}, u32[]{:S(2)}) collective-permute-start(bf16[128,2048]{1,0:T(8,128)(2,1)} %get-tuple-element.83), channel_id=1, source_target_pairs={{0,2},{1,3},{2,0},{3,1},{4,6},{5,7},{6,4},{7,5},{8,10},{9,11},{10,... | collective-permute-start | bytes 1572872 | tf_op jit(solution)/shard_map/ppermute | solution.py:18
  152.1 12.3 %collective-permute-start.18 = (bf16[256,2048]{1,0:T(8,128)(2,1)}, bf16[256,2048]{1,0:T(8,128)(2,1)}, u32[]{:S(2)}, u32[]{:S(2)}) collective-permute-start(bf16[256,2048]{1,0:T(8,128)(2,1)} %constant_dynamic-update-slice_fusion.6), channel_id=1, source_target_pairs={{0,1},{1,0},{2,3},{3,2},{4,5},{5,4},{6,7},{7,6},{8,9},{9,8},{10,11... | collective-permute-start | bytes 3145736 | tf_op jit(solution)/shard_map/ppermute | solution.py:18
  152.2 45.9 %collective-permute-start.21 = (bf16[512,1408]{1,0:T(8,128)(2,1)}, bf16[512,1408]{1,0:T(8,128)(2,1)}, u32[]{:S(2)}, u32[]{:S(2)}) collective-permute-start(bf16[512,1408]{1,0:T(8,128)(2,1)} %copy-done.29), channel_id=1, source_target_pairs={{0,4},{4,0},{8,12},{12,8},{16,20},{20,16},{24,28},{28,24},{1,5},{5... | collective-permute-start | bytes 4325384 | tf_op jit(solution)/shard_map/ppermute | solution.py:18
  153.0 23.6 %collective-permute-start.13 = (bf16[256,2048]{1,0:T(8,128)(2,1)}, bf16[256,2048]{1,0:T(8,128)(2,1)S(1)}, u32[]{:S(2)}, u32[]{:S(2)}) collective-permute-start(bf16[256,2048]{1,0:T(8,128)(2,1)} %copy-done.48), channel_id=1, source_target_pairs={{0,1},{1,0},{2,3},{3,2},{4,5},{5,4},{6,7},{7,6},{8,9},{9,8},{10,11... | collective-permute-start | bytes 3145736 | tf_op jit(solution)/shard_map/ppermute | solution.py:18
  154.6 48.7 %collective-permute-start.20 = (bf16[256,1024]{1,0:T(8,128)(2,1)S(1)}, bf16[256,1024]{1,0:T(8,128)(2,1)S(1)}, u32[]{:S(2)}, u32[]{:S(2)}) collective-permute-start(bf16[256,1024]{1,0:T(8,128)(2,1)S(1)} %pad_maximum_fusion.6), channel_id=1, source_target_pairs={{0,4},{4,0},{8,12},{12,8},{16,20},{20,16},{24,28},{28,24},{1,5},{5... | collective-permute-start | bytes 1572872 | tf_op jit(solution)/shard_map/ppermute | solution.py:18
  176.6 21.5 %copy-start.15 = (bf16[512,2048]{1,0:T(8,128)(2,1)S(1)}, bf16[512,2048]{1,0:T(8,128)(2,1)}, u32[]{:S(2)}) copy-start(bf16[512,2048]{1,0:T(8,128)(2,1)} %copy-done.14) | copy-start | bytes 6291460
  176.6 21.5 %copy-start.30 = (bf16[512,1408]{1,0:T(8,128)(2,1)S(1)}, bf16[512,1408]{1,0:T(8,128)(2,1)}, u32[]{:S(2)}) copy-start(bf16[512,1408]{1,0:T(8,128)(2,1)} %copy-done.29) | copy-start | bytes 4325380
  177.0 25.4 %copy-start.61 = (f32[256,2048]{1,0:T(8,128)}, f32[256,2048]{1,0:T(8,128)S(1)}, u32[]{:S(2)}) copy-start(f32[256,2048]{1,0:T(8,128)S(1)} %convert_add_fusion.1) | copy-start | bytes 6291460
  177.0 29.6 %collective-permute-start.24 = (bf16[128,512]{1,0:T(8,128)(2,1)S(1)}, bf16[128,512]{1,0:T(8,128)(2,1)S(1)}, u32[]{:S(2)}, u32[]{:S(2)}) collective-permute-start(bf16[128,512]{1,0:T(8,128)(2,1)S(1)} %get-tuple-element.95), channel_id=1, source_target_pairs={{0,12},{4,8},{8,4},{12,0},{16,28},{20,24},{24,20},{28,16},{1,13},{... | collective-permute-start | bytes 393224 | tf_op jit(solution)/shard_map/ppermute | solution.py:18
  197.5 12.0 %collective-permute-start.23 = (bf16[128,512]{1,0:T(8,128)(2,1)S(1)}, bf16[128,512]{1,0:T(8,128)(2,1)S(1)}, u32[]{:S(2)}, u32[]{:S(2)}) collective-permute-start(bf16[128,512]{1,0:T(8,128)(2,1)S(1)} %get-tuple-element.94), channel_id=1, source_target_pairs={{0,8},{4,12},{8,0},{12,4},{16,24},{20,28},{24,16},{28,20},{1,9},{5... | collective-permute-start | bytes 393224 | tf_op jit(solution)/shard_map/ppermute | solution.py:18
  197.5 12.0 %collective-permute-start.22 = (bf16[128,512]{1,0:T(8,128)(2,1)S(1)}, bf16[128,512]{1,0:T(8,128)(2,1)S(1)}, u32[]{:S(2)}, u32[]{:S(2)}) collective-permute-start(bf16[128,512]{1,0:T(8,128)(2,1)S(1)} %get-tuple-element.93), channel_id=1, source_target_pairs={{0,4},{4,0},{8,12},{12,8},{16,20},{20,16},{24,28},{28,24},{1,5},{5... | collective-permute-start | bytes 393224 | tf_op jit(solution)/shard_map/ppermute | solution.py:18
  213.4 10.7 %collective-permute-start.25 = (bf16[256,2048]{1,0:T(8,128)(2,1)}, bf16[256,2048]{1,0:T(8,128)(2,1)}, u32[]{:S(2)}, u32[]{:S(2)}) collective-permute-start(bf16[256,2048]{1,0:T(8,128)(2,1)} %fusion.5), channel_id=1, source_target_pairs={{0,1},{1,0},{2,3},{3,2},{4,5},{5,4},{6,7},{7,6},{8,9},{9,8},{10,11... | collective-permute-start | bytes 3145736 | tf_op jit(solution)/shard_map/ppermute | solution.py:18
  214.9 14.5 %collective-permute-start.19 = (bf16[128,2048]{1,0:T(8,128)(2,1)}, bf16[128,2048]{1,0:T(8,128)(2,1)S(1)}, u32[]{:S(2)}, u32[]{:S(2)}) collective-permute-start(bf16[128,2048]{1,0:T(8,128)(2,1)} %slice.322), channel_id=1, source_target_pairs={{0,2},{1,3},{2,0},{3,1},{4,6},{5,7},{6,4},{7,5},{8,10},{9,11},{10,... | collective-permute-start | bytes 1572872 | tf_op jit(solution)/shard_map/ppermute | solution.py:18
  216.4 34.9 %collective-permute-start.28 = (bf16[512,1408]{1,0:T(8,128)(2,1)}, bf16[512,1408]{1,0:T(8,128)(2,1)}, u32[]{:S(2)}, u32[]{:S(2)}) collective-permute-start(bf16[512,1408]{1,0:T(8,128)(2,1)} %copy-done.47), channel_id=1, source_target_pairs={{0,8},{4,12},{8,0},{12,4},{16,24},{20,28},{24,16},{28,20},{1,9},{5... | collective-permute-start | bytes 4325384 | tf_op jit(solution)/shard_map/ppermute | solution.py:18
  218.9 5.2 %collective-permute-start.26 = (bf16[256,1024]{1,0:T(8,128)(2,1)}, bf16[256,1024]{1,0:T(8,128)(2,1)S(1)}, u32[]{:S(2)}, u32[]{:S(2)}) collective-permute-start(bf16[256,1024]{1,0:T(8,128)(2,1)} %copy-done.72), channel_id=1, source_target_pairs={{0,1},{1,0},{2,3},{3,2},{4,5},{5,4},{6,7},{7,6},{8,9},{9,8},{10,11... | collective-permute-start | bytes 1572872 | tf_op jit(solution)/shard_map/ppermute | solution.py:18
  219.9 55.8 %collective-permute-start.33 = (bf16[640,512]{1,0:T(8,128)(2,1)S(1)}, bf16[640,512]{1,0:T(8,128)(2,1)}, u32[]{:S(2)}, u32[]{:S(2)}) collective-permute-start(bf16[640,512]{1,0:T(8,128)(2,1)S(1)} %pad_maximum_fusion.3.g), channel_id=1, source_target_pairs={{0,4},{4,0},{8,12},{12,8},{16,20},{20,16},{24,28},{28,24},{1,5},{5... | collective-permute-start | bytes 1966088 | tf_op jit(solution)/shard_map/ppermute | solution.py:18
  224.1 12.1 %copy-start.18 = (bf16[512,1024]{1,0:T(8,128)(2,1)}, bf16[512,1024]{1,0:T(8,128)(2,1)S(1)}, u32[]{:S(2)}) copy-start(bf16[512,1024]{1,0:T(8,128)(2,1)S(1)} %constant_dynamic-update-slice_fusion.10.x_far) | copy-start | bytes 3145732
  227.0 9.2 %copy-start.12 = (bf16[512,2048]{1,0:T(8,128)(2,1)S(1)}, bf16[512,2048]{1,0:T(8,128)(2,1)}, u32[]{:S(2)}) copy-start(bf16[512,2048]{1,0:T(8,128)(2,1)} %copy-done.11) | copy-start | bytes 6291460
  227.0 9.2 %copy-start.25 = (bf16[512,512]{1,0:T(8,128)(2,1)S(1)}, bf16[512,512]{1,0:T(8,128)(2,1)}, u32[]{:S(2)}) copy-start(bf16[512,512]{1,0:T(8,128)(2,1)} %copy-done.23) | copy-start | bytes 1572868
  227.0 9.2 %copy-start.34 = (bf16[512,512]{1,0:T(8,128)(2,1)S(1)}, bf16[512,512]{1,0:T(8,128)(2,1)}, u32[]{:S(2)}) copy-start(bf16[512,512]{1,0:T(8,128)(2,1)} %copy-done.33) | copy-start | bytes 1572868
  227.0 16.5 %collective-permute-start.27 = (bf16[128,2048]{1,0:T(8,128)(2,1)}, bf16[128,2048]{1,0:T(8,128)(2,1)}, u32[]{:S(2)}, u32[]{:S(2)}) collective-permute-start(bf16[128,2048]{1,0:T(8,128)(2,1)} %slice.321), channel_id=1, source_target_pairs={{0,2},{1,3},{2,0},{3,1},{4,6},{5,7},{6,4},{7,5},{8,10},{9,11},{10,... | collective-permute-start | bytes 1572872 | tf_op jit(solution)/shard_map/ppermute | solution.py:18
  231.5 36.8 %collective-permute-start.29 = (bf16[512,1408]{1,0:T(8,128)(2,1)}, bf16[512,1408]{1,0:T(8,128)(2,1)}, u32[]{:S(2)}, u32[]{:S(2)}) collective-permute-start(bf16[512,1408]{1,0:T(8,128)(2,1)} %weight_terms.14), channel_id=1, source_target_pairs={{0,4},{4,0},{8,12},{12,8},{16,20},{20,16},{24,28},{28,24},{1,5},{5... | collective-permute-start | bytes 4325384 | tf_op jit(solution)/shard_map/ppermute | solution.py:18
  245.4 25.0 %copy-start.77 = (f32[2048]{0:T(1024)}, f32[2048]{0:T(1024)S(1)}, u32[]{:S(2)}) copy-start(f32[2048]{0:T(1024)S(1)} %get-tuple-element.106) | copy-start | bytes 24580
  256.9 13.5 %copy-start.75 = (f32[2048]{0:T(1024)S(1)}, f32[2048]{0:T(1024)}, u32[]{:S(2)}) copy-start(f32[2048]{0:T(1024)} %get-tuple-element.124) | copy-start | bytes 24580
  271.0 3.3 collective-permute-start.30
  271.0 36.0 %collective-permute-start.36 = (bf16[256,1408]{1,0:T(8,128)(2,1)}, bf16[256,1408]{1,0:T(8,128)(2,1)S(1)}, u32[]{:S(2)}, u32[]{:S(2)}) collective-permute-start(bf16[256,1408]{1,0:T(8,128)(2,1)} %add_convert_fusion.1), channel_id=1, source_target_pairs={{0,16},{4,20},{8,24},{12,28},{16,0},{20,4},{24,8},{28,12},{1,17},{... | collective-permute-start | bytes 2162696 | tf_op jit(solution)/shard_map/ppermute | solution.py:18
  275.1 6.8 %collective-permute-start.31 = (f32[2,2048]{1,0:T(2,128)S(1)}, f32[2,2048]{1,0:T(2,128)S(1)}, u32[]{:S(2)}, u32[]{:S(2)}) collective-permute-start(f32[2,2048]{1,0:T(2,128)S(1)} %fusion.64), channel_id=1, source_target_pairs={{0,2},{1,3},{2,0},{3,1},{4,6},{5,7},{6,4},{7,5},{8,10},{9,11},{10,... | collective-permute-start | bytes 49160 | tf_op jit(solution)/shard_map/ppermute | solution.py:18
  282.7 3.7 collective-permute-start.32
  286.5 58.1 %copy-start.81 = (f32[2,1024]{1,0:T(2,128)}, f32[2,1024]{1,0:T(2,128)S(1)}, u32[]{:S(2)}) copy-start(f32[2,1024]{1,0:T(2,128)S(1)} %maximum_add_fusion) | copy-start | bytes 24580
  286.6 57.8 %collective-permute-start.34 = (bf16[528,1152]{1,0:T(8,128)(2,1)S(1)}, bf16[528,1152]{1,0:T(8,128)(2,1)S(1)}, u32[]{:S(2)}, u32[]{:S(2)}) collective-permute-start(bf16[528,1152]{1,0:T(8,128)(2,1)S(1)} %fusion.9), channel_id=1, source_target_pairs={{0,8},{4,12},{8,0},{12,4},{16,24},{20,28},{24,16},{28,20},{1,9},{5... | collective-permute-start | bytes 3649544 | tf_op jit(solution)/shard_map/ppermute | solution.py:18
  287.0 62.0 %collective-permute-start.37 = (bf16[256,1408]{1,0:T(8,128)(2,1)S(1)}, bf16[256,1408]{1,0:T(8,128)(2,1)S(1)}, u32[]{:S(2)}, u32[]{:S(2)}) collective-permute-start(bf16[256,1408]{1,0:T(8,128)(2,1)S(1)} %copy-done.71), channel_id=1, source_target_pairs={{0,16},{4,20},{8,24},{12,28},{16,0},{20,4},{24,8},{28,12},{1,17},{... | collective-permute-start | bytes 2162696 | tf_op jit(solution)/shard_map/ppermute | solution.py:18
  289.5 17.6 %copy-start.41 = (bf16[256,1408]{1,0:T(8,128)(2,1)S(1)}, bf16[256,1408]{1,0:T(8,128)(2,1)}, u32[]{:S(2)}) copy-start(bf16[256,1408]{1,0:T(8,128)(2,1)} %copy-done.40) | copy-start | bytes 2162692
  307.1 38.5 %copy-start.39 = (bf16[512,1024]{1,0:T(8,128)(2,1)S(1)}, bf16[512,1024]{1,0:T(8,128)(2,1)}, u32[]{:S(2)}) copy-start(bf16[512,1024]{1,0:T(8,128)(2,1)} %copy-done.36) | copy-start | bytes 3145732
  309.7 35.9 %copy-start.10 = (bf16[512,2048]{1,0:T(8,128)(2,1)S(1)}, bf16[512,2048]{1,0:T(8,128)(2,1)}, u32[]{:S(2)}) copy-start(bf16[512,2048]{1,0:T(8,128)(2,1)} %copy-done.6) | copy-start | bytes 6291460
  345.6 27.8 %collective-permute-start.35 = (bf16[272,1152]{1,0:T(8,128)(2,1)}, bf16[272,1152]{1,0:T(8,128)(2,1)}, u32[]{:S(2)}, u32[]{:S(2)}) collective-permute-start(bf16[272,1152]{1,0:T(8,128)(2,1)} %fusion.27), channel_id=1, source_target_pairs={{0,16},{4,20},{8,24},{12,28},{16,0},{20,4},{24,8},{28,12},{1,17},{... | collective-permute-start | bytes 1880072 | tf_op jit(solution)/shard_map/ppermute | solution.py:18
  (66 other events, 269.0 us)
Sparse Core Ops, SparseCore 0:
  153.1 62.9 reduce-scatter.1

commit v9 on v8

--- a/solution.py
+++ b/solution.py
@@ -338,7 +338,7 @@
         ),
         compiler_params=pltpu.CompilerParams(vmem_limit_bytes=24 << 20),
         cost_estimate=pl.CostEstimate(
-            flops=8 * rows * count * size * units, bytes_accessed=4 * rows * units, transcendentals=0
+            flops=24 * rows * count * size * units, bytes_accessed=4 * rows * units, transcendentals=0
         ),
         name="weight_terms",
     )(jnp.stack([*places, *far_places]).astype(jnp.int32), x, x_far, g, g_far)
@@ -480,7 +480,8 @@
     cot_send = pick(cot, down_places[1], dp, 1)
     cot_theirs = flip(cot_send, "dp", 2)
     own_inputs = own(tokens).astype(jnp.float32)
-    middle = own_inputs + (after(branch, cot_send) + branch_far)
+    grad_hidden = dot(after(cot, cot_send), w_down, 1, 1)
+    middle = own_inputs + (after(branch, cot_send, grad_hidden) + branch_far)
 
     scale_two = lax.rsqrt(jnp.mean(middle * middle, -1, keepdims=True) + EPSILON)
     own_two = (middle * scale_two * norm2_gain).astype(LOW)
@@ -489,8 +490,7 @@
     core_two = flip(pair_two, "tp", 1)
     two_send = pick(pair_two, halves[1], dp, 1)
     two_near = flip(two_send, "dp", 1)
-    grad_hidden = dot(after(cot, two_send), w_down, 1, 1)
-    normed_two = jnp.concatenate([after(pair_two, grad_hidden), core_two], 0)
+    normed_two = jnp.concatenate([after(pair_two, two_send), core_two], 0)
 
     gate_pre = dot(normed_two, w_gate, 1, 0)
     up_pre = dot(normed_two, w_up, 1, 0)
@@ -535,7 +535,10 @@
     grad_pair = jnp.concatenate([after(branch_grad, gate_terms), grad_far], 0)
     grad_core = flip(grad_pair, "tp", 1)
     branch_send = pick(grad_pair, halves[1], dp, 1)
-    branch_near = flip(branch_send, "dp", 1)
+
+    def near_flip(terms, bit):
+        half = terms.shape[0] // 2
+        return [flip(terms[half:], "dp", 1 << bit), flip(terms[:half], "dp", 1 << bit)]
 
     def down_terms(lo, hi, *late):
         g = after(hidden, *late)
@@ -544,6 +547,8 @@
         )
 
     down_sent = down_terms(half_count // 2, half_count, branch_send)
+    half = down_sent.shape[0] // 2
+    down_first = flip(down_sent[half:], "dp", 1)
     branch_all = jnp.concatenate([after(grad_pair, down_sent), grad_core], 0)
     grad_attended = dot(w_out, branch_all, 1, 1).astype(LOW)
     grads = attention_backward(
@@ -571,14 +576,29 @@
         return rest_terms(lo, hi, normed_two, two_theirs, after(grad_up_pre, *late), up_theirs)
 
     up_sent = up_terms(half_count // 2, half_count, grad_query_rows)
-    up_got = [flip(up_sent, "dp", 2)]
-    kv_total, branch_near = lax.optimization_barrier((kv_total, branch_near, up_sent, down_out))[:2]
+    up_first = flip(up_sent[half:], "dp", 2)
+
+    def exchange_mid(terms, first, order, *late):
+        got, left = [first], half_count // 2
+        for b in order[1:]:
+            send = terms(left // 2, left, *late).astype(jnp.float32)
+            rows = send.shape[0]
+            for other in got:
+                send = send + other[other.shape[0] - rows :]
+            send = send.astype(LOW)
+            got.append(flip(send, "dp", 1 << b))
+            left //= 2
+        return got[1:], send
+
+    down_late, down_last = exchange_mid(down_terms, down_first, down_bits, grad_query_rows)
+    kv_total = lax.optimization_barrier((kv_total, up_sent, down_out, down_last))[0]
     for back in kv_back:
         kv_total = kv_total + back
     key_grad = turn_back(kv_total[:size], cosine, sine)
     grad_kv_rows = jnp.concatenate([key_grad, kv_total[size:]], 0).astype(LOW)
     proj_rows = jnp.concatenate([grad_query_rows, grad_kv_rows], 0)
     proj_theirs = flip(proj_rows, "dp", 1)
+    branch_near = flip(after(branch_send, proj_rows), "dp", 1)
 
     own_order = pick(proj_rows, row_order, len(ROW_MASKS), 1)
 
@@ -588,7 +608,6 @@
 
     grad_normed_one, one_out = near_sum(one_terms)
     one_far = flip(one_out, "tp", 2)
-    down_got = [flip(after(down_sent, one_out), "dp", 1)]
     branch_theirs = jnp.concatenate([branch_near, flip(branch_near, "tp", 1)], 0)
     output_rows = (middle + (down + after(down_far, one_out))).astype(LOW)
     up_kept = up_terms(0, 1, one_out)
@@ -600,67 +619,74 @@
     grad_in_norm, gain_one = norm_back(grad_normed_one, own_inputs, own(scale_one), norm1_gain)
     input_rows = grad_middle + grad_in_norm
 
-    def exchange_rest(terms, got, order, *late):
-        left = half_count // 2
-        for b in order[1:]:
-            send = terms(left // 2, left, *late)
-            rows = send.shape[0]
-            for other in got:
-                keep = rows * (left // 2) // (left - left // 2)
-                send = send.astype(jnp.float32) + other[keep : keep + rows]
-            send = send.astype(LOW)
-            got.append(flip(send, "dp", 1 << b))
-            left //= 2
-        return send
-
-    def exchange_end(kept, got):
-        kept = kept.astype(jnp.float32)
-        for other in got:
-            kept = kept + other[:block]
-        return kept
-
-    up_last = exchange_rest(up_terms, up_got, rest_bits, input_rows)
-    down_last = exchange_rest(down_terms, down_got, down_bits, up_last)
-
-    gains = jnp.stack([after(gain_one, down_last), gain_two])
+    up_late, up_last = exchange_mid(up_terms, up_first, rest_bits, input_rows)
+    gain_one, *down_late = lax.optimization_barrier((gain_one, *down_late, up_last))[:-1]
+    gains = jnp.stack([gain_one, gain_two])
     for m in (1, 2):
         gains = gains + flip(gains, "tp", m)
     gains = pick(gains, rest_places[0], dp, 1) + flip(pick(gains, rest_places[1], dp, 1), "dp", 1)
 
     out_late, proj_late = lax.optimization_barrier((attended, proj_rows, up_last))[:2]
 
-    def last_terms(lo, hi):
+    def last_terms(lo, hi, *late):
+        first, second = after(proj_late, *late), after(out_late, *late)
         return jnp.concatenate(
             [
-                rest_terms(lo, hi, normed_one, one_theirs, proj_late, proj_theirs, True),
-                rest_terms(lo, hi, branch_all, branch_theirs, out_late, att_theirs, True),
+                rest_terms(lo, hi, normed_one, one_theirs, first, proj_theirs, True),
+                rest_terms(lo, hi, branch_all, branch_theirs, second, att_theirs, True),
             ],
             1,
         )
 
-    last_got, gains_got = [], []
-    left = half_count
-    for b in rest_bits:
-        send = last_terms(left // 2, left)
-        rows, columns = send.shape
-        extra = gains[:, left // 2 * block : left * block]
-        for other, other_gains in zip(last_got, gains_got):
-            send = send.astype(jnp.float32) + other[left // 2 * block : left * block]
-            extra = extra + other_gains[:, left // 2 * block : left * block]
-        extra = jnp.pad(extra, ((0, 14), (0, columns - extra.shape[1] % columns)))[:, :columns]
-        whole = jnp.concatenate([send.astype(LOW), extra.astype(LOW)], 0)
-        got = flip(whole, "dp", 1 << b)
-        last_got.append(got[:rows])
-        gains_got.append(got[rows : rows + 2])
-        left //= 2
-    proj_kept = rest_terms(0, 1, normed_one, one_theirs, after(proj_late, whole), proj_theirs, True)
-    down_kept = down_terms(0, 1, whole)
-    grad_last = exchange_end(jnp.concatenate([proj_kept, out_kept], 1), last_got)
-    gains = gains[:, :block]
-    for other in gains_got:
+    def with_gains(terms, lo, hi, *others):
+        extra = gains[:, lo * block : hi * block]
+        for other, other_gains in others:
+            terms = terms.astype(jnp.float32) + other
+            extra = extra + other_gains
+        columns = terms.shape[1]
+        extra = jnp.pad(extra, ((0, 14), (0, -extra.shape[1] % columns)))[:, :columns]
+        return jnp.concatenate([terms.astype(LOW), extra.astype(LOW)], 0)
+
+    def split(message, count):
+        rows = count * block
+        return message[:rows], message[rows : rows + 2, :rows]
+
+    quarter = half_count // 4
+    sent = last_terms(half_count // 2, half_count)
+    cut = quarter * block
+    firsts = with_gains(sent[cut:], 3 * quarter, half_count)
+    seconds = with_gains(sent[:cut], 2 * quarter, 3 * quarter)
+    mids = [split(flip(firsts, "dp", 2), quarter)]
+    proj_kept = rest_terms(0, 1, normed_one, one_theirs, after(proj_late, firsts), proj_theirs, True)
+    down_kept = down_terms(0, 1, firsts)
+    left = half_count // 2
+    for b in rest_bits[1:]:
+        count = left // 2
+        terms = last_terms(count, left, firsts)
+        terms, *up_late = lax.optimization_barrier((terms, *up_late, proj_kept, down_kept))[:-2]
+        send = with_gains(
+            terms, count, left, *((o[-count * block :], g[:, -count * block :]) for o, g in mids)
+        )
+        mids.append(split(flip(send, "dp", 1 << b), count))
+        left = count
+    last_second = split(flip(after(seconds, send), "dp", 2), quarter)
+    up_second, down_second = lax.optimization_barrier((up_sent[:half], down_sent[:half], send))[:2]
+    up_second, down_second = flip(up_second, "dp", 2), flip(down_second, "dp", 1)
+
+    def ending(kept, *others):
+        kept = kept.astype(jnp.float32)
+        for other in others:
+            kept = kept + other[:block]
+        return kept
+
+    grad_last = ending(
+        jnp.concatenate([proj_kept, out_kept], 1), last_second[0], *(m[0] for m in mids[1:])
+    )
+    gains = gains[:, :block] + last_second[1][:, :block]
+    for _, other in mids[1:]:
         gains = gains + other[:, :block]
-    grad_up = exchange_end(up_kept, up_got)
-    grad_down = exchange_end(down_kept, down_got)
+    grad_up = ending(up_kept, up_second, *up_late)
+    grad_down = ending(down_kept, down_second, *down_late)
     narrow = wide + 2 * size
 
     return (

time: 393 us -> 369 us (0.939)
  waiting for transfers between devices: 130 us -> 113 us
  other arithmetic: 42.3 us -> 32.3 us
  starting transfers between devices: 62 us -> 72 us
  local copies, waits for them, and re-layouts: 38.8 us -> 31.3 us
    ppermute x38 -> x41, waiting for transfers between devices: 130 us -> 113 us  [flip(): lax.ppermute(block, axis, [(i, i ^ mask) for i in range(lax.axis_size(axi...]
    ppermute x38 -> x41, starting transfers between devices: 62 us -> 72 us  [flip(): lax.ppermute(block, axis, [(i, i ^ mask) for i in range(lax.axis_size(axi...]
    unnamed x190 -> x172, local copies, waits for them, and re-layouts: 24.3 us -> 19.5 us
  transfers between devices with their start and end apart: 39 -> 42, of which waited for: 14 -> 15; matrix products, arithmetic and copies ran while one was open for 22% -> 21% of each run, Pallas kernels for 16% -> 17%
where the time goes in v9:
time: 369 us; the launch traced here: 364 us
  waiting for transfers between devices  113 us (31%)
  starting transfers between devices  72 us (20%)
  Pallas kernels  63.4 us (17%)
  matrix products  36.5 us (10%)
  other arithmetic  32.3 us (9%)
  local copies, waits for them, and re-layouts  31.3 us (8%)
  between operations  16.1 us (4%)
    ppermute x41, waiting for transfers between devices, flip(): lax.ppermute(block, axis, [(i, i ^ mask) for i in range(lax.axis_size(axi...  113 us
    ppermute x41, starting transfers between devices, flip(): lax.ppermute(block, axis, [(i, i ^ mask) for i in range(lax.axis_size(axi...  72 us
    pallas_call x13, Pallas kernels, weight_terms(): pl.pallas_call(functools.partial(terms_kernel, transposed), out_shape=(ja...  40.4 us
    dot_general x16, matrix products, dot(): lax.dot_general(left, right, (((left_dim,), (right_dim,)), ((), ())), pre...  36.5 us
    unnamed x172, local copies, waits for them, and re-layouts  19.5 us
    pallas_call x1, Pallas kernels, attention_backward(): pl.pallas_call(functools.partial(backward_kernel, heads, size), out_shape...  8.75 us
  transfers between devices with their start and end apart: 42, of which 15 were waited for; matrix products, arithmetic and copies ran while one was open for 21% of the time, Pallas kernels for 17%

profile of v9, /device:TPU:0, one launch (start us, length us, event | category | flops | bytes accessed | tf_op | source)
XLA Modules:
  0.0 364.2 jit_solution(9235735800259658421)
XLA Ops:
  7.3 2.2 fusion
  13.6 3.0 collective-permute-start
  20.7 1.9 collective-permute-start.3
  26.4 7.2 %attention_forward.1 = (bf16[512,512]{1,0:T(8,128)(2,1)S(1)}, f32[8,1,512]{2,1,0:T(1,128)S(1)}) custom-call(s32[2]{0:T(128)S(1)} %pad_add_fusion.at_ref, s32[1,512]{1,0:T(1,128)S(1)} %bitcast.58, bf16[512,512]{1,0:T(8,128)(2,1)S(1)} %bitcast.56, bf16[128,512]{1,0:T(8,128)(2,1)S(1)} %pad_maximum_fusion.12.kv0, bf16[128,512]{1,0:T(8,128)(2,1)S(1)} %collective-permute-done.kv1, ...), custom_call_target="tpu_custom_call" | custom-call | flops 17179869184 | bytes 1048576 | tf_op jit(solution)/shard_map/attention_forward/pallas_call | solution.py:214
  34.2 12.5 %collective-permute-done.3.x_far = bf16[512,1024]{1,0:T(8,128)(2,1)} collective-permute-done((bf16[512,1024]{1,0:T(8,128)(2,1)}, bf16[512,1024]{1,0:T(8,128)(2,1)}, u32[]{:S(2)}, u32[]{:S(2)}) %collective-permute-start.3) | collective-permute-done | bytes 1048608 | tf_op jit(solution)/shard_map/ppermute | solution.py:18
  46.7 1.7 convolution_convert_fusion
  49.2 2.3 collective-permute-done.4
  53.0 1.8 collective-permute-start.5
  59.2 5.0 %fusion.76 = f32[512,1408]{1,0:T(8,128)} fusion(bf16[512,2048]{1,0:T(8,128)(2,1)S(1)} %pad_maximum_fusion.x, bf16[1408,2048]{1,0:T(8,128)(2,1)S(1)} %bitcast.61), kind=kOutput, calls=%fused_computation.205 | convolution fusion | flops 2952790016 | bytes 10747904 | tf_op jit(solution)/shard_map/dot_general | solution.py:22
  64.2 1.7 collective-permute-start.6
  70.3 1.7 collective-permute-start.7
  72.3 5.9 %collective-permute-done.6.g_far = bf16[512,512]{1,0:T(8,128)(2,1)S(1)} collective-permute-done((bf16[512,512]{1,0:T(8,128)(2,1)S(1)}, bf16[512,512]{1,0:T(8,128)(2,1)S(1)}, u32[]{:S(2)}, u32[]{:S(2)}) %collective-permute-start.6) | collective-permute-done | bytes 524320 | tf_op jit(solution)/shard_map/ppermute | solution.py:18
  79.4 4.3 %collective-permute-done.7 = bf16[128,2048]{1,0:T(8,128)(2,1)} collective-permute-done((bf16[128,2048]{1,0:T(8,128)(2,1)}, bf16[128,2048]{1,0:T(8,128)(2,1)}, u32[]{:S(2)}, u32[]{:S(2)}) %collective-permute-start.7) | collective-permute-done | bytes 524320 | tf_op jit(solution)/shard_map/ppermute | solution.py:18
  85.3 1.8 collective-permute-start.9
  89.0 6.6 %fusion.77 = f32[512,1408]{1,0:T(8,128)S(1)} fusion(bf16[512,2048]{1,0:T(8,128)(2,1)S(1)} %constant_dynamic-update-slice_fusion.2.x, bf16[2048,1408]{1,0:T(8,128)(2,1)} %param.21), kind=kOutput, calls=%fused_computation.206 | convolution fusion | flops 2952790016 | bytes 10747904 | tf_op jit(solution)/shard_map/dot_general | solution.py:22
  95.7 6.0 %multiply_convert_fusion.1 = (bf16[512,1408]{1,0:T(8,128)(2,1)S(1)}, bf16[512,1408]{1,0:T(8,128)(2,1)}, bf16[512,1408]{1,0:T(8,128)(2,1)}) fusion(f32[512,1408]{1,0:T(8,128)S(1)} %copy-done.72, f32[512,1408]{1,0:T(8,128)S(1)} %fusion.77, bf16[512,2048]{1,0:T(8,128)(2,1)S(1)} %constant_dynamic-update-slice_fusion.2.x, bf16[2048,1408]{1,0:T(8,128)(2,1)S(1)} %bitcast.86), kind=kOutput, calls=%fused_computation.6 | convolution fusion | flops 2963603456 | bytes 17956864 | tf_op jit(solution)/shard_map/dot_general | solution.py:22
  101.7 2.9 fusion.23
  104.7 6.3 %collective-permute-done.9.x_far = bf16[512,1024]{1,0:T(8,128)(2,1)S(1)} collective-permute-done((bf16[512,1024]{1,0:T(8,128)(2,1)S(1)}, bf16[512,1024]{1,0:T(8,128)(2,1)S(1)}, u32[]{:S(2)}, u32[]{:S(2)}) %collective-permute-start.9) | collective-permute-done | bytes 1048608 | tf_op jit(solution)/shard_map/ppermute | solution.py:18
  111.9 1.8 fusion.4
  113.8 3.1 fusion.21
  116.9 1.7 collective-permute-start.15
  119.0 1.7 collective-permute-start.17
  120.8 1.8 convolution_add_fusion.2
  124.7 7.0 %row_terms.1 = (bf16[256,2048]{1,0:T(8,128)(2,1)S(1)}, f32[256,2048]{1,0:T(8,128)S(1)}) custom-call(bf16[512,1408]{1,0:T(8,128)(2,1)} %get-tuple-element.116.left.g, bf16[1408,2048]{1,0:T(8,128)(2,1)S(1)} %bitcast.63), custom_call_target="tpu_custom_call" | custom-call | flops 11811160064 | bytes 5767168 | tf_op jit(solution)/shard_map/row_terms/pallas_call | solution.py:357
  131.9 5.3 %collective-permute-done.12 = bf16[128,2048]{1,0:T(8,128)(2,1)S(1)} collective-permute-done((bf16[128,2048]{1,0:T(8,128)(2,1)S(1)}, bf16[128,2048]{1,0:T(8,128)(2,1)S(1)}, u32[]{:S(2)}, u32[]{:S(2)}) %collective-permute-start.12) | collective-permute-done | bytes 524320 | tf_op jit(solution)/shard_map/ppermute | solution.py:18
  137.6 2.6 fusion.69
  141.7 9.7 %collective-permute-done.15.g_far = bf16[512,1408]{1,0:T(8,128)(2,1)S(1)} collective-permute-done((bf16[512,1408]{1,0:T(8,128)(2,1)S(1)}, bf16[512,1408]{1,0:T(8,128)(2,1)S(1)}, u32[]{:S(2)}, u32[]{:S(2)}) %collective-permute-start.15) | collective-permute-done | bytes 1441824 | tf_op jit(solution)/shard_map/ppermute | solution.py:18
  151.4 5.9 %weight_terms.13 = bf16[1024,1408]{1,0:T(8,128)(2,1)} custom-call(s32[8]{0:T(128)S(1)} %stack.131.places, bf16[512,2048]{1,0:T(8,128)(2,1)S(1)} %constant_dynamic-update-slice_fusion.2.x, bf16[512,1024]{1,0:T(8,128)(2,1)S(1)} %constant_dynamic-update-slice_fusion.4.x_far, bf16[512,1408]{1,0:T(8,128)(2,1)S(1)} %get-tuple-element.79.g, ...), custom_call_target="tpu_custom_call" | custom-call | flops 17716740096 | bytes 2883584 | tf_op jit(solution)/shard_map/weight_terms/pallas_call | solution.py:325
  160.3 4.7 %weight_terms.14 = bf16[512,1408]{1,0:T(8,128)(2,1)S(1)} custom-call(s32[4]{0:T(128)S(1)} %pad_add_fusion.1.places, bf16[512,2048]{1,0:T(8,128)(2,1)S(1)} %copy-done.6, bf16[512,1024]{1,0:T(8,128)(2,1)S(1)} %copy-done.31, bf16[512,1408]{1,0:T(8,128)(2,1)} %get-tuple-element.116.left.g, bf16[512,1408]{1,0:T(8,128)(2,1)} %collective-permute-done.17.g_far), custom_call_target="tpu_custom_call" | custom-call | flops 8858370048 | bytes 2883584 | tf_op jit(solution)/shard_map/weight_terms/pallas_call | solution.py:325
  166.0 1.7 collective-permute-start.21
  167.9 2.1 fusion.9.do_in
  169.9 8.7 %attention_backward.1 = (bf16[512,512]{1,0:T(8,128)(2,1)S(1)}, f32[128,512]{1,0:T(8,128)S(1)}, bf16[128,512]{1,0:T(8,128)(2,1)S(1)}, bf16[128,512]{1,0:T(8,128)(2,1)S(1)}, bf16[128,512]{1,0:T(8,128)(2,1)S(1)}) custom-call(s32[2]{0:T(128)S(1)} %pad_add_fusion.at_ref, s32[1,512]{1,0:T(1,128)S(1)} %bitcast.59, bf16[512,512]{1,0:T(8,128)(2,1)} %bitcast.57, ...), custom_call_target="tpu_custom_call" | custom-call | flops 25769803776 | bytes 2621440 | tf_op jit(solution)/shard_map/attention_backward/pallas_call | solution.py:249
  180.8 20.1 %collective-permute-start.24 = (bf16[128,512]{1,0:T(8,128)(2,1)S(1)}, bf16[128,512]{1,0:T(8,128)(2,1)S(1)}, u32[]{:S(2)}, u32[]{:S(2)}) collective-permute-start(bf16[128,512]{1,0:T(8,128)(2,1)S(1)} %get-tuple-element.102), channel_id=1, source_target_pairs={{0,12},{4,8},{8,4},{12,0},{16,28},{20,24},{24,20},{28,16},{1,13},{... | collective-permute-start | bytes 393224 | tf_op jit(solution)/shard_map/ppermute | solution.py:18
  200.8 3.4 weight_terms.16
  206.0 2.6 collective-permute-start.29
  208.6 4.7 %weight_terms.15 = bf16[512,1408]{1,0:T(8,128)(2,1)S(1)} custom-call(s32[4]{0:T(128)S(1)} %pad_add_fusion.2.places, bf16[512,2048]{1,0:T(8,128)(2,1)S(1)} %copy-done.14, bf16[512,1024]{1,0:T(8,128)(2,1)S(1)} %constant_dynamic-update-slice_fusion.4.x_far, bf16[512,1408]{1,0:T(8,128)(2,1)} %get-tuple-element.110.g, bf16[512,1408]{1,0:T(8,128)(2,1)} %collective-permute-done.20.g_far), custom_call_target="tpu_custom_call" | custom-call | flops 8858370048 | bytes 2883584 | tf_op jit(solution)/shard_map/weight_terms/pallas_call | solution.py:325
  213.3 2.9 collective-permute-done.23
  220.5 9.0 %collective-permute-start.26 = (bf16[256,1024]{1,0:T(8,128)(2,1)S(1)}, bf16[256,1024]{1,0:T(8,128)(2,1)S(1)}, u32[]{:S(2)}, u32[]{:S(2)}) collective-permute-start(bf16[256,1024]{1,0:T(8,128)(2,1)S(1)} %pad_maximum_fusion.8), channel_id=1, source_target_pairs={{0,4},{4,0},{8,12},{12,8},{16,20},{20,16},{24,28},{28,24},{1,5},{5... | collective-permute-start | bytes 1572872 | tf_op jit(solution)/shard_map/ppermute | solution.py:18
  230.7 11.1 %collective-permute-done.26 = bf16[256,1024]{1,0:T(8,128)(2,1)S(1)} collective-permute-done((bf16[256,1024]{1,0:T(8,128)(2,1)S(1)}, bf16[256,1024]{1,0:T(8,128)(2,1)S(1)}, u32[]{:S(2)}, u32[]{:S(2)}) %collective-permute-start.26) | collective-permute-done | bytes 524320 | tf_op jit(solution)/shard_map/ppermute | solution.py:18
  241.8 1.7 collective-permute-start.34
  247.3 3.4 weight_terms.17
  252.5 2.5 convert_element_type.196
  255.0 4.6 %collective-permute-done.28 = bf16[128,2048]{1,0:T(8,128)(2,1)} collective-permute-done((bf16[128,2048]{1,0:T(8,128)(2,1)}, bf16[128,2048]{1,0:T(8,128)(2,1)}, u32[]{:S(2)}, u32[]{:S(2)}) %collective-permute-start.28) | collective-permute-done | bytes 524320 | tf_op jit(solution)/shard_map/ppermute | solution.py:18
  259.6 1.7 fusion.17
  261.4 2.6 fusion.14
  263.9 3.4 weight_terms.19
  268.8 2.3 collective-permute-start.35
  271.2 3.1 weight_terms.20
  274.4 1.8 collective-permute-start.32
  276.2 2.0 weight_terms.21
  278.4 1.8 collective-permute-start.33
  280.2 1.8 collective-permute-done.33
  283.6 2.1 weight_terms.22
  285.8 2.4 weight_terms.24
  288.2 3.4 weight_terms.25
  291.6 19.5 %collective-permute-done.36 = bf16[272,1152]{1,0:T(8,128)(2,1)S(1)} collective-permute-done((bf16[272,1152]{1,0:T(8,128)(2,1)S(1)}, bf16[272,1152]{1,0:T(8,128)(2,1)S(1)}, u32[]{:S(2)}, u32[]{:S(2)}) %collective-permute-start.36) | collective-permute-done | bytes 626720 | tf_op jit(solution)/shard_map/ppermute | solution.py:18
  311.5 2.1 collective-permute-start.37
  313.6 3.2 collective-permute-start.40
  316.8 21.9 %collective-permute-done.38 = bf16[272,1152]{1,0:T(8,128)(2,1)S(1)} collective-permute-done((bf16[272,1152]{1,0:T(8,128)(2,1)S(1)}, bf16[272,1152]{1,0:T(8,128)(2,1)S(1)}, u32[]{:S(2)}, u32[]{:S(2)}) %collective-permute-start.38) | collective-permute-done | bytes 626720 | tf_op jit(solution)/shard_map/ppermute | solution.py:18
  338.7 3.2 collective-permute-done.37
  344.6 2.1 slice_bitcast_fusion
  348.9 2.4 add_bitcast_fusion
  351.3 3.0 copy.27
  354.4 2.4 convert_add_fusion.5
  (322 shorter events, 61.1 us)
Async XLA Ops:
  7.2 39.5 %copy-start = (bf16[512,2048]{1,0:T(8,128)(2,1)S(1)}, bf16[512,2048]{1,0:T(8,128)(2,1)}, u32[]{:S(2)}) copy-start(bf16[512,2048]{1,0:T(8,128)(2,1)} %param.18) | copy-start | bytes 6291460
  7.2 245.3 %reduce-scatter.2.cloned.1.call-start = ((), (), s32[]{:S(2)}) async-start(), calls=%async_computation.1 | async-start | bytes 3604480 | tf_op jit(solution)/shard_map/reduce_scatter | solution.py:303
  7.3 15.3 %copy-start.70 = (f32[32]{0:T(128)}, f32[32]{0:T(128)S(1)}, u32[]{:S(2)}) copy-start(f32[32]{0:T(128)S(1)} %multiply_exponential_fusion) | copy-start | bytes 388
  13.2 9.4 %copy-start.68 = (f32[512]{0:T(512)}, f32[512]{0:T(512)S(1)}, u32[]{:S(2)}) copy-start(f32[512]{0:T(512)S(1)} %convert_element_type.168) | copy-start | bytes 6148
  13.5 11.9 %copy-start.28 = (bf16[128,512]{1,0:T(8,128)(2,1)}, bf16[128,512]{1,0:T(8,128)(2,1)S(1)}, u32[]{:S(2)}) copy-start(bf16[128,512]{1,0:T(8,128)(2,1)S(1)} %pad_maximum_fusion.12.kv0) | copy-start | bytes 393220
  13.6 11.1 %collective-permute-start = (bf16[128,512]{1,0:T(8,128)(2,1)S(1)}, bf16[128,512]{1,0:T(8,128)(2,1)S(1)}, u32[]{:S(2)}, u32[]{:S(2)}) collective-permute-start(bf16[128,512]{1,0:T(8,128)(2,1)S(1)} %pad_maximum_fusion.12.kv0), channel_id=1, source_target_pairs={{0,4},{4,0},{8,12},{12,8},{16,20},{20,16},{24,28},{28,24},{1,5},{5... | collective-permute-start | bytes 393224 | tf_op jit(solution)/shard_map/ppermute | solution.py:18
  16.6 8.1 %collective-permute-start.1 = (bf16[128,512]{1,0:T(8,128)(2,1)S(1)}, bf16[128,512]{1,0:T(8,128)(2,1)S(1)}, u32[]{:S(2)}, u32[]{:S(2)}) collective-permute-start(bf16[128,512]{1,0:T(8,128)(2,1)S(1)} %pad_maximum_fusion.12.kv0), channel_id=1, source_target_pairs={{0,8},{4,12},{8,0},{12,4},{16,24},{20,28},{24,16},{28,20},{1,9},{5... | collective-permute-start | bytes 393224 | tf_op jit(solution)/shard_map/ppermute | solution.py:18
  18.1 6.5 %collective-permute-start.2 = (bf16[128,512]{1,0:T(8,128)(2,1)S(1)}, bf16[128,512]{1,0:T(8,128)(2,1)S(1)}, u32[]{:S(2)}, u32[]{:S(2)}) collective-permute-start(bf16[128,512]{1,0:T(8,128)(2,1)S(1)} %pad_maximum_fusion.12.kv0), channel_id=1, source_target_pairs={{0,12},{4,8},{8,4},{12,0},{16,28},{20,24},{24,20},{28,16},{1,13},{... | collective-permute-start | bytes 393224 | tf_op jit(solution)/shard_map/ppermute | solution.py:18
  20.7 26.0 %collective-permute-start.3 = (bf16[512,1024]{1,0:T(8,128)(2,1)}, bf16[512,1024]{1,0:T(8,128)(2,1)}, u32[]{:S(2)}, u32[]{:S(2)}) collective-permute-start(bf16[512,1024]{1,0:T(8,128)(2,1)} %pad_maximum_fusion.1), channel_id=1, source_target_pairs={{0,4},{4,0},{8,12},{12,8},{16,20},{20,16},{24,28},{28,24},{1,5},{5... | collective-permute-start | bytes 3145736 | tf_op jit(solution)/shard_map/ppermute | solution.py:18
  24.6 9.0 %copy-start.12 = (bf16[8,2,32,512]{3,2,1,0:T(8,128)(2,1)}, bf16[8,2,32,512]{3,2,1,0:T(8,128)(2,1)S(1)}, u32[]{:S(2)}) copy-start(bf16[8,2,32,512]{3,2,1,0:T(8,128)(2,1)S(1)} %fusion.20) | copy-start | bytes 1572868
  24.7 8.9 %copy-start.37 = (bf16[128,512]{1,0:T(8,128)(2,1)}, bf16[128,512]{1,0:T(8,128)(2,1)S(1)}, u32[]{:S(2)}) copy-start(bf16[128,512]{1,0:T(8,128)(2,1)S(1)} %collective-permute-done.kv1) | copy-start | bytes 393220
  24.7 8.9 %copy-start.38 = (bf16[128,512]{1,0:T(8,128)(2,1)}, bf16[128,512]{1,0:T(8,128)(2,1)S(1)}, u32[]{:S(2)}) copy-start(bf16[128,512]{1,0:T(8,128)(2,1)S(1)} %collective-permute-done.1.kv2) | copy-start | bytes 393220
  34.2 30.0 %copy-start.18 = (bf16[512,512]{1,0:T(8,128)(2,1)}, bf16[512,512]{1,0:T(8,128)(2,1)S(1)}, u32[]{:S(2)}) copy-start(bf16[512,512]{1,0:T(8,128)(2,1)S(1)} %get-tuple-element.115.o_in.g) | copy-start | bytes 1572868
  48.4 3.0 collective-permute-start.4
  53.0 14.0 %collective-permute-start.5 = (bf16[128,2048]{1,0:T(8,128)(2,1)S(1)}, bf16[128,2048]{1,0:T(8,128)(2,1)S(1)}, u32[]{:S(2)}, u32[]{:S(2)}) collective-permute-start(bf16[128,2048]{1,0:T(8,128)(2,1)S(1)} %slice.333), channel_id=1, source_target_pairs={{0,2},{1,3},{2,0},{3,1},{4,6},{5,7},{6,4},{7,5},{8,10},{9,11},{10,... | collective-permute-start | bytes 1572872 | tf_op jit(solution)/shard_map/ppermute | solution.py:18
  64.2 14.0 %collective-permute-start.6 = (bf16[512,512]{1,0:T(8,128)(2,1)S(1)}, bf16[512,512]{1,0:T(8,128)(2,1)S(1)}, u32[]{:S(2)}, u32[]{:S(2)}) collective-permute-start(bf16[512,512]{1,0:T(8,128)(2,1)S(1)} %get-tuple-element.115.o_in.g), channel_id=1, source_target_pairs={{0,4},{4,0},{8,12},{12,8},{16,20},{20,16},{24,28},{28,24},{1,5},{5... | collective-permute-start | bytes 1572872 | tf_op jit(solution)/shard_map/ppermute | solution.py:18
  70.3 13.5 %collective-permute-start.7 = (bf16[128,2048]{1,0:T(8,128)(2,1)}, bf16[128,2048]{1,0:T(8,128)(2,1)}, u32[]{:S(2)}, u32[]{:S(2)}) collective-permute-start(bf16[128,2048]{1,0:T(8,128)(2,1)} %multiply_convert_fusion.3), channel_id=1, source_target_pairs={{0,2},{1,3},{2,0},{3,1},{4,6},{5,7},{6,4},{7,5},{8,10},{9,11},{10,... | collective-permute-start | bytes 1572872 | tf_op jit(solution)/shard_map/ppermute | solution.py:18
  72.2 13.1 %copy-start.58 = (bf16[512,1024]{1,0:T(8,128)(2,1)S(1)}, bf16[512,1024]{1,0:T(8,128)(2,1)}, u32[]{:S(2)}) copy-start(bf16[512,1024]{1,0:T(8,128)(2,1)} %pad_maximum_fusion.2) | copy-start | bytes 3145732
  84.9 4.0 %collective-permute-start.8 = (bf16[256,2048]{1,0:T(8,128)(2,1)S(1)}, bf16[256,2048]{1,0:T(8,128)(2,1)S(1)}, u32[]{:S(2)}, u32[]{:S(2)}) collective-permute-start(bf16[256,2048]{1,0:T(8,128)(2,1)S(1)} %constant_dynamic-update-slice_fusion), channel_id=1, source_target_pairs={{0,1},{1,0},{2,3},{3,2},{4,5},{5,4},{6,7},{7,6},{8,9},{9,8},{10,11... | collective-permute-start | bytes 3145736 | tf_op jit(solution)/shard_map/ppermute | solution.py:18
  85.3 25.6 %collective-permute-start.9 = (bf16[512,1024]{1,0:T(8,128)(2,1)S(1)}, bf16[512,1024]{1,0:T(8,128)(2,1)S(1)}, u32[]{:S(2)}, u32[]{:S(2)}) collective-permute-start(bf16[512,1024]{1,0:T(8,128)(2,1)S(1)} %copy-done.58), channel_id=1, source_target_pairs={{0,8},{4,12},{8,0},{12,4},{16,24},{20,28},{24,16},{28,20},{1,9},{5... | collective-permute-start | bytes 3145736 | tf_op jit(solution)/shard_map/ppermute | solution.py:18
  87.2 24.7 %collective-permute-start.10 = (bf16[256,1024]{1,0:T(8,128)(2,1)S(1)}, bf16[256,1024]{1,0:T(8,128)(2,1)S(1)}, u32[]{:S(2)}, u32[]{:S(2)}) collective-permute-start(bf16[256,1024]{1,0:T(8,128)(2,1)S(1)} %pad_maximum_fusion.7), channel_id=1, source_target_pairs={{0,4},{4,0},{8,12},{12,8},{16,20},{20,16},{24,28},{28,24},{1,5},{5... | collective-permute-start | bytes 1572872 | tf_op jit(solution)/shard_map/ppermute | solution.py:18
  89.0 62.4 %copy-start.13 = (bf16[512,2048]{1,0:T(8,128)(2,1)}, bf16[512,2048]{1,0:T(8,128)(2,1)S(1)}, u32[]{:S(2)}) copy-start(bf16[512,2048]{1,0:T(8,128)(2,1)S(1)} %constant_dynamic-update-slice_fusion.2.x) | copy-start | bytes 6291460
  89.0 12.7 %slice-start.5 = ((s8[5767168]{0:T(1024)(128)(4,1)}), s8[4194304]{0:T(1024)(128)(4,1)S(1)}, s32[]{:S(2)}) async-start(s8[5767168]{0:T(1024)(128)(4,1)} %bitcast.83), calls=%async_computation.7 | async-start | bytes 8388608
  113.7 9.0 %collective-permute-start.11 = (bf16[256,2048]{1,0:T(8,128)(2,1)S(1)}, bf16[256,2048]{1,0:T(8,128)(2,1)S(1)}, u32[]{:S(2)}, u32[]{:S(2)}) collective-permute-start(bf16[256,2048]{1,0:T(8,128)(2,1)S(1)} %fusion.4), channel_id=1, source_target_pairs={{0,1},{1,0},{2,3},{3,2},{4,5},{5,4},{6,7},{7,6},{8,9},{9,8},{10,11... | collective-permute-start | bytes 3145736 | tf_op jit(solution)/shard_map/ppermute | solution.py:18
  113.8 10.9 %slice-start.2 = ((s8[5767168]{0:T(1024)(128)(4,1)}), s8[4194304]{0:T(1024)(128)(4,1)S(1)}, s32[]{:S(2)}) async-start(s8[5767168]{0:T(1024)(128)(4,1)} %bitcast.62), calls=%async_computation.4 | async-start | bytes 8388608
  116.9 34.4 %collective-permute-start.15 = (bf16[512,1408]{1,0:T(8,128)(2,1)S(1)}, bf16[512,1408]{1,0:T(8,128)(2,1)S(1)}, u32[]{:S(2)}, u32[]{:S(2)}) collective-permute-start(bf16[512,1408]{1,0:T(8,128)(2,1)S(1)} %get-tuple-element.79.g), channel_id=1, source_target_pairs={{0,4},{4,0},{8,12},{12,8},{16,20},{20,16},{24,28},{28,24},{1,5},{5... | collective-permute-start | bytes 4325384 | tf_op jit(solution)/shard_map/ppermute | solution.py:18
  118.6 87.3 %collective-permute-start.20 = (bf16[512,1408]{1,0:T(8,128)(2,1)}, bf16[512,1408]{1,0:T(8,128)(2,1)}, u32[]{:S(2)}, u32[]{:S(2)}) collective-permute-start(bf16[512,1408]{1,0:T(8,128)(2,1)} %get-tuple-element.110.g), channel_id=1, source_target_pairs={{0,4},{4,0},{8,12},{12,8},{16,20},{20,16},{24,28},{28,24},{1,5},{5... | collective-permute-start | bytes 4325384 | tf_op jit(solution)/shard_map/ppermute | solution.py:18
  119.0 3.6 collective-permute-start.14
  119.0 41.2 %collective-permute-start.17 = (bf16[512,1408]{1,0:T(8,128)(2,1)}, bf16[512,1408]{1,0:T(8,128)(2,1)}, u32[]{:S(2)}, u32[]{:S(2)}) collective-permute-start(bf16[512,1408]{1,0:T(8,128)(2,1)} %get-tuple-element.116.left.g), channel_id=1, source_target_pairs={{0,8},{4,12},{8,0},{12,4},{16,24},{20,28},{24,16},{28,20},{1,9},{5... | collective-permute-start | bytes 4325384 | tf_op jit(solution)/shard_map/ppermute | solution.py:18
  122.7 85.9 %copy-start.25 = (bf16[512,1024]{1,0:T(8,128)(2,1)}, bf16[512,1024]{1,0:T(8,128)(2,1)S(1)}, u32[]{:S(2)}) copy-start(bf16[512,1024]{1,0:T(8,128)(2,1)S(1)} %constant_dynamic-update-slice_fusion.4.x_far) | copy-start | bytes 3145732
  123.1 14.1 %collective-permute-start.12 = (bf16[128,2048]{1,0:T(8,128)(2,1)S(1)}, bf16[128,2048]{1,0:T(8,128)(2,1)S(1)}, u32[]{:S(2)}, u32[]{:S(2)}) collective-permute-start(bf16[128,2048]{1,0:T(8,128)(2,1)S(1)} %slice.332), channel_id=1, source_target_pairs={{0,2},{1,3},{2,0},{3,1},{4,6},{5,7},{6,4},{7,5},{8,10},{9,11},{10,... | collective-permute-start | bytes 1572872 | tf_op jit(solution)/shard_map/ppermute | solution.py:18
  140.2 18.4 %collective-permute-start.16 = (bf16[128,2048]{1,0:T(8,128)(2,1)}, bf16[128,2048]{1,0:T(8,128)(2,1)}, u32[]{:S(2)}, u32[]{:S(2)}) collective-permute-start(bf16[128,2048]{1,0:T(8,128)(2,1)} %get-tuple-element.89), channel_id=1, source_target_pairs={{0,2},{1,3},{2,0},{3,1},{4,6},{5,7},{6,4},{7,5},{8,10},{9,11},{10,... | collective-permute-start | bytes 1572872 | tf_op jit(solution)/shard_map/ppermute | solution.py:18
  157.3 21.4 %collective-permute-start.13 = (bf16[256,2048]{1,0:T(8,128)(2,1)}, bf16[256,2048]{1,0:T(8,128)(2,1)S(1)}, u32[]{:S(2)}, u32[]{:S(2)}) collective-permute-start(bf16[256,2048]{1,0:T(8,128)(2,1)} %copy-done.33), channel_id=1, source_target_pairs={{0,1},{1,0},{2,3},{3,2},{4,5},{5,4},{6,7},{7,6},{8,9},{9,8},{10,11... | collective-permute-start | bytes 3145736 | tf_op jit(solution)/shard_map/ppermute | solution.py:18
  159.7 8.0 %collective-permute-start.18 = (bf16[256,2048]{1,0:T(8,128)(2,1)S(1)}, bf16[256,2048]{1,0:T(8,128)(2,1)S(1)}, u32[]{:S(2)}, u32[]{:S(2)}) collective-permute-start(bf16[256,2048]{1,0:T(8,128)(2,1)S(1)} %constant_dynamic-update-slice_fusion.6), channel_id=1, source_target_pairs={{0,1},{1,0},{2,3},{3,2},{4,5},{5,4},{6,7},{7,6},{8,9},{9,8},{10,11... | collective-permute-start | bytes 3145736 | tf_op jit(solution)/shard_map/ppermute | solution.py:18
  166.0 38.2 %collective-permute-start.21 = (bf16[256,1408]{1,0:T(8,128)(2,1)S(1)}, bf16[256,1408]{1,0:T(8,128)(2,1)S(1)}, u32[]{:S(2)}, u32[]{:S(2)}) collective-permute-start(bf16[256,1408]{1,0:T(8,128)(2,1)S(1)} %get-tuple-element.160), channel_id=1, source_target_pairs={{0,4},{4,0},{8,12},{12,8},{16,20},{20,16},{24,28},{28,24},{1,5},{5... | collective-permute-start | bytes 2162696 | tf_op jit(solution)/shard_map/ppermute | solution.py:18
  167.9 82.9 %copy-start.16 = (bf16[512,2048]{1,0:T(8,128)(2,1)}, bf16[512,2048]{1,0:T(8,128)(2,1)S(1)}, u32[]{:S(2)}) copy-start(bf16[512,2048]{1,0:T(8,128)(2,1)S(1)} %constant_dynamic-update-slice_fusion.8.x) | copy-start | bytes 6291460
  179.2 65.8 %collective-permute-start.19 = (bf16[128,2048]{1,0:T(8,128)(2,1)S(1)}, bf16[128,2048]{1,0:T(8,128)(2,1)S(1)}, u32[]{:S(2)}, u32[]{:S(2)}) collective-permute-start(bf16[128,2048]{1,0:T(8,128)(2,1)S(1)} %slice.331), channel_id=1, source_target_pairs={{0,2},{1,3},{2,0},{3,1},{4,6},{5,7},{6,4},{7,5},{8,10},{9,11},{10,... | collective-permute-start | bytes 1572872 | tf_op jit(solution)/shard_map/ppermute | solution.py:18
  180.8 32.6 %collective-permute-start.24 = (bf16[128,512]{1,0:T(8,128)(2,1)S(1)}, bf16[128,512]{1,0:T(8,128)(2,1)S(1)}, u32[]{:S(2)}, u32[]{:S(2)}) collective-permute-start(bf16[128,512]{1,0:T(8,128)(2,1)S(1)} %get-tuple-element.102), channel_id=1, source_target_pairs={{0,12},{4,8},{8,4},{12,0},{16,28},{20,24},{24,20},{28,16},{1,13},{... | collective-permute-start | bytes 393224 | tf_op jit(solution)/shard_map/ppermute | solution.py:18
  200.8 15.4 %collective-permute-start.23 = (bf16[128,512]{1,0:T(8,128)(2,1)S(1)}, bf16[128,512]{1,0:T(8,128)(2,1)S(1)}, u32[]{:S(2)}, u32[]{:S(2)}) collective-permute-start(bf16[128,512]{1,0:T(8,128)(2,1)S(1)} %get-tuple-element.101), channel_id=1, source_target_pairs={{0,8},{4,12},{8,0},{12,4},{16,24},{20,28},{24,16},{28,20},{1,9},{5... | collective-permute-start | bytes 393224 | tf_op jit(solution)/shard_map/ppermute | solution.py:18
  204.2 12.0 %collective-permute-start.22 = (bf16[128,512]{1,0:T(8,128)(2,1)S(1)}, bf16[128,512]{1,0:T(8,128)(2,1)S(1)}, u32[]{:S(2)}, u32[]{:S(2)}) collective-permute-start(bf16[128,512]{1,0:T(8,128)(2,1)S(1)} %get-tuple-element.100), channel_id=1, source_target_pairs={{0,4},{4,0},{8,12},{12,8},{16,20},{20,16},{24,28},{28,24},{1,5},{5... | collective-permute-start | bytes 393224 | tf_op jit(solution)/shard_map/ppermute | solution.py:18
  206.0 10.4 %copy-start.69 = (f32[512]{0:T(512)S(1)}, f32[512]{0:T(512)}, u32[]{:S(2)}) copy-start(f32[512]{0:T(512)} %copy-done.68) | copy-start | bytes 6148
  206.0 10.4 %copy-start.71 = (f32[32]{0:T(128)S(1)}, f32[32]{0:T(128)}, u32[]{:S(2)}) copy-start(f32[32]{0:T(128)} %copy-done.70) | copy-start | bytes 388
  206.0 65.1 %collective-permute-start.29 = (bf16[256,1408]{1,0:T(8,128)(2,1)}, bf16[256,1408]{1,0:T(8,128)(2,1)}, u32[]{:S(2)}, u32[]{:S(2)}) collective-permute-start(bf16[256,1408]{1,0:T(8,128)(2,1)} %add_convert_fusion.1), channel_id=1, source_target_pairs={{0,16},{4,20},{8,24},{12,28},{16,0},{20,4},{24,8},{28,12},{1,17},{... | collective-permute-start | bytes 2162696 | tf_op jit(solution)/shard_map/ppermute | solution.py:18
  219.1 24.5 %collective-permute-start.25 = (bf16[256,2048]{1,0:T(8,128)(2,1)S(1)}, bf16[256,2048]{1,0:T(8,128)(2,1)S(1)}, u32[]{:S(2)}, u32[]{:S(2)}) collective-permute-start(bf16[256,2048]{1,0:T(8,128)(2,1)S(1)} %fusion.5), channel_id=1, source_target_pairs={{0,1},{1,0},{2,3},{3,2},{4,5},{5,4},{6,7},{7,6},{8,9},{9,8},{10,11... | collective-permute-start | bytes 3145736 | tf_op jit(solution)/shard_map/ppermute | solution.py:18
  220.5 46.8 %collective-permute-start.30 = (bf16[256,1408]{1,0:T(8,128)(2,1)}, bf16[256,1408]{1,0:T(8,128)(2,1)}, u32[]{:S(2)}, u32[]{:S(2)}) collective-permute-start(bf16[256,1408]{1,0:T(8,128)(2,1)} %get-tuple-element.162), channel_id=1, source_target_pairs={{0,8},{4,12},{8,0},{12,4},{16,24},{20,28},{24,16},{28,20},{1,9},{5... | collective-permute-start | bytes 2162696 | tf_op jit(solution)/shard_map/ppermute | solution.py:18
  220.5 21.4 %collective-permute-start.26 = (bf16[256,1024]{1,0:T(8,128)(2,1)S(1)}, bf16[256,1024]{1,0:T(8,128)(2,1)S(1)}, u32[]{:S(2)}, u32[]{:S(2)}) collective-permute-start(bf16[256,1024]{1,0:T(8,128)(2,1)S(1)} %pad_maximum_fusion.8), channel_id=1, source_target_pairs={{0,4},{4,0},{8,12},{12,8},{16,20},{20,16},{24,28},{28,24},{1,5},{5... | collective-permute-start | bytes 1572872 | tf_op jit(solution)/shard_map/ppermute | solution.py:18
  241.8 29.4 %collective-permute-start.34 = (bf16[640,512]{1,0:T(8,128)(2,1)S(1)}, bf16[640,512]{1,0:T(8,128)(2,1)S(1)}, u32[]{:S(2)}, u32[]{:S(2)}) collective-permute-start(bf16[640,512]{1,0:T(8,128)(2,1)S(1)} %pad_maximum_fusion.3.g), channel_id=1, source_target_pairs={{0,4},{4,0},{8,12},{12,8},{16,20},{20,16},{24,28},{28,24},{1,5},{5... | collective-permute-start | bytes 1966088 | tf_op jit(solution)/shard_map/ppermute | solution.py:18
  243.6 7.0 %collective-permute-start.27 = (bf16[256,1024]{1,0:T(8,128)(2,1)S(1)}, bf16[256,1024]{1,0:T(8,128)(2,1)S(1)}, u32[]{:S(2)}, u32[]{:S(2)}) collective-permute-start(bf16[256,1024]{1,0:T(8,128)(2,1)S(1)} %collective-permute-done.26), channel_id=1, source_target_pairs={{0,1},{1,0},{2,3},{3,2},{4,5},{5,4},{6,7},{7,6},{8,9},{9,8},{10,11... | collective-permute-start | bytes 1572872 | tf_op jit(solution)/shard_map/ppermute | solution.py:18
  245.0 14.6 %collective-permute-start.28 = (bf16[128,2048]{1,0:T(8,128)(2,1)}, bf16[128,2048]{1,0:T(8,128)(2,1)}, u32[]{:S(2)}, u32[]{:S(2)}) collective-permute-start(bf16[128,2048]{1,0:T(8,128)(2,1)} %slice.330), channel_id=1, source_target_pairs={{0,2},{1,3},{2,0},{3,1},{4,6},{5,7},{6,4},{7,5},{8,10},{9,11},{10,... | collective-permute-start | bytes 1572872 | tf_op jit(solution)/shard_map/ppermute | solution.py:18
  252.5 8.8 %copy-start.47 = (f32[128,2048]{1,0:T(8,128)S(1)}, f32[128,2048]{1,0:T(8,128)}, u32[]{:S(2)}) copy-start(f32[128,2048]{1,0:T(8,128)} %slice.238) | copy-start | bytes 3145732
  252.5 8.8 %copy-start.52 = (f32[128,2048]{1,0:T(8,128)S(1)}, f32[128,2048]{1,0:T(8,128)}, u32[]{:S(2)}) copy-start(f32[128,2048]{1,0:T(8,128)} %get-tuple-element.141) | copy-start | bytes 3145732
  268.8 42.4 %collective-permute-start.35 = (bf16[256,1408]{1,0:T(8,128)(2,1)S(1)}, bf16[256,1408]{1,0:T(8,128)(2,1)S(1)}, u32[]{:S(2)}, u32[]{:S(2)}) collective-permute-start(bf16[256,1408]{1,0:T(8,128)(2,1)S(1)} %add_convert_fusion), channel_id=1, source_target_pairs={{0,16},{4,20},{8,24},{12,28},{16,0},{20,4},{24,8},{28,12},{1,17},{... | collective-permute-start | bytes 2162696 | tf_op jit(solution)/shard_map/ppermute | solution.py:18
  271.1 3.3 collective-permute-start.31
  274.4 3.8 %collective-permute-start.32 = (f32[2,2048]{1,0:T(2,128)S(1)}, f32[2,2048]{1,0:T(2,128)S(1)}, u32[]{:S(2)}, u32[]{:S(2)}) collective-permute-start(f32[2,2048]{1,0:T(2,128)S(1)} %fusion.67), channel_id=1, source_target_pairs={{0,2},{1,3},{2,0},{3,1},{4,6},{5,7},{6,4},{7,5},{8,10},{9,11},{10,... | collective-permute-start | bytes 49160 | tf_op jit(solution)/shard_map/ppermute | solution.py:18
  278.4 3.7 %collective-permute-start.33 = (f32[2,1024]{1,0:T(2,128)S(1)}, f32[2,1024]{1,0:T(2,128)S(1)}, u32[]{:S(2)}, u32[]{:S(2)}) collective-permute-start(f32[2,1024]{1,0:T(2,128)S(1)} %pad_maximum_fusion.20), channel_id=1, source_target_pairs={{0,4},{4,0},{8,12},{12,8},{16,20},{20,16},{24,28},{28,24},{1,5},{5... | collective-permute-start | bytes 24584 | tf_op jit(solution)/shard_map/ppermute | solution.py:18
  282.2 29.0 %collective-permute-start.36 = (bf16[272,1152]{1,0:T(8,128)(2,1)S(1)}, bf16[272,1152]{1,0:T(8,128)(2,1)S(1)}, u32[]{:S(2)}, u32[]{:S(2)}) collective-permute-start(bf16[272,1152]{1,0:T(8,128)(2,1)S(1)} %fusion.27), channel_id=1, source_target_pairs={{0,8},{4,12},{8,0},{12,4},{16,24},{20,28},{24,16},{28,20},{1,9},{5... | collective-permute-start | bytes 1880072 | tf_op jit(solution)/shard_map/ppermute | solution.py:18
  291.6 50.5 %copy-start.10 = (bf16[256,1408]{1,0:T(8,128)(2,1)}, bf16[256,1408]{1,0:T(8,128)(2,1)S(1)}, u32[]{:S(2)}) copy-start(bf16[256,1408]{1,0:T(8,128)(2,1)S(1)} %weight_terms.25) | copy-start | bytes 2162692
  291.6 22.0 %copy-start.61 = (bf16[256,1408]{1,0:T(8,128)(2,1)S(1)}, bf16[256,1408]{1,0:T(8,128)(2,1)}, u32[]{:S(2)}) copy-start(bf16[256,1408]{1,0:T(8,128)(2,1)} %get-tuple-element.121) | copy-start | bytes 2162692
  291.6 50.3 %copy-start.22 = (bf16[256,512]{1,0:T(8,128)(2,1)S(1)}, bf16[256,512]{1,0:T(8,128)(2,1)}, u32[]{:S(2)}) copy-start(bf16[256,512]{1,0:T(8,128)(2,1)} %copy-done.21) | copy-start | bytes 786436
  311.1 31.0 %copy-start.59 = (bf16[256,1408]{1,0:T(8,128)(2,1)}, bf16[256,1408]{1,0:T(8,128)(2,1)S(1)}, u32[]{:S(2)}) copy-start(bf16[256,1408]{1,0:T(8,128)(2,1)S(1)} %collective-permute-done.35) | copy-start | bytes 2162692
  311.4 27.3 %collective-permute-start.38 = (bf16[272,1152]{1,0:T(8,128)(2,1)S(1)}, bf16[272,1152]{1,0:T(8,128)(2,1)S(1)}, u32[]{:S(2)}, u32[]{:S(2)}) collective-permute-start(bf16[272,1152]{1,0:T(8,128)(2,1)S(1)} %fusion.29), channel_id=1, source_target_pairs={{0,16},{4,20},{8,24},{12,28},{16,0},{20,4},{24,8},{28,12},{1,17},{... | collective-permute-start | bytes 1880072 | tf_op jit(solution)/shard_map/ppermute | solution.py:18
  311.5 30.5 %collective-permute-start.37 = (bf16[272,1152]{1,0:T(8,128)(2,1)S(1)}, bf16[272,1152]{1,0:T(8,128)(2,1)S(1)}, u32[]{:S(2)}, u32[]{:S(2)}) collective-permute-start(bf16[272,1152]{1,0:T(8,128)(2,1)S(1)} %fusion.28), channel_id=1, source_target_pairs={{0,8},{4,12},{8,0},{12,4},{16,24},{20,28},{24,16},{28,20},{1,9},{5... | collective-permute-start | bytes 1880072 | tf_op jit(solution)/shard_map/ppermute | solution.py:18
  313.5 40.9 %collective-permute-start.39 = (bf16[256,1408]{1,0:T(8,128)(2,1)}, bf16[256,1408]{1,0:T(8,128)(2,1)}, u32[]{:S(2)}, u32[]{:S(2)}) collective-permute-start(bf16[256,1408]{1,0:T(8,128)(2,1)} %get-tuple-element.119), channel_id=1, source_target_pairs={{0,8},{4,12},{8,0},{12,4},{16,24},{20,28},{24,16},{28,20},{1,9},{5... | collective-permute-start | bytes 2162696 | tf_op jit(solution)/shard_map/ppermute | solution.py:18
  313.6 35.3 %collective-permute-start.40 = (bf16[256,1408]{1,0:T(8,128)(2,1)S(1)}, bf16[256,1408]{1,0:T(8,128)(2,1)S(1)}, u32[]{:S(2)}, u32[]{:S(2)}) collective-permute-start(bf16[256,1408]{1,0:T(8,128)(2,1)S(1)} %copy-done.61), channel_id=1, source_target_pairs={{0,4},{4,0},{8,12},{12,8},{16,20},{20,16},{24,28},{28,24},{1,5},{5... | collective-permute-start | bytes 2162696 | tf_op jit(solution)/shard_map/ppermute | solution.py:18
  (60 other events, 217.5 us)
Sparse Core Ops, SparseCore 0:
  157.4 71.1 reduce-scatter.1

commit v10 on v9

--- a/solution.py
+++ b/solution.py
@@ -344,6 +344,34 @@
     )(jnp.stack([*places, *far_places]).astype(jnp.int32), x, x_far, g, g_far)
 
 
+def copy_kernel(places, source, target):
+    del places
+    target[...] = source[...]
+
+
+def pick_columns(values, places):
+    rows, count = values.shape[0], len(places)
+    blocks = lax.axis_size("dp")
+    size = values.shape[1] // blocks
+    if size % 128:
+        return pick(values, places, blocks, 1)
+    return pl.pallas_call(
+        copy_kernel,
+        out_shape=jax.ShapeDtypeStruct((rows, count * size), values.dtype),
+        grid_spec=pltpu.PrefetchScalarGridSpec(
+            num_scalar_prefetch=1,
+            grid=(count,),
+            in_specs=[pl.BlockSpec((rows, size), lambda i, p: (0, p[i]))],
+            out_specs=pl.BlockSpec((rows, size), lambda i, p: (0, i)),
+        ),
+        compiler_params=pltpu.CompilerParams(vmem_limit_bytes=8 << 20),
+        cost_estimate=pl.CostEstimate(
+            flops=65536 * rows * count * size, bytes_accessed=4 * rows * count * size, transcendentals=0
+        ),
+        name="pick_columns",
+    )(jnp.stack(places).astype(jnp.int32), values)
+
+
 def row_kernel(left, right, send, kept):
     half = left.shape[0] // 2
     send[...] = dot(left[half:, :], right[...], 1, 0).astype(LOW)
@@ -465,7 +493,7 @@
         pair = kept + near
         return pair[:own_rows], pair[own_rows:].astype(LOW)
 
-    one_send = pick(after(normed_one, paired), halves[1], dp, 1)
+    one_send = pick_columns(after(normed_one, paired), halves[1])
     one_theirs = flip(one_send, "dp", 1)
     queries = after(queries, one_send)
     attended, lse = attention_forward(at, pos, queries, blocks, size, 2)
@@ -477,7 +505,7 @@
     branch_far = flip(branch_out, "tp", 2)
     att_theirs = flip(after(attended, branch_out), "dp", 1)
     cot = pick(after(cotangent, branch_out), row_order, len(ROW_MASKS), 0)
-    cot_send = pick(cot, down_places[1], dp, 1)
+    cot_send = pick_columns(cot, down_places[1])
     cot_theirs = flip(cot_send, "dp", 2)
     own_inputs = own(tokens).astype(jnp.float32)
     grad_hidden = dot(after(cot, cot_send), w_down, 1, 1)
@@ -488,7 +516,7 @@
     far_two = flip(own_two, "tp", 2)
     pair_two = jnp.concatenate([after(own_two, att_theirs), far_two], 0)
     core_two = flip(pair_two, "tp", 1)
-    two_send = pick(pair_two, halves[1], dp, 1)
+    two_send = pick_columns(pair_two, halves[1])
     two_near = flip(two_send, "dp", 1)
     normed_two = jnp.concatenate([after(pair_two, two_send), core_two], 0)
 
@@ -534,7 +562,7 @@
     grad_gate = parity_sum(gate_terms, 0)
     grad_pair = jnp.concatenate([after(branch_grad, gate_terms), grad_far], 0)
     grad_core = flip(grad_pair, "tp", 1)
-    branch_send = pick(grad_pair, halves[1], dp, 1)
+    branch_send = pick_columns(grad_pair, halves[1])
 
     def near_flip(terms, bit):
         half = terms.shape[0] // 2
@@ -608,18 +636,17 @@
 
     grad_normed_one, one_out = near_sum(one_terms)
     one_far = flip(one_out, "tp", 2)
-    branch_theirs = jnp.concatenate([branch_near, flip(branch_near, "tp", 1)], 0)
     output_rows = (middle + (down + after(down_far, one_out))).astype(LOW)
     up_kept = up_terms(0, 1, one_out)
-    out_kept = rest_terms(
-        0, 1, branch_all, branch_theirs, after(attended, one_out), att_theirs, True
-    )
     grad_gate = grad_gate.astype(jnp.float32)
-    grad_normed_one = after(grad_normed_one, output_rows, up_kept, out_kept, grad_gate) + one_far
+    grad_normed_one = after(grad_normed_one, output_rows, up_kept, grad_gate) + one_far
     grad_in_norm, gain_one = norm_back(grad_normed_one, own_inputs, own(scale_one), norm1_gain)
     input_rows = grad_middle + grad_in_norm
 
     up_late, up_last = exchange_mid(up_terms, up_first, rest_bits, input_rows)
+    branch_near, down_second = lax.optimization_barrier((branch_near, down_sent[:half], up_last))[:2]
+    branch_theirs = jnp.concatenate([branch_near, flip(branch_near, "tp", 1)], 0)
+    down_second = flip(down_second, "dp", 1)
     gain_one, *down_late = lax.optimization_barrier((gain_one, *down_late, up_last))[:-1]
     gains = jnp.stack([gain_one, gain_two])
     for m in (1, 2):
@@ -657,21 +684,23 @@
     firsts = with_gains(sent[cut:], 3 * quarter, half_count)
     seconds = with_gains(sent[:cut], 2 * quarter, 3 * quarter)
     mids = [split(flip(firsts, "dp", 2), quarter)]
+    last_second = split(flip(after(seconds, firsts), "dp", 2), quarter)
     proj_kept = rest_terms(0, 1, normed_one, one_theirs, after(proj_late, firsts), proj_theirs, True)
+    out_kept = rest_terms(0, 1, branch_all, branch_theirs, after(out_late, firsts), att_theirs, True)
     down_kept = down_terms(0, 1, firsts)
     left = half_count // 2
     for b in rest_bits[1:]:
         count = left // 2
         terms = last_terms(count, left, firsts)
-        terms, *up_late = lax.optimization_barrier((terms, *up_late, proj_kept, down_kept))[:-2]
+        terms, *up_late = lax.optimization_barrier((terms, *up_late, proj_kept, out_kept, down_kept))[
+            :-3
+        ]
         send = with_gains(
             terms, count, left, *((o[-count * block :], g[:, -count * block :]) for o, g in mids)
         )
         mids.append(split(flip(send, "dp", 1 << b), count))
         left = count
-    last_second = split(flip(after(seconds, send), "dp", 2), quarter)
-    up_second, down_second = lax.optimization_barrier((up_sent[:half], down_sent[:half], send))[:2]
-    up_second, down_second = flip(up_second, "dp", 2), flip(down_second, "dp", 1)
+    up_second = flip(after(up_sent[:half], send), "dp", 2)
 
     def ending(kept, *others):
         kept = kept.astype(jnp.float32)
@@ -679,6 +708,8 @@
             kept = kept + other[:block]
         return kept
 
+    down_kept, down_second = lax.optimization_barrier((down_kept, down_second, send))[:2]
+    grad_down = ending(down_kept, down_second, *down_late)
     grad_last = ending(
         jnp.concatenate([proj_kept, out_kept], 1), last_second[0], *(m[0] for m in mids[1:])
     )
@@ -686,7 +717,6 @@
     for _, other in mids[1:]:
         gains = gains + other[:, :block]
     grad_up = ending(up_kept, up_second, *up_late)
-    grad_down = ending(down_kept, down_second, *down_late)
     narrow = wide + 2 * size
 
     return (

time: 369 us -> 348 us (0.943)
  waiting for transfers between devices: 113 us -> 91.2 us
  starting transfers between devices: 72 us -> 61.8 us
  Pallas kernels: 63.4 us -> 69.7 us
  matrix products: 36.5 us -> 41.4 us
    ppermute x41, waiting for transfers between devices: 113 us -> 91.2 us  [flip(): lax.ppermute(block, axis, [(i, i ^ mask) for i in range(lax.axis_size(axi...]
    ppermute x41, starting transfers between devices: 72 us -> 61.8 us  [flip(): lax.ppermute(block, axis, [(i, i ^ mask) for i in range(lax.axis_size(axi...]
    pallas_call x0 -> x4, Pallas kernels: none -> 6.52 us  [pick_columns(): pl.pallas_call(copy_kernel, out_shape=jax.ShapeDtypeStruct((rows, count *...]
    dot_general x16, matrix products: 36.5 us -> 41.4 us  [dot(): lax.dot_general(left, right, (((left_dim,), (right_dim,)), ((), ())), pre...]
    unnamed x172 -> x150, local copies, waits for them, and re-layouts: 19.5 us -> 22.7 us
  transfers between devices with their start and end apart: 42 -> 42, of which waited for: 15 -> 14; matrix products, arithmetic and copies ran while one was open for 21% -> 23% of each run, Pallas kernels for 17% -> 20%
where the time goes in v10:
time: 348 us; the launch traced here: 344 us
  waiting for transfers between devices  91.2 us (26%)
  Pallas kernels  69.7 us (20%)
  starting transfers between devices  61.8 us (18%)
  matrix products  41.4 us (12%)
  local copies, waits for them, and re-layouts  32.3 us (9%)
  other arithmetic  32.2 us (9%)
  between operations  15.7 us (5%)
    ppermute x41, waiting for transfers between devices, flip(): lax.ppermute(block, axis, [(i, i ^ mask) for i in range(lax.axis_size(axi...  91.2 us
    ppermute x41, starting transfers between devices, flip(): lax.ppermute(block, axis, [(i, i ^ mask) for i in range(lax.axis_size(axi...  61.8 us
    dot_general x16, matrix products, dot(): lax.dot_general(left, right, (((left_dim,), (right_dim,)), ((), ())), pre...  41.4 us
    pallas_call x13, Pallas kernels, weight_terms(): pl.pallas_call(functools.partial(terms_kernel, transposed), out_shape=(ja...  40.7 us
    unnamed x150, local copies, waits for them, and re-layouts  22.7 us
    pallas_call x1, Pallas kernels, attention_backward(): pl.pallas_call(functools.partial(backward_kernel, heads, size), out_shape...  8.75 us
    pallas_call x1, Pallas kernels, row_terms(): pl.pallas_call(row_kernel, out_shape=(jax.ShapeDtypeStruct((half, width),...  7.04 us
  transfers between devices with their start and end apart: 42, of which 14 were waited for; matrix products, arithmetic and copies ran while one was open for 23% of the time, Pallas kernels for 20%

profile of v10, /device:TPU:0, one launch (start us, length us, event | category | flops | bytes accessed | tf_op | source)
XLA Modules:
  0.0 344.3 jit_solution(1930330673173571462)
XLA Ops:
  7.3 2.2 fusion
  13.5 4.0 %collective-permute-start.2 = (bf16[128,512]{1,0:T(8,128)(2,1)S(1)}, bf16[128,512]{1,0:T(8,128)(2,1)S(1)}, u32[]{:S(2)}, u32[]{:S(2)}) collective-permute-start(bf16[128,512]{1,0:T(8,128)(2,1)S(1)} %pad_maximum_fusion.8.kv0), channel_id=1, source_target_pairs={{0,12},{4,8},{8,4},{12,0},{16,28},{20,24},{24,20},{28,16},{1,13},{... | collective-permute-start | bytes 393224 | tf_op jit(solution)/shard_map/ppermute | solution.py:18
  18.3 1.6 copy-done.2
  19.9 2.4 pick_columns.4
  22.3 1.8 collective-permute-start.3
  27.9 6.7 %attention_forward.1 = (bf16[512,512]{1,0:T(8,128)(2,1)S(1)}, f32[8,1,512]{2,1,0:T(1,128)S(1)}) custom-call(s32[2]{0:T(128)S(1)} %pad_add_fusion.at_ref, s32[1,512]{1,0:T(1,128)S(1)} %bitcast.65, bf16[512,512]{1,0:T(8,128)(2,1)S(1)} %bitcast.63, bf16[128,512]{1,0:T(8,128)(2,1)S(1)} %pad_maximum_fusion.8.kv0, bf16[128,512]{1,0:T(8,128)(2,1)S(1)} %copy-done.37, ...), custom_call_target="tpu_custom_call" | custom-call | flops 17179869184 | bytes 1048576 | tf_op jit(solution)/shard_map/attention_forward/pallas_call | solution.py:214
  35.8 11.2 %collective-permute-done.3.x_far = bf16[512,1024]{1,0:T(8,128)(2,1)} collective-permute-done((bf16[512,1024]{1,0:T(8,128)(2,1)}, bf16[512,1024]{1,0:T(8,128)(2,1)}, u32[]{:S(2)}, u32[]{:S(2)}) %collective-permute-start.3) | collective-permute-done | bytes 1048608 | tf_op jit(solution)/shard_map/ppermute | solution.py:18
  46.9 1.7 convolution_convert_fusion
  51.6 1.6 convert_add_fusion.3
  53.3 1.6 collective-permute-start.5
  60.2 3.4 %fusion.76 = f32[512,1408]{1,0:T(8,128)S(1)} fusion(bf16[512,2048]{1,0:T(8,128)(2,1)S(1)} %pad_maximum_fusion.source.x, bf16[1408,2048]{1,0:T(8,128)(2,1)S(1)} %bitcast.68), kind=kOutput, calls=%fused_computation.187 | convolution fusion | flops 2952790016 | bytes 10747904 | tf_op jit(solution)/shard_map/dot_general | solution.py:22
  63.6 3.8 %collective-permute-done.5 = bf16[128,2048]{1,0:T(8,128)(2,1)S(1)} collective-permute-done((bf16[128,2048]{1,0:T(8,128)(2,1)S(1)}, bf16[128,2048]{1,0:T(8,128)(2,1)S(1)}, u32[]{:S(2)}, u32[]{:S(2)}) %collective-permute-start.5) | collective-permute-done | bytes 524320 | tf_op jit(solution)/shard_map/ppermute | solution.py:18
  68.9 1.6 collective-permute-start.7
  72.4 9.7 %collective-permute-done.7 = bf16[128,2048]{1,0:T(8,128)(2,1)S(1)} collective-permute-done((bf16[128,2048]{1,0:T(8,128)(2,1)S(1)}, bf16[128,2048]{1,0:T(8,128)(2,1)S(1)}, u32[]{:S(2)}, u32[]{:S(2)}) %collective-permute-start.7) | collective-permute-done | bytes 524320 | tf_op jit(solution)/shard_map/ppermute | solution.py:18
  83.3 1.6 collective-permute-start.10
  85.2 5.0 %fusion.77 = f32[512,1408]{1,0:T(8,128)} fusion(bf16[512,2048]{1,0:T(8,128)(2,1)S(1)} %constant_dynamic-update-slice_fusion.2.x, bf16[2048,1408]{1,0:T(8,128)(2,1)S(1)} %bitcast.89), kind=kOutput, calls=%fused_computation.188 | convolution fusion | flops 2952790016 | bytes 10747904 | tf_op jit(solution)/shard_map/dot_general | solution.py:22
  90.1 8.9 %multiply_convert_fusion.1 = (bf16[512,1408]{1,0:T(8,128)(2,1)S(1)}, bf16[512,1408]{1,0:T(8,128)(2,1)}, bf16[512,1408]{1,0:T(8,128)(2,1)}) fusion(f32[512,1408]{1,0:T(8,128)S(1)} %fusion.76, f32[512,1408]{1,0:T(8,128)} %fusion.77, bf16[512,2048]{1,0:T(8,128)(2,1)S(1)} %constant_dynamic-update-slice_fusion.2.x, bf16[2048,1408]{1,0:T(8,128)(2,1)} %param.20), kind=kOutput, calls=%fused_computation.6 | convolution fusion | flops 2963603456 | bytes 17956864 | tf_op jit(solution)/shard_map/dot_general | solution.py:22
  101.1 3.0 fusion.23
  105.0 4.5 %fusion.4 = bf16[256,2048]{1,0:T(8,128)(2,1)S(1)} fusion(f32[256,2048]{1,0:T(8,128)S(1)} %fusion.23, bf16[2048,1408]{1,0:T(8,128)(2,1)} %param.20, bf16[512,1408]{1,0:T(8,128)(2,1)S(1)} %get-tuple-element.81.g), kind=kOutput, calls=%fused_computation.14 | convolution fusion | flops 1477443584 | bytes 9633792 | tf_op jit(solution)/shard_map/dot_general | solution.py:22
  109.6 2.9 fusion.21
  113.1 2.0 collective-permute-start.17
  115.2 4.5 %convolution_add_fusion.2 = f32[256,2048]{1,0:T(8,128)S(1)} fusion(f32[256,2048]{1,0:T(8,128)S(1)} %fusion.21, bf16[2048,1408]{1,0:T(8,128)(2,1)} %param.20, bf16[512,1408]{1,0:T(8,128)(2,1)S(1)} %get-tuple-element.81.g), kind=kOutput, calls=%fused_computation.12 | convolution fusion | flops 1476919296 | bytes 10682368 | tf_op jit(solution)/shard_map/dot_general | solution.py:22
  121.8 7.0 %row_terms.1 = (bf16[256,2048]{1,0:T(8,128)(2,1)S(1)}, f32[256,2048]{1,0:T(8,128)S(1)}) custom-call(bf16[512,1408]{1,0:T(8,128)(2,1)} %get-tuple-element.119.left.g, bf16[1408,2048]{1,0:T(8,128)(2,1)S(1)} %bitcast.68), custom_call_target="tpu_custom_call" | custom-call | flops 11811160064 | bytes 5767168 | tf_op jit(solution)/shard_map/row_terms/pallas_call | solution.py:385
  129.0 4.9 %collective-permute-done.12 = bf16[128,2048]{1,0:T(8,128)(2,1)S(1)} collective-permute-done((bf16[128,2048]{1,0:T(8,128)(2,1)S(1)}, bf16[128,2048]{1,0:T(8,128)(2,1)S(1)}, u32[]{:S(2)}, u32[]{:S(2)}) %collective-permute-start.12) | collective-permute-done | bytes 524320 | tf_op jit(solution)/shard_map/ppermute | solution.py:18
  134.3 1.6 fusion.69
  137.4 6.3 %weight_terms.13 = bf16[1024,1408]{1,0:T(8,128)(2,1)} custom-call(s32[8]{0:T(128)S(1)} %stack.179.places, bf16[512,2048]{1,0:T(8,128)(2,1)S(1)} %constant_dynamic-update-slice_fusion.2.x, bf16[512,1024]{1,0:T(8,128)(2,1)S(1)} %constant_dynamic-update-slice_fusion.4.x_far, bf16[512,1408]{1,0:T(8,128)(2,1)S(1)} %get-tuple-element.81.g, ...), custom_call_target="tpu_custom_call" | custom-call | flops 17716740096 | bytes 2883584 | tf_op jit(solution)/shard_map/weight_terms/pallas_call | solution.py:325
  144.9 4.1 %collective-permute-done.16 = bf16[128,2048]{1,0:T(8,128)(2,1)} collective-permute-done((bf16[128,2048]{1,0:T(8,128)(2,1)}, bf16[128,2048]{1,0:T(8,128)(2,1)}, u32[]{:S(2)}, u32[]{:S(2)}) %collective-permute-start.16) | collective-permute-done | bytes 524320 | tf_op jit(solution)/shard_map/ppermute | solution.py:18
  150.3 2.1 pick_columns.7
  152.4 4.5 %weight_terms.14 = bf16[512,1408]{1,0:T(8,128)(2,1)S(1)} custom-call(s32[4]{0:T(128)S(1)} %pad_add_fusion.3.places, bf16[512,2048]{1,0:T(8,128)(2,1)S(1)} %copy-done.7, bf16[512,1024]{1,0:T(8,128)(2,1)S(1)} %copy-done.29, bf16[512,1408]{1,0:T(8,128)(2,1)} %get-tuple-element.119.left.g, bf16[512,1408]{1,0:T(8,128)(2,1)} %collective-permute-done.17.g_far), custom_call_target="tpu_custom_call" | custom-call | flops 8858370048 | bytes 2883584 | tf_op jit(solution)/shard_map/weight_terms/pallas_call | solution.py:325
  159.6 2.2 fusion.9.do_in
  161.8 8.7 %attention_backward.1 = (bf16[512,512]{1,0:T(8,128)(2,1)S(1)}, f32[128,512]{1,0:T(8,128)S(1)}, bf16[128,512]{1,0:T(8,128)(2,1)S(1)}, bf16[128,512]{1,0:T(8,128)(2,1)S(1)}, bf16[128,512]{1,0:T(8,128)(2,1)S(1)}) custom-call(s32[2]{0:T(128)S(1)} %copy-done.39, s32[1,512]{1,0:T(1,128)S(1)} %bitcast.66, bf16[512,512]{1,0:T(8,128)(2,1)} %bitcast.64, ...), custom_call_target="tpu_custom_call" | custom-call | flops 25769803776 | bytes 2621440 | tf_op jit(solution)/shard_map/attention_backward/pallas_call | solution.py:249
  170.8 6.8 %collective-permute-start.22 = (bf16[128,512]{1,0:T(8,128)(2,1)S(1)}, bf16[128,512]{1,0:T(8,128)(2,1)S(1)}, u32[]{:S(2)}, u32[]{:S(2)}) collective-permute-start(bf16[128,512]{1,0:T(8,128)(2,1)S(1)} %get-tuple-element.102), channel_id=1, source_target_pairs={{0,4},{4,0},{8,12},{12,8},{16,20},{20,16},{24,28},{28,24},{1,5},{5... | collective-permute-start | bytes 393224 | tf_op jit(solution)/shard_map/ppermute | solution.py:18
  177.6 12.9 %collective-permute-start.23 = (bf16[128,512]{1,0:T(8,128)(2,1)S(1)}, bf16[128,512]{1,0:T(8,128)(2,1)S(1)}, u32[]{:S(2)}, u32[]{:S(2)}) collective-permute-start(bf16[128,512]{1,0:T(8,128)(2,1)S(1)} %get-tuple-element.103), channel_id=1, source_target_pairs={{0,8},{4,12},{8,0},{12,4},{16,24},{20,28},{24,16},{28,20},{1,9},{5... | collective-permute-start | bytes 393224 | tf_op jit(solution)/shard_map/ppermute | solution.py:18
  190.6 3.4 weight_terms.16
  194.0 1.6 collective-permute-start.19
  196.7 2.5 collective-permute-start.27
  199.3 4.7 %weight_terms.15 = bf16[512,1408]{1,0:T(8,128)(2,1)S(1)} custom-call(s32[4]{0:T(128)S(1)} %pad_add_fusion.4.places, bf16[512,2048]{1,0:T(8,128)(2,1)S(1)} %copy-done.13, bf16[512,1024]{1,0:T(8,128)(2,1)S(1)} %constant_dynamic-update-slice_fusion.4.x_far, bf16[512,1408]{1,0:T(8,128)(2,1)} %get-tuple-element.110.g, bf16[512,1408]{1,0:T(8,128)(2,1)} %collective-permute-done.20.g_far), custom_call_target="tpu_custom_call" | custom-call | flops 8858370048 | bytes 2883584 | tf_op jit(solution)/shard_map/weight_terms/pallas_call | solution.py:325
  204.0 3.8 %collective-permute-done.24 = bf16[128,512]{1,0:T(8,128)(2,1)S(1)} collective-permute-done((bf16[128,512]{1,0:T(8,128)(2,1)S(1)}, bf16[128,512]{1,0:T(8,128)(2,1)S(1)}, u32[]{:S(2)}, u32[]{:S(2)}) %collective-permute-start.24) | collective-permute-done | bytes 131104 | tf_op jit(solution)/shard_map/ppermute | solution.py:18
  217.5 2.3 collective-permute-start.26
  219.9 3.4 weight_terms.17
  224.3 2.5 convert_element_type.196
  226.7 5.4 %collective-permute-done.26 = bf16[128,2048]{1,0:T(8,128)(2,1)} collective-permute-done((bf16[128,2048]{1,0:T(8,128)(2,1)}, bf16[128,2048]{1,0:T(8,128)(2,1)}, u32[]{:S(2)}, u32[]{:S(2)}) %collective-permute-start.26) | collective-permute-done | bytes 524320 | tf_op jit(solution)/shard_map/ppermute | solution.py:18
  232.2 1.7 fusion.17
  234.0 2.6 fusion.14
  236.5 3.4 weight_terms.18
  239.9 1.8 collective-permute-done.28
  241.7 2.2 add_convert_fusion
  244.6 2.2 collective-permute-start.40
  248.3 1.6 copy-done.4
  249.9 3.0 weight_terms.19
  254.6 9.3 %collective-permute-done.31 = f32[2,1024]{1,0:T(2,128)S(1)} collective-permute-done((f32[2,1024]{1,0:T(2,128)S(1)}, f32[2,1024]{1,0:T(2,128)S(1)}, u32[]{:S(2)}, u32[]{:S(2)}) %collective-permute-start.31) | collective-permute-done | bytes 8224 | tf_op jit(solution)/shard_map/ppermute | solution.py:18
  264.0 1.9 weight_terms.20
  266.0 2.6 collective-permute-start.37
  271.1 2.3 weight_terms.21
  275.1 2.6 weight_terms.23
  278.4 3.4 weight_terms.25
  281.8 10.4 %collective-permute-done.37 = bf16[272,1152]{1,0:T(8,128)(2,1)S(1)} collective-permute-done((bf16[272,1152]{1,0:T(8,128)(2,1)S(1)}, bf16[272,1152]{1,0:T(8,128)(2,1)S(1)}, u32[]{:S(2)}, u32[]{:S(2)}) %collective-permute-start.37) | collective-permute-done | bytes 626720 | tf_op jit(solution)/shard_map/ppermute | solution.py:18
  293.3 2.5 add_bitcast_fusion
  295.8 3.0 copy.27
  298.8 2.2 collective-permute-start.39
  301.0 5.4 %collective-permute-done.35 = bf16[272,1152]{1,0:T(8,128)(2,1)} collective-permute-done((bf16[272,1152]{1,0:T(8,128)(2,1)}, bf16[272,1152]{1,0:T(8,128)(2,1)}, u32[]{:S(2)}, u32[]{:S(2)}) %collective-permute-start.35) | collective-permute-done | bytes 626720 | tf_op jit(solution)/shard_map/ppermute | solution.py:18
  306.4 17.1 %collective-permute-done.38 = bf16[272,1152]{1,0:T(8,128)(2,1)} collective-permute-done((bf16[272,1152]{1,0:T(8,128)(2,1)}, bf16[272,1152]{1,0:T(8,128)(2,1)}, u32[]{:S(2)}, u32[]{:S(2)}) %collective-permute-start.38) | collective-permute-done | bytes 626720 | tf_op jit(solution)/shard_map/ppermute | solution.py:18
  331.7 2.9 collective-permute-done.39
  334.6 2.7 convert_add_fusion.5
  (296 shorter events, 65.4 us)
Async XLA Ops:
  7.2 39.8 %copy-start = (bf16[512,2048]{1,0:T(8,128)(2,1)S(1)}, bf16[512,2048]{1,0:T(8,128)(2,1)}, u32[]{:S(2)}) copy-start(bf16[512,2048]{1,0:T(8,128)(2,1)} %param.18) | copy-start | bytes 6291460
  7.2 217.1 %reduce-scatter.2.cloned.1.call-start = ((), (), s32[]{:S(2)}) async-start(), calls=%async_computation.1 | async-start | bytes 3604480 | tf_op jit(solution)/shard_map/reduce_scatter | solution.py:303
  7.3 16.9 %copy-start.63 = (f32[32]{0:T(128)}, f32[32]{0:T(128)S(1)}, u32[]{:S(2)}) copy-start(f32[32]{0:T(128)S(1)} %multiply_exponential_fusion) | copy-start | bytes 388
  13.1 11.0 %copy-start.61 = (f32[512]{0:T(512)}, f32[512]{0:T(512)S(1)}, u32[]{:S(2)}) copy-start(f32[512]{0:T(512)S(1)} %convert_element_type.168) | copy-start | bytes 6148
  13.5 13.5 %copy-start.26 = (bf16[128,512]{1,0:T(8,128)(2,1)}, bf16[128,512]{1,0:T(8,128)(2,1)S(1)}, u32[]{:S(2)}) copy-start(bf16[128,512]{1,0:T(8,128)(2,1)S(1)} %pad_maximum_fusion.8.kv0) | copy-start | bytes 393220
  13.5 12.7 %collective-permute-start.2 = (bf16[128,512]{1,0:T(8,128)(2,1)S(1)}, bf16[128,512]{1,0:T(8,128)(2,1)S(1)}, u32[]{:S(2)}, u32[]{:S(2)}) collective-permute-start(bf16[128,512]{1,0:T(8,128)(2,1)S(1)} %pad_maximum_fusion.8.kv0), channel_id=1, source_target_pairs={{0,12},{4,8},{8,4},{12,0},{16,28},{20,24},{24,20},{28,16},{1,13},{... | collective-permute-start | bytes 393224 | tf_op jit(solution)/shard_map/ppermute | solution.py:18
  17.5 8.7 %collective-permute-start.1 = (bf16[128,512]{1,0:T(8,128)(2,1)S(1)}, bf16[128,512]{1,0:T(8,128)(2,1)S(1)}, u32[]{:S(2)}, u32[]{:S(2)}) collective-permute-start(bf16[128,512]{1,0:T(8,128)(2,1)S(1)} %pad_maximum_fusion.8.kv0), channel_id=1, source_target_pairs={{0,8},{4,12},{8,0},{12,4},{16,24},{20,28},{24,16},{28,20},{1,9},{5... | collective-permute-start | bytes 393224 | tf_op jit(solution)/shard_map/ppermute | solution.py:18
  18.0 8.2 %collective-permute-start = (bf16[128,512]{1,0:T(8,128)(2,1)S(1)}, bf16[128,512]{1,0:T(8,128)(2,1)S(1)}, u32[]{:S(2)}, u32[]{:S(2)}) collective-permute-start(bf16[128,512]{1,0:T(8,128)(2,1)S(1)} %pad_maximum_fusion.8.kv0), channel_id=1, source_target_pairs={{0,4},{4,0},{8,12},{12,8},{16,20},{20,16},{24,28},{28,24},{1,5},{5... | collective-permute-start | bytes 393224 | tf_op jit(solution)/shard_map/ppermute | solution.py:18
  22.3 24.7 %collective-permute-start.3 = (bf16[512,1024]{1,0:T(8,128)(2,1)}, bf16[512,1024]{1,0:T(8,128)(2,1)}, u32[]{:S(2)}, u32[]{:S(2)}) collective-permute-start(bf16[512,1024]{1,0:T(8,128)(2,1)} %pick_columns.4), channel_id=1, source_target_pairs={{0,4},{4,0},{8,12},{12,8},{16,20},{20,16},{24,28},{28,24},{1,5},{5... | collective-permute-start | bytes 3145736 | tf_op jit(solution)/shard_map/ppermute | solution.py:18
  35.8 19.2 %copy-start.17 = (bf16[512,512]{1,0:T(8,128)(2,1)}, bf16[512,512]{1,0:T(8,128)(2,1)S(1)}, u32[]{:S(2)}) copy-start(bf16[512,512]{1,0:T(8,128)(2,1)S(1)} %get-tuple-element.118.o_in.g) | copy-start | bytes 1572868
  48.6 3.0 collective-permute-start.4
  53.3 14.0 %collective-permute-start.5 = (bf16[128,2048]{1,0:T(8,128)(2,1)S(1)}, bf16[128,2048]{1,0:T(8,128)(2,1)S(1)}, u32[]{:S(2)}, u32[]{:S(2)}) collective-permute-start(bf16[128,2048]{1,0:T(8,128)(2,1)S(1)} %slice.333), channel_id=1, source_target_pairs={{0,2},{1,3},{2,0},{3,1},{4,6},{5,7},{6,4},{7,5},{8,10},{9,11},{10,... | collective-permute-start | bytes 1572872 | tf_op jit(solution)/shard_map/ppermute | solution.py:18
  55.0 17.4 %collective-permute-start.6 = (bf16[512,512]{1,0:T(8,128)(2,1)S(1)}, bf16[512,512]{1,0:T(8,128)(2,1)S(1)}, u32[]{:S(2)}, u32[]{:S(2)}) collective-permute-start(bf16[512,512]{1,0:T(8,128)(2,1)S(1)} %get-tuple-element.118.o_in.g), channel_id=1, source_target_pairs={{0,4},{4,0},{8,12},{12,8},{16,20},{20,16},{24,28},{28,24},{1,5},{5... | collective-permute-start | bytes 1572872 | tf_op jit(solution)/shard_map/ppermute | solution.py:18
  68.7 65.6 %copy-start.41 = (f32[128,2048]{1,0:T(8,128)}, f32[128,2048]{1,0:T(8,128)S(1)}, u32[]{:S(2)}) copy-start(f32[128,2048]{1,0:T(8,128)S(1)} %get-tuple-element.147) | copy-start | bytes 3145732
  68.9 13.2 %collective-permute-start.7 = (bf16[128,2048]{1,0:T(8,128)(2,1)S(1)}, bf16[128,2048]{1,0:T(8,128)(2,1)S(1)}, u32[]{:S(2)}, u32[]{:S(2)}) collective-permute-start(bf16[128,2048]{1,0:T(8,128)(2,1)S(1)} %multiply_convert_fusion.3), channel_id=1, source_target_pairs={{0,2},{1,3},{2,0},{3,1},{4,6},{5,7},{6,4},{7,5},{8,10},{9,11},{10,... | collective-permute-start | bytes 1572872 | tf_op jit(solution)/shard_map/ppermute | solution.py:18
  70.8 33.3 %collective-permute-start.9 = (bf16[512,1024]{1,0:T(8,128)(2,1)S(1)}, bf16[512,1024]{1,0:T(8,128)(2,1)S(1)}, u32[]{:S(2)}, u32[]{:S(2)}) collective-permute-start(bf16[512,1024]{1,0:T(8,128)(2,1)S(1)} %pick_columns.5), channel_id=1, source_target_pairs={{0,8},{4,12},{8,0},{12,4},{16,24},{20,28},{24,16},{28,20},{1,9},{5... | collective-permute-start | bytes 3145736 | tf_op jit(solution)/shard_map/ppermute | solution.py:18
  72.4 10.9 %copy-start.32 = (bf16[512,512]{1,0:T(8,128)(2,1)}, bf16[512,512]{1,0:T(8,128)(2,1)S(1)}, u32[]{:S(2)}) copy-start(bf16[512,512]{1,0:T(8,128)(2,1)S(1)} %collective-permute-done.6.g_far) | copy-start | bytes 1572868
  82.2 2.8 collective-permute-start.8
  83.3 21.7 %collective-permute-start.10 = (bf16[256,1024]{1,0:T(8,128)(2,1)S(1)}, bf16[256,1024]{1,0:T(8,128)(2,1)S(1)}, u32[]{:S(2)}, u32[]{:S(2)}) collective-permute-start(bf16[256,1024]{1,0:T(8,128)(2,1)S(1)} %pick_columns.6), channel_id=1, source_target_pairs={{0,4},{4,0},{8,12},{12,8},{16,20},{20,16},{24,28},{28,24},{1,5},{5... | collective-permute-start | bytes 1572872 | tf_op jit(solution)/shard_map/ppermute | solution.py:18
  85.2 52.2 %copy-start.12 = (bf16[512,2048]{1,0:T(8,128)(2,1)}, bf16[512,2048]{1,0:T(8,128)(2,1)S(1)}, u32[]{:S(2)}) copy-start(bf16[512,2048]{1,0:T(8,128)(2,1)S(1)} %constant_dynamic-update-slice_fusion.2.x) | copy-start | bytes 6291460
  99.1 38.3 %collective-permute-start.15 = (bf16[512,1408]{1,0:T(8,128)(2,1)S(1)}, bf16[512,1408]{1,0:T(8,128)(2,1)S(1)}, u32[]{:S(2)}, u32[]{:S(2)}) collective-permute-start(bf16[512,1408]{1,0:T(8,128)(2,1)S(1)} %get-tuple-element.81.g), channel_id=1, source_target_pairs={{0,4},{4,0},{8,12},{12,8},{16,20},{20,16},{24,28},{28,24},{1,5},{5... | collective-permute-start | bytes 4325384 | tf_op jit(solution)/shard_map/ppermute | solution.py:18
  100.5 96.2 %collective-permute-start.20 = (bf16[512,1408]{1,0:T(8,128)(2,1)}, bf16[512,1408]{1,0:T(8,128)(2,1)}, u32[]{:S(2)}, u32[]{:S(2)}) collective-permute-start(bf16[512,1408]{1,0:T(8,128)(2,1)} %get-tuple-element.110.g), channel_id=1, source_target_pairs={{0,4},{4,0},{8,12},{12,8},{16,20},{20,16},{24,28},{28,24},{1,5},{5... | collective-permute-start | bytes 4325384 | tf_op jit(solution)/shard_map/ppermute | solution.py:18
  109.6 10.2 %collective-permute-start.11 = (bf16[256,2048]{1,0:T(8,128)(2,1)S(1)}, bf16[256,2048]{1,0:T(8,128)(2,1)S(1)}, u32[]{:S(2)}, u32[]{:S(2)}) collective-permute-start(bf16[256,2048]{1,0:T(8,128)(2,1)S(1)} %fusion.4), channel_id=1, source_target_pairs={{0,1},{1,0},{2,3},{3,2},{4,5},{5,4},{6,7},{7,6},{8,9},{9,8},{10,11... | collective-permute-start | bytes 3145736 | tf_op jit(solution)/shard_map/ppermute | solution.py:18
  112.6 7.1 %collective-permute-start.14 = (bf16[256,1024]{1,0:T(8,128)(2,1)S(1)}, bf16[256,1024]{1,0:T(8,128)(2,1)S(1)}, u32[]{:S(2)}, u32[]{:S(2)}) collective-permute-start(bf16[256,1024]{1,0:T(8,128)(2,1)S(1)} %collective-permute-done.10), channel_id=1, source_target_pairs={{0,1},{1,0},{2,3},{3,2},{4,5},{5,4},{6,7},{7,6},{8,9},{9,8},{10,11... | collective-permute-start | bytes 1572872 | tf_op jit(solution)/shard_map/ppermute | solution.py:18
  113.1 39.3 %collective-permute-start.17 = (bf16[512,1408]{1,0:T(8,128)(2,1)}, bf16[512,1408]{1,0:T(8,128)(2,1)}, u32[]{:S(2)}, u32[]{:S(2)}) collective-permute-start(bf16[512,1408]{1,0:T(8,128)(2,1)} %get-tuple-element.119.left.g), channel_id=1, source_target_pairs={{0,8},{4,12},{8,0},{12,4},{16,24},{20,28},{24,16},{28,20},{1,9},{5... | collective-permute-start | bytes 4325384 | tf_op jit(solution)/shard_map/ppermute | solution.py:18
  119.7 79.5 %copy-start.23 = (bf16[512,1024]{1,0:T(8,128)(2,1)}, bf16[512,1024]{1,0:T(8,128)(2,1)S(1)}, u32[]{:S(2)}) copy-start(bf16[512,1024]{1,0:T(8,128)(2,1)S(1)} %constant_dynamic-update-slice_fusion.4.x_far) | copy-start | bytes 3145732
  120.2 13.7 %collective-permute-start.12 = (bf16[128,2048]{1,0:T(8,128)(2,1)S(1)}, bf16[128,2048]{1,0:T(8,128)(2,1)S(1)}, u32[]{:S(2)}, u32[]{:S(2)}) collective-permute-start(bf16[128,2048]{1,0:T(8,128)(2,1)S(1)} %slice.332), channel_id=1, source_target_pairs={{0,2},{1,3},{2,0},{3,1},{4,6},{5,7},{6,4},{7,5},{8,10},{9,11},{10,... | collective-permute-start | bytes 1572872 | tf_op jit(solution)/shard_map/ppermute | solution.py:18
  135.9 13.2 %collective-permute-start.16 = (bf16[128,2048]{1,0:T(8,128)(2,1)}, bf16[128,2048]{1,0:T(8,128)(2,1)}, u32[]{:S(2)}, u32[]{:S(2)}) collective-permute-start(bf16[128,2048]{1,0:T(8,128)(2,1)} %get-tuple-element.91), channel_id=1, source_target_pairs={{0,2},{1,3},{2,0},{3,1},{4,6},{5,7},{6,4},{7,5},{8,10},{9,11},{10,... | collective-permute-start | bytes 1572872 | tf_op jit(solution)/shard_map/ppermute | solution.py:18
  143.8 26.8 %collective-permute-start.13 = (bf16[256,2048]{1,0:T(8,128)(2,1)}, bf16[256,2048]{1,0:T(8,128)(2,1)S(1)}, u32[]{:S(2)}, u32[]{:S(2)}) collective-permute-start(bf16[256,2048]{1,0:T(8,128)(2,1)} %copy-done.31), channel_id=1, source_target_pairs={{0,1},{1,0},{2,3},{3,2},{4,5},{5,4},{6,7},{7,6},{8,9},{9,8},{10,11... | collective-permute-start | bytes 3145736 | tf_op jit(solution)/shard_map/ppermute | solution.py:18
  150.2 9.2 %collective-permute-start.18 = (bf16[256,2048]{1,0:T(8,128)(2,1)S(1)}, bf16[256,2048]{1,0:T(8,128)(2,1)S(1)}, u32[]{:S(2)}, u32[]{:S(2)}) collective-permute-start(bf16[256,2048]{1,0:T(8,128)(2,1)S(1)} %constant_dynamic-update-slice_fusion.6.source), channel_id=1, source_target_pairs={{0,1},{1,0},{2,3},{3,2},{4,5},{5,4},{6,7},{7,6},{8,9},{9,8},{10,11... | collective-permute-start | bytes 3145736 | tf_op jit(solution)/shard_map/ppermute | solution.py:18
  157.9 36.1 %collective-permute-start.21 = (bf16[256,1408]{1,0:T(8,128)(2,1)S(1)}, bf16[256,1408]{1,0:T(8,128)(2,1)S(1)}, u32[]{:S(2)}, u32[]{:S(2)}) collective-permute-start(bf16[256,1408]{1,0:T(8,128)(2,1)S(1)} %get-tuple-element.158), channel_id=1, source_target_pairs={{0,4},{4,0},{8,12},{12,8},{16,20},{20,16},{24,28},{28,24},{1,5},{5... | collective-permute-start | bytes 2162696 | tf_op jit(solution)/shard_map/ppermute | solution.py:18
  161.8 8.8 %copy-start.10 = (f32[256,2048]{1,0:T(8,128)S(1)}, f32[256,2048]{1,0:T(8,128)}, u32[]{:S(2)}) copy-start(f32[256,2048]{1,0:T(8,128)} %copy-done.9) | copy-start | bytes 6291460
  170.8 33.2 %collective-permute-start.22 = (bf16[128,512]{1,0:T(8,128)(2,1)S(1)}, bf16[128,512]{1,0:T(8,128)(2,1)S(1)}, u32[]{:S(2)}, u32[]{:S(2)}) collective-permute-start(bf16[128,512]{1,0:T(8,128)(2,1)S(1)} %get-tuple-element.102), channel_id=1, source_target_pairs={{0,4},{4,0},{8,12},{12,8},{16,20},{20,16},{24,28},{28,24},{1,5},{5... | collective-permute-start | bytes 393224 | tf_op jit(solution)/shard_map/ppermute | solution.py:18
  177.6 26.4 %collective-permute-start.23 = (bf16[128,512]{1,0:T(8,128)(2,1)S(1)}, bf16[128,512]{1,0:T(8,128)(2,1)S(1)}, u32[]{:S(2)}, u32[]{:S(2)}) collective-permute-start(bf16[128,512]{1,0:T(8,128)(2,1)S(1)} %get-tuple-element.103), channel_id=1, source_target_pairs={{0,8},{4,12},{8,0},{12,4},{16,24},{20,28},{24,16},{28,20},{1,9},{5... | collective-permute-start | bytes 393224 | tf_op jit(solution)/shard_map/ppermute | solution.py:18
  190.5 17.2 %collective-permute-start.24 = (bf16[128,512]{1,0:T(8,128)(2,1)S(1)}, bf16[128,512]{1,0:T(8,128)(2,1)S(1)}, u32[]{:S(2)}, u32[]{:S(2)}) collective-permute-start(bf16[128,512]{1,0:T(8,128)(2,1)S(1)} %get-tuple-element.104), channel_id=1, source_target_pairs={{0,12},{4,8},{8,4},{12,0},{16,28},{20,24},{24,20},{28,16},{1,13},{... | collective-permute-start | bytes 393224 | tf_op jit(solution)/shard_map/ppermute | solution.py:18
  194.0 23.5 %collective-permute-start.19 = (bf16[128,2048]{1,0:T(8,128)(2,1)S(1)}, bf16[128,2048]{1,0:T(8,128)(2,1)S(1)}, u32[]{:S(2)}, u32[]{:S(2)}) collective-permute-start(bf16[128,2048]{1,0:T(8,128)(2,1)S(1)} %slice.331), channel_id=1, source_target_pairs={{0,2},{1,3},{2,0},{3,1},{4,6},{5,7},{6,4},{7,5},{8,10},{9,11},{10,... | collective-permute-start | bytes 1572872 | tf_op jit(solution)/shard_map/ppermute | solution.py:18
  196.7 11.2 %copy-start.62 = (f32[512]{0:T(512)S(1)}, f32[512]{0:T(512)}, u32[]{:S(2)}) copy-start(f32[512]{0:T(512)} %copy-done.61) | copy-start | bytes 6148
  196.7 11.2 %copy-start.64 = (f32[32]{0:T(128)S(1)}, f32[32]{0:T(128)}, u32[]{:S(2)}) copy-start(f32[32]{0:T(128)} %copy-done.63) | copy-start | bytes 388
  196.7 47.2 %collective-permute-start.27 = (bf16[256,1408]{1,0:T(8,128)(2,1)}, bf16[256,1408]{1,0:T(8,128)(2,1)}, u32[]{:S(2)}, u32[]{:S(2)}) collective-permute-start(bf16[256,1408]{1,0:T(8,128)(2,1)} %add_convert_fusion.1), channel_id=1, source_target_pairs={{0,16},{4,20},{8,24},{12,28},{16,0},{20,4},{24,8},{28,12},{1,17},{... | collective-permute-start | bytes 2162696 | tf_op jit(solution)/shard_map/ppermute | solution.py:18
  210.7 3.8 %collective-permute-start.25 = (bf16[256,2048]{1,0:T(8,128)(2,1)S(1)}, bf16[256,2048]{1,0:T(8,128)(2,1)S(1)}, u32[]{:S(2)}, u32[]{:S(2)}) collective-permute-start(bf16[256,2048]{1,0:T(8,128)(2,1)S(1)} %fusion.5), channel_id=1, source_target_pairs={{0,1},{1,0},{2,3},{3,2},{4,5},{5,4},{6,7},{7,6},{8,9},{9,8},{10,11... | collective-permute-start | bytes 3145736 | tf_op jit(solution)/shard_map/ppermute | solution.py:18
  212.0 29.7 %collective-permute-start.28 = (bf16[256,1408]{1,0:T(8,128)(2,1)}, bf16[256,1408]{1,0:T(8,128)(2,1)}, u32[]{:S(2)}, u32[]{:S(2)}) collective-permute-start(bf16[256,1408]{1,0:T(8,128)(2,1)} %get-tuple-element.156), channel_id=1, source_target_pairs={{0,8},{4,12},{8,0},{12,4},{16,24},{20,28},{24,16},{28,20},{1,9},{5... | collective-permute-start | bytes 2162696 | tf_op jit(solution)/shard_map/ppermute | solution.py:18
  212.0 36.3 %collective-permute-start.32 = (bf16[640,512]{1,0:T(8,128)(2,1)S(1)}, bf16[640,512]{1,0:T(8,128)(2,1)}, u32[]{:S(2)}, u32[]{:S(2)}) collective-permute-start(bf16[640,512]{1,0:T(8,128)(2,1)S(1)} %pad_maximum_fusion.1.g), channel_id=1, source_target_pairs={{0,4},{4,0},{8,12},{12,8},{16,20},{20,16},{24,28},{28,24},{1,5},{5... | collective-permute-start | bytes 1966088 | tf_op jit(solution)/shard_map/ppermute | solution.py:18
  214.5 29.9 %collective-permute-start.33 = (bf16[256,1024]{1,0:T(8,128)(2,1)}, bf16[256,1024]{1,0:T(8,128)(2,1)}, u32[]{:S(2)}, u32[]{:S(2)}) collective-permute-start(bf16[256,1024]{1,0:T(8,128)(2,1)} %pick_columns.7), channel_id=1, source_target_pairs={{0,4},{4,0},{8,12},{12,8},{16,20},{20,16},{24,28},{28,24},{1,5},{5... | collective-permute-start | bytes 1572872 | tf_op jit(solution)/shard_map/ppermute | solution.py:18
  217.5 14.6 %collective-permute-start.26 = (bf16[128,2048]{1,0:T(8,128)(2,1)}, bf16[128,2048]{1,0:T(8,128)(2,1)}, u32[]{:S(2)}, u32[]{:S(2)}) collective-permute-start(bf16[128,2048]{1,0:T(8,128)(2,1)} %slice.330), channel_id=1, source_target_pairs={{0,2},{1,3},{2,0},{3,1},{4,6},{5,7},{6,4},{7,5},{8,10},{9,11},{10,... | collective-permute-start | bytes 1572872 | tf_op jit(solution)/shard_map/ppermute | solution.py:18
  223.3 8.9 %copy-start.60 = (f32[2048]{0:T(1024)S(1)}, f32[2048]{0:T(1024)}, u32[]{:S(2)}) copy-start(f32[2048]{0:T(1024)} %param.14) | copy-start | bytes 24580
  223.3 8.9 %copy-start.65 = (f32[128]{0:T(128)S(1)}, f32[128]{0:T(128)}, u32[]{:S(2)}) copy-start(f32[128]{0:T(128)} %dynamic-slice.3) | copy-start | bytes 1540
  224.3 9.6 %copy-start.45 = (f32[128,2048]{1,0:T(8,128)S(1)}, f32[128,2048]{1,0:T(8,128)}, u32[]{:S(2)}) copy-start(f32[128,2048]{1,0:T(8,128)} %slice.238) | copy-start | bytes 3145732
  224.3 9.6 %copy-start.50 = (f32[128,2048]{1,0:T(8,128)S(1)}, f32[128,2048]{1,0:T(8,128)}, u32[]{:S(2)}) copy-start(f32[128,2048]{1,0:T(8,128)} %get-tuple-element.145) | copy-start | bytes 3145732
  243.9 2.9 collective-permute-start.29
  244.1 37.7 %collective-permute-start.36 = (bf16[256,1408]{1,0:T(8,128)(2,1)}, bf16[256,1408]{1,0:T(8,128)(2,1)S(1)}, u32[]{:S(2)}, u32[]{:S(2)}) collective-permute-start(bf16[256,1408]{1,0:T(8,128)(2,1)} %add_convert_fusion), channel_id=1, source_target_pairs={{0,16},{4,20},{8,24},{12,28},{16,0},{20,4},{24,8},{28,12},{1,17},{... | collective-permute-start | bytes 2162696 | tf_op jit(solution)/shard_map/ppermute | solution.py:18
  244.4 19.5 %collective-permute-start.34 = (bf16[256,1024]{1,0:T(8,128)(2,1)}, bf16[256,1024]{1,0:T(8,128)(2,1)S(1)}, u32[]{:S(2)}, u32[]{:S(2)}) collective-permute-start(bf16[256,1024]{1,0:T(8,128)(2,1)} %collective-permute-done.33), channel_id=1, source_target_pairs={{0,1},{1,0},{2,3},{3,2},{4,5},{5,4},{6,7},{7,6},{8,9},{9,8},{10,11... | collective-permute-start | bytes 1572872 | tf_op jit(solution)/shard_map/ppermute | solution.py:18
  244.6 48.6 %collective-permute-start.40 = (bf16[256,1408]{1,0:T(8,128)(2,1)}, bf16[256,1408]{1,0:T(8,128)(2,1)S(1)}, u32[]{:S(2)}, u32[]{:S(2)}) collective-permute-start(bf16[256,1408]{1,0:T(8,128)(2,1)} %get-tuple-element.123), channel_id=1, source_target_pairs={{0,4},{4,0},{8,12},{12,8},{16,20},{20,16},{24,28},{28,24},{1,5},{5... | collective-permute-start | bytes 2162696 | tf_op jit(solution)/shard_map/ppermute | solution.py:18
  246.9 6.0 %collective-permute-start.30 = (f32[2,2048]{1,0:T(2,128)S(1)}, f32[2,2048]{1,0:T(2,128)S(1)}, u32[]{:S(2)}, u32[]{:S(2)}) collective-permute-start(f32[2,2048]{1,0:T(2,128)S(1)} %fusion.67), channel_id=1, source_target_pairs={{0,2},{1,3},{2,0},{3,1},{4,6},{5,7},{6,4},{7,5},{8,10},{9,11},{10,... | collective-permute-start | bytes 49160 | tf_op jit(solution)/shard_map/ppermute | solution.py:18
  249.9 14.1 %copy-start.18 = (bf16[512,512]{1,0:T(8,128)(2,1)S(1)}, bf16[512,512]{1,0:T(8,128)(2,1)}, u32[]{:S(2)}) copy-start(bf16[512,512]{1,0:T(8,128)(2,1)} %copy-done.17) | copy-start | bytes 1572868
  249.9 14.1 %copy-start.33 = (bf16[512,512]{1,0:T(8,128)(2,1)S(1)}, bf16[512,512]{1,0:T(8,128)(2,1)}, u32[]{:S(2)}) copy-start(bf16[512,512]{1,0:T(8,128)(2,1)} %copy-done.32) | copy-start | bytes 1572868
  252.9 11.1 %copy-start.16 = (bf16[512,2048]{1,0:T(8,128)(2,1)S(1)}, bf16[512,2048]{1,0:T(8,128)(2,1)}, u32[]{:S(2)}) copy-start(bf16[512,2048]{1,0:T(8,128)(2,1)} %copy-done.15) | copy-start | bytes 6291460
  253.0 10.9 %collective-permute-start.31 = (f32[2,1024]{1,0:T(2,128)S(1)}, f32[2,1024]{1,0:T(2,128)S(1)}, u32[]{:S(2)}, u32[]{:S(2)}) collective-permute-start(f32[2,1024]{1,0:T(2,128)S(1)} %pad_maximum_fusion.16), channel_id=1, source_target_pairs={{0,4},{4,0},{8,12},{12,8},{16,20},{20,16},{24,28},{28,24},{1,5},{5... | collective-permute-start | bytes 24584 | tf_op jit(solution)/shard_map/ppermute | solution.py:18
  266.0 26.2 %collective-permute-start.37 = (bf16[272,1152]{1,0:T(8,128)(2,1)S(1)}, bf16[272,1152]{1,0:T(8,128)(2,1)S(1)}, u32[]{:S(2)}, u32[]{:S(2)}) collective-permute-start(bf16[272,1152]{1,0:T(8,128)(2,1)S(1)} %fusion.27), channel_id=1, source_target_pairs={{0,8},{4,12},{8,0},{12,4},{16,24},{20,28},{24,16},{28,20},{1,9},{5... | collective-permute-start | bytes 1880072 | tf_op jit(solution)/shard_map/ppermute | solution.py:18
  269.5 36.9 %collective-permute-start.35 = (bf16[272,1152]{1,0:T(8,128)(2,1)}, bf16[272,1152]{1,0:T(8,128)(2,1)}, u32[]{:S(2)}, u32[]{:S(2)}) collective-permute-start(bf16[272,1152]{1,0:T(8,128)(2,1)} %fusion.28), channel_id=1, source_target_pairs={{0,8},{4,12},{8,0},{12,4},{16,24},{20,28},{24,16},{28,20},{1,9},{5... | collective-permute-start | bytes 1880072 | tf_op jit(solution)/shard_map/ppermute | solution.py:18
  281.8 11.5 %copy-start.56 = (bf16[256,1408]{1,0:T(8,128)(2,1)}, bf16[256,1408]{1,0:T(8,128)(2,1)S(1)}, u32[]{:S(2)}) copy-start(bf16[256,1408]{1,0:T(8,128)(2,1)S(1)} %collective-permute-done.36) | copy-start | bytes 2162692
  293.3 30.2 %collective-permute-start.38 = (bf16[272,1152]{1,0:T(8,128)(2,1)}, bf16[272,1152]{1,0:T(8,128)(2,1)}, u32[]{:S(2)}, u32[]{:S(2)}) collective-permute-start(bf16[272,1152]{1,0:T(8,128)(2,1)} %fusion.29), channel_id=1, source_target_pairs={{0,16},{4,20},{8,24},{12,28},{16,0},{20,4},{24,8},{28,12},{1,17},{... | collective-permute-start | bytes 1880072 | tf_op jit(solution)/shard_map/ppermute | solution.py:18
  295.8 27.7 %copy-start.20 = (bf16[256,640]{1,0:T(8,128)(2,1)S(1)}, bf16[256,640]{1,0:T(8,128)(2,1)}, u32[]{:S(2)}) copy-start(bf16[256,640]{1,0:T(8,128)(2,1)} %copy-done.19) | copy-start | bytes 983044
  295.8 27.7 %copy-start.22 = (bf16[256,512]{1,0:T(8,128)(2,1)S(1)}, bf16[256,512]{1,0:T(8,128)(2,1)}, u32[]{:S(2)}) copy-start(bf16[256,512]{1,0:T(8,128)(2,1)} %copy-done.21) | copy-start | bytes 786436
  298.8 35.8 %collective-permute-start.39 = (bf16[256,1408]{1,0:T(8,128)(2,1)}, bf16[256,1408]{1,0:T(8,128)(2,1)}, u32[]{:S(2)}, u32[]{:S(2)}) collective-permute-start(bf16[256,1408]{1,0:T(8,128)(2,1)} %get-tuple-element.121), channel_id=1, source_target_pairs={{0,8},{4,12},{8,0},{12,4},{16,24},{20,28},{24,16},{28,20},{1,9},{5... | collective-permute-start | bytes 2162696 | tf_op jit(solution)/shard_map/ppermute | solution.py:18
  (49 other events, 154.4 us)
Sparse Core Ops, SparseCore 0:
  143.9 59.7 reduce-scatter.1
